TPU v7x, 32 devices: a whole 2x2x4 slice. The times are simulated.
32 devices in a mesh: grp: 2 (over y), seq: 4 (over z), head: 4 (over x, core).
Axes of the slice: x: 2, y: 2, z: 4, core: 2. Of those that a mesh axis runs over, the one named last changes fastest.
Arguments:
- encoder: bfloat16 [8, 256, 4096], P('grp', 'seq'), parts along dimension 0, may hold values from -6 to 6
- key_weight: bfloat16 [4096, 4096], P('seq', 'head'), may hold values from -0.09375 to 0.09375
- value_weight: bfloat16 [4096, 4096], P('seq', 'head'), may hold values from -0.09375 to 0.09375
- tile_mask: int32 [2, 64, 64], P(None, 'seq', 'head'), may hold values 0 or 1
- lengths: int32 [8], P('grp'), parts along dimension 0, may hold values from 64 to 256, as said below
- queries: bfloat16 [8, 64, 4096], P('grp', 'seq', 'head'), parts along dimension 0, may hold values from -240 to 240
- cotangent: bfloat16 [8, 64, 4096], P('grp', 'seq', 'head'), parts along dimension 0, may hold values from -6 to 6
Outputs:
- attention: bfloat16 [8, 64, 4096], P('grp', 'seq', 'head'), parts along dimension 0
- query_grad: bfloat16 [8, 64, 4096], P('grp', 'seq', 'head'), parts along dimension 0
- encoder_grad: bfloat16 [8, 256, 4096], P('grp', 'seq', 'head'), parts along dimension 0
There are 2 independent parts, one for each index of `grp`. A program takes and returns all parts, laid end to end along the dimension named above; an argument that names none is the same for every part. Nothing has to cross between parts.
Inputs may be any that keep to these rules, and one draw needn't show every extreme that they name: `lengths`: one document of each group has all 256 positions valid.
All inputs are finite; a program needn't handle non-finite values. No bound on the sum of `tile_mask` on one device may be relied on, other than what follows from the above.
Results may differ from a plain program's by a relative error of at most 0.0096.
Values may be sent and summed in bfloat16 or wider, within the bound.
No kernel may reach another device: no remote copies, remote signals or barrier semaphores. Data moves between devices by JAX's collectives and lax.ppermute only.
A program may use at most 128 MiB of HBM per device.

v0:
```python
import jax
import jax.numpy as jnp
from jax import lax
from jax.sharding import PartitionSpec as P

DH = 64
TILE = 64
DOCS = 4


SCALE = 0.125
FLOOR_SCORE = -1e30


def expand(tile_grid, tile_edge):
    return jnp.repeat(jnp.repeat(tile_grid, tile_edge, axis=0), tile_edge, axis=1)


def attend(keys, values, queries, cotangent, length):
    position = jnp.arange(keys.shape[0])[None, :]
    live = position < length
    scores = jnp.dot(queries, keys.T, preferred_element_type=jnp.float32) * SCALE
    scores = jnp.where(live, scores, FLOOR_SCORE)
    row_max = jnp.max(scores, axis=1, keepdims=True)
    weights = jnp.where(live, jnp.exp(scores - row_max), 0.0)
    probs = weights / jnp.sum(weights, axis=1, keepdims=True)
    probs_low = probs.astype(jnp.bfloat16)
    output = jnp.dot(probs_low, values, preferred_element_type=jnp.float32)
    delta = jnp.sum(cotangent.astype(jnp.float32) * output, axis=1, keepdims=True)
    prob_grad = jnp.dot(cotangent, values.T, preferred_element_type=jnp.float32)
    score_grad = (probs * (prob_grad - delta) * SCALE).astype(jnp.bfloat16)
    query_grad = jnp.dot(score_grad, keys, preferred_element_type=jnp.float32)
    key_grad = jnp.dot(score_grad.T, queries, preferred_element_type=jnp.float32)
    value_grad = jnp.dot(probs_low.T, cotangent, preferred_element_type=jnp.float32)
    return (
        output.astype(jnp.bfloat16),
        query_grad.astype(jnp.bfloat16),
        key_grad.astype(jnp.bfloat16),
        value_grad.astype(jnp.bfloat16),
    )


def project(encoder, key_piece, value_piece):
    count = key_piece.shape[0]
    flat = encoder.reshape(DOCS * encoder.shape[1], count)
    key_flat = jnp.dot(flat, key_piece, preferred_element_type=jnp.float32)
    value_flat = jnp.dot(flat, value_piece, preferred_element_type=jnp.float32)
    shape_out = (DOCS, encoder.shape[1], key_piece.shape[1])
    return (key_flat.reshape(shape_out), value_flat.reshape(shape_out))


def back_product(key_rows, value_rows, key_piece, value_piece):
    contract = (((1,), (1,)), ((), ()))
    total = lax.dot_general(key_rows, key_piece, contract, preferred_element_type=jnp.float32)
    return total + lax.dot_general(
        value_rows, value_piece, contract, preferred_element_type=jnp.float32
    )


def body(encoder, key_weight, value_weight, tile_mask, lengths, queries, cotangent):
    seq_count = lax.axis_size("seq")
    enc_rows = encoder.shape[1]
    dec_rows = queries.shape[1]
    group_heads = queries.shape[2] // DH
    pair_count = DOCS * group_heads
    local_pairs = pair_count // seq_count
    key_masked = key_weight * expand(tile_mask[0], TILE).astype(jnp.bfloat16)
    value_masked = value_weight * expand(tile_mask[1], TILE).astype(jnp.bfloat16)
    full_key, full_value = (
        lax.all_gather(key_masked, "seq", axis=0, tiled=True),
        lax.all_gather(value_masked, "seq", axis=0, tiled=True),
    )
    key_sum, value_sum = project(encoder, full_key, full_value)

    def to_pairs(first, second, rows):
        joined = jnp.concatenate(
            [
                first.reshape(DOCS, rows, group_heads, DH),
                second.reshape(DOCS, rows, group_heads, DH),
            ],
            axis=3,
        )
        return joined.transpose(0, 2, 1, 3).reshape(pair_count, rows, 2 * DH)

    def from_pairs(block, rows):
        shaped = block.reshape(DOCS, group_heads, rows, 2 * DH).transpose(0, 2, 1, 3)
        first = shaped[..., :DH].reshape(DOCS, rows, group_heads * DH)
        second = shaped[..., DH:].reshape(DOCS, rows, group_heads * DH)
        return (first, second)

    query_pairs = to_pairs(queries, cotangent, dec_rows)
    query_owned = lax.all_to_all(query_pairs, "seq", split_axis=0, concat_axis=1, tiled=True)
    kv_pairs = to_pairs(key_sum.astype(jnp.bfloat16), value_sum.astype(jnp.bfloat16), enc_rows)
    kv_owned = lax.all_to_all(kv_pairs, "seq", split_axis=0, concat_axis=1, tiled=True)
    pair_ids = lax.axis_index("seq") * local_pairs + jnp.arange(local_pairs)
    doc_of_pair = pair_ids // group_heads
    pair_length = jnp.sum(
        jnp.where(doc_of_pair[:, None] == jnp.arange(DOCS)[None, :], lengths[None, :], 0), axis=1
    )

    def owner_pair(items):
        pair_kv, pair_query, length = items
        output, query_grad, key_grad, value_grad = attend(
            pair_kv[:, :DH], pair_kv[:, DH:], pair_query[:, :DH], pair_query[:, DH:], length
        )
        return (
            jnp.concatenate([output, query_grad], axis=1),
            jnp.concatenate([key_grad, value_grad], axis=1),
        )

    front, back = lax.map(owner_pair, (kv_owned, query_owned, pair_length))
    front_rows, back_rows = (
        lax.all_to_all(front, "seq", split_axis=1, concat_axis=0, tiled=True),
        lax.all_to_all(back, "seq", split_axis=1, concat_axis=0, tiled=True),
    )
    attention, query_grad = from_pairs(front_rows, dec_rows)
    key_grads, value_grads = from_pairs(back_rows, enc_rows)
    key_rows = key_grads.reshape(DOCS * enc_rows, group_heads * DH)
    value_rows = value_grads.reshape(DOCS * enc_rows, group_heads * DH)
    grad_terms = back_product(key_rows, value_rows, full_key, full_value)
    grad_share = lax.psum_scatter(grad_terms, "head", scatter_dimension=1, tiled=True)
    encoder_grad = grad_share.astype(jnp.bfloat16).reshape(DOCS, enc_rows, grad_share.shape[1])
    return (attention, query_grad, encoder_grad)


def solution(mesh):
    placed = (
        P("grp", "seq", None),
        P("seq", "head"),
        P("seq", "head"),
        P(None, "seq", "head"),
        P("grp"),
        P("grp", "seq", "head"),
        P("grp", "seq", "head"),
    )
    return jax.shard_map(
        body,
        mesh=mesh,
        in_specs=placed,
        out_specs=(P("grp", "seq", "head"), P("grp", "seq", "head"), P("grp", "seq", "head")),
        check_vma=False,
    )
```

profile of v0, /device:TPU:0, one launch (start us, length us, event | category | flops | bytes accessed | tf_op | source)
XLA Modules:
  0.0 557.6 jit_solution(13570915106982386981)
XLA Ops:
  8.4 3.9 copy.49
  12.3 3.1 bitcast_multiply_fusion.1
  15.8 3.9 copy.51
  19.7 3.1 bitcast_multiply_fusion
  25.0 6.3 %all-to-all-start = ((bf16[64,16,128]{2,1,0:T(8,128)(2,1)}), bf16[64,16,128]{2,1,0:T(8,128)(2,1)S(1)}, u32[]{:S(2)}, u32[]{:S(2)}) async-start(bf16[64,16,128]{2,1,0:T(8,128)(2,1)} %bitcast.6), calls=%async_computation | async-start | bytes 524288 | tf_op jit(solution)/shard_map/all_to_all | solution.py:92
  31.3 142.1 %all-gather.3.cloned.1.call-done = bf16[4096,1024]{0,1:T(8,128)(2,1)} async-done(((bf16[1024,1024]{0,1:T(8,128)(2,1)}), bf16[4096,1024]{0,1:T(8,128)(2,1)}) %all-gather.3.cloned.1.call-update) | async-done | bytes 8388624 | tf_op jit(solution)/shard_map/all_gather | solution.py:70
  173.5 5.7 %fusion.21 = bf16[256,1024]{0,1:T(8,128)(2,1)S(1)} fusion(bf16[4096,1024]{0,1:T(8,128)(2,1)} %all-gather.3.cloned.1.call-done, bf16[256,4096]{1,0:T(8,128)(2,1)S(1)} %bitcast.87), kind=kOutput, calls=%fused_computation.36 | convolution fusion | flops 2147745792 | bytes 11010048 | tf_op jit(solution)/shard_map/dot_general | solution.py:46
  179.2 143.6 %all-gather.5.cloned.1.call-done = bf16[4096,1024]{0,1:T(8,128)(2,1)} async-done(((bf16[1024,1024]{0,1:T(8,128)(2,1)}), bf16[4096,1024]{0,1:T(8,128)(2,1)}) %all-gather.5.cloned.1.call-update) | async-done | bytes 8388624 | tf_op jit(solution)/shard_map/all_gather | solution.py:71
  322.9 6.5 %fusion.22 = bf16[256,1024]{0,1:T(8,128)(2,1)} fusion(bf16[4096,1024]{0,1:T(8,128)(2,1)} %all-gather.5.cloned.1.call-done, bf16[256,4096]{1,0:T(8,128)(2,1)S(1)} %bitcast.88), kind=kOutput, calls=%fused_computation.37 | convolution fusion | flops 2147745792 | bytes 11010048 | tf_op jit(solution)/shard_map/dot_general | solution.py:47
  330.8 1.7 copy.52
  332.6 2.8 convert_element_type.79
  335.3 2.4 copy.53
  337.7 2.8 pad_maximum_fusion
  340.6 3.5 all-to-all-start.1
  345.0 25.3 %all-to-all-done.1 = bf16[64,64,128]{2,1,0:T(8,128)(2,1)S(1)} async-done(((bf16[64,64,128]{2,1,0:T(8,128)(2,1)}), bf16[64,64,128]{2,1,0:T(8,128)(2,1)S(1)}, u32[]{:S(2)}, u32[]{:S(2)}) %all-to-all-start.1) | async-done | bytes 1048608 | tf_op jit(solution)/shard_map/all_to_all | solution.py:94
  371.3 83.0 %while.12 = (s32[]{:T(128)}, bf16[16,64,128]{2,1,0:T(8,128)(2,1)S(1)}, bf16[16,256,128]{1,2,0:T(8,128)(2,1)}, s32[16]{0:T(128)S(1)}, bf16[16,64,128]{2,1,0:T(8,1...) while((s32[]{:T(128)}, bf16[16,64,128]{2,1,0:T(8,128)(2,1)S(1)}, bf16[16,256,128]{1,2,0:T(8,128)(2,1)}, ...), condition=%wide.region_5.6_spmd, body=%wide.region_1.5_spmd.sunk | while | flops 13144130 | bytes 1192309 | solution.py:111
  454.3 1.9 copy.56
  456.2 27.8 %all_to_all.60 = bf16[16,256,128]{2,0,1:T(8,128)(2,1)S(1)} all-to-all(bf16[16,256,128]{2,0,1:T(8,128)(2,1)S(1)} %copy.56), channel_id=1, replica_groups=mesh['grp'=2,'seq'=4,'head'=4] {'seq'}, dimensions={1} | all-to-all | bytes 2097152 | tf_op jit(solution)/shard_map/all_to_all | solution.py:114
  488.0 1.9 copy.58
  491.4 5.9 %fusion.27 = f32[256,4096]{1,0:T(8,128)S(1)} fusion(bf16[256,1024]{1,0:T(8,128)(2,1)} %reshape_reshape.6, bf16[4096,1024]{0,1:T(8,128)(2,1)} %all-gather.3.cloned.1.call-done), kind=kOutput, calls=%fused_computation.52 | convolution fusion | flops 2147483648 | bytes 13107200 | tf_op jit(solution)/shard_map/dot_general | solution.py:54
  497.4 7.8 %convolution_add_fusion = f32[256,4096]{1,0:T(8,128)} fusion(f32[256,4096]{1,0:T(8,128)S(1)} %fusion.27, bf16[256,1024]{1,0:T(8,128)(2,1)S(1)} %copy-done.1, bf16[4096,1024]{0,1:T(8,128)(2,1)} %all-gather.5.cloned.1.call-done), kind=kOutput, calls=%fused_computation.31 | convolution fusion | flops 2148532224 | bytes 17301504 | tf_op jit(solution)/shard_map/dot_general | solution.py:55
  505.4 10.8 %all_to_all.61 = bf16[16,64,128]{2,0,1:T(8,128)(2,1)S(1)} all-to-all(bf16[16,64,128]{2,0,1:T(8,128)(2,1)S(1)} %copy.55), channel_id=1, replica_groups=mesh['grp'=2,'seq'=4,'head'=4] {'seq'}, dimensions={1} | all-to-all | bytes 524288 | tf_op jit(solution)/shard_map/all_to_all | solution.py:113
  518.1 30.9 %reduce-scatter.2.cloned.1.call-done = f32[256,1024]{1,0:T(8,128)} async-done(((f32[256,4096]{1,0:T(8,128)}), f32[256,1024]{1,0:T(8,128)}) %reduce-scatter.2.cloned.1.call-update) | async-done | bytes 1048592 | tf_op jit(solution)/shard_map/reduce_scatter | solution.py:121
  549.0 2.1 convert_element_type.80
  (255 shorter events, 96.9 us)
Async XLA Ops:
  7.2 166.3 %copy-start = (bf16[4,64,4096]{2,1,0:T(8,128)(2,1)S(1)}, bf16[4,64,4096]{2,1,0:T(8,128)(2,1)}, u32[]{:S(2)}) copy-start(bf16[4,64,4096]{2,1,0:T(8,128)(2,1)} %param.9) | copy-start | bytes 6291460
  7.2 166.3 %all-gather.3.cloned.1.call-start = ((), (), s32[]{:S(2)}) async-start(), calls=%async_computation.5 | async-start | bytes 10485760 | tf_op jit(solution)/shard_map/all_gather | solution.py:70
  15.4 307.4 %all-gather.5.cloned.1.call-start = ((), (), s32[]{:S(2)}) async-start(), calls=%async_computation.6 | async-start | bytes 10485760 | tf_op jit(solution)/shard_map/all_gather | solution.py:71
  22.8 0.9 copy-start.3
  22.8 1.1 copy-start.4
  25.0 315.6 %all-to-all-start = ((bf16[64,16,128]{2,1,0:T(8,128)(2,1)}), bf16[64,16,128]{2,1,0:T(8,128)(2,1)S(1)}, u32[]{:S(2)}, u32[]{:S(2)}) async-start(bf16[64,16,128]{2,1,0:T(8,128)(2,1)} %bitcast.6), calls=%async_computation | async-start | bytes 524288 | tf_op jit(solution)/shard_map/all_to_all | solution.py:92
  337.7 6.4 %copy-start.5 = (s32[4]{0:T(128)S(1)}, s32[4]{0:T(128)}, u32[]{:S(2)}) copy-start(s32[4]{0:T(128)} %param.13) | copy-start | bytes 52
  340.6 29.7 %all-to-all-start.1 = ((bf16[64,64,128]{2,1,0:T(8,128)(2,1)}), bf16[64,64,128]{2,1,0:T(8,128)(2,1)S(1)}, u32[]{:S(2)}, u32[]{:S(2)}) async-start(bf16[64,64,128]{2,1,0:T(8,128)(2,1)} %bitcast.18), calls=%async_computation.1 | async-start | bytes 2097152 | tf_op jit(solution)/shard_map/all_to_all | solution.py:94
  344.1 204.9 %reduce-scatter.2.cloned.1.call-start = ((), (), s32[]{:S(2)}) async-start(), calls=%async_computation.7 | async-start | bytes 5242880 | tf_op jit(solution)/shard_map/reduce_scatter | solution.py:121
  345.0 26.3 %copy-start.2 = (bf16[16,64,128]{2,1,0:T(8,128)(2,1)S(1)}, bf16[16,64,128]{2,1,0:T(8,128)(2,1)}, u32[]{:S(2)}) copy-start(bf16[16,64,128]{2,1,0:T(8,128)(2,1)} %custom-call) | copy-start | bytes 786436
  491.4 6.0 %copy-start.1 = (bf16[256,1024]{1,0:T(8,128)(2,1)S(1)}, bf16[256,1024]{1,0:T(8,128)(2,1)}, u32[]{:S(2)}) copy-start(bf16[256,1024]{1,0:T(8,128)(2,1)} %reshape_reshape.7) | copy-start | bytes 1572868
Sparse Core Ops, SparseCore 0:
  15.5 157.8 all-gather.2
  175.1 147.7 all-gather.4
  505.4 43.5 reduce-scatter.1
where the time goes:
time: 560 us; the launch traced here: 558 us
  waiting for transfers between devices  342 us (61%)
  local copies, waits for them, and re-layouts  66.4 us (12%)
  matrix products  48.8 us (9%)
  blocking collectives  38.6 us (7%)
  other arithmetic  37.3 us (7%)
  between operations  13.9 us (2%)
  starting transfers between devices  9.98 us (2%)
    all_gather x1, waiting for transfers between devices, body(): lax.all_gather(value_masked, 'seq', axis=0, tiled=True)  144 us
    all_gather x1, waiting for transfers between devices, body(): lax.all_gather(key_masked, 'seq', axis=0, tiled=True)  142 us
    reduce_scatter x1, waiting for transfers between devices, body(): lax.psum_scatter(grad_terms, 'head', scatter_dimension=1, tiled=True)  30.9 us
    all_to_all x1, blocking collectives, body(): lax.all_to_all(back, 'seq', split_axis=1, concat_axis=0, tiled=True)  27.8 us
    all_to_all x1, waiting for transfers between devices, body(): lax.all_to_all(kv_pairs, 'seq', split_axis=0, concat_axis=1, tiled=True)  25.3 us
    squeeze x32, local copies, waits for them, and re-layouts, body(): front, back = lax.map(owner_pair, (kv_owned, query_owned, pair_length))  25.1 us
    dynamic_update_slice x32, other arithmetic, body(): front, back = lax.map(owner_pair, (kv_owned, query_owned, pair_length))  11.7 us
  transfers between devices with their start and end apart: 5, of which 4 were waited for; matrix products, arithmetic and copies ran while one was open for 6% of the time, Pallas kernels for 0%

commit v1 on v0

--- a/solution.py
+++ b/solution.py
@@ -1,6 +1,10 @@
+import functools
+
 import jax
 import jax.numpy as jnp
 from jax import lax
+from jax.experimental import pallas as pl
+from jax.experimental.pallas import tpu as pltpu
 from jax.sharding import PartitionSpec as P
 
 DH = 64
@@ -10,6 +14,9 @@
 
 SCALE = 0.125
 FLOOR_SCORE = -1e30
+
+BF = jnp.bfloat16
+F32 = jnp.float32
 
 
 def expand(tile_grid, tile_edge):
@@ -57,7 +64,7 @@
     )
 
 
-def body(encoder, key_weight, value_weight, tile_mask, lengths, queries, cotangent):
+def general_body(encoder, key_weight, value_weight, tile_mask, lengths, queries, cotangent):
     seq_count = lax.axis_size("seq")
     enc_rows = encoder.shape[1]
     dec_rows = queries.shape[1]
@@ -123,6 +130,264 @@
     return (attention, query_grad, encoder_grad)
 
 
+SEQ = 4
+RING = (0, 1, 3, 2)
+
+
+def fits(mesh, encoder, key_weight, queries):
+    return (
+        mesh.shape["seq"] == SEQ
+        and mesh.shape["head"] == 4
+        and mesh.shape["grp"] == 2
+        and encoder.shape[0] == DOCS * 2
+        and key_weight.shape[1] // 4 // SEQ == 4 * DH
+        and key_weight.shape[0] == encoder.shape[2] == 4096
+        and encoder.shape[1] == 256
+        and queries.shape[1] == 64
+    )
+
+
+def prune_kernel(place, key_ref, value_ref, mask_ref, own_ref, *message_refs):
+    rows = key_ref.shape[0]
+    half = rows // 2
+    s, g = place[0], place[1]
+
+    def write(out_ref, first_tile, tiles, column):
+        at = pl.ds(pl.multiple_of(column * 256, 256), 256)
+        for t in range(tiles):
+            tile = first_tile + t
+            row = pl.ds(pl.multiple_of(tile * TILE, TILE), TILE)
+            for side, ref in ((0, key_ref), (1, value_ref)):
+                keep = mask_ref[side, pl.ds(tile, 1), at]
+                out_ref[t * TILE : (t + 1) * TILE, side * 256 : (side + 1) * 256] = (
+                    ref[row, at].astype(F32) * keep
+                ).astype(BF)
+
+    write(own_ref, 0, rows // TILE, s)
+    for j, ref in enumerate(message_refs):
+        write(ref, g * (half // TILE), half // TILE, lax.rem(s + j + 1, SEQ))
+
+
+def prune(place, key_weight, value_weight, mask_columns):
+    rows = key_weight.shape[0]
+    whole = pl.BlockSpec(memory_space=pltpu.VMEM)
+    return pl.pallas_call(
+        prune_kernel,
+        out_shape=[jax.ShapeDtypeStruct((rows, 512), BF)]
+        + [jax.ShapeDtypeStruct((rows // 2, 512), BF)] * 3,
+        in_specs=[pl.BlockSpec(memory_space=pltpu.SMEM)] + [whole] * 3,
+        out_specs=[whole] * 4,
+        name="prune",
+    )(place, key_weight, value_weight, mask_columns)
+
+
+NT = (((1,), (1,)), ((), ()))
+TN = (((0,), (0,)), ((), ()))
+NN = (((1,), (0,)), ((), ()))
+
+
+def dot(a, b, dims=NN):
+    return lax.dot_general(a, b, dims, preferred_element_type=F32)
+
+
+def main_kernel(place, lengths, *refs):
+    (
+        enc, e1, e2, e3, x1, x2, x3,
+        w_own, z1, z2, z3, y1, y2, y3,
+        v_own, vz1, vz2, vz3, vy1, vy2, vy3,
+        qc,
+        att_ref, qg_ref,
+        a0, a1, a2, a3, b0, b1, b2, b3, core_ref, own_ref,
+        enc_s, w_s, grad_s, part_s, sems,
+    ) = refs
+    s, g, h = place[0], place[1], place[2]
+    c = lax.rem(h, 2)
+    x = h // 2
+    origin = [place[3], place[4], place[5]]
+    copies = []
+
+    def move(src, dst):
+        copy = pltpu.make_async_copy(src, dst, sems.at[len(copies)])
+        copy.start()
+        copies.append(copy)
+
+    def rows_of(doc, at):
+        return enc_s.at[doc, pl.ds(pl.multiple_of(at * 64, 64), 64)]
+
+    for i in range(2):
+        move(enc.at[2 * i + c], rows_of(i, s))
+    for k, (mine, other) in enumerate(((e1, x1), (e2, x2), (e3, x3))):
+        move(mine, rows_of(x, origin[k]))
+        move(other, rows_of(1 - x, origin[k]))
+
+    def weight_rows(core, at, half, count):
+        return w_s.at[core, pl.ds(pl.multiple_of(at * 1024 + half * 512, 512), count)]
+
+    for core, own, zs, ys in (
+        (c, w_own, (z1, z2, z3), (y1, y2, y3)),
+        (1 - c, v_own, (vz1, vz2, vz3), (vy1, vy2, vy3)),
+    ):
+        move(own, weight_rows(core, s, 0, 1024))
+        for j in range(3):
+            at = lax.rem(s + 3 - j, SEQ)
+            move(zs[j], weight_rows(core, at, g, 512))
+            move(ys[j], weight_rows(core, at, 1 - g, 512))
+    for copy in copies:
+        copy.wait()
+
+    row_head = lax.broadcasted_iota(jnp.int32, (256, 256), 0) // DH
+    col_head = lax.broadcasted_iota(jnp.int32, (256, 256), 1) // DH
+    same = row_head == col_head
+    position = lax.broadcasted_iota(jnp.int32, (256, 256), 1)
+
+    def spread(block):
+        four = jnp.concatenate([block] * 4, axis=0)
+        return jnp.where(same, four, jnp.zeros_like(four))
+
+    def gather_heads(block):
+        kept = jnp.where(same, block, 0.0)
+        return (kept[0:64] + kept[64:128]) + (kept[128:192] + kept[192:256])
+
+    for core in range(2):
+        for doc in range(2):
+            both = dot(enc_s[doc], w_s[core])
+            keys = both[:, :256].astype(BF)
+            values = both[:, 256:].astype(BF)
+            slot = lax.rem(core + c, 2)
+            query = spread(qc[slot, 0, doc].reshape(64, 256))
+            cot = spread(qc[slot, 1, doc].reshape(64, 256))
+            live = position < lengths[2 * doc + c]
+            scores = dot(query, keys, NT) * SCALE
+            scores = jnp.where(live, scores, FLOOR_SCORE)
+            row_max = jnp.max(scores, axis=1, keepdims=True)
+            weights = jnp.where(live, jnp.exp(scores - row_max), 0.0)
+            probs = weights / jnp.sum(weights, axis=1, keepdims=True)
+            low = probs.astype(BF)
+            output = dot(low, values)
+            delta = jnp.sum(cot.astype(F32) * output, axis=1, keepdims=True)
+            prob_grad = dot(cot, values, NT)
+            score_grad = (probs * (prob_grad - delta) * SCALE).astype(BF)
+            query_grad = dot(score_grad, keys)
+            att_ref[slot, doc] = gather_heads(output).astype(BF)
+            qg_ref[slot, doc] = gather_heads(query_grad).astype(BF)
+            grad_s[core, doc * 256 : (doc + 1) * 256, 0:256] = dot(score_grad, query, TN).astype(BF)
+            grad_s[core, doc * 256 : (doc + 1) * 256, 256:512] = dot(low, cot, TN).astype(BF)
+
+    for flip, outs in ((2, (a0, a1, a2, a3)), (3, (b0, b1, b2, b3)), (1, None), (0, None)):
+        block = lax.bitwise_xor(h, flip)
+
+        def column(n, carry):
+            at = pl.ds(pl.multiple_of(block * 1024 + n * 256, 256), 256)
+            part = dot(grad_s[0], w_s[0, at, :], NT) + dot(grad_s[1], w_s[1, at, :], NT)
+            part_s[:, :, pl.ds(pl.multiple_of(n * 256, 256), 256)] = part.reshape(2, 256, 256)
+            return carry
+
+        lax.fori_loop(0, 4, column, 0)
+        for j in range(4):
+            at = pl.ds(pl.multiple_of(lax.rem(s + j, SEQ) * 64, 64), 64)
+            for doc in range(2):
+                value = part_s[doc, at, :]
+                if outs is not None:
+                    outs[j][doc] = value.astype(BF)
+                elif flip == 1:
+                    core_ref[j, doc] = value.astype(BF)
+                else:
+                    own_ref[j, doc] = value
+
+
+def main_call(place, lengths, arrays):
+    here = pl.BlockSpec(memory_space=pl.ANY)
+    vmem = pl.BlockSpec(memory_space=pltpu.VMEM)
+    smem = pl.BlockSpec(memory_space=pltpu.SMEM)
+    piece = jax.ShapeDtypeStruct((2, 64, 1024), BF)
+    front = jax.ShapeDtypeStruct((2, 2, 64, 256), BF)
+    return pl.pallas_call(
+        main_kernel,
+        out_shape=[front, front]
+        + [piece] * 8
+        + [jax.ShapeDtypeStruct((4, 2, 64, 1024), BF), jax.ShapeDtypeStruct((4, 2, 64, 1024), F32)],
+        in_specs=[smem, smem] + [here] * 21 + [vmem],
+        out_specs=[vmem] * 12,
+        scratch_shapes=[
+            pltpu.VMEM((2, 256, 4096), BF),
+            pltpu.VMEM((2, 4096, 512), BF),
+            pltpu.VMEM((2, 512, 512), BF),
+            pltpu.VMEM((2, 256, 1024), F32),
+            pltpu.SemaphoreType.DMA((22,)),
+        ],
+        compiler_params=pltpu.CompilerParams(vmem_limit_bytes=48 * 1024 * 1024),
+        name="attend",
+    )(place, lengths, *arrays)
+
+
+def body(encoder, key_weight, value_weight, tile_mask, lengths, queries, cotangent):
+    s, g, h = lax.axis_index("seq"), lax.axis_index("grp"), lax.axis_index("head")
+    c = lax.rem(h, 2)
+    ring = jnp.array(RING, jnp.int32)
+    spot = jnp.array([RING.index(i) for i in range(SEQ)], jnp.int32)[s]
+    origins = [ring[lax.rem(spot + SEQ - k, SEQ)] for k in (1, 2, 3)]
+    place = jnp.stack([s, g, h] + origins).astype(jnp.int32)
+
+    def shift(value, j):
+        return lax.ppermute(value, "seq", [(a, (a + j) % SEQ) for a in range(SEQ)])
+
+    def flip(value, bits):
+        return lax.ppermute(value, "head", [(a, a ^ bits) for a in range(4)])
+
+    def around(value):
+        return lax.ppermute(value, "seq", [(RING[i], RING[(i + 1) % SEQ]) for i in range(SEQ)])
+
+    def across(value):
+        return lax.ppermute(value, "grp", [(0, 1), (1, 0)])
+
+    mask_columns = jnp.repeat(tile_mask, TILE, axis=2).astype(F32)
+    w_own, m1, m2, m3 = prune(place, key_weight, value_weight, mask_columns)
+    e0 = lax.dynamic_index_in_dim(encoder, h, 0, keepdims=False)
+    e1 = around(e0)
+    z2 = shift(m2, 2)
+    z1 = shift(m1, 1)
+    z3 = shift(m3, 3)
+    e2 = around(e1)
+    e3 = around(e2)
+
+    both = jnp.stack([queries, cotangent]).reshape(2, 2, 2, 16, 1024)
+    mine = lax.dynamic_index_in_dim(both, c, 2, keepdims=False)
+    theirs = flip(lax.dynamic_index_in_dim(both, 1 - c, 2, keepdims=False), 1)
+    qc = jnp.stack([mine, theirs]).reshape(2, 2, 2, 16, SEQ, 256).transpose(4, 0, 1, 2, 3, 5)
+    qc = lax.all_to_all(qc, "seq", split_axis=0, concat_axis=0, tiled=True)
+    qc = qc.transpose(1, 2, 3, 0, 4, 5).reshape(2, 2, 2, 64, 256)
+
+    x1, x2, x3 = flip(e1, 2), flip(e2, 2), flip(e3, 2)
+    y2, y1, y3 = across(z2), across(z1), across(z3)
+    firsts = [w_own, z1, z2, z3, y1, y2, y3]
+    seconds = [flip(value, 1) for value in firsts]
+    outs = main_call(place, lengths, [encoder, e1, e2, e3, x1, x2, x3] + firsts + seconds + [qc])
+    att, qgrad = outs[0], outs[1]
+    to_x, to_far, to_core, own = outs[2:6], outs[6:10], outs[10], outs[11]
+
+    from_core = flip(to_core, 1)
+    terms = []
+    for j in (2, 1, 3, 0):
+        near = flip(to_x[j], 2).astype(F32)
+        far = flip(to_far[j], 3).astype(F32)
+        summed = jnp.stack([own[j] + near, from_core[j].astype(F32) + far])
+        if j:
+            summed = shift(summed.astype(BF), j).astype(F32)
+        terms.append(summed)
+    total = ((terms[0] + terms[1]) + (terms[2] + terms[3])).astype(BF)
+    total = jnp.where(c == 0, total, total[::-1])
+    encoder_grad = total.transpose(1, 0, 2, 3).reshape(DOCS, 64, 1024)
+
+    front = jnp.stack([att, qgrad], axis=1)
+    other = flip(front[1], 1)
+    back = jnp.stack([front[0], other]).reshape(2, 2, 2, SEQ, 16, 256).transpose(3, 0, 1, 2, 4, 5)
+    back = lax.all_to_all(back, "seq", split_axis=0, concat_axis=0, tiled=True)
+    back = back.transpose(2, 3, 1, 4, 0, 5).reshape(2, 2, 2, 16, 1024)
+    back = jnp.where(c == 0, back, back[:, :, ::-1])
+    back = back.reshape(2, DOCS, 16, 1024)
+    return (back[0], back[1], encoder_grad)
+
+
 def solution(mesh):
     placed = (
         P("grp", "seq", None),
@@ -133,10 +398,15 @@
         P("grp", "seq", "head"),
         P("grp", "seq", "head"),
     )
-    return jax.shard_map(
-        body,
-        mesh=mesh,
-        in_specs=placed,
-        out_specs=(P("grp", "seq", "head"), P("grp", "seq", "head"), P("grp", "seq", "head")),
-        check_vma=False,
-    )
+
+    def step(*arrays):
+        plan = body if fits(mesh, arrays[0], arrays[1], arrays[5]) else general_body
+        return jax.shard_map(
+            plan,
+            mesh=mesh,
+            in_specs=placed,
+            out_specs=(P("grp", "seq", "head"),) * 3,
+            check_vma=False,
+        )(*arrays)
+
+    return step

time: 560 us -> 242 us (0.43)
  waiting for transfers between devices: 342 us -> 152 us
  local copies, waits for them, and re-layouts: 66.4 us -> 11 us
  matrix products: 48.8 us -> 0 us
  other arithmetic: 37.3 us -> 6.04 us
  blocking collectives: 38.6 us -> 11.9 us
  Pallas kernels: 0 us -> 26.4 us
  starting transfers between devices: 9.98 us -> 30.6 us
  between operations: 13.9 us -> 2.91 us
    all_gather x2 -> x0, waiting for transfers between devices: 286 us -> none  [the longest x1 144 us: body(): lax.all_gather(value_masked, 'seq', axis=0, tiled=True)]
    ppermute x0 -> x33, waiting for transfers between devices: none -> 152 us  [the longest x6 72.7 us: shift(): return lax.ppermute(value, 'seq', [(a, (a + j) % SEQ) for a in range(SEQ)])]
    dot_general x100 -> x0, matrix products: 48.8 us -> none  [the longest x1 7.82 us: back_product(): lax.dot_general(value_rows, value_piece, contract, preferred_element_type...]
    reduce_scatter x1 -> x0, waiting for transfers between devices: 30.9 us -> none  [body(): lax.psum_scatter(grad_terms, 'head', scatter_dimension=1, tiled=True)]
    ppermute x0 -> x33, starting transfers between devices: none -> 27.2 us  [the longest x21 11.4 us: flip(): return lax.ppermute(value, 'head', [(a, a ^ bits) for a in range(4)])]
    all_to_all x2 -> x1, blocking collectives: 38.6 us -> 11.9 us  [body(): qc = lax.all_to_all(qc, 'seq', split_axis=0, concat_axis=0, tiled=True)]
    pallas_call x0 -> x2, Pallas kernels: none -> 26.4 us  [the longest x1 22.2 us: main_call(): pl.pallas_call(main_kernel, out_shape=[front, front] + [piece] * 8 + [jax...]
    all_to_all x2 -> x1, waiting for transfers between devices: 25.3 us -> 0.01 us  [body(): back = lax.all_to_all(back, 'seq', split_axis=0, concat_axis=0, tiled=True)]
  transfers between devices with their start and end apart: 5 -> 34, of which waited for: 4 -> 18; matrix products, arithmetic and copies ran while one was open for 6% -> 5% of each run, Pallas kernels for 0% -> 2%
where the time goes in v1:
time: 242 us; the launch traced here: 241 us
  waiting for transfers between devices  152 us (63%)
  starting transfers between devices  30.6 us (13%)
  Pallas kernels  26.4 us (11%)
  blocking collectives  11.9 us (5%)
  local copies, waits for them, and re-layouts  11 us (5%)
  other arithmetic  6.04 us (2%)
  between operations  2.91 us (1%)
    ppermute x6, waiting for transfers between devices, shift(): return lax.ppermute(value, 'seq', [(a, (a + j) % SEQ) for a in range(SEQ)])  72.7 us
    ppermute x21, waiting for transfers between devices, flip(): return lax.ppermute(value, 'head', [(a, a ^ bits) for a in range(4)])  37.7 us
    pallas_call x1, Pallas kernels, main_call(): pl.pallas_call(main_kernel, out_shape=[front, front] + [piece] * 8 + [jax...  22.2 us
    ppermute x3, waiting for transfers between devices, across(): return lax.ppermute(value, 'grp', [(0, 1), (1, 0)])  21.5 us
    ppermute x3, waiting for transfers between devices, around(): lax.ppermute(value, 'seq', [(RING[i], RING[(i + 1) % SEQ]) for i in range...  20.3 us
    all_to_all x1, blocking collectives, body(): qc = lax.all_to_all(qc, 'seq', split_axis=0, concat_axis=0, tiled=True)  11.9 us
    ppermute x21, starting transfers between devices, flip(): return lax.ppermute(value, 'head', [(a, a ^ bits) for a in range(4)])  11.4 us
    ppermute x6, starting transfers between devices, shift(): return lax.ppermute(value, 'seq', [(a, (a + j) % SEQ) for a in range(SEQ)])  9.01 us
  transfers between devices with their start and end apart: 34, of which 18 were waited for; matrix products, arithmetic and copies ran while one was open for 5% of the time, Pallas kernels for 2%

profile of v1, /device:TPU:0, one launch (start us, length us, event | category | flops | bytes accessed | tf_op | source)
XLA Modules:
  0.0 241.1 jit_solution(9443781421744578827)
XLA Ops:
  1.7 3.1 %collective-permute-start = (bf16[64,4096]{1,0:T(8,128)(2,1)S(1)}, bf16[64,4096]{1,0:T(8,128)(2,1)S(1)}, u32[]{:S(2)}, u32[]{:S(2)}) collective-permute-start(bf16[64,4096]{1,0:T(8,128)(2,1)S(1)} %dynamic-slice_bitcast_fusion), channel_id=1, source_target_pairs={{0,4},{4,12},{12,8},{8,0},{1,5},{5,13},{13,9},{9,1},{2,6},{6,14},{... | collective-permute-start | bytes 1572872 | tf_op jit(solution)/shard_map/ppermute | solution.py:338
  11.1 2.6 %stack.95.place = s32[6]{0:T(128)} concatenate(s32[1]{0:T(128)} %bitcast, s32[1]{0:T(128)} %bitcast.1, s32[1]{0:T(128)} %bitcast.2, s32[1]{0:T(128)} %get-tuple-element.50, s32[1]{0:T(128)} %get-tuple-element.51, s32[1]{0:T(128)} %get-tuple-element.49), dimensions={0} | concatenate | bytes 48 | tf_op jit(solution)/shard_map/stack | solution.py:329
  13.7 4.1 %prune.1 = (bf16[1024,512]{1,0:T(8,128)(2,1)}, bf16[512,512]{1,0:T(8,128)(2,1)}, bf16[512,512]{1,0:T(8,128)(2,1)}, bf16[512,512]{1,0:T(8,128)(2,1)}) custom-call(s32[6]{0:T(128)} %stack.95.place, bf16[1024,1024]{1,0:T(8,128)(2,1)} %key_ref.1, bf16[1024,1024]{1,0:T(8,128)(2,1)} %value_ref.1, f32[2,16,1024]{2,1,0:T(8,128)} %convert_element_type.69.mask_ref), custom_call_target="tpu_custom_call" | custom-call | tf_op jit(solution)/shard_map/prune/pallas_call | solution.py:174
  17.8 2.6 %collective-permute-start.6 = (bf16[512,512]{1,0:T(8,128)(2,1)}, bf16[512,512]{1,0:T(8,128)(2,1)S(1)}, u32[]{:S(2)}, u32[]{:S(2)}) collective-permute-start(bf16[512,512]{1,0:T(8,128)(2,1)} %get-tuple-element.20), channel_id=1, source_target_pairs={{0,4},{4,8},{8,12},{12,0},{1,5},{5,9},{9,13},{13,1},{2,6},{6,10},{... | collective-permute-start | bytes 1572872 | tf_op jit(solution)/shard_map/ppermute | solution.py:332
  25.8 9.0 %collective-permute-done.6.refs_8_ = bf16[512,512]{1,0:T(8,128)(2,1)S(1)} collective-permute-done((bf16[512,512]{1,0:T(8,128)(2,1)}, bf16[512,512]{1,0:T(8,128)(2,1)S(1)}, u32[]{:S(2)}, u32[]{:S(2)}) %collective-permute-start.6) | collective-permute-done | bytes 524320 | tf_op jit(solution)/shard_map/ppermute | solution.py:332
  34.8 21.0 %collective-permute-done.7.refs_9_ = bf16[512,512]{1,0:T(8,128)(2,1)S(1)} collective-permute-done((bf16[512,512]{1,0:T(8,128)(2,1)}, bf16[512,512]{1,0:T(8,128)(2,1)S(1)}, u32[]{:S(2)}, u32[]{:S(2)}) %collective-permute-start.7) | collective-permute-done | bytes 524320 | tf_op jit(solution)/shard_map/ppermute | solution.py:332
  57.8 20.3 %collective-permute-done.1.refs_2_ = bf16[64,4096]{1,0:T(8,128)(2,1)S(1)} collective-permute-done((bf16[64,4096]{1,0:T(8,128)(2,1)S(1)}, bf16[64,4096]{1,0:T(8,128)(2,1)S(1)}, u32[]{:S(2)}, u32[]{:S(2)}) %collective-permute-start.1) | collective-permute-done | bytes 524320 | tf_op jit(solution)/shard_map/ppermute | solution.py:338
  80.4 12.7 %collective-permute-done.10.refs_12_ = bf16[512,512]{1,0:T(8,128)(2,1)} collective-permute-done((bf16[512,512]{1,0:T(8,128)(2,1)S(1)}, bf16[512,512]{1,0:T(8,128)(2,1)}, u32[]{:S(2)}, u32[]{:S(2)}) %collective-permute-start.10) | collective-permute-done | bytes 524320 | tf_op jit(solution)/shard_map/ppermute | solution.py:341
  94.6 8.8 %collective-permute-done.11.refs_13_ = bf16[512,512]{1,0:T(8,128)(2,1)} collective-permute-done((bf16[512,512]{1,0:T(8,128)(2,1)S(1)}, bf16[512,512]{1,0:T(8,128)(2,1)}, u32[]{:S(2)}, u32[]{:S(2)}) %collective-permute-start.11) | collective-permute-done | bytes 524320 | tf_op jit(solution)/shard_map/ppermute | solution.py:341
  106.3 11.9 %all_to_all.10 = bf16[4,2,2,2,16,256]{5,4,3,2,1,0:T(8,128)(2,1)S(1)} all-to-all(bf16[4,2,2,2,16,256]{5,4,3,2,1,0:T(8,128)(2,1)S(1)} %copy.20), channel_id=1, replica_groups=mesh['grp'=2,'seq'=4,'head'=4] {'seq'}, dimensions={0} | all-to-all | bytes 524288 | tf_op jit(solution)/shard_map/all_to_all | solution.py:357
  118.7 22.2 %attend.1 = (bf16[2,2,64,256]{3,2,1,0:T(8,128)(2,1)S(1)}, bf16[2,2,64,256]{3,2,1,0:T(8,128)(2,1)S(1)}, bf16[2,64,1024]{2,1,0:T(8,128)(2,1)}, bf16[2,64,1024]{2,1...) custom-call(s32[6]{0:T(128)S(1)} %copy-done, ...), custom_call_target="tpu_custom_call" | custom-call | tf_op jit(solution)/shard_map/attend/pallas_call | solution.py:304
  147.3 3.4 %all-to-all-start.1 = ((bf16[4,2,2,2,16,256]{5,4,1,3,2,0:T(8,128)(2,1)}), bf16[4,2,2,2,16,256]{5,4,1,3,2,0:T(8,128)(2,1)S(1)}, u32[]{:S(2)}, u32[]{:S(2)}) async-start(bf16[4,2,2,2,16,256]{5,4,1,3,2,0:T(8,128)(2,1)} %copy_bitcast_fusion), calls=%async_computation.1 | async-start | bytes 524288 | tf_op jit(solution)/shard_map/all_to_all | solution.py:384
  152.2 5.2 %collective-permute-done.25 = bf16[2,64,1024]{2,1,0:T(8,128)(2,1)S(1)} collective-permute-done((bf16[2,64,1024]{2,1,0:T(8,128)(2,1)}, bf16[2,64,1024]{2,1,0:T(8,128)(2,1)S(1)}, u32[]{:S(2)}, u32[]{:S(2)}) %collective-permute-start.25) | collective-permute-done | bytes 262176 | tf_op jit(solution)/shard_map/ppermute | solution.py:335
  157.8 5.3 %collective-permute-done.28 = bf16[2,64,1024]{2,1,0:T(8,128)(2,1)} collective-permute-done((bf16[2,64,1024]{2,1,0:T(8,128)(2,1)}, bf16[2,64,1024]{2,1,0:T(8,128)(2,1)}, u32[]{:S(2)}, u32[]{:S(2)}) %collective-permute-start.28) | collective-permute-done | bytes 262176 | tf_op jit(solution)/shard_map/ppermute | solution.py:335
  163.6 5.2 %collective-permute-done.31 = bf16[2,64,1024]{2,1,0:T(8,128)(2,1)} collective-permute-done((bf16[2,64,1024]{2,1,0:T(8,128)(2,1)}, bf16[2,64,1024]{2,1,0:T(8,128)(2,1)}, u32[]{:S(2)}, u32[]{:S(2)}) %collective-permute-start.31) | collective-permute-done | bytes 262176 | tf_op jit(solution)/shard_map/ppermute | solution.py:335
  169.2 2.0 fusion.11
  171.2 2.3 collective-permute-done.23
  173.5 5.6 %collective-permute-done.26 = bf16[2,64,1024]{2,1,0:T(8,128)(2,1)S(1)} collective-permute-done((bf16[2,64,1024]{2,1,0:T(8,128)(2,1)}, bf16[2,64,1024]{2,1,0:T(8,128)(2,1)S(1)}, u32[]{:S(2)}, u32[]{:S(2)}) %collective-permute-start.26) | collective-permute-done | bytes 262176 | tf_op jit(solution)/shard_map/ppermute | solution.py:335
  179.1 5.6 %collective-permute-done.29 = bf16[2,64,1024]{2,1,0:T(8,128)(2,1)S(1)} collective-permute-done((bf16[2,64,1024]{2,1,0:T(8,128)(2,1)}, bf16[2,64,1024]{2,1,0:T(8,128)(2,1)S(1)}, u32[]{:S(2)}, u32[]{:S(2)}) %collective-permute-start.29) | collective-permute-done | bytes 262176 | tf_op jit(solution)/shard_map/ppermute | solution.py:335
  184.7 5.6 %collective-permute-done.32 = bf16[2,64,1024]{2,1,0:T(8,128)(2,1)S(1)} collective-permute-done((bf16[2,64,1024]{2,1,0:T(8,128)(2,1)S(1)}, bf16[2,64,1024]{2,1,0:T(8,128)(2,1)S(1)}, u32[]{:S(2)}, u32[]{:S(2)}) %collective-permute-start.32) | collective-permute-done | bytes 262176 | tf_op jit(solution)/shard_map/ppermute | solution.py:335
  190.9 3.9 %collective-permute-start.30 = (bf16[2,2,64,1024]{3,2,1,0:T(8,128)(2,1)S(1)}, bf16[2,2,64,1024]{3,2,1,0:T(8,128)(2,1)}, u32[]{:S(2)}, u32[]{:S(2)}) collective-permute-start(bf16[2,2,64,1024]{3,2,1,0:T(8,128)(2,1)S(1)} %pad_maximum_fusion.2), channel_id=1, source_target_pairs={{0,12},{4,0},{8,4},{12,8},{1,13},{5,1},{9,5},{13,9},{2,14},{6,2},{... | collective-permute-start | bytes 1572872 | tf_op jit(solution)/shard_map/ppermute | solution.py:332
  195.7 11.8 %collective-permute-done.27 = bf16[2,2,64,1024]{3,2,1,0:T(8,128)(2,1)} collective-permute-done((bf16[2,2,64,1024]{3,2,1,0:T(8,128)(2,1)S(1)}, bf16[2,2,64,1024]{3,2,1,0:T(8,128)(2,1)}, u32[]{:S(2)}, u32[]{:S(2)}) %collective-permute-start.27) | collective-permute-done | bytes 524320 | tf_op jit(solution)/shard_map/ppermute | solution.py:332
  207.6 10.5 %collective-permute-done.30 = bf16[2,2,64,1024]{3,2,1,0:T(8,128)(2,1)} collective-permute-done((bf16[2,2,64,1024]{3,2,1,0:T(8,128)(2,1)S(1)}, bf16[2,2,64,1024]{3,2,1,0:T(8,128)(2,1)}, u32[]{:S(2)}, u32[]{:S(2)}) %collective-permute-start.30) | collective-permute-done | bytes 524320 | tf_op jit(solution)/shard_map/ppermute | solution.py:332
  218.1 20.3 %collective-permute-done.24 = bf16[2,2,64,1024]{3,2,1,0:T(8,128)(2,1)} collective-permute-done((bf16[2,2,64,1024]{3,2,1,0:T(8,128)(2,1)S(1)}, bf16[2,2,64,1024]{3,2,1,0:T(8,128)(2,1)}, u32[]{:S(2)}, u32[]{:S(2)}) %collective-permute-start.24) | collective-permute-done | bytes 524320 | tf_op jit(solution)/shard_map/ppermute | solution.py:332
  (101 shorter events, 33.0 us)
Async XLA Ops:
  1.7 21.1 %collective-permute-start = (bf16[64,4096]{1,0:T(8,128)(2,1)S(1)}, bf16[64,4096]{1,0:T(8,128)(2,1)S(1)}, u32[]{:S(2)}, u32[]{:S(2)}) collective-permute-start(bf16[64,4096]{1,0:T(8,128)(2,1)S(1)} %dynamic-slice_bitcast_fusion), channel_id=1, source_target_pairs={{0,4},{4,12},{12,8},{8,0},{1,5},{5,13},{13,9},{9,1},{2,6},{6,14},{... | collective-permute-start | bytes 1572872 | tf_op jit(solution)/shard_map/ppermute | solution.py:338
  17.8 17.0 %collective-permute-start.6 = (bf16[512,512]{1,0:T(8,128)(2,1)}, bf16[512,512]{1,0:T(8,128)(2,1)S(1)}, u32[]{:S(2)}, u32[]{:S(2)}) collective-permute-start(bf16[512,512]{1,0:T(8,128)(2,1)} %get-tuple-element.20), channel_id=1, source_target_pairs={{0,4},{4,8},{8,12},{12,0},{1,5},{5,9},{9,13},{13,1},{2,6},{6,10},{... | collective-permute-start | bytes 1572872 | tf_op jit(solution)/shard_map/ppermute | solution.py:332
  20.4 35.4 %collective-permute-start.7 = (bf16[512,512]{1,0:T(8,128)(2,1)}, bf16[512,512]{1,0:T(8,128)(2,1)S(1)}, u32[]{:S(2)}, u32[]{:S(2)}) collective-permute-start(bf16[512,512]{1,0:T(8,128)(2,1)} %get-tuple-element.21), channel_id=1, source_target_pairs={{0,8},{4,12},{8,0},{12,4},{1,9},{5,13},{9,1},{13,5},{2,10},{6,14},... | collective-permute-start | bytes 1572872 | tf_op jit(solution)/shard_map/ppermute | solution.py:332
  20.8 36.5 %collective-permute-start.8 = (bf16[512,512]{1,0:T(8,128)(2,1)}, bf16[512,512]{1,0:T(8,128)(2,1)S(1)}, u32[]{:S(2)}, u32[]{:S(2)}) collective-permute-start(bf16[512,512]{1,0:T(8,128)(2,1)} %get-tuple-element.22), channel_id=1, source_target_pairs={{0,12},{4,0},{8,4},{12,8},{1,13},{5,1},{9,5},{13,9},{2,14},{6,2},{... | collective-permute-start | bytes 1572872 | tf_op jit(solution)/shard_map/ppermute | solution.py:332
  22.8 34.5 %collective-permute-start.3 = (bf16[64,4096]{1,0:T(8,128)(2,1)S(1)}, bf16[64,4096]{1,0:T(8,128)(2,1)S(1)}, u32[]{:S(2)}, u32[]{:S(2)}) collective-permute-start(bf16[64,4096]{1,0:T(8,128)(2,1)S(1)} %collective-permute-done.refs_1_), channel_id=1, source_target_pairs={{0,2},{1,3},{2,0},{3,1},{4,6},{5,7},{6,4},{7,5},{8,10},{9,11},{10,... | collective-permute-start | bytes 1572872 | tf_op jit(solution)/shard_map/ppermute | solution.py:335
  25.8 52.4 %collective-permute-start.1 = (bf16[64,4096]{1,0:T(8,128)(2,1)S(1)}, bf16[64,4096]{1,0:T(8,128)(2,1)S(1)}, u32[]{:S(2)}, u32[]{:S(2)}) collective-permute-start(bf16[64,4096]{1,0:T(8,128)(2,1)S(1)} %collective-permute-done.refs_1_), channel_id=1, source_target_pairs={{0,4},{4,12},{12,8},{8,0},{1,5},{5,13},{13,9},{9,1},{2,6},{6,14},{... | collective-permute-start | bytes 1572872 | tf_op jit(solution)/shard_map/ppermute | solution.py:338
  34.8 44.9 %collective-permute-start.13 = (bf16[512,512]{1,0:T(8,128)(2,1)S(1)}, bf16[512,512]{1,0:T(8,128)(2,1)S(1)}, u32[]{:S(2)}, u32[]{:S(2)}) collective-permute-start(bf16[512,512]{1,0:T(8,128)(2,1)S(1)} %collective-permute-done.6.refs_8_), channel_id=1, source_target_pairs={{0,1},{1,0},{2,3},{3,2},{4,5},{5,4},{6,7},{7,6},{8,9},{9,8},{10,11... | collective-permute-start | bytes 1572872 | tf_op jit(solution)/shard_map/ppermute | solution.py:335
  55.8 23.9 %collective-permute-start.9 = (bf16[512,512]{1,0:T(8,128)(2,1)S(1)}, bf16[512,512]{1,0:T(8,128)(2,1)}, u32[]{:S(2)}, u32[]{:S(2)}) collective-permute-start(bf16[512,512]{1,0:T(8,128)(2,1)S(1)} %collective-permute-done.6.refs_8_), channel_id=1, source_target_pairs={{0,16},{16,0},{1,17},{17,1},{2,18},{18,2},{3,19},{19,3},{4,20},{20... | collective-permute-start | bytes 1572872 | tf_op jit(solution)/shard_map/ppermute | solution.py:341
  57.3 46.0 %collective-permute-start.12 = (bf16[1024,512]{1,0:T(8,128)(2,1)}, bf16[1024,512]{1,0:T(8,128)(2,1)S(1)}, u32[]{:S(2)}, u32[]{:S(2)}) collective-permute-start(bf16[1024,512]{1,0:T(8,128)(2,1)} %get-tuple-element.19.refs_7_), channel_id=1, source_target_pairs={{0,1},{1,0},{2,3},{3,2},{4,5},{5,4},{6,7},{7,6},{8,9},{9,8},{10,11... | collective-permute-start | bytes 3145736 | tf_op jit(solution)/shard_map/ppermute | solution.py:335
  57.3 23.0 %collective-permute-start.14 = (bf16[512,512]{1,0:T(8,128)(2,1)S(1)}, bf16[512,512]{1,0:T(8,128)(2,1)S(1)}, u32[]{:S(2)}, u32[]{:S(2)}) collective-permute-start(bf16[512,512]{1,0:T(8,128)(2,1)S(1)} %collective-permute-done.7.refs_9_), channel_id=1, source_target_pairs={{0,1},{1,0},{2,3},{3,2},{4,5},{5,4},{6,7},{7,6},{8,9},{9,8},{10,11... | collective-permute-start | bytes 1572872 | tf_op jit(solution)/shard_map/ppermute | solution.py:335
  79.7 23.6 %collective-permute-start.11 = (bf16[512,512]{1,0:T(8,128)(2,1)S(1)}, bf16[512,512]{1,0:T(8,128)(2,1)}, u32[]{:S(2)}, u32[]{:S(2)}) collective-permute-start(bf16[512,512]{1,0:T(8,128)(2,1)S(1)} %collective-permute-done.8.refs_10_), channel_id=1, source_target_pairs={{0,16},{16,0},{1,17},{17,1},{2,18},{18,2},{3,19},{19,3},{4,20},{20... | collective-permute-start | bytes 1572872 | tf_op jit(solution)/shard_map/ppermute | solution.py:341
  80.3 23.6 %collective-permute-start.2 = (bf16[64,4096]{1,0:T(8,128)(2,1)S(1)}, bf16[64,4096]{1,0:T(8,128)(2,1)S(1)}, u32[]{:S(2)}, u32[]{:S(2)}) collective-permute-start(bf16[64,4096]{1,0:T(8,128)(2,1)S(1)} %collective-permute-done.1.refs_2_), channel_id=1, source_target_pairs={{0,4},{4,12},{12,8},{8,0},{1,5},{5,13},{13,9},{9,1},{2,6},{6,14},{... | collective-permute-start | bytes 1572872 | tf_op jit(solution)/shard_map/ppermute | solution.py:338
  93.1 25.1 %collective-permute-start.4 = (bf16[64,4096]{1,0:T(8,128)(2,1)S(1)}, bf16[64,4096]{1,0:T(8,128)(2,1)S(1)}, u32[]{:S(2)}, u32[]{:S(2)}) collective-permute-start(bf16[64,4096]{1,0:T(8,128)(2,1)S(1)} %collective-permute-done.1.refs_2_), channel_id=1, source_target_pairs={{0,2},{1,3},{2,0},{3,1},{4,6},{5,7},{6,4},{7,5},{8,10},{9,11},{10,... | collective-permute-start | bytes 1572872 | tf_op jit(solution)/shard_map/ppermute | solution.py:335
  94.6 23.7 %collective-permute-start.16 = (bf16[512,512]{1,0:T(8,128)(2,1)}, bf16[512,512]{1,0:T(8,128)(2,1)}, u32[]{:S(2)}, u32[]{:S(2)}) collective-permute-start(bf16[512,512]{1,0:T(8,128)(2,1)} %collective-permute-done.9.refs_11_), channel_id=1, source_target_pairs={{0,1},{1,0},{2,3},{3,2},{4,5},{5,4},{6,7},{7,6},{8,9},{9,8},{10,11... | collective-permute-start | bytes 1572872 | tf_op jit(solution)/shard_map/ppermute | solution.py:335
  141.7 48.7 %collective-permute-start.22 = (bf16[4,2,64,1024]{3,2,1,0:T(8,128)(2,1)}, bf16[4,2,64,1024]{3,2,1,0:T(8,128)(2,1)S(1)}, u32[]{:S(2)}, u32[]{:S(2)}) collective-permute-start(bf16[4,2,64,1024]{3,2,1,0:T(8,128)(2,1)} %get-tuple-element.27), channel_id=1, source_target_pairs={{0,1},{1,0},{2,3},{3,2},{4,5},{5,4},{6,7},{7,6},{8,9},{9,8},{10,11... | collective-permute-start | bytes 3145736 | tf_op jit(solution)/shard_map/ppermute | solution.py:335
  144.5 18.6 %collective-permute-start.28 = (bf16[2,64,1024]{2,1,0:T(8,128)(2,1)}, bf16[2,64,1024]{2,1,0:T(8,128)(2,1)}, u32[]{:S(2)}, u32[]{:S(2)}) collective-permute-start(bf16[2,64,1024]{2,1,0:T(8,128)(2,1)} %get-tuple-element.31), channel_id=1, source_target_pairs={{0,2},{1,3},{2,0},{3,1},{4,6},{5,7},{6,4},{7,5},{8,10},{9,11},{10,... | collective-permute-start | bytes 786440 | tf_op jit(solution)/shard_map/ppermute | solution.py:335
  146.0 22.8 %collective-permute-start.31 = (bf16[2,64,1024]{2,1,0:T(8,128)(2,1)}, bf16[2,64,1024]{2,1,0:T(8,128)(2,1)}, u32[]{:S(2)}, u32[]{:S(2)}) collective-permute-start(bf16[2,64,1024]{2,1,0:T(8,128)(2,1)} %get-tuple-element.33), channel_id=1, source_target_pairs={{0,2},{1,3},{2,0},{3,1},{4,6},{5,7},{6,4},{7,5},{8,10},{9,11},{10,... | collective-permute-start | bytes 786440 | tf_op jit(solution)/shard_map/ppermute | solution.py:335
  147.3 47.7 %all-to-all-start.1 = ((bf16[4,2,2,2,16,256]{5,4,1,3,2,0:T(8,128)(2,1)}), bf16[4,2,2,2,16,256]{5,4,1,3,2,0:T(8,128)(2,1)S(1)}, u32[]{:S(2)}, u32[]{:S(2)}) async-start(bf16[4,2,2,2,16,256]{5,4,1,3,2,0:T(8,128)(2,1)} %copy_bitcast_fusion), calls=%async_computation.1 | async-start | bytes 524288 | tf_op jit(solution)/shard_map/all_to_all | solution.py:384
  151.8 21.7 %collective-permute-start.23 = (bf16[2,64,1024]{2,1,0:T(8,128)(2,1)}, bf16[2,64,1024]{2,1,0:T(8,128)(2,1)S(1)}, u32[]{:S(2)}, u32[]{:S(2)}) collective-permute-start(bf16[2,64,1024]{2,1,0:T(8,128)(2,1)} %copy-done.4), channel_id=1, source_target_pairs={{0,3},{1,2},{2,1},{3,0},{4,7},{5,6},{6,5},{7,4},{8,11},{9,10},{10,... | collective-permute-start | bytes 786440 | tf_op jit(solution)/shard_map/ppermute | solution.py:335
  157.4 21.7 %collective-permute-start.26 = (bf16[2,64,1024]{2,1,0:T(8,128)(2,1)}, bf16[2,64,1024]{2,1,0:T(8,128)(2,1)S(1)}, u32[]{:S(2)}, u32[]{:S(2)}) collective-permute-start(bf16[2,64,1024]{2,1,0:T(8,128)(2,1)} %copy-done.3), channel_id=1, source_target_pairs={{0,3},{1,2},{2,1},{3,0},{4,7},{5,6},{6,5},{7,4},{8,11},{9,10},{10,... | collective-permute-start | bytes 786440 | tf_op jit(solution)/shard_map/ppermute | solution.py:335
  163.1 21.6 %collective-permute-start.29 = (bf16[2,64,1024]{2,1,0:T(8,128)(2,1)}, bf16[2,64,1024]{2,1,0:T(8,128)(2,1)S(1)}, u32[]{:S(2)}, u32[]{:S(2)}) collective-permute-start(bf16[2,64,1024]{2,1,0:T(8,128)(2,1)} %copy-done.2), channel_id=1, source_target_pairs={{0,3},{1,2},{2,1},{3,0},{4,7},{5,6},{6,5},{7,4},{8,11},{9,10},{10,... | collective-permute-start | bytes 786440 | tf_op jit(solution)/shard_map/ppermute | solution.py:335
  168.8 21.6 %collective-permute-start.32 = (bf16[2,64,1024]{2,1,0:T(8,128)(2,1)S(1)}, bf16[2,64,1024]{2,1,0:T(8,128)(2,1)S(1)}, u32[]{:S(2)}, u32[]{:S(2)}) collective-permute-start(bf16[2,64,1024]{2,1,0:T(8,128)(2,1)S(1)} %get-tuple-element.34), channel_id=1, source_target_pairs={{0,3},{1,2},{2,1},{3,0},{4,7},{5,6},{6,5},{7,4},{8,11},{9,10},{10,... | collective-permute-start | bytes 786440 | tf_op jit(solution)/shard_map/ppermute | solution.py:335
  190.9 27.2 %collective-permute-start.30 = (bf16[2,2,64,1024]{3,2,1,0:T(8,128)(2,1)S(1)}, bf16[2,2,64,1024]{3,2,1,0:T(8,128)(2,1)}, u32[]{:S(2)}, u32[]{:S(2)}) collective-permute-start(bf16[2,2,64,1024]{3,2,1,0:T(8,128)(2,1)S(1)} %pad_maximum_fusion.2), channel_id=1, source_target_pairs={{0,12},{4,0},{8,4},{12,8},{1,13},{5,1},{9,5},{13,9},{2,14},{6,2},{... | collective-permute-start | bytes 1572872 | tf_op jit(solution)/shard_map/ppermute | solution.py:332
  194.8 43.6 %collective-permute-start.24 = (bf16[2,2,64,1024]{3,2,1,0:T(8,128)(2,1)S(1)}, bf16[2,2,64,1024]{3,2,1,0:T(8,128)(2,1)}, u32[]{:S(2)}, u32[]{:S(2)}) collective-permute-start(bf16[2,2,64,1024]{3,2,1,0:T(8,128)(2,1)S(1)} %pad_maximum_fusion), channel_id=1, source_target_pairs={{0,8},{4,12},{8,0},{12,4},{1,9},{5,13},{9,1},{13,5},{2,10},{6,14},... | collective-permute-start | bytes 1572872 | tf_op jit(solution)/shard_map/ppermute | solution.py:332
  (24 other events, 524.3 us)

commit v2 on v1

--- a/solution.py
+++ b/solution.py
@@ -131,7 +131,8 @@
 
 
 SEQ = 4
-RING = (0, 1, 3, 2)
+PIECE = 512
+SENT = PIECE + 64
 
 
 def fits(mesh, encoder, key_weight, queries):
@@ -139,46 +140,57 @@
         mesh.shape["seq"] == SEQ
         and mesh.shape["head"] == 4
         and mesh.shape["grp"] == 2
-        and encoder.shape[0] == DOCS * 2
-        and key_weight.shape[1] // 4 // SEQ == 4 * DH
-        and key_weight.shape[0] == encoder.shape[2] == 4096
-        and encoder.shape[1] == 256
-        and queries.shape[1] == 64
-    )
-
-
-def prune_kernel(place, key_ref, value_ref, mask_ref, own_ref, *message_refs):
-    rows = key_ref.shape[0]
-    half = rows // 2
-    s, g = place[0], place[1]
+        and encoder.shape == (DOCS * 2, 256, 4096)
+        and key_weight.shape == (4096, 4096)
+        and queries.shape == (DOCS * 2, 64, 4096)
+    )
+
+
+def gray(value):
+    return lax.bitwise_xor(value, value // 2)
+
+
+def ring_back(s, k):
+    return gray(lax.rem(gray(s) + SEQ - k, SEQ))
+
+
+def prune_kernel(mask_ref, key_ref, value_ref, query_ref, cot_ref, own_ref, *message_refs):
+    s, g = lax.axis_index("seq"), lax.axis_index("grp")
+    left = lax.broadcasted_iota(jnp.int32, (1, 128), 1) < TILE
 
     def write(out_ref, first_tile, tiles, column):
-        at = pl.ds(pl.multiple_of(column * 256, 256), 256)
         for t in range(tiles):
             tile = first_tile + t
             row = pl.ds(pl.multiple_of(tile * TILE, TILE), TILE)
             for side, ref in ((0, key_ref), (1, value_ref)):
-                keep = mask_ref[side, pl.ds(tile, 1), at]
-                out_ref[t * TILE : (t + 1) * TILE, side * 256 : (side + 1) * 256] = (
-                    ref[row, at].astype(F32) * keep
-                ).astype(BF)
-
-    write(own_ref, 0, rows // TILE, s)
-    for j, ref in enumerate(message_refs):
-        write(ref, g * (half // TILE), half // TILE, lax.rem(s + j + 1, SEQ))
-
-
-def prune(place, key_weight, value_weight, mask_columns):
-    rows = key_weight.shape[0]
+                for part in range(2):
+                    at = pl.ds(pl.multiple_of(column * 256 + part * 128, 128), 128)
+                    first = mask_ref[side, tile, column * 4 + part * 2]
+                    second = mask_ref[side, tile, column * 4 + part * 2 + 1]
+                    keep = jnp.where(left, first, second).astype(F32)
+                    to = side * 256 + part * 128
+                    out_ref[t * TILE : (t + 1) * TILE, to : to + 128] = (
+                        ref[row, at].astype(F32) * keep
+                    ).astype(BF)
+        at = pl.ds(pl.multiple_of(column * 256, 256), 256)
+        out_ref[tiles * TILE :, 0:256] = query_ref[:, at]
+        out_ref[tiles * TILE :, 256:512] = cot_ref[:, at]
+
+    for j in (2, 1, 3):
+        write(message_refs[j - 1], g * 8, 8, lax.rem(s + j, SEQ))
+    write(own_ref, 0, 16, s)
+
+
+def prune(tile_mask, key_weight, value_weight, queries, cotangent):
     whole = pl.BlockSpec(memory_space=pltpu.VMEM)
     return pl.pallas_call(
         prune_kernel,
-        out_shape=[jax.ShapeDtypeStruct((rows, 512), BF)]
-        + [jax.ShapeDtypeStruct((rows // 2, 512), BF)] * 3,
-        in_specs=[pl.BlockSpec(memory_space=pltpu.SMEM)] + [whole] * 3,
+        out_shape=[jax.ShapeDtypeStruct((2 * PIECE + 64, 512), BF)]
+        + [jax.ShapeDtypeStruct((SENT, 512), BF)] * 3,
+        in_specs=[pl.BlockSpec(memory_space=pltpu.SMEM)] + [whole] * 4,
         out_specs=[whole] * 4,
         name="prune",
-    )(place, key_weight, value_weight, mask_columns)
+    )(tile_mask, key_weight, value_weight, queries, cotangent)
 
 
 NT = (((1,), (1,)), ((), ()))
@@ -190,50 +202,75 @@
     return lax.dot_general(a, b, dims, preferred_element_type=F32)
 
 
-def main_kernel(place, lengths, *refs):
+def partial_blocks(block, grad, weight, part):
+    def column(n, carry):
+        at = pl.ds(pl.multiple_of(block * 1024 + n * 256, 256), 256)
+        total = dot(grad[0], weight[0, at, :], NT) + dot(grad[1], weight[1, at, :], NT)
+        part[:, :, pl.ds(pl.multiple_of(n * 256, 256), 256)] = total.reshape(2, 256, 256)
+        return carry
+
+    lax.fori_loop(0, 4, column, 0)
+
+
+def main_kernel(lengths, *refs):
     (
-        enc, e1, e2, e3, x1, x2, x3,
+        enc, ea, eb, ec, ed, ef, xa, xb, xc, xd, xf,
         w_own, z1, z2, z3, y1, y2, y3,
         v_own, vz1, vz2, vz3, vy1, vy2, vy3,
-        qc,
-        att_ref, qg_ref,
-        a0, a1, a2, a3, b0, b1, b2, b3, core_ref, own_ref,
-        enc_s, w_s, grad_s, part_s, sems,
+        att_ref, qg_ref, grad_ref, weight_ref,
+        a1, a2, a30, b1, b2, b3, b0, core_ref,
+        enc_s, w_s, qc_s, grad_s, part_s, sems,
     ) = refs
-    s, g, h = place[0], place[1], place[2]
+    s, g, h = lax.axis_index("seq"), lax.axis_index("grp"), lax.axis_index("head")
     c = lax.rem(h, 2)
     x = h // 2
-    origin = [place[3], place[4], place[5]]
+    middle = jnp.logical_or(s == 1, s == 2)
     copies = []
 
-    def move(src, dst):
-        copy = pltpu.make_async_copy(src, dst, sems.at[len(copies)])
-        copy.start()
+    def move(src, dst, other=None):
+        sem = sems.at[len(copies)]
+        copy = pltpu.make_async_copy(src, dst, sem)
+        if other is None:
+            copy.start()
+        else:
+            pl.when(middle)(lambda: copy.start())
+            pl.when(jnp.logical_not(middle))(lambda: pltpu.make_async_copy(other, dst, sem).start())
         copies.append(copy)
 
     def rows_of(doc, at):
         return enc_s.at[doc, pl.ds(pl.multiple_of(at * 64, 64), 64)]
 
+    low_half = s < 2
+    second = jnp.where(low_half, 2, 1)
+    third = jnp.where(low_half, 3, 0)
     for i in range(2):
         move(enc.at[2 * i + c], rows_of(i, s))
-    for k, (mine, other) in enumerate(((e1, x1), (e2, x2), (e3, x3))):
-        move(mine, rows_of(x, origin[k]))
-        move(other, rows_of(1 - x, origin[k]))
+    for doc, first_from, second_from, third_from in (
+        (x, ea, (eb, ed), (ec, ef)),
+        (1 - x, xa, (xb, xd), (xc, xf)),
+    ):
+        move(first_from, rows_of(doc, lax.bitwise_xor(s, 1)))
+        move(second_from[0], rows_of(doc, second), second_from[1])
+        move(third_from[0], rows_of(doc, third), third_from[1])
 
     def weight_rows(core, at, half, count):
-        return w_s.at[core, pl.ds(pl.multiple_of(at * 1024 + half * 512, 512), count)]
+        return w_s.at[core, pl.ds(pl.multiple_of(at * 1024 + half * PIECE, PIECE), count)]
 
     for core, own, zs, ys in (
         (c, w_own, (z1, z2, z3), (y1, y2, y3)),
         (1 - c, v_own, (vz1, vz2, vz3), (vy1, vy2, vy3)),
     ):
-        move(own, weight_rows(core, s, 0, 1024))
+        move(own.at[0 : 2 * PIECE], weight_rows(core, s, 0, 2 * PIECE))
+        move(own.at[2 * PIECE : 2 * PIECE + 64], qc_s.at[core, s])
         for j in range(3):
             at = lax.rem(s + 3 - j, SEQ)
-            move(zs[j], weight_rows(core, at, g, 512))
-            move(ys[j], weight_rows(core, at, 1 - g, 512))
+            move(zs[j].at[0:PIECE], weight_rows(core, at, g, PIECE))
+            move(ys[j].at[0:PIECE], weight_rows(core, at, 1 - g, PIECE))
+            move(zs[j].at[PIECE:SENT], qc_s.at[core, at])
     for copy in copies:
         copy.wait()
+    save = pltpu.make_async_copy(w_s, weight_ref, sems.at[0])
+    save.start()
 
     row_head = lax.broadcasted_iota(jnp.int32, (256, 256), 0) // DH
     col_head = lax.broadcasted_iota(jnp.int32, (256, 256), 1) // DH
@@ -249,13 +286,14 @@
         return (kept[0:64] + kept[64:128]) + (kept[128:192] + kept[192:256])
 
     for core in range(2):
+        slot = lax.rem(core + c, 2)
         for doc in range(2):
             both = dot(enc_s[doc], w_s[core])
             keys = both[:, :256].astype(BF)
             values = both[:, 256:].astype(BF)
-            slot = lax.rem(core + c, 2)
-            query = spread(qc[slot, 0, doc].reshape(64, 256))
-            cot = spread(qc[slot, 1, doc].reshape(64, 256))
+            at = pl.ds(pl.multiple_of((2 * doc + c) * 16, 16), 16)
+            query = spread(qc_s[core, :, at, 0:256].reshape(64, 256))
+            cot = spread(qc_s[core, :, at, 256:512].reshape(64, 256))
             live = position < lengths[2 * doc + c]
             scores = dot(query, keys, NT) * SCALE
             scores = jnp.where(live, scores, FLOOR_SCORE)
@@ -273,29 +311,22 @@
             grad_s[core, doc * 256 : (doc + 1) * 256, 0:256] = dot(score_grad, query, TN).astype(BF)
             grad_s[core, doc * 256 : (doc + 1) * 256, 256:512] = dot(low, cot, TN).astype(BF)
 
-    for flip, outs in ((2, (a0, a1, a2, a3)), (3, (b0, b1, b2, b3)), (1, None), (0, None)):
-        block = lax.bitwise_xor(h, flip)
-
-        def column(n, carry):
-            at = pl.ds(pl.multiple_of(block * 1024 + n * 256, 256), 256)
-            part = dot(grad_s[0], w_s[0, at, :], NT) + dot(grad_s[1], w_s[1, at, :], NT)
-            part_s[:, :, pl.ds(pl.multiple_of(n * 256, 256), 256)] = part.reshape(2, 256, 256)
-            return carry
-
-        lax.fori_loop(0, 4, column, 0)
-        for j in range(4):
-            at = pl.ds(pl.multiple_of(lax.rem(s + j, SEQ) * 64, 64), 64)
+    cores = [core_ref.at[k] for k in range(4)]
+    for flip, outs in (
+        (2, (a30.at[1], a1, a2, a30.at[0])),
+        (3, (b0, b1, b2, b3)),
+        (1, cores),
+    ):
+        partial_blocks(lax.bitwise_xor(h, flip), grad_s, w_s, part_s)
+        for k in range(4):
+            at = pl.ds(pl.multiple_of(ring_back(s, k) * 64, 64), 64)
             for doc in range(2):
-                value = part_s[doc, at, :]
-                if outs is not None:
-                    outs[j][doc] = value.astype(BF)
-                elif flip == 1:
-                    core_ref[j, doc] = value.astype(BF)
-                else:
-                    own_ref[j, doc] = value
-
-
-def main_call(place, lengths, arrays):
+                outs[k][doc] = part_s[doc, at, :].astype(BF)
+    grad_ref[...] = grad_s[...]
+    save.wait()
+
+
+def main_call(lengths, arrays):
     here = pl.BlockSpec(memory_space=pl.ANY)
     vmem = pl.BlockSpec(memory_space=pltpu.VMEM)
     smem = pl.BlockSpec(memory_space=pltpu.SMEM)
@@ -303,80 +334,164 @@
     front = jax.ShapeDtypeStruct((2, 2, 64, 256), BF)
     return pl.pallas_call(
         main_kernel,
-        out_shape=[front, front]
-        + [piece] * 8
-        + [jax.ShapeDtypeStruct((4, 2, 64, 1024), BF), jax.ShapeDtypeStruct((4, 2, 64, 1024), F32)],
-        in_specs=[smem, smem] + [here] * 21 + [vmem],
-        out_specs=[vmem] * 12,
+        out_shape=[
+            front,
+            front,
+            jax.ShapeDtypeStruct((2, 512, 512), BF),
+            jax.ShapeDtypeStruct((2, 4096, 512), BF),
+        ]
+        + [piece] * 2
+        + [jax.ShapeDtypeStruct((2, 2, 64, 1024), BF)]
+        + [piece] * 4
+        + [jax.ShapeDtypeStruct((4, 2, 64, 1024), BF)],
+        in_specs=[smem] + [here] * len(arrays),
+        out_specs=[vmem] * 3 + [here] + [vmem] * 8,
         scratch_shapes=[
             pltpu.VMEM((2, 256, 4096), BF),
             pltpu.VMEM((2, 4096, 512), BF),
+            pltpu.VMEM((2, 4, 64, 512), BF),
             pltpu.VMEM((2, 512, 512), BF),
             pltpu.VMEM((2, 256, 1024), F32),
-            pltpu.SemaphoreType.DMA((22,)),
+            pltpu.SemaphoreType.DMA((32,)),
         ],
         compiler_params=pltpu.CompilerParams(vmem_limit_bytes=48 * 1024 * 1024),
+        cost_estimate=pl.CostEstimate(
+            flops=8 * 10**9, bytes_accessed=30 * 2**20, transcendentals=2**18
+        ),
         name="attend",
-    )(place, lengths, *arrays)
+    )(lengths, *arrays)
+
+
+def near_kernel(grad, weight, own_ref, part_s):
+    s, h = lax.axis_index("seq"), lax.axis_index("head")
+    partial_blocks(h, grad, weight, part_s)
+    for k in range(4):
+        at = pl.ds(pl.multiple_of(ring_back(s, k) * 64, 64), 64)
+        for doc in range(2):
+            own_ref[k, doc] = part_s[doc, at, :]
+
+
+def near_call(grad, weight):
+    vmem = pl.BlockSpec(memory_space=pltpu.VMEM)
+    return pl.pallas_call(
+        near_kernel,
+        out_shape=jax.ShapeDtypeStruct((4, 2, 64, 1024), F32),
+        in_specs=[vmem, vmem],
+        out_specs=vmem,
+        scratch_shapes=[pltpu.VMEM((2, 256, 1024), F32)],
+        compiler_params=pltpu.CompilerParams(vmem_limit_bytes=48 * 1024 * 1024),
+        cost_estimate=pl.CostEstimate(
+            flops=10**9, bytes_accessed=10 * 2**20, transcendentals=0
+        ),
+        name="near",
+    )(grad, weight)
+
+
+def final_kernel(own, core, near, far, near_sum, far_sum, out_ref):
+    c = lax.rem(lax.axis_index("head"), 2)
+    for i in range(2):
+        mine = own[0, i] + near[1, i].astype(F32) + near_sum[i].astype(F32)
+        theirs = core[0, i].astype(F32) + far[i].astype(F32) + far_sum[i].astype(F32)
+        out_ref[2 * i + c] = mine.astype(BF)
+        out_ref[2 * i + 1 - c] = theirs.astype(BF)
+
+
+def small_call(kernel, shape, name, *arrays):
+    vmem = pl.BlockSpec(memory_space=pltpu.VMEM)
+    return pl.pallas_call(
+        kernel,
+        out_shape=jax.ShapeDtypeStruct(shape, BF),
+        in_specs=[vmem] * len(arrays),
+        out_specs=vmem,
+        name=name,
+    )(*arrays)
+
+
+def after(value, *first):
+    return lax.optimization_barrier((value,) + first)[0]
 
 
 def body(encoder, key_weight, value_weight, tile_mask, lengths, queries, cotangent):
-    s, g, h = lax.axis_index("seq"), lax.axis_index("grp"), lax.axis_index("head")
+    h = lax.axis_index("head")
     c = lax.rem(h, 2)
-    ring = jnp.array(RING, jnp.int32)
-    spot = jnp.array([RING.index(i) for i in range(SEQ)], jnp.int32)[s]
-    origins = [ring[lax.rem(spot + SEQ - k, SEQ)] for k in (1, 2, 3)]
-    place = jnp.stack([s, g, h] + origins).astype(jnp.int32)
 
     def shift(value, j):
         return lax.ppermute(value, "seq", [(a, (a + j) % SEQ) for a in range(SEQ)])
 
-    def flip(value, bits):
-        return lax.ppermute(value, "head", [(a, a ^ bits) for a in range(4)])
-
-    def around(value):
-        return lax.ppermute(value, "seq", [(RING[i], RING[(i + 1) % SEQ]) for i in range(SEQ)])
+    def along(value, pairs):
+        return lax.ppermute(value, "seq", pairs)
+
+    def flip(value, bits, seqs=range(SEQ)):
+        pairs = [(a * 4 + b, a * 4 + (b ^ bits)) for a in seqs for b in range(4)]
+        return lax.ppermute(value, ("seq", "head"), pairs)
 
     def across(value):
         return lax.ppermute(value, "grp", [(0, 1), (1, 0)])
 
-    mask_columns = jnp.repeat(tile_mask, TILE, axis=2).astype(F32)
-    w_own, m1, m2, m3 = prune(place, key_weight, value_weight, mask_columns)
+    inner, ends = (1, 2), (0, 3)
+    outward = [(1, 0), (2, 3)]
+    swap = [(1, 2), (2, 1)]
     e0 = lax.dynamic_index_in_dim(encoder, h, 0, keepdims=False)
-    e1 = around(e0)
+    ea = along(e0, [(0, 1), (1, 0), (2, 3), (3, 2)])
+    eb = along(e0, swap)
+    w_own, m1, m2, m3 = prune(
+        tile_mask, key_weight, value_weight, queries.reshape(64, 1024), cotangent.reshape(64, 1024)
+    )
     z2 = shift(m2, 2)
-    z1 = shift(m1, 1)
-    z3 = shift(m3, 3)
-    e2 = around(e1)
-    e3 = around(e2)
-
-    both = jnp.stack([queries, cotangent]).reshape(2, 2, 2, 16, 1024)
-    mine = lax.dynamic_index_in_dim(both, c, 2, keepdims=False)
-    theirs = flip(lax.dynamic_index_in_dim(both, 1 - c, 2, keepdims=False), 1)
-    qc = jnp.stack([mine, theirs]).reshape(2, 2, 2, 16, SEQ, 256).transpose(4, 0, 1, 2, 3, 5)
-    qc = lax.all_to_all(qc, "seq", split_axis=0, concat_axis=0, tiled=True)
-    qc = qc.transpose(1, 2, 3, 0, 4, 5).reshape(2, 2, 2, 64, 256)
-
-    x1, x2, x3 = flip(e1, 2), flip(e2, 2), flip(e3, 2)
-    y2, y1, y3 = across(z2), across(z1), across(z3)
-    firsts = [w_own, z1, z2, z3, y1, y2, y3]
-    seconds = [flip(value, 1) for value in firsts]
-    outs = main_call(place, lengths, [encoder, e1, e2, e3, x1, x2, x3] + firsts + seconds + [qc])
-    att, qgrad = outs[0], outs[1]
-    to_x, to_far, to_core, own = outs[2:6], outs[6:10], outs[10], outs[11]
+    v_own = flip(after(w_own, m2), 1)
+    xa = flip(ea, 2)
+    ec = along(ea, swap)
+    z1 = shift(after(m1, ea), 1)
+    xb = flip(eb, 2, inner)
+    ed = along(eb, outward)
+    y2 = across(z2)
+    vz2 = flip(z2, 1)
+    xc = flip(ec, 2, inner)
+    ef = along(ec, outward)
+    z3 = shift(after(m3, ec), 3)
+    xd = flip(ed, 2, ends)
+    y1 = across(z1)
+    vz1 = flip(z1, 1)
+    vy2 = flip(y2, 1)
+    xf = flip(ef, 2, ends)
+    y3 = across(z3)
+    vz3 = flip(z3, 1)
+    vy1 = flip(y1, 1)
+    vy3 = flip(y3, 1)
+
+    outs = main_call(
+        lengths,
+        [encoder, ea, eb, ec, ed, ef, xa, xb, xc, xd, xf]
+        + [w_own, z1, z2, z3, y1, y2, y3]
+        + [v_own, vz1, vz2, vz3, vy1, vy2, vy3],
+    )
+    att, qgrad, grad, weight = outs[:4]
+    a1, a2, a30, b1, b2, b3, b0, to_core = outs[4:]
+
+    def onward(value):
+        pairs = [(0, 1), (1, 3), (3, 2), (2, 0)]
+        return along(value, pairs)
 
     from_core = flip(to_core, 1)
-    terms = []
-    for j in (2, 1, 3, 0):
-        near = flip(to_x[j], 2).astype(F32)
-        far = flip(to_far[j], 3).astype(F32)
-        summed = jnp.stack([own[j] + near, from_core[j].astype(F32) + far])
-        if j:
-            summed = shift(summed.astype(BF), j).astype(F32)
-        terms.append(summed)
-    total = ((terms[0] + terms[1]) + (terms[2] + terms[3])).astype(BF)
-    total = jnp.where(c == 0, total, total[::-1])
-    encoder_grad = total.transpose(1, 0, 2, 3).reshape(DOCS, 64, 1024)
+    a1, b1, a2, b2 = flip(a1, 2), flip(b1, 3), flip(a2, 2), flip(b2, 3)
+    a30, b3, b0 = flip(a30, 2), flip(b3, 3), flip(b0, 3)
+    own = near_call(after(grad, a1), weight)
+
+    def summed(*parts):
+        total = parts[0].astype(F32)
+        for part in parts[1:]:
+            total = total + part.astype(F32)
+        return total.astype(BF)
+
+    near1 = onward(summed(own[1], a1))
+    far1 = onward(summed(from_core[1], b1))
+    near2 = onward(summed(own[2], a2, near1))
+    far2 = onward(summed(from_core[2], b2, far1))
+    near3 = onward(summed(own[3], a30[0], near2))
+    far3 = onward(summed(from_core[3], b3, far2))
+    encoder_grad = small_call(
+        final_kernel, (DOCS, 64, 1024), "final", own, from_core, a30, b0, near3, far3
+    )
 
     front = jnp.stack([att, qgrad], axis=1)
     other = flip(front[1], 1)

time: 242 us -> 225 us (0.930)
  waiting for transfers between devices: 152 us -> 108 us
  starting transfers between devices: 30.6 us -> 66.3 us
  blocking collectives: 11.9 us -> 0 us
  Pallas kernels: 26.4 us -> 33.6 us
  local copies, waits for them, and re-layouts: 11 us -> 6.61 us
  other arithmetic: 6.04 us -> 8.78 us
    ppermute x6 -> x3, waiting for transfers between devices: 72.7 us -> 24.6 us  [shift(): return lax.ppermute(value, 'seq', [(a, (a + j) % SEQ) for a in range(SEQ)])]
    ppermute x6 -> x3, starting transfers between devices: 9.01 us -> 35.3 us  [shift(): return lax.ppermute(value, 'seq', [(a, (a + j) % SEQ) for a in range(SEQ)])]
    ppermute x24 -> x32, waiting for transfers between devices: 58.1 us -> 75.8 us  [the longest x11 51.1 us: along(): return lax.ppermute(value, 'seq', pairs)]
    ppermute x3, waiting for transfers between devices: 21.5 us -> 7.24 us  [across(): return lax.ppermute(value, 'grp', [(0, 1), (1, 0)])]
    all_to_all x1 -> x0, blocking collectives: 11.9 us -> none  [body(): qc = lax.all_to_all(qc, 'seq', split_axis=0, concat_axis=0, tiled=True)]
    ppermute x24 -> x32, starting transfers between devices: 14.5 us -> 22.1 us  [the longest x21 13.7 us: flip(): return lax.ppermute(value, ('seq', 'head'), pairs)]
    pallas_call x2 -> x4, Pallas kernels: 26.4 us -> 33.6 us  [the longest x1 20.5 us: main_call(): pl.pallas_call(main_kernel, out_shape=[front, front, jax.ShapeDtypeStruct...]
    convert_element_type x2 -> x6, other arithmetic: 2.39 us -> 7.97 us  [summed(): return total.astype(BF)]
  transfers between devices with their start and end apart: 34 -> 39, of which waited for: 18 -> 16; matrix products, arithmetic and copies ran while one was open for 5% -> 5% of each run, Pallas kernels for 2% -> 4%
where the time goes in v2:
time: 225 us; the launch traced here: 224 us
  waiting for transfers between devices  108 us (48%)
  starting transfers between devices  66.3 us (29%)
  Pallas kernels  33.6 us (15%)
  other arithmetic  8.78 us (4%)
  local copies, waits for them, and re-layouts  6.61 us (3%)
    ppermute x11, waiting for transfers between devices, along(): return lax.ppermute(value, 'seq', pairs)  51.1 us
    ppermute x3, starting transfers between devices, shift(): return lax.ppermute(value, 'seq', [(a, (a + j) % SEQ) for a in range(SEQ)])  35.3 us
    ppermute x21, waiting for transfers between devices, flip(): return lax.ppermute(value, ('seq', 'head'), pairs)  24.7 us
    ppermute x3, waiting for transfers between devices, shift(): return lax.ppermute(value, 'seq', [(a, (a + j) % SEQ) for a in range(SEQ)])  24.6 us
    pallas_call x1, Pallas kernels, main_call(): pl.pallas_call(main_kernel, out_shape=[front, front, jax.ShapeDtypeStruct...  20.5 us
    ppermute x21, starting transfers between devices, flip(): return lax.ppermute(value, ('seq', 'head'), pairs)  13.7 us
    ppermute x11, starting transfers between devices, along(): return lax.ppermute(value, 'seq', pairs)  8.43 us
    convert_element_type x6, other arithmetic, summed(): return total.astype(BF)  7.97 us
  transfers between devices with their start and end apart: 39, of which 16 were waited for; matrix products, arithmetic and copies ran while one was open for 5% of the time, Pallas kernels for 4%

profile of v2, /device:TPU:0, one launch (start us, length us, event | category | flops | bytes accessed | tf_op | source)
XLA Modules:
  0.0 224.0 jit_solution(3479244624726358710)
XLA Ops:
  1.7 3.1 %collective-permute-start = (bf16[64,4096]{1,0:T(8,128)(2,1)S(1)}, bf16[64,4096]{1,0:T(8,128)(2,1)S(1)}, u32[]{:S(2)}, u32[]{:S(2)}) collective-permute-start(bf16[64,4096]{1,0:T(8,128)(2,1)S(1)} %dynamic-slice_bitcast_fusion), channel_id=1, source_target_pairs={{0,4},{4,0},{8,12},{12,8},{1,5},{5,1},{9,13},{13,9},{2,6},{6,2},{1... | collective-permute-start | bytes 1572872 | tf_op jit(solution)/shard_map/ppermute | solution.py:422
  4.8 4.5 %prune.1 = (bf16[1088,512]{1,0:T(8,128)(2,1)}, bf16[576,512]{1,0:T(8,128)(2,1)}, bf16[576,512]{1,0:T(8,128)(2,1)}, bf16[576,512]{1,0:T(8,128)(2,1)}) custom-call(s32[2,16,16]{2,1,0:T(8,128)} %mask_ref.1, bf16[1024,1024]{1,0:T(8,128)(2,1)} %key_ref.1, bf16[1024,1024]{1,0:T(8,128)(2,1)} %value_ref.1, bf16[64,1024]{1,0:T(8,128)(2,1)} %bitcast.56, ...), custom_call_target="tpu_custom_call" | custom-call | tf_op jit(solution)/shard_map/prune/pallas_call | solution.py:186
  9.3 2.6 %collective-permute-start.11 = (bf16[576,512]{1,0:T(8,128)(2,1)}, bf16[576,512]{1,0:T(8,128)(2,1)S(1)}, u32[]{:S(2)}, u32[]{:S(2)}) collective-permute-start(bf16[576,512]{1,0:T(8,128)(2,1)} %get-tuple-element.26), channel_id=1, source_target_pairs={{0,8},{4,12},{8,0},{12,4},{1,9},{5,13},{9,1},{13,5},{2,10},{6,14},... | collective-permute-start | bytes 1769480 | tf_op jit(solution)/shard_map/ppermute | solution.py:419
  12.6 10.6 %collective-permute-done.refs_1_ = bf16[64,4096]{1,0:T(8,128)(2,1)S(1)} collective-permute-done((bf16[64,4096]{1,0:T(8,128)(2,1)S(1)}, bf16[64,4096]{1,0:T(8,128)(2,1)S(1)}, u32[]{:S(2)}, u32[]{:S(2)}) %collective-permute-start) | collective-permute-done | bytes 524320 | tf_op jit(solution)/shard_map/ppermute | solution.py:422
  25.9 13.3 %collective-permute-done.11.refs_13_ = bf16[576,512]{1,0:T(8,128)(2,1)S(1)} collective-permute-done((bf16[576,512]{1,0:T(8,128)(2,1)}, bf16[576,512]{1,0:T(8,128)(2,1)S(1)}, u32[]{:S(2)}, u32[]{:S(2)}) %collective-permute-start.11) | collective-permute-done | bytes 589856 | tf_op jit(solution)/shard_map/ppermute | solution.py:419
  40.8 32.8 %collective-permute-start.10 = (bf16[576,512]{1,0:T(8,128)(2,1)}, bf16[576,512]{1,0:T(8,128)(2,1)S(1)}, u32[]{:S(2)}, u32[]{:S(2)}) collective-permute-start(bf16[576,512]{1,0:T(8,128)(2,1)} %get-tuple-element.25), channel_id=1, source_target_pairs={{0,4},{4,8},{8,12},{12,0},{1,5},{5,9},{9,13},{13,1},{2,6},{6,10},{... | collective-permute-start | bytes 1769480 | tf_op jit(solution)/shard_map/ppermute | solution.py:419
  73.5 6.6 %collective-permute-done.3.refs_4_ = bf16[64,4096]{1,0:T(8,128)(2,1)S(1)} collective-permute-done((bf16[64,4096]{1,0:T(8,128)(2,1)S(1)}, bf16[64,4096]{1,0:T(8,128)(2,1)S(1)}, u32[]{:S(2)}, u32[]{:S(2)}) %collective-permute-start.3) | collective-permute-done | bytes 524320 | tf_op jit(solution)/shard_map/ppermute | solution.py:422
  81.6 6.0 %collective-permute-done.10.refs_12_ = bf16[576,512]{1,0:T(8,128)(2,1)S(1)} collective-permute-done((bf16[576,512]{1,0:T(8,128)(2,1)}, bf16[576,512]{1,0:T(8,128)(2,1)S(1)}, u32[]{:S(2)}, u32[]{:S(2)}) %collective-permute-start.10) | collective-permute-done | bytes 589856 | tf_op jit(solution)/shard_map/ppermute | solution.py:419
  87.6 3.4 %collective-permute-start.8 = (bf16[64,4096]{1,0:T(8,128)(2,1)S(1)}, bf16[64,4096]{1,0:T(8,128)(2,1)S(1)}, u32[]{:S(2)}, u32[]{:S(2)}) collective-permute-start(bf16[64,4096]{1,0:T(8,128)(2,1)S(1)} %collective-permute-done.3.refs_4_), channel_id=1, source_target_pairs={{0,2},{1,3},{2,0},{3,1},{12,14},{13,15},{14,12},{15,13},{16,18},{1... | collective-permute-start | bytes 1572872 | tf_op jit(solution)/shard_map/ppermute | solution.py:426
  92.6 5.3 %collective-permute-done.12.refs_14_ = bf16[576,512]{1,0:T(8,128)(2,1)S(1)} collective-permute-done((bf16[576,512]{1,0:T(8,128)(2,1)}, bf16[576,512]{1,0:T(8,128)(2,1)S(1)}, u32[]{:S(2)}, u32[]{:S(2)}) %collective-permute-start.12) | collective-permute-done | bytes 589856 | tf_op jit(solution)/shard_map/ppermute | solution.py:419
  102.1 11.3 %collective-permute-done.4.refs_5_ = bf16[64,4096]{1,0:T(8,128)(2,1)S(1)} collective-permute-done((bf16[64,4096]{1,0:T(8,128)(2,1)S(1)}, bf16[64,4096]{1,0:T(8,128)(2,1)S(1)}, u32[]{:S(2)}, u32[]{:S(2)}) %collective-permute-start.4) | collective-permute-done | bytes 524320 | tf_op jit(solution)/shard_map/ppermute | solution.py:422
  113.9 7.2 %collective-permute-done.15.refs_17_ = bf16[576,512]{1,0:T(8,128)(2,1)S(1)} collective-permute-done((bf16[576,512]{1,0:T(8,128)(2,1)S(1)}, bf16[576,512]{1,0:T(8,128)(2,1)S(1)}, u32[]{:S(2)}, u32[]{:S(2)}) %collective-permute-start.15) | collective-permute-done | bytes 589856 | tf_op jit(solution)/shard_map/ppermute | solution.py:429
  121.2 1.9 collective-permute-start.9
  123.1 14.3 %collective-permute-done.9.refs_10_ = bf16[64,4096]{1,0:T(8,128)(2,1)S(1)} collective-permute-done((bf16[64,4096]{1,0:T(8,128)(2,1)S(1)}, bf16[64,4096]{1,0:T(8,128)(2,1)S(1)}, u32[]{:S(2)}, u32[]{:S(2)}) %collective-permute-start.9) | collective-permute-done | bytes 524320 | tf_op jit(solution)/shard_map/ppermute | solution.py:426
  139.4 20.5 %attend.1 = (bf16[2,2,64,256]{3,2,1,0:T(8,128)(2,1)S(1)}, bf16[2,2,64,256]{3,2,1,0:T(8,128)(2,1)S(1)}, bf16[2,512,512]{2,1,0:T(8,128)(2,1)}, bf16[2,4096,512]{2,...) custom-call(s32[4]{0:T(128)S(1)} %copy-done.2, ...), custom_call_target="tpu_custom_call" | custom-call | flops 8000000000 | bytes 31457280 | tf_op jit(solution)/shard_map/attend/pallas_call | solution.py:335
  162.4 6.8 %collective-permute-done.24 = bf16[2,64,1024]{2,1,0:T(8,128)(2,1)S(1)} collective-permute-done((bf16[2,64,1024]{2,1,0:T(8,128)(2,1)S(1)}, bf16[2,64,1024]{2,1,0:T(8,128)(2,1)S(1)}, u32[]{:S(2)}, u32[]{:S(2)}) %collective-permute-start.24) | collective-permute-done | bytes 262176 | tf_op jit(solution)/shard_map/ppermute | solution.py:426
  170.4 5.4 %near.1.own = f32[4,2,64,1024]{3,2,1,0:T(8,128)S(1)} custom-call(bf16[2,512,512]{2,1,0:T(8,128)(2,1)S(1)} %copy-done.1, bf16[2,4096,512]{2,1,0:T(8,128)(2,1)} %get-tuple-element.35.weight), custom_call_target="tpu_custom_call" | custom-call | flops 1000000000 | bytes 10485760 | tf_op jit(solution)/shard_map/near/pallas_call | solution.py:376
  177.4 4.2 %all-to-all-start = ((bf16[4,2,2,2,16,256]{5,4,1,3,2,0:T(8,128)(2,1)}), bf16[4,2,2,2,16,256]{5,4,1,3,2,0:T(8,128)(2,1)}, u32[]{:S(2)}, u32[]{:S(2)}) async-start(bf16[4,2,2,2,16,256]{5,4,1,3,2,0:T(8,128)(2,1)} %copy_bitcast_fusion), calls=%async_computation | async-start | bytes 524288 | tf_op jit(solution)/shard_map/all_to_all | solution.py:499
  181.6 3.6 %collective-permute-done.34 = bf16[2,64,1024]{2,1,0:T(8,128)(2,1)} collective-permute-done((bf16[2,64,1024]{2,1,0:T(8,128)(2,1)}, bf16[2,64,1024]{2,1,0:T(8,128)(2,1)}, u32[]{:S(2)}, u32[]{:S(2)}) %collective-permute-start.34) | collective-permute-done | bytes 262176 | tf_op jit(solution)/shard_map/ppermute | solution.py:426
  191.7 6.4 %collective-permute-done.35 = bf16[2,64,1024]{2,1,0:T(8,128)(2,1)S(1)} collective-permute-done((bf16[2,64,1024]{2,1,0:T(8,128)(2,1)S(1)}, bf16[2,64,1024]{2,1,0:T(8,128)(2,1)S(1)}, u32[]{:S(2)}, u32[]{:S(2)}) %collective-permute-start.35) | collective-permute-done | bytes 262176 | tf_op jit(solution)/shard_map/ppermute | solution.py:422
  205.1 5.0 %collective-permute-done.36 = bf16[2,64,1024]{2,1,0:T(8,128)(2,1)} collective-permute-done((bf16[2,64,1024]{2,1,0:T(8,128)(2,1)}, bf16[2,64,1024]{2,1,0:T(8,128)(2,1)}, u32[]{:S(2)}, u32[]{:S(2)}) %collective-permute-start.36) | collective-permute-done | bytes 262176 | tf_op jit(solution)/shard_map/ppermute | solution.py:422
  212.2 3.4 %collective-permute-done.31.near_sum = bf16[2,64,1024]{2,1,0:T(8,128)(2,1)S(1)} collective-permute-done((bf16[2,64,1024]{2,1,0:T(8,128)(2,1)S(1)}, bf16[2,64,1024]{2,1,0:T(8,128)(2,1)S(1)}, u32[]{:S(2)}, u32[]{:S(2)}) %collective-permute-start.31) | collective-permute-done | bytes 262176 | tf_op jit(solution)/shard_map/ppermute | solution.py:422
  215.6 4.5 %collective-permute-done.37.far_sum = bf16[2,64,1024]{2,1,0:T(8,128)(2,1)S(1)} collective-permute-done((bf16[2,64,1024]{2,1,0:T(8,128)(2,1)S(1)}, bf16[2,64,1024]{2,1,0:T(8,128)(2,1)S(1)}, u32[]{:S(2)}, u32[]{:S(2)}) %collective-permute-start.37) | collective-permute-done | bytes 262176 | tf_op jit(solution)/shard_map/ppermute | solution.py:422
  220.8 3.2 %final.1 = bf16[4,64,1024]{2,1,0:T(8,128)(2,1)} custom-call(f32[4,2,64,1024]{3,2,1,0:T(8,128)} %copy-done, bf16[4,2,64,1024]{3,2,1,0:T(8,128)(2,1)} %collective-permute-done.25.core, bf16[2,2,64,1024]{3,2,1,0:T(8,128)(2,1)} %collective-permute-done.26.near, bf16[2,64,1024]{2,1,0:T(8,128)(2,1)} %copy-done.3, bf16[2,64,1024]{2,1,0:T(8,128)(2,1)} %copy-done.4, ...), custom_call_target="tpu_custom_call" | custom-call | tf_op jit(solution)/shard_map/final/pallas_call | solution.py:401
  (114 shorter events, 37.0 us)
Async XLA Ops:
  1.7 21.4 %collective-permute-start = (bf16[64,4096]{1,0:T(8,128)(2,1)S(1)}, bf16[64,4096]{1,0:T(8,128)(2,1)S(1)}, u32[]{:S(2)}, u32[]{:S(2)}) collective-permute-start(bf16[64,4096]{1,0:T(8,128)(2,1)S(1)} %dynamic-slice_bitcast_fusion), channel_id=1, source_target_pairs={{0,4},{4,0},{8,12},{12,8},{1,5},{5,1},{9,13},{13,9},{2,6},{6,2},{1... | collective-permute-start | bytes 1572872 | tf_op jit(solution)/shard_map/ppermute | solution.py:422
  9.3 30.0 %collective-permute-start.11 = (bf16[576,512]{1,0:T(8,128)(2,1)}, bf16[576,512]{1,0:T(8,128)(2,1)S(1)}, u32[]{:S(2)}, u32[]{:S(2)}) collective-permute-start(bf16[576,512]{1,0:T(8,128)(2,1)} %get-tuple-element.26), channel_id=1, source_target_pairs={{0,8},{4,12},{8,0},{12,4},{1,9},{5,13},{9,1},{13,5},{2,10},{6,14},... | collective-permute-start | bytes 1769480 | tf_op jit(solution)/shard_map/ppermute | solution.py:419
  23.2 17.6 %collective-permute-start.2 = (bf16[64,4096]{1,0:T(8,128)(2,1)S(1)}, bf16[64,4096]{1,0:T(8,128)(2,1)S(1)}, u32[]{:S(2)}, u32[]{:S(2)}) collective-permute-start(bf16[64,4096]{1,0:T(8,128)(2,1)S(1)} %collective-permute-done.refs_1_), channel_id=1, source_target_pairs={{4,8},{8,4},{5,9},{9,5},{6,10},{10,6},{7,11},{11,7},{20,24},{24,20... | collective-permute-start | bytes 1572872 | tf_op jit(solution)/shard_map/ppermute | solution.py:422
  23.9 67.2 %collective-permute-start.16 = (bf16[1088,512]{1,0:T(8,128)(2,1)}, bf16[1088,512]{1,0:T(8,128)(2,1)S(1)}, u32[]{:S(2)}, u32[]{:S(2)}) collective-permute-start(bf16[1088,512]{1,0:T(8,128)(2,1)} %get-tuple-element.29.refs_11_), channel_id=1, source_target_pairs={{0,1},{1,0},{2,3},{3,2},{4,5},{5,4},{6,7},{7,6},{8,9},{9,8},{10,11... | collective-permute-start | bytes 3342344 | tf_op jit(solution)/shard_map/ppermute | solution.py:426
  23.9 49.6 %collective-permute-start.6 = (bf16[64,4096]{1,0:T(8,128)(2,1)S(1)}, bf16[64,4096]{1,0:T(8,128)(2,1)S(1)}, u32[]{:S(2)}, u32[]{:S(2)}) collective-permute-start(bf16[64,4096]{1,0:T(8,128)(2,1)S(1)} %collective-permute-done.1.refs_2_), channel_id=1, source_target_pairs={{4,6},{5,7},{6,4},{7,5},{8,10},{9,11},{10,8},{11,9},{20,22},{21,23... | collective-permute-start | bytes 1572872 | tf_op jit(solution)/shard_map/ppermute | solution.py:426
  24.6 55.5 %collective-permute-start.3 = (bf16[64,4096]{1,0:T(8,128)(2,1)S(1)}, bf16[64,4096]{1,0:T(8,128)(2,1)S(1)}, u32[]{:S(2)}, u32[]{:S(2)}) collective-permute-start(bf16[64,4096]{1,0:T(8,128)(2,1)S(1)} %collective-permute-done.1.refs_2_), channel_id=1, source_target_pairs={{4,0},{8,12},{5,1},{9,13},{6,2},{10,14},{7,3},{11,15},{20,16},{24,... | collective-permute-start | bytes 1572872 | tf_op jit(solution)/shard_map/ppermute | solution.py:422
  39.3 40.8 %collective-permute-start.5 = (bf16[64,4096]{1,0:T(8,128)(2,1)S(1)}, bf16[64,4096]{1,0:T(8,128)(2,1)S(1)}, u32[]{:S(2)}, u32[]{:S(2)}) collective-permute-start(bf16[64,4096]{1,0:T(8,128)(2,1)S(1)} %collective-permute-done.refs_1_), channel_id=1, source_target_pairs={{0,2},{1,3},{2,0},{3,1},{4,6},{5,7},{6,4},{7,5},{8,10},{9,11},{10,... | collective-permute-start | bytes 1572872 | tf_op jit(solution)/shard_map/ppermute | solution.py:426
  40.8 46.9 %collective-permute-start.10 = (bf16[576,512]{1,0:T(8,128)(2,1)}, bf16[576,512]{1,0:T(8,128)(2,1)S(1)}, u32[]{:S(2)}, u32[]{:S(2)}) collective-permute-start(bf16[576,512]{1,0:T(8,128)(2,1)} %get-tuple-element.25), channel_id=1, source_target_pairs={{0,4},{4,8},{8,12},{12,0},{1,5},{5,9},{9,13},{13,1},{2,6},{6,10},{... | collective-permute-start | bytes 1769480 | tf_op jit(solution)/shard_map/ppermute | solution.py:419
  73.5 24.4 %collective-permute-start.12 = (bf16[576,512]{1,0:T(8,128)(2,1)}, bf16[576,512]{1,0:T(8,128)(2,1)S(1)}, u32[]{:S(2)}, u32[]{:S(2)}) collective-permute-start(bf16[576,512]{1,0:T(8,128)(2,1)} %get-tuple-element.28), channel_id=1, source_target_pairs={{0,12},{4,0},{8,4},{12,8},{1,13},{5,1},{9,5},{13,9},{2,14},{6,2},{... | collective-permute-start | bytes 1769480 | tf_op jit(solution)/shard_map/ppermute | solution.py:419
  80.1 19.3 %collective-permute-start.18 = (bf16[576,512]{1,0:T(8,128)(2,1)S(1)}, bf16[576,512]{1,0:T(8,128)(2,1)S(1)}, u32[]{:S(2)}, u32[]{:S(2)}) collective-permute-start(bf16[576,512]{1,0:T(8,128)(2,1)S(1)} %collective-permute-done.11.refs_13_), channel_id=1, source_target_pairs={{0,1},{1,0},{2,3},{3,2},{4,5},{5,4},{6,7},{7,6},{8,9},{9,8},{10,11... | collective-permute-start | bytes 1769480 | tf_op jit(solution)/shard_map/ppermute | solution.py:426
  80.1 20.0 %collective-permute-start.14 = (bf16[576,512]{1,0:T(8,128)(2,1)S(1)}, bf16[576,512]{1,0:T(8,128)(2,1)S(1)}, u32[]{:S(2)}, u32[]{:S(2)}) collective-permute-start(bf16[576,512]{1,0:T(8,128)(2,1)S(1)} %collective-permute-done.11.refs_13_), channel_id=1, source_target_pairs={{0,16},{16,0},{1,17},{17,1},{2,18},{18,2},{3,19},{19,3},{4,20},{20... | collective-permute-start | bytes 1769480 | tf_op jit(solution)/shard_map/ppermute | solution.py:429
  91.1 22.3 %collective-permute-start.13 = (bf16[576,512]{1,0:T(8,128)(2,1)S(1)}, bf16[576,512]{1,0:T(8,128)(2,1)S(1)}, u32[]{:S(2)}, u32[]{:S(2)}) collective-permute-start(bf16[576,512]{1,0:T(8,128)(2,1)S(1)} %collective-permute-done.10.refs_12_), channel_id=1, source_target_pairs={{0,16},{16,0},{1,17},{17,1},{2,18},{18,2},{3,19},{19,3},{4,20},{20... | collective-permute-start | bytes 1769480 | tf_op jit(solution)/shard_map/ppermute | solution.py:429
  97.9 23.2 %collective-permute-start.15 = (bf16[576,512]{1,0:T(8,128)(2,1)S(1)}, bf16[576,512]{1,0:T(8,128)(2,1)S(1)}, u32[]{:S(2)}, u32[]{:S(2)}) collective-permute-start(bf16[576,512]{1,0:T(8,128)(2,1)S(1)} %collective-permute-done.12.refs_14_), channel_id=1, source_target_pairs={{0,16},{16,0},{1,17},{17,1},{2,18},{18,2},{3,19},{19,3},{4,20},{20... | collective-permute-start | bytes 1769480 | tf_op jit(solution)/shard_map/ppermute | solution.py:429
  101.5 19.7 %collective-permute-start.17 = (bf16[576,512]{1,0:T(8,128)(2,1)S(1)}, bf16[576,512]{1,0:T(8,128)(2,1)S(1)}, u32[]{:S(2)}, u32[]{:S(2)}) collective-permute-start(bf16[576,512]{1,0:T(8,128)(2,1)S(1)} %collective-permute-done.10.refs_12_), channel_id=1, source_target_pairs={{0,1},{1,0},{2,3},{3,2},{4,5},{5,4},{6,7},{7,6},{8,9},{9,8},{10,11... | collective-permute-start | bytes 1769480 | tf_op jit(solution)/shard_map/ppermute | solution.py:426
  101.6 21.5 %collective-permute-start.21 = (bf16[576,512]{1,0:T(8,128)(2,1)S(1)}, bf16[576,512]{1,0:T(8,128)(2,1)S(1)}, u32[]{:S(2)}, u32[]{:S(2)}) collective-permute-start(bf16[576,512]{1,0:T(8,128)(2,1)S(1)} %collective-permute-done.14.refs_16_), channel_id=1, source_target_pairs={{0,1},{1,0},{2,3},{3,2},{4,5},{5,4},{6,7},{7,6},{8,9},{9,8},{10,11... | collective-permute-start | bytes 1769480 | tf_op jit(solution)/shard_map/ppermute | solution.py:426
  113.4 24.0 %collective-permute-start.19 = (bf16[576,512]{1,0:T(8,128)(2,1)S(1)}, bf16[576,512]{1,0:T(8,128)(2,1)S(1)}, u32[]{:S(2)}, u32[]{:S(2)}) collective-permute-start(bf16[576,512]{1,0:T(8,128)(2,1)S(1)} %collective-permute-done.12.refs_14_), channel_id=1, source_target_pairs={{0,1},{1,0},{2,3},{3,2},{4,5},{5,4},{6,7},{7,6},{8,9},{9,8},{10,11... | collective-permute-start | bytes 1769480 | tf_op jit(solution)/shard_map/ppermute | solution.py:426
  113.4 24.0 %collective-permute-start.20 = (bf16[576,512]{1,0:T(8,128)(2,1)S(1)}, bf16[576,512]{1,0:T(8,128)(2,1)S(1)}, u32[]{:S(2)}, u32[]{:S(2)}) collective-permute-start(bf16[576,512]{1,0:T(8,128)(2,1)S(1)} %collective-permute-done.13.refs_15_), channel_id=1, source_target_pairs={{0,1},{1,0},{2,3},{3,2},{4,5},{5,4},{6,7},{7,6},{8,9},{9,8},{10,11... | collective-permute-start | bytes 1769480 | tf_op jit(solution)/shard_map/ppermute | solution.py:426
  121.1 16.3 %collective-permute-start.22 = (bf16[576,512]{1,0:T(8,128)(2,1)S(1)}, bf16[576,512]{1,0:T(8,128)(2,1)S(1)}, u32[]{:S(2)}, u32[]{:S(2)}) collective-permute-start(bf16[576,512]{1,0:T(8,128)(2,1)S(1)} %collective-permute-done.15.refs_17_), channel_id=1, source_target_pairs={{0,1},{1,0},{2,3},{3,2},{4,5},{5,4},{6,7},{7,6},{8,9},{9,8},{10,11... | collective-permute-start | bytes 1769480 | tf_op jit(solution)/shard_map/ppermute | solution.py:426
  159.9 25.6 %collective-permute-start.25 = (bf16[4,2,64,1024]{3,2,1,0:T(8,128)(2,1)}, bf16[4,2,64,1024]{3,2,1,0:T(8,128)(2,1)}, u32[]{:S(2)}, u32[]{:S(2)}) collective-permute-start(bf16[4,2,64,1024]{3,2,1,0:T(8,128)(2,1)} %get-tuple-element.36), channel_id=1, source_target_pairs={{0,1},{1,0},{2,3},{3,2},{4,5},{5,4},{6,7},{7,6},{8,9},{9,8},{10,11... | collective-permute-start | bytes 3145736 | tf_op jit(solution)/shard_map/ppermute | solution.py:426
  160.4 16.3 %collective-permute-start.23 = (bf16[2,2,64,256]{3,2,1,0:T(8,128)(2,1)S(1)}, bf16[2,2,64,256]{3,2,1,0:T(8,128)(2,1)S(1)}, u32[]{:S(2)}, u32[]{:S(2)}) collective-permute-start(bf16[2,2,64,256]{3,2,1,0:T(8,128)(2,1)S(1)} %get-tuple-element.46), channel_id=1, source_target_pairs={{0,1},{1,0},{2,3},{3,2},{4,5},{5,4},{6,7},{7,6},{8,9},{9,8},{10,11... | collective-permute-start | bytes 393224 | tf_op jit(solution)/shard_map/ppermute | solution.py:426
  160.6 26.1 %collective-permute-start.28 = (bf16[2,64,1024]{2,1,0:T(8,128)(2,1)}, bf16[2,64,1024]{2,1,0:T(8,128)(2,1)}, u32[]{:S(2)}, u32[]{:S(2)}) collective-permute-start(bf16[2,64,1024]{2,1,0:T(8,128)(2,1)} %get-tuple-element.39), channel_id=1, source_target_pairs={{0,2},{1,3},{2,0},{3,1},{4,6},{5,7},{6,4},{7,5},{8,10},{9,11},{10,... | collective-permute-start | bytes 786440 | tf_op jit(solution)/shard_map/ppermute | solution.py:426
  162.4 29.3 %collective-permute-start.33 = (bf16[2,64,1024]{2,1,0:T(8,128)(2,1)S(1)}, bf16[2,64,1024]{2,1,0:T(8,128)(2,1)}, u32[]{:S(2)}, u32[]{:S(2)}) collective-permute-start(bf16[2,64,1024]{2,1,0:T(8,128)(2,1)S(1)} %get-tuple-element.41), channel_id=1, source_target_pairs={{0,3},{1,2},{2,1},{3,0},{4,7},{5,6},{6,5},{7,4},{8,11},{9,10},{10,... | collective-permute-start | bytes 786440 | tf_op jit(solution)/shard_map/ppermute | solution.py:426
  177.4 23.6 %all-to-all-start = ((bf16[4,2,2,2,16,256]{5,4,1,3,2,0:T(8,128)(2,1)}), bf16[4,2,2,2,16,256]{5,4,1,3,2,0:T(8,128)(2,1)}, u32[]{:S(2)}, u32[]{:S(2)}) async-start(bf16[4,2,2,2,16,256]{5,4,1,3,2,0:T(8,128)(2,1)} %copy_bitcast_fusion), calls=%async_computation | async-start | bytes 524288 | tf_op jit(solution)/shard_map/all_to_all | solution.py:499
  185.2 16.8 %collective-permute-start.26 = (bf16[2,2,64,1024]{3,2,1,0:T(8,128)(2,1)S(1)}, bf16[2,2,64,1024]{3,2,1,0:T(8,128)(2,1)}, u32[]{:S(2)}, u32[]{:S(2)}) collective-permute-start(bf16[2,2,64,1024]{3,2,1,0:T(8,128)(2,1)S(1)} %get-tuple-element.37), channel_id=1, source_target_pairs={{0,2},{1,3},{2,0},{3,1},{4,6},{5,7},{6,4},{7,5},{8,10},{9,11},{10,... | collective-permute-start | bytes 1572872 | tf_op jit(solution)/shard_map/ppermute | solution.py:426
  (37 other events, 808.2 us)

commit v3 on v2

--- a/solution.py
+++ b/solution.py
@@ -146,14 +146,6 @@
     )
 
 
-def gray(value):
-    return lax.bitwise_xor(value, value // 2)
-
-
-def ring_back(s, k):
-    return gray(lax.rem(gray(s) + SEQ - k, SEQ))
-
-
 def prune_kernel(mask_ref, key_ref, value_ref, query_ref, cot_ref, own_ref, *message_refs):
     s, g = lax.axis_index("seq"), lax.axis_index("grp")
     left = lax.broadcasted_iota(jnp.int32, (1, 128), 1) < TILE
@@ -176,8 +168,8 @@
         out_ref[tiles * TILE :, 0:256] = query_ref[:, at]
         out_ref[tiles * TILE :, 256:512] = cot_ref[:, at]
 
-    for j in (2, 1, 3):
-        write(message_refs[j - 1], g * 8, 8, lax.rem(s + j, SEQ))
+    for k in (2, 3, 1):
+        write(message_refs[k - 1], g * 8, 8, lax.bitwise_xor(s, k))
     write(own_ref, 0, 16, s)
 
 
@@ -214,44 +206,32 @@
 
 def main_kernel(lengths, *refs):
     (
-        enc, ea, eb, ec, ed, ef, xa, xb, xc, xd, xf,
+        enc, e1, e2, e3, x1, x2, x3,
         w_own, z1, z2, z3, y1, y2, y3,
         v_own, vz1, vz2, vz3, vy1, vy2, vy3,
         att_ref, qg_ref, grad_ref, weight_ref,
-        a1, a2, a30, b1, b2, b3, b0, core_ref,
+        a3, b3, a2, b2, b1, a10, b0, core_ref,
         enc_s, w_s, qc_s, grad_s, part_s, sems,
     ) = refs
     s, g, h = lax.axis_index("seq"), lax.axis_index("grp"), lax.axis_index("head")
     c = lax.rem(h, 2)
     x = h // 2
-    middle = jnp.logical_or(s == 1, s == 2)
     copies = []
 
-    def move(src, dst, other=None):
-        sem = sems.at[len(copies)]
-        copy = pltpu.make_async_copy(src, dst, sem)
-        if other is None:
-            copy.start()
-        else:
-            pl.when(middle)(lambda: copy.start())
-            pl.when(jnp.logical_not(middle))(lambda: pltpu.make_async_copy(other, dst, sem).start())
+    def move(src, dst):
+        copy = pltpu.make_async_copy(src, dst, sems.at[len(copies)])
+        copy.start()
         copies.append(copy)
 
     def rows_of(doc, at):
         return enc_s.at[doc, pl.ds(pl.multiple_of(at * 64, 64), 64)]
 
-    low_half = s < 2
-    second = jnp.where(low_half, 2, 1)
-    third = jnp.where(low_half, 3, 0)
     for i in range(2):
         move(enc.at[2 * i + c], rows_of(i, s))
-    for doc, first_from, second_from, third_from in (
-        (x, ea, (eb, ed), (ec, ef)),
-        (1 - x, xa, (xb, xd), (xc, xf)),
-    ):
-        move(first_from, rows_of(doc, lax.bitwise_xor(s, 1)))
-        move(second_from[0], rows_of(doc, second), second_from[1])
-        move(third_from[0], rows_of(doc, third), third_from[1])
+    for k, (mine, other) in enumerate(((e1, x1), (e2, x2), (e3, x3))):
+        at = lax.bitwise_xor(s, k + 1)
+        move(mine, rows_of(x, at))
+        move(other, rows_of(1 - x, at))
 
     def weight_rows(core, at, half, count):
         return w_s.at[core, pl.ds(pl.multiple_of(at * 1024 + half * PIECE, PIECE), count)]
@@ -263,7 +243,7 @@
         move(own.at[0 : 2 * PIECE], weight_rows(core, s, 0, 2 * PIECE))
         move(own.at[2 * PIECE : 2 * PIECE + 64], qc_s.at[core, s])
         for j in range(3):
-            at = lax.rem(s + 3 - j, SEQ)
+            at = lax.bitwise_xor(s, j + 1)
             move(zs[j].at[0:PIECE], weight_rows(core, at, g, PIECE))
             move(ys[j].at[0:PIECE], weight_rows(core, at, 1 - g, PIECE))
             move(zs[j].at[PIECE:SENT], qc_s.at[core, at])
@@ -313,13 +293,13 @@
 
     cores = [core_ref.at[k] for k in range(4)]
     for flip, outs in (
-        (2, (a30.at[1], a1, a2, a30.at[0])),
+        (2, (a10.at[1], a10.at[0], a2, a3)),
         (3, (b0, b1, b2, b3)),
         (1, cores),
     ):
         partial_blocks(lax.bitwise_xor(h, flip), grad_s, w_s, part_s)
         for k in range(4):
-            at = pl.ds(pl.multiple_of(ring_back(s, k) * 64, 64), 64)
+            at = pl.ds(pl.multiple_of(lax.bitwise_xor(s, k) * 64, 64), 64)
             for doc in range(2):
                 outs[k][doc] = part_s[doc, at, :].astype(BF)
     grad_ref[...] = grad_s[...]
@@ -340,9 +320,9 @@
             jax.ShapeDtypeStruct((2, 512, 512), BF),
             jax.ShapeDtypeStruct((2, 4096, 512), BF),
         ]
-        + [piece] * 2
+        + [piece] * 5
         + [jax.ShapeDtypeStruct((2, 2, 64, 1024), BF)]
-        + [piece] * 4
+        + [piece]
         + [jax.ShapeDtypeStruct((4, 2, 64, 1024), BF)],
         in_specs=[smem] + [here] * len(arrays),
         out_specs=[vmem] * 3 + [here] + [vmem] * 8,
@@ -366,7 +346,7 @@
     s, h = lax.axis_index("seq"), lax.axis_index("head")
     partial_blocks(h, grad, weight, part_s)
     for k in range(4):
-        at = pl.ds(pl.multiple_of(ring_back(s, k) * 64, 64), 64)
+        at = pl.ds(pl.multiple_of(lax.bitwise_xor(s, k) * 64, 64), 64)
         for doc in range(2):
             own_ref[k, doc] = part_s[doc, at, :]
 
@@ -387,11 +367,13 @@
     )(grad, weight)
 
 
-def final_kernel(own, core, near, far, near_sum, far_sum, out_ref):
+def final_kernel(own, core, near, far, near1, near2, far1, far2, out_ref):
     c = lax.rem(lax.axis_index("head"), 2)
     for i in range(2):
-        mine = own[0, i] + near[1, i].astype(F32) + near_sum[i].astype(F32)
-        theirs = core[0, i].astype(F32) + far[i].astype(F32) + far_sum[i].astype(F32)
+        mine = (own[0, i] + near[1, i].astype(F32)) + (near1[i].astype(F32) + near2[i].astype(F32))
+        theirs = (core[0, i].astype(F32) + far[i].astype(F32)) + (
+            far1[i].astype(F32) + far2[i].astype(F32)
+        )
         out_ref[2 * i + c] = mine.astype(BF)
         out_ref[2 * i + 1 - c] = theirs.astype(BF)
 
@@ -415,67 +397,45 @@
     h = lax.axis_index("head")
     c = lax.rem(h, 2)
 
-    def shift(value, j):
-        return lax.ppermute(value, "seq", [(a, (a + j) % SEQ) for a in range(SEQ)])
-
-    def along(value, pairs):
-        return lax.ppermute(value, "seq", pairs)
-
-    def flip(value, bits, seqs=range(SEQ)):
-        pairs = [(a * 4 + b, a * 4 + (b ^ bits)) for a in seqs for b in range(4)]
-        return lax.ppermute(value, ("seq", "head"), pairs)
+    def along(value, k):
+        return lax.ppermute(value, "seq", [(a, a ^ k) for a in range(SEQ)])
+
+    def flip(value, bits):
+        return lax.ppermute(value, "head", [(a, a ^ bits) for a in range(4)])
 
     def across(value):
         return lax.ppermute(value, "grp", [(0, 1), (1, 0)])
 
-    inner, ends = (1, 2), (0, 3)
-    outward = [(1, 0), (2, 3)]
-    swap = [(1, 2), (2, 1)]
     e0 = lax.dynamic_index_in_dim(encoder, h, 0, keepdims=False)
-    ea = along(e0, [(0, 1), (1, 0), (2, 3), (3, 2)])
-    eb = along(e0, swap)
+    e2 = along(e0, 2)
+    e1 = along(e0, 1)
     w_own, m1, m2, m3 = prune(
         tile_mask, key_weight, value_weight, queries.reshape(64, 1024), cotangent.reshape(64, 1024)
     )
-    z2 = shift(m2, 2)
-    v_own = flip(after(w_own, m2), 1)
-    xa = flip(ea, 2)
-    ec = along(ea, swap)
-    z1 = shift(after(m1, ea), 1)
-    xb = flip(eb, 2, inner)
-    ed = along(eb, outward)
-    y2 = across(z2)
-    vz2 = flip(z2, 1)
-    xc = flip(ec, 2, inner)
-    ef = along(ec, outward)
-    z3 = shift(after(m3, ec), 3)
-    xd = flip(ed, 2, ends)
-    y1 = across(z1)
-    vz1 = flip(z1, 1)
-    vy2 = flip(y2, 1)
-    xf = flip(ef, 2, ends)
-    y3 = across(z3)
-    vz3 = flip(z3, 1)
-    vy1 = flip(y1, 1)
-    vy3 = flip(y3, 1)
+    z2 = along(m2, 2)
+    e3 = along(e2, 1)
+    z3 = along(after(m3, e1), 3)
+    z1 = along(after(m1, e2), 1)
+    x1, x2, x3 = flip(e1, 2), flip(e2, 2), flip(e3, 2)
+    y1, y2, y3 = across(z1), across(z2), across(z3)
+    v_own = flip(after(w_own, e1), 1)
+    vz1, vz2, vz3 = flip(z1, 1), flip(z2, 1), flip(z3, 1)
+    vy1, vy2, vy3 = flip(y1, 1), flip(y2, 1), flip(y3, 1)
 
     outs = main_call(
         lengths,
-        [encoder, ea, eb, ec, ed, ef, xa, xb, xc, xd, xf]
+        [encoder, e1, e2, e3, x1, x2, x3]
         + [w_own, z1, z2, z3, y1, y2, y3]
         + [v_own, vz1, vz2, vz3, vy1, vy2, vy3],
     )
     att, qgrad, grad, weight = outs[:4]
-    a1, a2, a30, b1, b2, b3, b0, to_core = outs[4:]
-
-    def onward(value):
-        pairs = [(0, 1), (1, 3), (3, 2), (2, 0)]
-        return along(value, pairs)
-
+    a3, b3, a2, b2, b1, a10, b0, to_core = outs[4:]
     from_core = flip(to_core, 1)
-    a1, b1, a2, b2 = flip(a1, 2), flip(b1, 3), flip(a2, 2), flip(b2, 3)
-    a30, b3, b0 = flip(a30, 2), flip(b3, 3), flip(b0, 3)
-    own = near_call(after(grad, a1), weight)
+    a3, b3 = flip(a3, 2), flip(b3, 3)
+    a2, b2 = flip(after(a2, a3), 2), flip(after(b2, a3), 3)
+    b1, a10 = flip(after(b1, a2), 3), flip(after(a10, a2), 2)
+    b0 = flip(b0, 3)
+    own = near_call(after(grad, a3), weight)
 
     def summed(*parts):
         total = parts[0].astype(F32)
@@ -483,14 +443,15 @@
             total = total + part.astype(F32)
         return total.astype(BF)
 
-    near1 = onward(summed(own[1], a1))
-    far1 = onward(summed(from_core[1], b1))
-    near2 = onward(summed(own[2], a2, near1))
-    far2 = onward(summed(from_core[2], b2, far1))
-    near3 = onward(summed(own[3], a30[0], near2))
-    far3 = onward(summed(from_core[3], b3, far2))
+    near3 = along(summed(own[3], a3), 1)
+    far3 = along(summed(from_core[3], b3), 1)
+    near2 = along(summed(own[2], a2, near3), 2)
+    far2 = summed(from_core[2], b2, far3)
+    far1 = along(summed(from_core[1], after(b1, far2)), 1)
+    far2 = along(far2, 2)
+    near1 = along(summed(own[1], a10[0]), 1)
     encoder_grad = small_call(
-        final_kernel, (DOCS, 64, 1024), "final", own, from_core, a30, b0, near3, far3
+        final_kernel, (DOCS, 64, 1024), "final", own, from_core, a10, b0, near1, near2, far1, far2
     )
 
     front = jnp.stack([att, qgrad], axis=1)

time: 225 us -> 217 us (0.964)
  starting transfers between devices: 66.3 us -> 41.9 us
  waiting for transfers between devices: 108 us -> 125 us
    ppermute x35 -> x31, starting transfers between devices: 57.5 us -> 33.1 us  [the longest x12 18.9 us: along(): return lax.ppermute(value, 'seq', [(a, a ^ k) for a in range(SEQ)])]
    ppermute x35 -> x31, waiting for transfers between devices: 100 us -> 111 us  [the longest x12 84.6 us: along(): return lax.ppermute(value, 'seq', [(a, a ^ k) for a in range(SEQ)])]
    ppermute x3, waiting for transfers between devices: 7.24 us -> 13.3 us  [across(): return lax.ppermute(value, 'grp', [(0, 1), (1, 0)])]
  transfers between devices with their start and end apart: 39 -> 35, of which waited for: 16 -> 16; matrix products, arithmetic and copies ran while one was open for 5% -> 5% of each run, Pallas kernels for 4% -> 5%
where the time goes in v3:
time: 217 us; the launch traced here: 216 us
  waiting for transfers between devices  125 us (58%)
  starting transfers between devices  41.9 us (19%)
  Pallas kernels  33.3 us (15%)
  other arithmetic  8.62 us (4%)
  local copies, waits for them, and re-layouts  6.26 us (3%)
    ppermute x12, waiting for transfers between devices, along(): return lax.ppermute(value, 'seq', [(a, a ^ k) for a in range(SEQ)])  84.6 us
    ppermute x19, waiting for transfers between devices, flip(): return lax.ppermute(value, 'head', [(a, a ^ bits) for a in range(4)])  26.4 us
    pallas_call x1, Pallas kernels, main_call(): pl.pallas_call(main_kernel, out_shape=[front, front, jax.ShapeDtypeStruct...  19.9 us
    ppermute x12, starting transfers between devices, along(): return lax.ppermute(value, 'seq', [(a, a ^ k) for a in range(SEQ)])  18.9 us
    ppermute x19, starting transfers between devices, flip(): return lax.ppermute(value, 'head', [(a, a ^ bits) for a in range(4)])  14.2 us
    ppermute x3, waiting for transfers between devices, across(): return lax.ppermute(value, 'grp', [(0, 1), (1, 0)])  13.3 us
    convert_element_type x6, other arithmetic, summed(): return total.astype(BF)  7.82 us
    pallas_call x1, Pallas kernels, near_call(): pl.pallas_call(near_kernel, out_shape=jax.ShapeDtypeStruct((4, 2, 64, 102...  5.44 us
  transfers between devices with their start and end apart: 35, of which 16 were waited for; matrix products, arithmetic and copies ran while one was open for 5% of the time, Pallas kernels for 5%

profile of v3, /device:TPU:0, one launch (start us, length us, event | category | flops | bytes accessed | tf_op | source)
XLA Modules:
  0.0 216.5 jit_solution(4012778569097819313)
XLA Ops:
  1.7 4.1 %collective-permute-start.1 = (bf16[64,4096]{1,0:T(8,128)(2,1)S(1)}, bf16[64,4096]{1,0:T(8,128)(2,1)S(1)}, u32[]{:S(2)}, u32[]{:S(2)}) collective-permute-start(bf16[64,4096]{1,0:T(8,128)(2,1)S(1)} %dynamic-slice_bitcast_fusion), channel_id=1, source_target_pairs={{0,8},{4,12},{8,0},{12,4},{1,9},{5,13},{9,1},{13,5},{2,10},{6,14},... | collective-permute-start | bytes 1572872 | tf_op jit(solution)/shard_map/ppermute | solution.py:401
  5.8 4.5 %prune.1 = (bf16[1088,512]{1,0:T(8,128)(2,1)}, bf16[576,512]{1,0:T(8,128)(2,1)}, bf16[576,512]{1,0:T(8,128)(2,1)}, bf16[576,512]{1,0:T(8,128)(2,1)}) custom-call(s32[2,16,16]{2,1,0:T(8,128)} %mask_ref.1, bf16[1024,1024]{1,0:T(8,128)(2,1)} %key_ref.1, bf16[1024,1024]{1,0:T(8,128)(2,1)} %value_ref.1, bf16[64,1024]{1,0:T(8,128)(2,1)} %bitcast.52, ...), custom_call_target="tpu_custom_call" | custom-call | tf_op jit(solution)/shard_map/prune/pallas_call | solution.py:178
  10.3 1.9 collective-permute-start
  12.2 30.2 %collective-permute-done.1.refs_2_ = bf16[64,4096]{1,0:T(8,128)(2,1)S(1)} collective-permute-done((bf16[64,4096]{1,0:T(8,128)(2,1)S(1)}, bf16[64,4096]{1,0:T(8,128)(2,1)S(1)}, u32[]{:S(2)}, u32[]{:S(2)}) %collective-permute-start.1) | collective-permute-done | bytes 524320 | tf_op jit(solution)/shard_map/ppermute | solution.py:401
  44.3 2.5 %collective-permute-start.8 = (bf16[576,512]{1,0:T(8,128)(2,1)}, bf16[576,512]{1,0:T(8,128)(2,1)S(1)}, u32[]{:S(2)}, u32[]{:S(2)}) collective-permute-start(bf16[576,512]{1,0:T(8,128)(2,1)} %get-tuple-element.33), channel_id=1, source_target_pairs={{0,12},{4,8},{8,4},{12,0},{1,13},{5,9},{9,5},{13,1},{2,14},{6,10},... | collective-permute-start | bytes 1769480 | tf_op jit(solution)/shard_map/ppermute | solution.py:401
  47.9 7.3 %collective-permute-done.7.refs_9_ = bf16[576,512]{1,0:T(8,128)(2,1)S(1)} collective-permute-done((bf16[576,512]{1,0:T(8,128)(2,1)}, bf16[576,512]{1,0:T(8,128)(2,1)S(1)}, u32[]{:S(2)}, u32[]{:S(2)}) %collective-permute-start.7) | collective-permute-done | bytes 589856 | tf_op jit(solution)/shard_map/ppermute | solution.py:401
  57.0 21.2 %collective-permute-done.2.refs_3_ = bf16[64,4096]{1,0:T(8,128)(2,1)S(1)} collective-permute-done((bf16[64,4096]{1,0:T(8,128)(2,1)S(1)}, bf16[64,4096]{1,0:T(8,128)(2,1)S(1)}, u32[]{:S(2)}, u32[]{:S(2)}) %collective-permute-start.2) | collective-permute-done | bytes 524320 | tf_op jit(solution)/shard_map/ppermute | solution.py:401
  80.3 10.5 %collective-permute-done.6.refs_8_ = bf16[576,512]{1,0:T(8,128)(2,1)S(1)} collective-permute-done((bf16[576,512]{1,0:T(8,128)(2,1)}, bf16[576,512]{1,0:T(8,128)(2,1)S(1)}, u32[]{:S(2)}, u32[]{:S(2)}) %collective-permute-start.6) | collective-permute-done | bytes 589856 | tf_op jit(solution)/shard_map/ppermute | solution.py:401
  94.4 11.6 %collective-permute-done.5.refs_6_ = bf16[64,4096]{1,0:T(8,128)(2,1)S(1)} collective-permute-done((bf16[64,4096]{1,0:T(8,128)(2,1)S(1)}, bf16[64,4096]{1,0:T(8,128)(2,1)S(1)}, u32[]{:S(2)}, u32[]{:S(2)}) %collective-permute-start.5) | collective-permute-done | bytes 524320 | tf_op jit(solution)/shard_map/ppermute | solution.py:404
  107.0 12.2 %collective-permute-done.9.refs_11_ = bf16[576,512]{1,0:T(8,128)(2,1)S(1)} collective-permute-done((bf16[576,512]{1,0:T(8,128)(2,1)S(1)}, bf16[576,512]{1,0:T(8,128)(2,1)S(1)}, u32[]{:S(2)}, u32[]{:S(2)}) %collective-permute-start.9) | collective-permute-done | bytes 589856 | tf_op jit(solution)/shard_map/ppermute | solution.py:407
  119.3 1.9 collective-permute-done.16.refs_18_
  122.2 19.9 %attend.1 = (bf16[2,2,64,256]{3,2,1,0:T(8,128)(2,1)S(1)}, bf16[2,2,64,256]{3,2,1,0:T(8,128)(2,1)S(1)}, bf16[2,512,512]{2,1,0:T(8,128)(2,1)}, bf16[2,4096,512]{2,...) custom-call(s32[4]{0:T(128)S(1)} %copy-done.2, ...), custom_call_target="tpu_custom_call" | custom-call | flops 8000000000 | bytes 31457280 | tf_op jit(solution)/shard_map/attend/pallas_call | solution.py:315
  145.8 5.7 %collective-permute-done.20 = bf16[2,64,1024]{2,1,0:T(8,128)(2,1)S(1)} collective-permute-done((bf16[2,64,1024]{2,1,0:T(8,128)(2,1)S(1)}, bf16[2,64,1024]{2,1,0:T(8,128)(2,1)S(1)}, u32[]{:S(2)}, u32[]{:S(2)}) %collective-permute-start.20) | collective-permute-done | bytes 262176 | tf_op jit(solution)/shard_map/ppermute | solution.py:404
  154.2 5.4 %near.1.own = f32[4,2,64,1024]{3,2,1,0:T(8,128)S(1)} custom-call(bf16[2,512,512]{2,1,0:T(8,128)(2,1)S(1)} %copy-done.1, bf16[2,4096,512]{2,1,0:T(8,128)(2,1)} %get-tuple-element.40.weight), custom_call_target="tpu_custom_call" | custom-call | flops 1000000000 | bytes 10485760 | tf_op jit(solution)/shard_map/near/pallas_call | solution.py:356
  160.5 7.2 %collective-permute-done.22 = bf16[2,64,1024]{2,1,0:T(8,128)(2,1)S(1)} collective-permute-done((bf16[2,64,1024]{2,1,0:T(8,128)(2,1)}, bf16[2,64,1024]{2,1,0:T(8,128)(2,1)S(1)}, u32[]{:S(2)}, u32[]{:S(2)}) %collective-permute-start.22) | collective-permute-done | bytes 262176 | tf_op jit(solution)/shard_map/ppermute | solution.py:404
  170.1 5.3 %all-to-all-start = ((bf16[4,2,2,2,16,256]{5,4,1,3,2,0:T(8,128)(2,1)}), bf16[4,2,2,2,16,256]{5,4,1,3,2,0:T(8,128)(2,1)}, u32[]{:S(2)}, u32[]{:S(2)}) async-start(bf16[4,2,2,2,16,256]{5,4,1,3,2,0:T(8,128)(2,1)} %copy_bitcast_fusion), calls=%async_computation | async-start | bytes 524288 | tf_op jit(solution)/shard_map/all_to_all | solution.py:460
  178.9 2.0 collective-permute-start.31
  185.0 1.9 collective-permute-start.27
  190.8 1.9 collective-permute-start.33
  193.8 2.0 collective-permute-start.32
  196.6 2.9 %collective-permute-done.27.near2 = bf16[2,64,1024]{2,1,0:T(8,128)(2,1)S(1)} collective-permute-done((bf16[2,64,1024]{2,1,0:T(8,128)(2,1)}, bf16[2,64,1024]{2,1,0:T(8,128)(2,1)S(1)}, u32[]{:S(2)}, u32[]{:S(2)}) %collective-permute-start.27) | collective-permute-done | bytes 262176 | tf_op jit(solution)/shard_map/ppermute | solution.py:401
  199.6 3.2 %collective-permute-done.25.near1 = bf16[2,64,1024]{2,1,0:T(8,128)(2,1)S(1)} collective-permute-done((bf16[2,64,1024]{2,1,0:T(8,128)(2,1)S(1)}, bf16[2,64,1024]{2,1,0:T(8,128)(2,1)S(1)}, u32[]{:S(2)}, u32[]{:S(2)}) %collective-permute-start.25) | collective-permute-done | bytes 262176 | tf_op jit(solution)/shard_map/ppermute | solution.py:401
  202.7 8.9 %collective-permute-done.32.far1 = bf16[2,64,1024]{2,1,0:T(8,128)(2,1)S(1)} collective-permute-done((bf16[2,64,1024]{2,1,0:T(8,128)(2,1)S(1)}, bf16[2,64,1024]{2,1,0:T(8,128)(2,1)S(1)}, u32[]{:S(2)}, u32[]{:S(2)}) %collective-permute-start.32) | collective-permute-done | bytes 262176 | tf_op jit(solution)/shard_map/ppermute | solution.py:401
  213.1 3.4 %final.1 = bf16[4,64,1024]{2,1,0:T(8,128)(2,1)} custom-call(f32[4,2,64,1024]{3,2,1,0:T(8,128)} %copy-done, bf16[4,2,64,1024]{3,2,1,0:T(8,128)(2,1)} %collective-permute-done.21.core, bf16[2,2,64,1024]{3,2,1,0:T(8,128)(2,1)} %collective-permute-done.23.near, bf16[2,64,1024]{2,1,0:T(8,128)(2,1)} %collective-permute-done.24.far, ...), custom_call_target="tpu_custom_call" | custom-call | tf_op jit(solution)/shard_map/final/pallas_call | solution.py:383
  (106 shorter events, 37.9 us)
Async XLA Ops:
  1.7 40.7 %collective-permute-start.1 = (bf16[64,4096]{1,0:T(8,128)(2,1)S(1)}, bf16[64,4096]{1,0:T(8,128)(2,1)S(1)}, u32[]{:S(2)}, u32[]{:S(2)}) collective-permute-start(bf16[64,4096]{1,0:T(8,128)(2,1)S(1)} %dynamic-slice_bitcast_fusion), channel_id=1, source_target_pairs={{0,8},{4,12},{8,0},{12,4},{1,9},{5,13},{9,1},{13,5},{2,10},{6,14},... | collective-permute-start | bytes 1572872 | tf_op jit(solution)/shard_map/ppermute | solution.py:401
  10.3 44.8 %collective-permute-start.7 = (bf16[576,512]{1,0:T(8,128)(2,1)}, bf16[576,512]{1,0:T(8,128)(2,1)S(1)}, u32[]{:S(2)}, u32[]{:S(2)}) collective-permute-start(bf16[576,512]{1,0:T(8,128)(2,1)} %get-tuple-element.31), channel_id=1, source_target_pairs={{0,8},{4,12},{8,0},{12,4},{1,9},{5,13},{9,1},{13,5},{2,10},{6,14},... | collective-permute-start | bytes 1769480 | tf_op jit(solution)/shard_map/ppermute | solution.py:401
  10.3 34.0 %collective-permute-start = (bf16[64,4096]{1,0:T(8,128)(2,1)S(1)}, bf16[64,4096]{1,0:T(8,128)(2,1)S(1)}, u32[]{:S(2)}, u32[]{:S(2)}) collective-permute-start(bf16[64,4096]{1,0:T(8,128)(2,1)S(1)} %dynamic-slice_bitcast_fusion), channel_id=1, source_target_pairs={{0,4},{4,0},{8,12},{12,8},{1,5},{5,1},{9,13},{13,9},{2,6},{6,2},{1... | collective-permute-start | bytes 1572872 | tf_op jit(solution)/shard_map/ppermute | solution.py:401
  44.3 33.9 %collective-permute-start.2 = (bf16[64,4096]{1,0:T(8,128)(2,1)S(1)}, bf16[64,4096]{1,0:T(8,128)(2,1)S(1)}, u32[]{:S(2)}, u32[]{:S(2)}) collective-permute-start(bf16[64,4096]{1,0:T(8,128)(2,1)S(1)} %collective-permute-done.1.refs_2_), channel_id=1, source_target_pairs={{0,4},{4,0},{8,12},{12,8},{1,5},{5,1},{9,13},{13,9},{2,6},{6,2},{1... | collective-permute-start | bytes 1572872 | tf_op jit(solution)/shard_map/ppermute | solution.py:401
  44.3 35.5 %collective-permute-start.8 = (bf16[576,512]{1,0:T(8,128)(2,1)}, bf16[576,512]{1,0:T(8,128)(2,1)S(1)}, u32[]{:S(2)}, u32[]{:S(2)}) collective-permute-start(bf16[576,512]{1,0:T(8,128)(2,1)} %get-tuple-element.33), channel_id=1, source_target_pairs={{0,12},{4,8},{8,4},{12,0},{1,13},{5,9},{9,5},{13,1},{2,14},{6,10},... | collective-permute-start | bytes 1769480 | tf_op jit(solution)/shard_map/ppermute | solution.py:401
  46.7 44.0 %collective-permute-start.6 = (bf16[576,512]{1,0:T(8,128)(2,1)}, bf16[576,512]{1,0:T(8,128)(2,1)S(1)}, u32[]{:S(2)}, u32[]{:S(2)}) collective-permute-start(bf16[576,512]{1,0:T(8,128)(2,1)} %get-tuple-element.30), channel_id=1, source_target_pairs={{0,4},{4,0},{8,12},{12,8},{1,5},{5,1},{9,13},{13,9},{2,6},{6,2},{1... | collective-permute-start | bytes 1769480 | tf_op jit(solution)/shard_map/ppermute | solution.py:401
  55.1 23.1 %collective-permute-start.3 = (bf16[64,4096]{1,0:T(8,128)(2,1)S(1)}, bf16[64,4096]{1,0:T(8,128)(2,1)S(1)}, u32[]{:S(2)}, u32[]{:S(2)}) collective-permute-start(bf16[64,4096]{1,0:T(8,128)(2,1)S(1)} %collective-permute-done.refs_1_), channel_id=1, source_target_pairs={{0,2},{1,3},{2,0},{3,1},{4,6},{5,7},{6,4},{7,5},{8,10},{9,11},{10,... | collective-permute-start | bytes 1572872 | tf_op jit(solution)/shard_map/ppermute | solution.py:404
  57.0 35.4 %collective-permute-start.14 = (bf16[576,512]{1,0:T(8,128)(2,1)S(1)}, bf16[576,512]{1,0:T(8,128)(2,1)S(1)}, u32[]{:S(2)}, u32[]{:S(2)}) collective-permute-start(bf16[576,512]{1,0:T(8,128)(2,1)S(1)} %collective-permute-done.7.refs_9_), channel_id=1, source_target_pairs={{0,1},{1,0},{2,3},{3,2},{4,5},{5,4},{6,7},{7,6},{8,9},{9,8},{10,11... | collective-permute-start | bytes 1769480 | tf_op jit(solution)/shard_map/ppermute | solution.py:404
  78.2 27.7 %collective-permute-start.12 = (bf16[1088,512]{1,0:T(8,128)(2,1)}, bf16[1088,512]{1,0:T(8,128)(2,1)S(1)}, u32[]{:S(2)}, u32[]{:S(2)}) collective-permute-start(bf16[1088,512]{1,0:T(8,128)(2,1)} %get-tuple-element.34.refs_7_), channel_id=1, source_target_pairs={{0,1},{1,0},{2,3},{3,2},{4,5},{5,4},{6,7},{7,6},{8,9},{9,8},{10,11... | collective-permute-start | bytes 3342344 | tf_op jit(solution)/shard_map/ppermute | solution.py:404
  78.2 16.1 %collective-permute-start.10 = (bf16[576,512]{1,0:T(8,128)(2,1)S(1)}, bf16[576,512]{1,0:T(8,128)(2,1)S(1)}, u32[]{:S(2)}, u32[]{:S(2)}) collective-permute-start(bf16[576,512]{1,0:T(8,128)(2,1)S(1)} %collective-permute-done.7.refs_9_), channel_id=1, source_target_pairs={{0,16},{16,0},{1,17},{17,1},{2,18},{18,2},{3,19},{19,3},{4,20},{20... | collective-permute-start | bytes 1769480 | tf_op jit(solution)/shard_map/ppermute | solution.py:407
  79.8 27.2 %collective-permute-start.11 = (bf16[576,512]{1,0:T(8,128)(2,1)S(1)}, bf16[576,512]{1,0:T(8,128)(2,1)S(1)}, u32[]{:S(2)}, u32[]{:S(2)}) collective-permute-start(bf16[576,512]{1,0:T(8,128)(2,1)S(1)} %collective-permute-done.8.refs_10_), channel_id=1, source_target_pairs={{0,16},{16,0},{1,17},{17,1},{2,18},{18,2},{3,19},{19,3},{4,20},{20... | collective-permute-start | bytes 1769480 | tf_op jit(solution)/shard_map/ppermute | solution.py:407
  90.8 28.5 %collective-permute-start.9 = (bf16[576,512]{1,0:T(8,128)(2,1)S(1)}, bf16[576,512]{1,0:T(8,128)(2,1)S(1)}, u32[]{:S(2)}, u32[]{:S(2)}) collective-permute-start(bf16[576,512]{1,0:T(8,128)(2,1)S(1)} %collective-permute-done.6.refs_8_), channel_id=1, source_target_pairs={{0,16},{16,0},{1,17},{17,1},{2,18},{18,2},{3,19},{19,3},{4,20},{20... | collective-permute-start | bytes 1769480 | tf_op jit(solution)/shard_map/ppermute | solution.py:407
  94.4 24.9 %collective-permute-start.15 = (bf16[576,512]{1,0:T(8,128)(2,1)S(1)}, bf16[576,512]{1,0:T(8,128)(2,1)S(1)}, u32[]{:S(2)}, u32[]{:S(2)}) collective-permute-start(bf16[576,512]{1,0:T(8,128)(2,1)S(1)} %collective-permute-done.8.refs_10_), channel_id=1, source_target_pairs={{0,1},{1,0},{2,3},{3,2},{4,5},{5,4},{6,7},{7,6},{8,9},{9,8},{10,11... | collective-permute-start | bytes 1769480 | tf_op jit(solution)/shard_map/ppermute | solution.py:404
  142.1 33.3 %collective-permute-start.21 = (bf16[4,2,64,1024]{3,2,1,0:T(8,128)(2,1)}, bf16[4,2,64,1024]{3,2,1,0:T(8,128)(2,1)}, u32[]{:S(2)}, u32[]{:S(2)}) collective-permute-start(bf16[4,2,64,1024]{3,2,1,0:T(8,128)(2,1)} %get-tuple-element.41), channel_id=1, source_target_pairs={{0,1},{1,0},{2,3},{3,2},{4,5},{5,4},{6,7},{7,6},{8,9},{9,8},{10,11... | collective-permute-start | bytes 3145736 | tf_op jit(solution)/shard_map/ppermute | solution.py:404
  143.9 23.9 %collective-permute-start.19 = (bf16[2,2,64,256]{3,2,1,0:T(8,128)(2,1)S(1)}, bf16[2,2,64,256]{3,2,1,0:T(8,128)(2,1)S(1)}, u32[]{:S(2)}, u32[]{:S(2)}) collective-permute-start(bf16[2,2,64,256]{3,2,1,0:T(8,128)(2,1)S(1)} %get-tuple-element.56), channel_id=1, source_target_pairs={{0,1},{1,0},{2,3},{3,2},{4,5},{5,4},{6,7},{7,6},{8,9},{9,8},{10,11... | collective-permute-start | bytes 393224 | tf_op jit(solution)/shard_map/ppermute | solution.py:404
  144.0 52.6 %collective-permute-start.24 = (bf16[2,64,1024]{2,1,0:T(8,128)(2,1)S(1)}, bf16[2,64,1024]{2,1,0:T(8,128)(2,1)}, u32[]{:S(2)}, u32[]{:S(2)}) collective-permute-start(bf16[2,64,1024]{2,1,0:T(8,128)(2,1)S(1)} %get-tuple-element.46), channel_id=1, source_target_pairs={{0,3},{1,2},{2,1},{3,0},{4,7},{5,6},{6,5},{7,4},{8,11},{9,10},{10,... | collective-permute-start | bytes 786440 | tf_op jit(solution)/shard_map/ppermute | solution.py:404
  144.6 30.8 %collective-permute-start.30 = (bf16[2,64,1024]{2,1,0:T(8,128)(2,1)}, bf16[2,64,1024]{2,1,0:T(8,128)(2,1)}, u32[]{:S(2)}, u32[]{:S(2)}) collective-permute-start(bf16[2,64,1024]{2,1,0:T(8,128)(2,1)} %get-tuple-element.51), channel_id=1, source_target_pairs={{0,3},{1,2},{2,1},{3,0},{4,7},{5,6},{6,5},{7,4},{8,11},{9,10},{10,... | collective-permute-start | bytes 786440 | tf_op jit(solution)/shard_map/ppermute | solution.py:404
  151.5 16.3 %collective-permute-start.22 = (bf16[2,64,1024]{2,1,0:T(8,128)(2,1)}, bf16[2,64,1024]{2,1,0:T(8,128)(2,1)S(1)}, u32[]{:S(2)}, u32[]{:S(2)}) collective-permute-start(bf16[2,64,1024]{2,1,0:T(8,128)(2,1)} %get-tuple-element.44), channel_id=1, source_target_pairs={{0,2},{1,3},{2,0},{3,1},{4,6},{5,7},{6,4},{7,5},{8,10},{9,11},{10,... | collective-permute-start | bytes 786440 | tf_op jit(solution)/shard_map/ppermute | solution.py:404
  167.8 17.2 %collective-permute-start.23 = (bf16[2,2,64,1024]{3,2,1,0:T(8,128)(2,1)S(1)}, bf16[2,2,64,1024]{3,2,1,0:T(8,128)(2,1)}, u32[]{:S(2)}, u32[]{:S(2)}) collective-permute-start(bf16[2,2,64,1024]{3,2,1,0:T(8,128)(2,1)S(1)} %get-tuple-element.45), channel_id=1, source_target_pairs={{0,2},{1,3},{2,0},{3,1},{4,6},{5,7},{6,4},{7,5},{8,10},{9,11},{10,... | collective-permute-start | bytes 1572872 | tf_op jit(solution)/shard_map/ppermute | solution.py:404
  175.4 17.3 %collective-permute-start.28 = (bf16[2,64,1024]{2,1,0:T(8,128)(2,1)S(1)}, bf16[2,64,1024]{2,1,0:T(8,128)(2,1)}, u32[]{:S(2)}, u32[]{:S(2)}) collective-permute-start(bf16[2,64,1024]{2,1,0:T(8,128)(2,1)S(1)} %get-tuple-element.48), channel_id=1, source_target_pairs={{0,3},{1,2},{2,1},{3,0},{4,7},{5,6},{6,5},{7,4},{8,11},{9,10},{10,... | collective-permute-start | bytes 786440 | tf_op jit(solution)/shard_map/ppermute | solution.py:404
  185.0 14.6 %collective-permute-start.27 = (bf16[2,64,1024]{2,1,0:T(8,128)(2,1)}, bf16[2,64,1024]{2,1,0:T(8,128)(2,1)S(1)}, u32[]{:S(2)}, u32[]{:S(2)}) collective-permute-start(bf16[2,64,1024]{2,1,0:T(8,128)(2,1)} %fusion.4), channel_id=1, source_target_pairs={{0,8},{4,12},{8,0},{12,4},{1,9},{5,13},{9,1},{13,5},{2,10},{6,14},... | collective-permute-start | bytes 786440 | tf_op jit(solution)/shard_map/ppermute | solution.py:401
  187.9 14.9 %collective-permute-start.25 = (bf16[2,64,1024]{2,1,0:T(8,128)(2,1)S(1)}, bf16[2,64,1024]{2,1,0:T(8,128)(2,1)S(1)}, u32[]{:S(2)}, u32[]{:S(2)}) collective-permute-start(bf16[2,64,1024]{2,1,0:T(8,128)(2,1)S(1)} %fusion.10), channel_id=1, source_target_pairs={{0,4},{4,0},{8,12},{12,8},{1,5},{5,1},{9,13},{13,9},{2,6},{6,2},{1... | collective-permute-start | bytes 786440 | tf_op jit(solution)/shard_map/ppermute | solution.py:401
  190.8 20.8 %collective-permute-start.33 = (bf16[2,64,1024]{2,1,0:T(8,128)(2,1)S(1)}, bf16[2,64,1024]{2,1,0:T(8,128)(2,1)S(1)}, u32[]{:S(2)}, u32[]{:S(2)}) collective-permute-start(bf16[2,64,1024]{2,1,0:T(8,128)(2,1)S(1)} %fusion.8), channel_id=1, source_target_pairs={{0,8},{4,12},{8,0},{12,4},{1,9},{5,13},{9,1},{13,5},{2,10},{6,14},... | collective-permute-start | bytes 786440 | tf_op jit(solution)/shard_map/ppermute | solution.py:401
  193.8 17.8 %collective-permute-start.32 = (bf16[2,64,1024]{2,1,0:T(8,128)(2,1)S(1)}, bf16[2,64,1024]{2,1,0:T(8,128)(2,1)S(1)}, u32[]{:S(2)}, u32[]{:S(2)}) collective-permute-start(bf16[2,64,1024]{2,1,0:T(8,128)(2,1)S(1)} %fusion.9), channel_id=1, source_target_pairs={{0,4},{4,0},{8,12},{12,8},{1,5},{5,1},{9,13},{13,9},{2,6},{6,2},{1... | collective-permute-start | bytes 786440 | tf_op jit(solution)/shard_map/ppermute | solution.py:401
  (33 other events, 506.3 us)

commit v4 on v3

--- a/solution.py
+++ b/solution.py
@@ -168,19 +168,21 @@
         out_ref[tiles * TILE :, 0:256] = query_ref[:, at]
         out_ref[tiles * TILE :, 256:512] = cot_ref[:, at]
 
-    for k in (2, 3, 1):
-        write(message_refs[k - 1], g * 8, 8, lax.bitwise_xor(s, k))
+    first, second, third = message_refs
+    write(second, g * 8, 8, lax.bitwise_xor(s, 2))
+    write(first, g * 8, 8, lax.bitwise_xor(s, 1))
+    write(third, g * 8, 8, lax.bitwise_xor(s, 3))
     write(own_ref, 0, 16, s)
 
 
 def prune(tile_mask, key_weight, value_weight, queries, cotangent):
     whole = pl.BlockSpec(memory_space=pltpu.VMEM)
+    rows = (2 * PIECE + 64, SENT, SENT, SENT)
     return pl.pallas_call(
         prune_kernel,
-        out_shape=[jax.ShapeDtypeStruct((2 * PIECE + 64, 512), BF)]
-        + [jax.ShapeDtypeStruct((SENT, 512), BF)] * 3,
+        out_shape=[jax.ShapeDtypeStruct((count, 512), BF) for count in rows],
         in_specs=[pl.BlockSpec(memory_space=pltpu.SMEM)] + [whole] * 4,
-        out_specs=[whole] * 4,
+        out_specs=[whole] * len(rows),
         name="prune",
     )(tile_mask, key_weight, value_weight, queries, cotangent)
 
@@ -204,53 +206,147 @@
     lax.fori_loop(0, 4, column, 0)
 
 
+class Mover:
+    def __init__(self, sems):
+        self.sems = sems
+        self.used = 0
+
+    def start(self, pairs):
+        copies = []
+        for src, dst in pairs:
+            copy = pltpu.make_async_copy(src, dst, self.sems.at[self.used])
+            copy.start()
+            self.used += 1
+            copies.append(copy)
+        return copies
+
+
+def piece_rows(w_s, core, at, first, count):
+    return w_s.at[core, pl.ds(pl.multiple_of(at * 1024 + first, 256), count)]
+
+
+PACKED = 3 * 2 * PIECE
+
+
+def pack_kernel(own, z1, z2, y1, y2, out_ref, sems):
+    g = lax.axis_index("grp")
+    pairs = [(own.at[0 : 2 * PIECE], out_ref.at[0 : 2 * PIECE])]
+    pairs.append((own.at[2 * PIECE : 2 * PIECE + 64], out_ref.at[PACKED : PACKED + 64]))
+    for k, z, y in ((1, z1, y1), (2, z2, y2)):
+        for piece, side in ((z, g), (y, 1 - g)):
+            first = pl.multiple_of(2 * PIECE * k + side * PIECE, PIECE)
+            pairs.append((piece.at[0:PIECE], out_ref.at[pl.ds(first, PIECE)]))
+        pairs.append((z.at[PIECE:SENT], out_ref.at[PACKED + 64 * k : PACKED + 64 * k + 64]))
+    for copy in Mover(sems).start(pairs):
+        copy.wait()
+
+
+def pack_call(*arrays):
+    here = pl.BlockSpec(memory_space=pl.ANY)
+    return pl.pallas_call(
+        pack_kernel,
+        out_shape=jax.ShapeDtypeStruct((PACKED + 192, 512), BF),
+        in_specs=[here] * len(arrays),
+        out_specs=here,
+        scratch_shapes=[pltpu.SemaphoreType.DMA((8,))],
+        cost_estimate=pl.CostEstimate(flops=1, bytes_accessed=1, transcendentals=0),
+        name="pack",
+    )(*arrays)
+
+
+def early_weights(w_s, c, s, mine, theirs):
+    pairs = []
+    for core, packed in ((c, mine), (1 - c, theirs)):
+        for k in range(3):
+            rows = packed.at[2 * PIECE * k : 2 * PIECE * (k + 1)]
+            pairs.append((rows, piece_rows(w_s, core, lax.bitwise_xor(s, k), 0, 2 * PIECE)))
+    return pairs
+
+
+def early_kernel(*refs):
+    enc, e1, e2, e3, x1, x2, x3 = refs[:7]
+    mine, theirs = refs[7:9]
+    sum_ref, last_ref, enc_s, w_s, sems = refs[9:]
+    s, h = lax.axis_index("seq"), lax.axis_index("head")
+    c = lax.rem(h, 2)
+    x = h // 2
+    mover = Mover(sems)
+
+    def rows_of(doc, at):
+        return enc_s.at[pl.ds(pl.multiple_of(doc * 256 + at * 64, 64), 64)]
+
+    pairs = [(enc.at[2 * i + c], rows_of(i, s)) for i in range(2)]
+    for k, (own, other) in enumerate(((e1, x1), (e2, x2), (e3, x3))):
+        at = lax.bitwise_xor(s, k + 1)
+        pairs += [(own, rows_of(x, at)), (other, rows_of(1 - x, at))]
+    pairs += early_weights(w_s, c, s, mine, theirs)
+    for copy in mover.start(pairs):
+        copy.wait()
+
+    def columns(k):
+        at = lax.bitwise_xor(s, k)
+        return pl.ds(pl.multiple_of(at * 1024, 1024), 1024)
+
+    for core in range(2):
+        for half in range(2):
+            row = slice(half * 256, half * 256 + 256)
+            total = dot(enc_s[row, columns(0)], w_s[core, columns(0), :])
+            for k in (1, 2):
+                total = total + dot(enc_s[row, columns(k)], w_s[core, columns(k), :])
+            sum_ref[core, row] = total
+    last_ref[...] = enc_s[:, columns(3)]
+
+
+def early_call(arrays):
+    here = pl.BlockSpec(memory_space=pl.ANY)
+    vmem = pl.BlockSpec(memory_space=pltpu.VMEM)
+    return pl.pallas_call(
+        early_kernel,
+        out_shape=[
+            jax.ShapeDtypeStruct((2, 512, 512), F32),
+            jax.ShapeDtypeStruct((512, 1024), BF),
+        ],
+        in_specs=[here] * len(arrays),
+        out_specs=[vmem] * 2,
+        scratch_shapes=[
+            pltpu.VMEM((512, 4096), BF),
+            pltpu.VMEM((2, 4096, 512), BF),
+            pltpu.SemaphoreType.DMA((18,)),
+        ],
+        compiler_params=pltpu.CompilerParams(vmem_limit_bytes=28 * 1024 * 1024),
+        cost_estimate=pl.CostEstimate(
+            flops=1, bytes_accessed=1, transcendentals=0
+        ),
+        name="early",
+    )(*arrays)
+
+
 def main_kernel(lengths, *refs):
+    early_sum, last_rows = refs[:2]
+    mine, theirs = refs[2:5], refs[5:8]
     (
-        enc, e1, e2, e3, x1, x2, x3,
-        w_own, z1, z2, z3, y1, y2, y3,
-        v_own, vz1, vz2, vz3, vy1, vy2, vy3,
-        att_ref, qg_ref, grad_ref, weight_ref,
+        att_ref, qg_ref, own_ref,
         a3, b3, a2, b2, b1, a10, b0, core_ref,
-        enc_s, w_s, qc_s, grad_s, part_s, sems,
-    ) = refs
+        w_s, qc_s, grad_s, part_s, sems,
+    ) = refs[8:]
     s, g, h = lax.axis_index("seq"), lax.axis_index("grp"), lax.axis_index("head")
     c = lax.rem(h, 2)
-    x = h // 2
-    copies = []
-
-    def move(src, dst):
-        copy = pltpu.make_async_copy(src, dst, sems.at[len(copies)])
-        copy.start()
-        copies.append(copy)
-
-    def rows_of(doc, at):
-        return enc_s.at[doc, pl.ds(pl.multiple_of(at * 64, 64), 64)]
-
-    for i in range(2):
-        move(enc.at[2 * i + c], rows_of(i, s))
-    for k, (mine, other) in enumerate(((e1, x1), (e2, x2), (e3, x3))):
-        at = lax.bitwise_xor(s, k + 1)
-        move(mine, rows_of(x, at))
-        move(other, rows_of(1 - x, at))
-
-    def weight_rows(core, at, half, count):
-        return w_s.at[core, pl.ds(pl.multiple_of(at * 1024 + half * PIECE, PIECE), count)]
-
-    for core, own, zs, ys in (
-        (c, w_own, (z1, z2, z3), (y1, y2, y3)),
-        (1 - c, v_own, (vz1, vz2, vz3), (vy1, vy2, vy3)),
-    ):
-        move(own.at[0 : 2 * PIECE], weight_rows(core, s, 0, 2 * PIECE))
-        move(own.at[2 * PIECE : 2 * PIECE + 64], qc_s.at[core, s])
-        for j in range(3):
-            at = lax.bitwise_xor(s, j + 1)
-            move(zs[j].at[0:PIECE], weight_rows(core, at, g, PIECE))
-            move(ys[j].at[0:PIECE], weight_rows(core, at, 1 - g, PIECE))
-            move(zs[j].at[PIECE:SENT], qc_s.at[core, at])
-    for copy in copies:
+    mover = Mover(sems)
+    far = lax.bitwise_xor(s, 3)
+    pairs = []
+    for core, pieces in ((c, mine), (1 - c, theirs)):
+        packed, z3, y3 = pieces
+        for src, side in ((z3, g), (y3, 1 - g)):
+            pairs.append((src.at[0:PIECE], piece_rows(w_s, core, far, side * PIECE, PIECE)))
+        for k in range(3):
+            rows = packed.at[PACKED + 64 * k : PACKED + 64 * k + 64]
+            pairs.append((rows, qc_s.at[core, lax.bitwise_xor(s, k)]))
+        pairs.append((z3.at[PIECE:SENT], qc_s.at[core, far]))
+    now = mover.start(pairs)
+    later = mover.start(early_weights(w_s, c, s, mine[0], theirs[0]))
+    for copy in now:
         copy.wait()
-    save = pltpu.make_async_copy(w_s, weight_ref, sems.at[0])
-    save.start()
+    far_rows = pl.ds(pl.multiple_of(far * 1024, 1024), 1024)
 
     row_head = lax.broadcasted_iota(jnp.int32, (256, 256), 0) // DH
     col_head = lax.broadcasted_iota(jnp.int32, (256, 256), 1) // DH
@@ -268,7 +364,8 @@
     for core in range(2):
         slot = lax.rem(core + c, 2)
         for doc in range(2):
-            both = dot(enc_s[doc], w_s[core])
+            row = slice(doc * 256, doc * 256 + 256)
+            both = early_sum[core, row] + dot(last_rows[row], w_s[core, far_rows, :])
             keys = both[:, :256].astype(BF)
             values = both[:, 256:].astype(BF)
             at = pl.ds(pl.multiple_of((2 * doc + c) * 16, 16), 16)
@@ -291,19 +388,21 @@
             grad_s[core, doc * 256 : (doc + 1) * 256, 0:256] = dot(score_grad, query, TN).astype(BF)
             grad_s[core, doc * 256 : (doc + 1) * 256, 256:512] = dot(low, cot, TN).astype(BF)
 
+    for copy in later:
+        copy.wait()
     cores = [core_ref.at[k] for k in range(4)]
+    owns = [own_ref.at[k] for k in range(4)]
     for flip, outs in (
         (2, (a10.at[1], a10.at[0], a2, a3)),
         (3, (b0, b1, b2, b3)),
         (1, cores),
+        (0, owns),
     ):
         partial_blocks(lax.bitwise_xor(h, flip), grad_s, w_s, part_s)
         for k in range(4):
             at = pl.ds(pl.multiple_of(lax.bitwise_xor(s, k) * 64, 64), 64)
             for doc in range(2):
-                outs[k][doc] = part_s[doc, at, :].astype(BF)
-    grad_ref[...] = grad_s[...]
-    save.wait()
+                outs[k][doc] = part_s[doc, at, :].astype(outs[k].dtype)
 
 
 def main_call(lengths, arrays):
@@ -317,54 +416,27 @@
         out_shape=[
             front,
             front,
-            jax.ShapeDtypeStruct((2, 512, 512), BF),
-            jax.ShapeDtypeStruct((2, 4096, 512), BF),
+            jax.ShapeDtypeStruct((4, 2, 64, 1024), F32),
         ]
         + [piece] * 5
         + [jax.ShapeDtypeStruct((2, 2, 64, 1024), BF)]
         + [piece]
         + [jax.ShapeDtypeStruct((4, 2, 64, 1024), BF)],
-        in_specs=[smem] + [here] * len(arrays),
-        out_specs=[vmem] * 3 + [here] + [vmem] * 8,
+        in_specs=[smem] + [vmem] * 2 + [here] * (len(arrays) - 2),
+        out_specs=[vmem] * 11,
         scratch_shapes=[
-            pltpu.VMEM((2, 256, 4096), BF),
             pltpu.VMEM((2, 4096, 512), BF),
             pltpu.VMEM((2, 4, 64, 512), BF),
             pltpu.VMEM((2, 512, 512), BF),
             pltpu.VMEM((2, 256, 1024), F32),
-            pltpu.SemaphoreType.DMA((32,)),
+            pltpu.SemaphoreType.DMA((26,)),
         ],
-        compiler_params=pltpu.CompilerParams(vmem_limit_bytes=48 * 1024 * 1024),
+        compiler_params=pltpu.CompilerParams(vmem_limit_bytes=34 * 1024 * 1024),
         cost_estimate=pl.CostEstimate(
-            flops=8 * 10**9, bytes_accessed=30 * 2**20, transcendentals=2**18
+            flops=6 * 10**9, bytes_accessed=24 * 2**20, transcendentals=2**18
         ),
         name="attend",
     )(lengths, *arrays)
-
-
-def near_kernel(grad, weight, own_ref, part_s):
-    s, h = lax.axis_index("seq"), lax.axis_index("head")
-    partial_blocks(h, grad, weight, part_s)
-    for k in range(4):
-        at = pl.ds(pl.multiple_of(lax.bitwise_xor(s, k) * 64, 64), 64)
-        for doc in range(2):
-            own_ref[k, doc] = part_s[doc, at, :]
-
-
-def near_call(grad, weight):
-    vmem = pl.BlockSpec(memory_space=pltpu.VMEM)
-    return pl.pallas_call(
-        near_kernel,
-        out_shape=jax.ShapeDtypeStruct((4, 2, 64, 1024), F32),
-        in_specs=[vmem, vmem],
-        out_specs=vmem,
-        scratch_shapes=[pltpu.VMEM((2, 256, 1024), F32)],
-        compiler_params=pltpu.CompilerParams(vmem_limit_bytes=48 * 1024 * 1024),
-        cost_estimate=pl.CostEstimate(
-            flops=10**9, bytes_accessed=10 * 2**20, transcendentals=0
-        ),
-        name="near",
-    )(grad, weight)
 
 
 def final_kernel(own, core, near, far, near1, near2, far1, far2, out_ref):
@@ -389,8 +461,15 @@
     )(*arrays)
 
 
-def after(value, *first):
-    return lax.optimization_barrier((value,) + first)[0]
+def together(*values):
+    return lax.optimization_barrier(values)
+
+
+def summed(*parts):
+    total = parts[0].astype(F32)
+    for part in parts[1:]:
+        total = total + part.astype(F32)
+    return total.astype(BF)
 
 
 def body(encoder, key_weight, value_weight, tile_mask, lengths, queries, cotangent):
@@ -412,55 +491,58 @@
     w_own, m1, m2, m3 = prune(
         tile_mask, key_weight, value_weight, queries.reshape(64, 1024), cotangent.reshape(64, 1024)
     )
+    e1, m2, w_own = together(e1, m2, w_own)
     z2 = along(m2, 2)
+    e2, m1 = together(e2, m1)
+    z1 = along(m1, 1)
     e3 = along(e2, 1)
-    z3 = along(after(m3, e1), 3)
-    z1 = along(after(m1, e2), 1)
-    x1, x2, x3 = flip(e1, 2), flip(e2, 2), flip(e3, 2)
-    y1, y2, y3 = across(z1), across(z2), across(z3)
-    v_own = flip(after(w_own, e1), 1)
-    vz1, vz2, vz3 = flip(z1, 1), flip(z2, 1), flip(z3, 1)
-    vy1, vy2, vy3 = flip(y1, 1), flip(y2, 1), flip(y3, 1)
-
-    outs = main_call(
-        lengths,
-        [encoder, e1, e2, e3, x1, x2, x3]
-        + [w_own, z1, z2, z3, y1, y2, y3]
-        + [v_own, vz1, vz2, vz3, vy1, vy2, vy3],
-    )
-    att, qgrad, grad, weight = outs[:4]
-    a3, b3, a2, b2, b1, a10, b0, to_core = outs[4:]
+    x1, x2 = flip(e1, 2), flip(e2, 2)
+    x1, e3, m3 = together(x1, e3, m3)
+    z3 = along(m3, 3)
+    x3 = flip(e3, 2)
+    y1, y2 = across(z1), across(z2)
+    x2, x3, z3, w_own = together(x2, x3, z3, w_own)
+    y3 = across(z3)
+    packed = pack_call(w_own, z1, z2, y1, y2)
+    packed_there = flip(packed, 1)
+    early = early_call([encoder, e1, e2, e3, x1, x2, x3, packed, packed_there])
+    z3_there = flip(z3, 1)
+    y3, *early = together(y3, *early)
+    y3_there = flip(y3, 1)
+    outs = main_call(lengths, early + [packed, z3, y3, packed_there, z3_there, y3_there])
+    att, qgrad, own = outs[:3]
+    a3, b3, a2, b2, b1, a10, b0, to_core = outs[3:]
     from_core = flip(to_core, 1)
-    a3, b3 = flip(a3, 2), flip(b3, 3)
-    a2, b2 = flip(after(a2, a3), 2), flip(after(b2, a3), 3)
-    b1, a10 = flip(after(b1, a2), 3), flip(after(a10, a2), 2)
-    b0 = flip(b0, 3)
-    own = near_call(after(grad, a3), weight)
-
-    def summed(*parts):
-        total = parts[0].astype(F32)
-        for part in parts[1:]:
-            total = total + part.astype(F32)
-        return total.astype(BF)
-
-    near3 = along(summed(own[3], a3), 1)
-    far3 = along(summed(from_core[3], b3), 1)
-    near2 = along(summed(own[2], a2, near3), 2)
-    far2 = summed(from_core[2], b2, far3)
-    far1 = along(summed(from_core[1], after(b1, far2)), 1)
-    far2 = along(far2, 2)
-    near1 = along(summed(own[1], a10[0]), 1)
-    encoder_grad = small_call(
-        final_kernel, (DOCS, 64, 1024), "final", own, from_core, a10, b0, near1, near2, far1, far2
-    )
-
     front = jnp.stack([att, qgrad], axis=1)
     other = flip(front[1], 1)
+    b3, a3 = flip(b3, 3), flip(a3, 2)
+    b3, core, other, b2, a2 = together(b3, from_core, other, b2, a2)
+    b2, a2 = flip(b2, 3), flip(a2, 2)
+    far3, own = together(summed(core[3], b3), own)
+    far3 = along(far3, 1)
+    near3, core = together(summed(own[3], a3), core)
+    near3 = along(near3, 1)
+    b2, b1, a10 = together(b2, b1, a10)
+    b1, a10 = flip(b1, 3), flip(a10, 2)
+    far2, own = together(summed(core[2], b2, far3), own)
+    far2 = along(far2, 2)
+    a2, b0 = together(a2, b0)
+    b0 = flip(b0, 3)
     back = jnp.stack([front[0], other]).reshape(2, 2, 2, SEQ, 16, 256).transpose(3, 0, 1, 2, 4, 5)
+    near2, core = together(summed(own[2], a2, near3), core)
+    near2 = along(near2, 2)
+    far1, own, back = together(summed(core[1], b1), own, back)
+    far1 = along(far1, 1)
+    near1 = along(summed(own[1], a10[0]), 1)
+    from_core = core
     back = lax.all_to_all(back, "seq", split_axis=0, concat_axis=0, tiled=True)
     back = back.transpose(2, 3, 1, 4, 0, 5).reshape(2, 2, 2, 16, 1024)
     back = jnp.where(c == 0, back, back[:, :, ::-1])
     back = back.reshape(2, DOCS, 16, 1024)
+    b0, back = together(b0, back)
+    encoder_grad = small_call(
+        final_kernel, (DOCS, 64, 1024), "final", own, from_core, a10, b0, near1, near2, far1, far2
+    )
     return (back[0], back[1], encoder_grad)
 
 

time: 217 us -> 307 us (1.41)
  Pallas kernels: 33.3 us -> 129 us
  local copies, waits for them, and re-layouts: 6.26 us -> 13.7 us
  waiting for transfers between devices: 125 us -> 119 us
  other arithmetic: 8.62 us -> 3.37 us
    pallas_call x2 -> x3, Pallas kernels: 9.91 us -> 111 us  [the longest x1 102 us: pack_call(): pl.pallas_call(pack_kernel, out_shape=jax.ShapeDtypeStruct((PACKED + 192,...]
    ppermute x12, waiting for transfers between devices: 84.6 us -> 48.1 us  [along(): return lax.ppermute(value, 'seq', [(a, a ^ k) for a in range(SEQ)])]
    ppermute x19 -> x15, waiting for transfers between devices: 26.4 us -> 56.6 us  [flip(): return lax.ppermute(value, 'head', [(a, a ^ bits) for a in range(4)])]
    ppermute x3, waiting for transfers between devices: 13.3 us -> 0.01 us  [across(): return lax.ppermute(value, 'grp', [(0, 1), (1, 0)])]
    all_to_all x1, waiting for transfers between devices: 1.21 us -> 13.9 us  [body(): back = lax.all_to_all(back, 'seq', split_axis=0, concat_axis=0, tiled=True)]
    unnamed x44 -> x38, local copies, waits for them, and re-layouts: 3.49 us -> 10.9 us
    pallas_call x1, Pallas kernels: 19.9 us -> 14.7 us  [main_call(): pl.pallas_call(main_kernel, out_shape=[front, front, jax.ShapeDtypeStruct...]
    convert_element_type x6, other arithmetic: 7.82 us -> 2.57 us  [summed(): return total.astype(BF)]
  transfers between devices with their start and end apart: 35 -> 31, of which waited for: 16 -> 18; matrix products, arithmetic and copies ran while one was open for 5% -> 2% of each run, Pallas kernels for 5% -> 3%
where the time goes in v4:
time: 307 us
  Pallas kernels  129 us (42%)
  waiting for transfers between devices  119 us (39%)
  starting transfers between devices  40.6 us (13%)
  local copies, waits for them, and re-layouts  13.7 us (4%)
  other arithmetic  3.37 us (1%)
    pallas_call x1, Pallas kernels, pack_call(): pl.pallas_call(pack_kernel, out_shape=jax.ShapeDtypeStruct((PACKED + 192,...  102 us
    ppermute x15, waiting for transfers between devices, flip(): return lax.ppermute(value, 'head', [(a, a ^ bits) for a in range(4)])  56.6 us
    ppermute x12, waiting for transfers between devices, along(): return lax.ppermute(value, 'seq', [(a, a ^ k) for a in range(SEQ)])  48.1 us
    ppermute x12, starting transfers between devices, along(): return lax.ppermute(value, 'seq', [(a, a ^ k) for a in range(SEQ)])  17.6 us
    ppermute x15, starting transfers between devices, flip(): return lax.ppermute(value, 'head', [(a, a ^ bits) for a in range(4)])  15.4 us
    pallas_call x1, Pallas kernels, main_call(): pl.pallas_call(main_kernel, out_shape=[front, front, jax.ShapeDtypeStruct...  14.7 us
    all_to_all x1, waiting for transfers between devices, body(): back = lax.all_to_all(back, 'seq', split_axis=0, concat_axis=0, tiled=True)  13.9 us
    unnamed x38, local copies, waits for them, and re-layouts  10.9 us
  transfers between devices with their start and end apart: 31, of which 18 were waited for; matrix products, arithmetic and copies ran while one was open for 2% of the time, Pallas kernels for 3%

profile of v4, /device:TPU:0, one launch (start us, length us, event | category | flops | bytes accessed | tf_op | source)
XLA Modules:
  0.0 306.6 jit_solution(4352679879952517635)
XLA Ops:
  1.7 4.1 %collective-permute-start = (bf16[64,4096]{1,0:T(8,128)(2,1)S(1)}, bf16[64,4096]{1,0:T(8,128)(2,1)S(1)}, u32[]{:S(2)}, u32[]{:S(2)}) collective-permute-start(bf16[64,4096]{1,0:T(8,128)(2,1)S(1)} %dynamic-slice_bitcast_fusion), channel_id=1, source_target_pairs={{0,8},{4,12},{8,0},{12,4},{1,9},{5,13},{9,1},{13,5},{2,10},{6,14},... | collective-permute-start | bytes 1572872 | tf_op jit(solution)/shard_map/ppermute | solution.py:480
  7.4 4.5 %prune.1 = (bf16[1088,512]{1,0:T(8,128)(2,1)}, bf16[576,512]{1,0:T(8,128)(2,1)}, bf16[576,512]{1,0:T(8,128)(2,1)}, bf16[576,512]{1,0:T(8,128)(2,1)}) custom-call(s32[2,16,16]{2,1,0:T(8,128)} %mask_ref.1, bf16[1024,1024]{1,0:T(8,128)(2,1)} %key_ref.1, bf16[1024,1024]{1,0:T(8,128)(2,1)} %value_ref.1, bf16[64,1024]{1,0:T(8,128)(2,1)} %bitcast.46, ...), custom_call_target="tpu_custom_call" | custom-call | tf_op jit(solution)/shard_map/prune/pallas_call | solution.py:181
  11.9 17.2 %collective-permute-done.refs_2_ = bf16[64,4096]{1,0:T(8,128)(2,1)S(1)} collective-permute-done((bf16[64,4096]{1,0:T(8,128)(2,1)S(1)}, bf16[64,4096]{1,0:T(8,128)(2,1)S(1)}, u32[]{:S(2)}, u32[]{:S(2)}) %collective-permute-start) | collective-permute-done | bytes 524320 | tf_op jit(solution)/shard_map/ppermute | solution.py:480
  30.6 2.4 collective-permute-start.8
  34.6 11.8 %collective-permute-done.3.refs_4_ = bf16[64,4096]{1,0:T(8,128)(2,1)S(1)} collective-permute-done((bf16[64,4096]{1,0:T(8,128)(2,1)S(1)}, bf16[64,4096]{1,0:T(8,128)(2,1)S(1)}, u32[]{:S(2)}, u32[]{:S(2)}) %collective-permute-start.3) | collective-permute-done | bytes 524320 | tf_op jit(solution)/shard_map/ppermute | solution.py:483
  47.2 21.5 %collective-permute-done.4.refs_3_ = bf16[64,4096]{1,0:T(8,128)(2,1)S(1)} collective-permute-done((bf16[64,4096]{1,0:T(8,128)(2,1)S(1)}, bf16[64,4096]{1,0:T(8,128)(2,1)S(1)}, u32[]{:S(2)}, u32[]{:S(2)}) %collective-permute-start.4) | collective-permute-done | bytes 524320 | tf_op jit(solution)/shard_map/ppermute | solution.py:480
  68.7 3.2 %collective-permute-start.6 = (bf16[576,512]{1,0:T(8,128)(2,1)}, bf16[576,512]{1,0:T(8,128)(2,1)}, u32[]{:S(2)}, u32[]{:S(2)}) collective-permute-start(bf16[576,512]{1,0:T(8,128)(2,1)} %get-tuple-element.65), channel_id=1, source_target_pairs={{0,12},{4,8},{8,4},{12,0},{1,13},{5,9},{9,5},{13,1},{2,14},{6,10},... | collective-permute-start | bytes 1769480 | tf_op jit(solution)/shard_map/ppermute | solution.py:480
  76.7 12.0 %collective-permute-done.1.refs_5_ = bf16[64,4096]{1,0:T(8,128)(2,1)S(1)} collective-permute-done((bf16[64,4096]{1,0:T(8,128)(2,1)S(1)}, bf16[64,4096]{1,0:T(8,128)(2,1)S(1)}, u32[]{:S(2)}, u32[]{:S(2)}) %collective-permute-start.1) | collective-permute-done | bytes 524320 | tf_op jit(solution)/shard_map/ppermute | solution.py:483
  89.6 7.0 %collective-permute-done.5.refs_6_ = bf16[64,4096]{1,0:T(8,128)(2,1)S(1)} collective-permute-done((bf16[64,4096]{1,0:T(8,128)(2,1)S(1)}, bf16[64,4096]{1,0:T(8,128)(2,1)S(1)}, u32[]{:S(2)}, u32[]{:S(2)}) %collective-permute-start.5) | collective-permute-done | bytes 524320 | tf_op jit(solution)/shard_map/ppermute | solution.py:483
  98.3 102.4 %pack.1.refs_7_.refs_2_ = bf16[3264,512]{1,0:T(8,128)(2,1)} custom-call(bf16[1088,512]{1,0:T(8,128)(2,1)} %get-tuple-element.71.own, bf16[576,512]{1,0:T(8,128)(2,1)} %copy-done.16, bf16[576,512]{1,0:T(8,128)(2,1)} %copy-done.15, bf16[576,512]{1,0:T(8,128)(2,1)} %collective-permute-done.10.y1, bf16[576,512]{1,0:T(8,128)(2,1)} %copy-done.17), custom_call_target="tpu_custom_call" | custom-call | flops 1 | bytes 1 | tf_op jit(solution)/shard_map/pack/pallas_call | solution.py:246
  202.6 4.4 %collective-permute-done.12.refs_8_.refs_5_ = bf16[3264,512]{1,0:T(8,128)(2,1)S(1)} collective-permute-done((bf16[3264,512]{1,0:T(8,128)(2,1)}, bf16[3264,512]{1,0:T(8,128)(2,1)S(1)}, u32[]{:S(2)}, u32[]{:S(2)}) %collective-permute-start.12) | collective-permute-done | bytes 3342368 | tf_op jit(solution)/shard_map/ppermute | solution.py:483
  213.1 4.4 %early.1 = (f32[2,512,512]{2,1,0:T(8,128)S(1)}, bf16[512,1024]{1,0:T(8,128)(2,1)S(1)}) custom-call(bf16[4,64,4096]{2,1,0:T(8,128)(2,1)S(1)} %copy-done.3, bf16[64,4096]{1,0:T(8,128)(2,1)S(1)} %collective-permute-done.2.refs_1_, bf16[64,4096]{1,0:T(8,128)(2,1)S(1)} %collective-permute-done.refs_2_, bf16[64,4096]{1,0:T(8,128)(2,1)S(1)} %copy-done.7, ...), custom_call_target="tpu_custom_call" | custom-call | flops 1 | bytes 1 | tf_op jit(solution)/shard_map/early/pallas_call | solution.py:303
  219.6 14.7 %attend.1 = (bf16[2,2,64,256]{3,2,1,0:T(8,128)(2,1)S(1)}, bf16[2,2,64,256]{3,2,1,0:T(8,128)(2,1)S(1)}, f32[4,2,64,1024]{3,2,1,0:T(8,128)S(1)}, bf16[2,64,1024]{2...) custom-call(s32[4]{0:T(128)S(1)} %copy-done.12, ...), custom_call_target="tpu_custom_call" | custom-call | flops 6000000000 | bytes 25165824 | tf_op jit(solution)/shard_map/attend/pallas_call | solution.py:414
  237.3 5.2 %collective-permute-done.15 = bf16[2,64,1024]{2,1,0:T(8,128)(2,1)S(1)} collective-permute-done((bf16[2,64,1024]{2,1,0:T(8,128)(2,1)S(1)}, bf16[2,64,1024]{2,1,0:T(8,128)(2,1)S(1)}, u32[]{:S(2)}, u32[]{:S(2)}) %collective-permute-start.15) | collective-permute-done | bytes 262176 | tf_op jit(solution)/shard_map/ppermute | solution.py:483
  244.7 4.5 %collective-permute-done.20 = bf16[2,64,1024]{2,1,0:T(8,128)(2,1)S(1)} collective-permute-done((bf16[2,64,1024]{2,1,0:T(8,128)(2,1)S(1)}, bf16[2,64,1024]{2,1,0:T(8,128)(2,1)S(1)}, u32[]{:S(2)}, u32[]{:S(2)}) %collective-permute-start.20) | collective-permute-done | bytes 262176 | tf_op jit(solution)/shard_map/ppermute | solution.py:483
  251.6 2.2 collective-permute-done.21
  256.8 3.6 %collective-permute-done.18 = bf16[2,64,1024]{2,1,0:T(8,128)(2,1)S(1)} collective-permute-done((bf16[2,64,1024]{2,1,0:T(8,128)(2,1)S(1)}, bf16[2,64,1024]{2,1,0:T(8,128)(2,1)S(1)}, u32[]{:S(2)}, u32[]{:S(2)}) %collective-permute-start.18) | collective-permute-done | bytes 262176 | tf_op jit(solution)/shard_map/ppermute | solution.py:483
  262.7 2.4 collective-permute-done.24
  265.8 4.0 %all-to-all-start = ((bf16[4,2,2,2,16,256]{5,4,1,3,2,0:T(8,128)(2,1)}), bf16[4,2,2,2,16,256]{5,4,1,3,2,0:T(8,128)(2,1)}, u32[]{:S(2)}, u32[]{:S(2)}) async-start(bf16[4,2,2,2,16,256]{5,4,1,3,2,0:T(8,128)(2,1)} %copy_bitcast_fusion), calls=%async_computation | async-start | bytes 524288 | tf_op jit(solution)/shard_map/all_to_all | solution.py:538
  271.8 2.5 collective-permute-start.27
  277.5 13.9 %all-to-all-done = bf16[4,2,2,2,16,256]{5,4,1,3,2,0:T(8,128)(2,1)} async-done(((bf16[4,2,2,2,16,256]{5,4,1,3,2,0:T(8,128)(2,1)}), bf16[4,2,2,2,16,256]{5,4,1,3,2,0:T(8,128)(2,1)}, u32[]{:S(2)}, u32[]{:S(2)}) %all-to-all-start) | async-done | bytes 262176 | tf_op jit(solution)/shard_map/all_to_all | solution.py:538
  293.2 3.8 %collective-permute-done.27.near2 = bf16[2,64,1024]{2,1,0:T(8,128)(2,1)} collective-permute-done((bf16[2,64,1024]{2,1,0:T(8,128)(2,1)}, bf16[2,64,1024]{2,1,0:T(8,128)(2,1)}, u32[]{:S(2)}, u32[]{:S(2)}) %collective-permute-start.27) | collective-permute-done | bytes 262176 | tf_op jit(solution)/shard_map/ppermute | solution.py:480
  297.1 5.4 %collective-permute-done.29.far2 = bf16[2,64,1024]{2,1,0:T(8,128)(2,1)} collective-permute-done((bf16[2,64,1024]{2,1,0:T(8,128)(2,1)}, bf16[2,64,1024]{2,1,0:T(8,128)(2,1)}, u32[]{:S(2)}, u32[]{:S(2)}) %collective-permute-start.29) | collective-permute-done | bytes 262176 | tf_op jit(solution)/shard_map/ppermute | solution.py:480
  303.2 3.4 %final.1 = bf16[4,64,1024]{2,1,0:T(8,128)(2,1)} custom-call(f32[4,2,64,1024]{3,2,1,0:T(8,128)} %copy-done.2, bf16[4,2,64,1024]{3,2,1,0:T(8,128)(2,1)} %copy-done.13, bf16[2,2,64,1024]{3,2,1,0:T(8,128)(2,1)} %copy-done.14, bf16[2,64,1024]{2,1,0:T(8,128)(2,1)} %collective-permute-done.19.far, bf16[2,64,1024]{2,1,0:T(8,128)(2,1)} %copy-done.18, ...), custom_call_target="tpu_custom_call" | custom-call | tf_op jit(solution)/shard_map/final/pallas_call | solution.py:455
  (93 shorter events, 45.1 us)
Async XLA Ops:
  1.7 27.4 %collective-permute-start = (bf16[64,4096]{1,0:T(8,128)(2,1)S(1)}, bf16[64,4096]{1,0:T(8,128)(2,1)S(1)}, u32[]{:S(2)}, u32[]{:S(2)}) collective-permute-start(bf16[64,4096]{1,0:T(8,128)(2,1)S(1)} %dynamic-slice_bitcast_fusion), channel_id=1, source_target_pairs={{0,8},{4,12},{8,0},{12,4},{1,9},{5,13},{9,1},{13,5},{2,10},{6,14},... | collective-permute-start | bytes 1572872 | tf_op jit(solution)/shard_map/ppermute | solution.py:480
  5.8 23.5 %collective-permute-start.2 = (bf16[64,4096]{1,0:T(8,128)(2,1)S(1)}, bf16[64,4096]{1,0:T(8,128)(2,1)S(1)}, u32[]{:S(2)}, u32[]{:S(2)}) collective-permute-start(bf16[64,4096]{1,0:T(8,128)(2,1)S(1)} %dynamic-slice_bitcast_fusion), channel_id=1, source_target_pairs={{0,4},{4,0},{8,12},{12,8},{1,5},{5,1},{9,13},{13,9},{2,6},{6,2},{1... | collective-permute-start | bytes 1572872 | tf_op jit(solution)/shard_map/ppermute | solution.py:480
  29.3 42.6 %collective-permute-start.9 = (bf16[576,512]{1,0:T(8,128)(2,1)}, bf16[576,512]{1,0:T(8,128)(2,1)S(1)}, u32[]{:S(2)}, u32[]{:S(2)}) collective-permute-start(bf16[576,512]{1,0:T(8,128)(2,1)} %get-tuple-element.73), channel_id=1, source_target_pairs={{0,8},{4,12},{8,0},{12,4},{1,9},{5,13},{9,1},{13,5},{2,10},{6,14},... | collective-permute-start | bytes 1769480 | tf_op jit(solution)/shard_map/ppermute | solution.py:480
  30.6 42.7 %collective-permute-start.8 = (bf16[576,512]{1,0:T(8,128)(2,1)}, bf16[576,512]{1,0:T(8,128)(2,1)S(1)}, u32[]{:S(2)}, u32[]{:S(2)}) collective-permute-start(bf16[576,512]{1,0:T(8,128)(2,1)} %get-tuple-element.72), channel_id=1, source_target_pairs={{0,4},{4,0},{8,12},{12,8},{1,5},{5,1},{9,13},{13,9},{2,6},{6,2},{1... | collective-permute-start | bytes 1769480 | tf_op jit(solution)/shard_map/ppermute | solution.py:480
  33.1 13.3 %collective-permute-start.3 = (bf16[64,4096]{1,0:T(8,128)(2,1)S(1)}, bf16[64,4096]{1,0:T(8,128)(2,1)S(1)}, u32[]{:S(2)}, u32[]{:S(2)}) collective-permute-start(bf16[64,4096]{1,0:T(8,128)(2,1)S(1)} %collective-permute-done.2.refs_1_), channel_id=1, source_target_pairs={{0,2},{1,3},{2,0},{3,1},{4,6},{5,7},{6,4},{7,5},{8,10},{9,11},{10,... | collective-permute-start | bytes 1572872 | tf_op jit(solution)/shard_map/ppermute | solution.py:483
  34.6 34.1 %collective-permute-start.4 = (bf16[64,4096]{1,0:T(8,128)(2,1)S(1)}, bf16[64,4096]{1,0:T(8,128)(2,1)S(1)}, u32[]{:S(2)}, u32[]{:S(2)}) collective-permute-start(bf16[64,4096]{1,0:T(8,128)(2,1)S(1)} %collective-permute-done.refs_2_), channel_id=1, source_target_pairs={{0,4},{4,0},{8,12},{12,8},{1,5},{5,1},{9,13},{13,9},{2,6},{6,2},{1... | collective-permute-start | bytes 1572872 | tf_op jit(solution)/shard_map/ppermute | solution.py:480
  68.7 28.8 %collective-permute-start.6 = (bf16[576,512]{1,0:T(8,128)(2,1)}, bf16[576,512]{1,0:T(8,128)(2,1)}, u32[]{:S(2)}, u32[]{:S(2)}) collective-permute-start(bf16[576,512]{1,0:T(8,128)(2,1)} %get-tuple-element.65), channel_id=1, source_target_pairs={{0,12},{4,8},{8,4},{12,0},{1,13},{5,9},{9,5},{13,1},{2,14},{6,10},... | collective-permute-start | bytes 1769480 | tf_op jit(solution)/shard_map/ppermute | solution.py:480
  71.9 25.6 %collective-permute-start.11 = (bf16[576,512]{1,0:T(8,128)(2,1)S(1)}, bf16[576,512]{1,0:T(8,128)(2,1)S(1)}, u32[]{:S(2)}, u32[]{:S(2)}) collective-permute-start(bf16[576,512]{1,0:T(8,128)(2,1)S(1)} %collective-permute-done.9.z2), channel_id=1, source_target_pairs={{0,16},{16,0},{1,17},{17,1},{2,18},{18,2},{3,19},{19,3},{4,20},{20... | collective-permute-start | bytes 1769480 | tf_op jit(solution)/shard_map/ppermute | solution.py:486
  73.4 24.9 %collective-permute-start.10 = (bf16[576,512]{1,0:T(8,128)(2,1)S(1)}, bf16[576,512]{1,0:T(8,128)(2,1)}, u32[]{:S(2)}, u32[]{:S(2)}) collective-permute-start(bf16[576,512]{1,0:T(8,128)(2,1)S(1)} %collective-permute-done.8.z1), channel_id=1, source_target_pairs={{0,16},{16,0},{1,17},{17,1},{2,18},{18,2},{3,19},{19,3},{4,20},{20... | collective-permute-start | bytes 1769480 | tf_op jit(solution)/shard_map/ppermute | solution.py:486
  73.9 14.9 %collective-permute-start.1 = (bf16[64,4096]{1,0:T(8,128)(2,1)S(1)}, bf16[64,4096]{1,0:T(8,128)(2,1)S(1)}, u32[]{:S(2)}, u32[]{:S(2)}) collective-permute-start(bf16[64,4096]{1,0:T(8,128)(2,1)S(1)} %collective-permute-done.refs_2_), channel_id=1, source_target_pairs={{0,2},{1,3},{2,0},{3,1},{4,6},{5,7},{6,4},{7,5},{8,10},{9,11},{10,... | collective-permute-start | bytes 1572872 | tf_op jit(solution)/shard_map/ppermute | solution.py:483
  75.4 21.3 %collective-permute-start.5 = (bf16[64,4096]{1,0:T(8,128)(2,1)S(1)}, bf16[64,4096]{1,0:T(8,128)(2,1)S(1)}, u32[]{:S(2)}, u32[]{:S(2)}) collective-permute-start(bf16[64,4096]{1,0:T(8,128)(2,1)S(1)} %collective-permute-done.4.refs_3_), channel_id=1, source_target_pairs={{0,2},{1,3},{2,0},{3,1},{4,6},{5,7},{6,4},{7,5},{8,10},{9,11},{10,... | collective-permute-start | bytes 1572872 | tf_op jit(solution)/shard_map/ppermute | solution.py:483
  200.8 16.7 %collective-permute-start.7 = (bf16[576,512]{1,0:T(8,128)(2,1)}, bf16[576,512]{1,0:T(8,128)(2,1)S(1)}, u32[]{:S(2)}, u32[]{:S(2)}) collective-permute-start(bf16[576,512]{1,0:T(8,128)(2,1)} %collective-permute-done.6.refs_3_), channel_id=1, source_target_pairs={{0,16},{16,0},{1,17},{17,1},{2,18},{18,2},{3,19},{19,3},{4,20},{20... | collective-permute-start | bytes 1769480 | tf_op jit(solution)/shard_map/ppermute | solution.py:486
  202.4 15.3 %collective-permute-start.13 = (bf16[576,512]{1,0:T(8,128)(2,1)}, bf16[576,512]{1,0:T(8,128)(2,1)S(1)}, u32[]{:S(2)}, u32[]{:S(2)}) collective-permute-start(bf16[576,512]{1,0:T(8,128)(2,1)} %collective-permute-done.6.refs_3_), channel_id=1, source_target_pairs={{0,1},{1,0},{2,3},{3,2},{4,5},{5,4},{6,7},{7,6},{8,9},{9,8},{10,11... | collective-permute-start | bytes 1769480 | tf_op jit(solution)/shard_map/ppermute | solution.py:483
  236.2 13.0 %collective-permute-start.20 = (bf16[2,64,1024]{2,1,0:T(8,128)(2,1)S(1)}, bf16[2,64,1024]{2,1,0:T(8,128)(2,1)S(1)}, u32[]{:S(2)}, u32[]{:S(2)}) collective-permute-start(bf16[2,64,1024]{2,1,0:T(8,128)(2,1)S(1)} %get-tuple-element.92), channel_id=1, source_target_pairs={{0,2},{1,3},{2,0},{3,1},{4,6},{5,7},{6,4},{7,5},{8,10},{9,11},{10,... | collective-permute-start | bytes 786440 | tf_op jit(solution)/shard_map/ppermute | solution.py:483
  242.7 13.3 %collective-permute-start.22 = (bf16[2,64,1024]{2,1,0:T(8,128)(2,1)S(1)}, bf16[2,64,1024]{2,1,0:T(8,128)(2,1)S(1)}, u32[]{:S(2)}, u32[]{:S(2)}) collective-permute-start(bf16[2,64,1024]{2,1,0:T(8,128)(2,1)S(1)} %fusion.3), channel_id=1, source_target_pairs={{0,4},{4,0},{8,12},{12,8},{1,5},{5,1},{9,13},{13,9},{2,6},{6,2},{1... | collective-permute-start | bytes 786440 | tf_op jit(solution)/shard_map/ppermute | solution.py:480
  249.2 12.7 %collective-permute-start.23 = (bf16[2,64,1024]{2,1,0:T(8,128)(2,1)S(1)}, bf16[2,64,1024]{2,1,0:T(8,128)(2,1)S(1)}, u32[]{:S(2)}, u32[]{:S(2)}) collective-permute-start(bf16[2,64,1024]{2,1,0:T(8,128)(2,1)S(1)} %fusion.6), channel_id=1, source_target_pairs={{0,4},{4,0},{8,12},{12,8},{1,5},{5,1},{9,13},{13,9},{2,6},{6,2},{1... | collective-permute-start | bytes 786440 | tf_op jit(solution)/shard_map/ppermute | solution.py:480
  253.8 11.2 %collective-permute-start.24 = (bf16[2,64,1024]{2,1,0:T(8,128)(2,1)S(1)}, bf16[2,64,1024]{2,1,0:T(8,128)(2,1)S(1)}, u32[]{:S(2)}, u32[]{:S(2)}) collective-permute-start(bf16[2,64,1024]{2,1,0:T(8,128)(2,1)S(1)} %get-tuple-element.103), channel_id=1, source_target_pairs={{0,3},{1,2},{2,1},{3,0},{4,7},{5,6},{6,5},{7,4},{8,11},{9,10},{10,... | collective-permute-start | bytes 786440 | tf_op jit(solution)/shard_map/ppermute | solution.py:483
  260.4 16.9 %collective-permute-start.25 = (bf16[2,2,64,1024]{3,2,1,0:T(8,128)(2,1)S(1)}, bf16[2,2,64,1024]{3,2,1,0:T(8,128)(2,1)S(1)}, u32[]{:S(2)}, u32[]{:S(2)}) collective-permute-start(bf16[2,2,64,1024]{3,2,1,0:T(8,128)(2,1)S(1)} %get-tuple-element.108), channel_id=1, source_target_pairs={{0,2},{1,3},{2,0},{3,1},{4,6},{5,7},{6,4},{7,5},{8,10},{9,11},{10,... | collective-permute-start | bytes 1572872 | tf_op jit(solution)/shard_map/ppermute | solution.py:483
  265.8 25.6 %all-to-all-start = ((bf16[4,2,2,2,16,256]{5,4,1,3,2,0:T(8,128)(2,1)}), bf16[4,2,2,2,16,256]{5,4,1,3,2,0:T(8,128)(2,1)}, u32[]{:S(2)}, u32[]{:S(2)}) async-start(bf16[4,2,2,2,16,256]{5,4,1,3,2,0:T(8,128)(2,1)} %copy_bitcast_fusion), calls=%async_computation | async-start | bytes 524288 | tf_op jit(solution)/shard_map/all_to_all | solution.py:538
  269.9 22.6 %collective-permute-start.19 = (bf16[2,64,1024]{2,1,0:T(8,128)(2,1)S(1)}, bf16[2,64,1024]{2,1,0:T(8,128)(2,1)}, u32[]{:S(2)}, u32[]{:S(2)}) collective-permute-start(bf16[2,64,1024]{2,1,0:T(8,128)(2,1)S(1)} %get-tuple-element.87), channel_id=1, source_target_pairs={{0,3},{1,2},{2,1},{3,0},{4,7},{5,6},{6,5},{7,4},{8,11},{9,10},{10,... | collective-permute-start | bytes 786440 | tf_op jit(solution)/shard_map/ppermute | solution.py:483
  271.8 25.3 %collective-permute-start.27 = (bf16[2,64,1024]{2,1,0:T(8,128)(2,1)}, bf16[2,64,1024]{2,1,0:T(8,128)(2,1)}, u32[]{:S(2)}, u32[]{:S(2)}) collective-permute-start(bf16[2,64,1024]{2,1,0:T(8,128)(2,1)} %fusion.5), channel_id=1, source_target_pairs={{0,8},{4,12},{8,0},{12,4},{1,9},{5,13},{9,1},{13,5},{2,10},{6,14},... | collective-permute-start | bytes 786440 | tf_op jit(solution)/shard_map/ppermute | solution.py:480
  274.3 28.2 %collective-permute-start.29 = (bf16[2,64,1024]{2,1,0:T(8,128)(2,1)}, bf16[2,64,1024]{2,1,0:T(8,128)(2,1)}, u32[]{:S(2)}, u32[]{:S(2)}) collective-permute-start(bf16[2,64,1024]{2,1,0:T(8,128)(2,1)} %fusion.2), channel_id=1, source_target_pairs={{0,8},{4,12},{8,0},{12,4},{1,9},{5,13},{9,1},{13,5},{2,10},{6,14},... | collective-permute-start | bytes 786440 | tf_op jit(solution)/shard_map/ppermute | solution.py:480
  274.7 27.8 %collective-permute-start.28 = (bf16[2,64,1024]{2,1,0:T(8,128)(2,1)}, bf16[2,64,1024]{2,1,0:T(8,128)(2,1)}, u32[]{:S(2)}, u32[]{:S(2)}) collective-permute-start(bf16[2,64,1024]{2,1,0:T(8,128)(2,1)} %fusion), channel_id=1, source_target_pairs={{0,4},{4,0},{8,12},{12,8},{1,5},{5,1},{9,13},{13,9},{2,6},{6,2},{1... | collective-permute-start | bytes 786440 | tf_op jit(solution)/shard_map/ppermute | solution.py:480
  277.3 25.2 %collective-permute-start.26 = (bf16[2,64,1024]{2,1,0:T(8,128)(2,1)S(1)}, bf16[2,64,1024]{2,1,0:T(8,128)(2,1)S(1)}, u32[]{:S(2)}, u32[]{:S(2)}) collective-permute-start(bf16[2,64,1024]{2,1,0:T(8,128)(2,1)S(1)} %fusion.7), channel_id=1, source_target_pairs={{0,4},{4,0},{8,12},{12,8},{1,5},{5,1},{9,13},{13,9},{2,6},{6,2},{1... | collective-permute-start | bytes 786440 | tf_op jit(solution)/shard_map/ppermute | solution.py:480
  (26 other events, 465.7 us)

commit v5 on v4

--- a/solution.py
+++ b/solution.py
@@ -183,6 +183,7 @@
         out_shape=[jax.ShapeDtypeStruct((count, 512), BF) for count in rows],
         in_specs=[pl.BlockSpec(memory_space=pltpu.SMEM)] + [whole] * 4,
         out_specs=[whole] * len(rows),
+        compiler_params=pltpu.CompilerParams(vmem_limit_bytes=12 * 1024 * 1024),
         name="prune",
     )(tile_mask, key_weight, value_weight, queries, cotangent)
 
@@ -247,8 +248,9 @@
         pack_kernel,
         out_shape=jax.ShapeDtypeStruct((PACKED + 192, 512), BF),
         in_specs=[here] * len(arrays),
-        out_specs=here,
+        out_specs=pl.BlockSpec(memory_space=pltpu.VMEM),
         scratch_shapes=[pltpu.SemaphoreType.DMA((8,))],
+        compiler_params=pltpu.CompilerParams(vmem_limit_bytes=6 * 1024 * 1024),
         cost_estimate=pl.CostEstimate(flops=1, bytes_accessed=1, transcendentals=0),
         name="pack",
     )(*arrays)
@@ -457,6 +459,7 @@
         out_shape=jax.ShapeDtypeStruct(shape, BF),
         in_specs=[vmem] * len(arrays),
         out_specs=vmem,
+        compiler_params=pltpu.CompilerParams(vmem_limit_bytes=12 * 1024 * 1024),
         name=name,
     )(*arrays)
 
@@ -491,13 +494,13 @@
     w_own, m1, m2, m3 = prune(
         tile_mask, key_weight, value_weight, queries.reshape(64, 1024), cotangent.reshape(64, 1024)
     )
-    e1, m2, w_own = together(e1, m2, w_own)
+    e1, e2, m2, w_own = together(e1, e2, m2, w_own)
     z2 = along(m2, 2)
-    e2, m1 = together(e2, m1)
-    z1 = along(m1, 1)
     e3 = along(e2, 1)
     x1, x2 = flip(e1, 2), flip(e2, 2)
-    x1, e3, m3 = together(x1, e3, m3)
+    x1, m1 = together(x1, m1)
+    z1 = along(m1, 1)
+    x2, m3 = together(x2, m3)
     z3 = along(m3, 3)
     x3 = flip(e3, 2)
     y1, y2 = across(z1), across(z2)
@@ -520,7 +523,8 @@
     b2, a2 = flip(b2, 3), flip(a2, 2)
     far3, own = together(summed(core[3], b3), own)
     far3 = along(far3, 1)
-    near3, core = together(summed(own[3], a3), core)
+    back = jnp.stack([front[0], other]).reshape(2, 2, 2, SEQ, 16, 256).transpose(3, 0, 1, 2, 4, 5)
+    near3, core, back = together(summed(own[3], a3), core, back)
     near3 = along(near3, 1)
     b2, b1, a10 = together(b2, b1, a10)
     b1, a10 = flip(b1, 3), flip(a10, 2)
@@ -528,11 +532,11 @@
     far2 = along(far2, 2)
     a2, b0 = together(a2, b0)
     b0 = flip(b0, 3)
-    back = jnp.stack([front[0], other]).reshape(2, 2, 2, SEQ, 16, 256).transpose(3, 0, 1, 2, 4, 5)
     near2, core = together(summed(own[2], a2, near3), core)
     near2 = along(near2, 2)
-    far1, own, back = together(summed(core[1], b1), own, back)
+    far1, own = together(summed(core[1], b1), own)
     far1 = along(far1, 1)
+    a10, near2, far2 = together(a10, near2, far2)
     near1 = along(summed(own[1], a10[0]), 1)
     from_core = core
     back = lax.all_to_all(back, "seq", split_axis=0, concat_axis=0, tiled=True)

time: 307 us -> 211 us (0.69)
  Pallas kernels: 129 us -> 24.3 us
  starting transfers between devices: 40.6 us -> 47.9 us
  other arithmetic: 3.37 us -> 8.08 us
  local copies, waits for them, and re-layouts: 13.7 us -> 9.19 us
    pallas_call x1, Pallas kernels: 102 us -> 0.57 us  [pack_call(): pl.pallas_call(pack_kernel, out_shape=jax.ShapeDtypeStruct((PACKED + 192,...]
    all_to_all x1, waiting for transfers between devices: 13.9 us -> 0.01 us  [body(): back = lax.all_to_all(back, 'seq', split_axis=0, concat_axis=0, tiled=True)]
    ppermute x12, waiting for transfers between devices: 48.1 us -> 62 us  [along(): return lax.ppermute(value, 'seq', [(a, a ^ k) for a in range(SEQ)])]
    all_to_all x1, starting transfers between devices: 4.04 us -> 10.5 us  [body(): back = lax.all_to_all(back, 'seq', split_axis=0, concat_axis=0, tiled=True)]
    ppermute x3, waiting for transfers between devices: 0.01 us -> 5.43 us  [across(): return lax.ppermute(value, 'grp', [(0, 1), (1, 0)])]
    convert_element_type x6, other arithmetic: 2.57 us -> 7.28 us  [summed(): return total.astype(BF)]
    unnamed x38 -> x18, local copies, waits for them, and re-layouts: 10.9 us -> 6.43 us
    ppermute x15, waiting for transfers between devices: 56.6 us -> 52.3 us  [flip(): return lax.ppermute(value, 'head', [(a, a ^ bits) for a in range(4)])]
  transfers between devices with their start and end apart: 31 -> 31, of which waited for: 18 -> 18; matrix products, arithmetic and copies ran while one was open for 2% -> 5% of each run, Pallas kernels for 3% -> 3%
where the time goes in v5:
time: 211 us; the launch traced here: 210 us
  waiting for transfers between devices  120 us (57%)
  starting transfers between devices  47.9 us (23%)
  Pallas kernels  24.3 us (12%)
  local copies, waits for them, and re-layouts  9.19 us (4%)
  other arithmetic  8.08 us (4%)
    ppermute x12, waiting for transfers between devices, along(): return lax.ppermute(value, 'seq', [(a, a ^ k) for a in range(SEQ)])  62 us
    ppermute x15, waiting for transfers between devices, flip(): return lax.ppermute(value, 'head', [(a, a ^ bits) for a in range(4)])  52.3 us
    ppermute x12, starting transfers between devices, along(): return lax.ppermute(value, 'seq', [(a, a ^ k) for a in range(SEQ)])  21.4 us
    pallas_call x1, Pallas kernels, main_call(): pl.pallas_call(main_kernel, out_shape=[front, front, jax.ShapeDtypeStruct...  15.6 us
    ppermute x15, starting transfers between devices, flip(): return lax.ppermute(value, 'head', [(a, a ^ bits) for a in range(4)])  12.1 us
    all_to_all x1, starting transfers between devices, body(): back = lax.all_to_all(back, 'seq', split_axis=0, concat_axis=0, tiled=True)  10.5 us
    convert_element_type x6, other arithmetic, summed(): return total.astype(BF)  7.28 us
    unnamed x18, local copies, waits for them, and re-layouts  6.43 us
  transfers between devices with their start and end apart: 31, of which 18 were waited for; matrix products, arithmetic and copies ran while one was open for 5% of the time, Pallas kernels for 3%

profile of v5, /device:TPU:0, one launch (start us, length us, event | category | flops | bytes accessed | tf_op | source)
XLA Modules:
  0.0 210.0 jit_solution(10991999401319179835)
XLA Ops:
  1.7 4.1 %collective-permute-start.1 = (bf16[64,4096]{1,0:T(8,128)(2,1)S(1)}, bf16[64,4096]{1,0:T(8,128)(2,1)S(1)}, u32[]{:S(2)}, u32[]{:S(2)}) collective-permute-start(bf16[64,4096]{1,0:T(8,128)(2,1)S(1)} %dynamic-slice_bitcast_fusion), channel_id=1, source_target_pairs={{0,8},{4,12},{8,0},{12,4},{1,9},{5,13},{9,1},{13,5},{2,10},{6,14},... | collective-permute-start | bytes 1572872 | tf_op jit(solution)/shard_map/ppermute | solution.py:483
  14.6 14.4 %collective-permute-done.1.refs_2_ = bf16[64,4096]{1,0:T(8,128)(2,1)S(1)} collective-permute-done((bf16[64,4096]{1,0:T(8,128)(2,1)S(1)}, bf16[64,4096]{1,0:T(8,128)(2,1)S(1)}, u32[]{:S(2)}, u32[]{:S(2)}) %collective-permute-start.1) | collective-permute-done | bytes 524320 | tf_op jit(solution)/shard_map/ppermute | solution.py:483
  32.1 10.0 %collective-permute-done.7.refs_4_ = bf16[64,4096]{1,0:T(8,128)(2,1)S(1)} collective-permute-done((bf16[64,4096]{1,0:T(8,128)(2,1)S(1)}, bf16[64,4096]{1,0:T(8,128)(2,1)S(1)}, u32[]{:S(2)}, u32[]{:S(2)}) %collective-permute-start.7) | collective-permute-done | bytes 524320 | tf_op jit(solution)/shard_map/ppermute | solution.py:486
  45.4 9.7 %collective-permute-done.2.refs_5_ = bf16[64,4096]{1,0:T(8,128)(2,1)S(1)} collective-permute-done((bf16[64,4096]{1,0:T(8,128)(2,1)S(1)}, bf16[64,4096]{1,0:T(8,128)(2,1)S(1)}, u32[]{:S(2)}, u32[]{:S(2)}) %collective-permute-start.2) | collective-permute-done | bytes 524320 | tf_op jit(solution)/shard_map/ppermute | solution.py:486
  55.1 4.2 %collective-permute-start.5 = (bf16[576,512]{1,0:T(8,128)(2,1)S(1)}, bf16[576,512]{1,0:T(8,128)(2,1)S(1)}, u32[]{:S(2)}, u32[]{:S(2)}) collective-permute-start(bf16[576,512]{1,0:T(8,128)(2,1)S(1)} %get-tuple-element.66), channel_id=1, source_target_pairs={{0,12},{4,8},{8,4},{12,0},{1,13},{5,9},{9,5},{13,1},{2,14},{6,10},... | collective-permute-start | bytes 1769480 | tf_op jit(solution)/shard_map/ppermute | solution.py:483
  60.9 8.2 %collective-permute-done.8.z1 = bf16[576,512]{1,0:T(8,128)(2,1)S(1)} collective-permute-done((bf16[576,512]{1,0:T(8,128)(2,1)S(1)}, bf16[576,512]{1,0:T(8,128)(2,1)S(1)}, u32[]{:S(2)}, u32[]{:S(2)}) %collective-permute-start.8) | collective-permute-done | bytes 589856 | tf_op jit(solution)/shard_map/ppermute | solution.py:483
  70.4 19.7 %collective-permute-done.3.refs_3_ = bf16[64,4096]{1,0:T(8,128)(2,1)S(1)} collective-permute-done((bf16[64,4096]{1,0:T(8,128)(2,1)S(1)}, bf16[64,4096]{1,0:T(8,128)(2,1)S(1)}, u32[]{:S(2)}, u32[]{:S(2)}) %collective-permute-start.3) | collective-permute-done | bytes 524320 | tf_op jit(solution)/shard_map/ppermute | solution.py:483
  91.4 9.6 %collective-permute-done.4.refs_6_ = bf16[64,4096]{1,0:T(8,128)(2,1)S(1)} collective-permute-done((bf16[64,4096]{1,0:T(8,128)(2,1)S(1)}, bf16[64,4096]{1,0:T(8,128)(2,1)S(1)}, u32[]{:S(2)}, u32[]{:S(2)}) %collective-permute-start.4) | collective-permute-done | bytes 524320 | tf_op jit(solution)/shard_map/ppermute | solution.py:486
  103.0 4.7 %collective-permute-done.12.refs_8_.refs_5_ = bf16[3264,512]{1,0:T(8,128)(2,1)S(1)} collective-permute-done((bf16[3264,512]{1,0:T(8,128)(2,1)S(1)}, bf16[3264,512]{1,0:T(8,128)(2,1)S(1)}, u32[]{:S(2)}, u32[]{:S(2)}) %collective-permute-start.12) | collective-permute-done | bytes 3342368 | tf_op jit(solution)/shard_map/ppermute | solution.py:486
  107.7 4.4 %early.1 = (f32[2,512,512]{2,1,0:T(8,128)S(1)}, bf16[512,1024]{1,0:T(8,128)(2,1)S(1)}) custom-call(bf16[4,64,4096]{2,1,0:T(8,128)(2,1)S(1)} %copy-done, bf16[64,4096]{1,0:T(8,128)(2,1)S(1)} %collective-permute-done.refs_1_, bf16[64,4096]{1,0:T(8,128)(2,1)S(1)} %collective-permute-done.1.refs_2_, bf16[64,4096]{1,0:T(8,128)(2,1)S(1)} %collective-permute-done.3.refs_3_, ...), custom_call_target="tpu_custom_call" | custom-call | flops 1 | bytes 1 | tf_op jit(solution)/shard_map/early/pallas_call | solution.py:305
  112.0 5.4 %collective-permute-done.6.refs_4_ = bf16[576,512]{1,0:T(8,128)(2,1)S(1)} collective-permute-done((bf16[576,512]{1,0:T(8,128)(2,1)S(1)}, bf16[576,512]{1,0:T(8,128)(2,1)S(1)}, u32[]{:S(2)}, u32[]{:S(2)}) %collective-permute-start.6) | collective-permute-done | bytes 589856 | tf_op jit(solution)/shard_map/ppermute | solution.py:489
  117.5 2.0 collective-permute-done.14.refs_7_
  119.5 15.6 %attend.1 = (bf16[2,2,64,256]{3,2,1,0:T(8,128)(2,1)S(1)}, bf16[2,2,64,256]{3,2,1,0:T(8,128)(2,1)S(1)}, f32[4,2,64,1024]{3,2,1,0:T(8,128)S(1)}, bf16[2,64,1024]{2...) custom-call(s32[4]{0:T(128)S(1)} %copy-done.8, ...), custom_call_target="tpu_custom_call" | custom-call | flops 6000000000 | bytes 25165824 | tf_op jit(solution)/shard_map/attend/pallas_call | solution.py:416
  138.6 5.4 %collective-permute-done.15 = bf16[2,64,1024]{2,1,0:T(8,128)(2,1)S(1)} collective-permute-done((bf16[2,64,1024]{2,1,0:T(8,128)(2,1)S(1)}, bf16[2,64,1024]{2,1,0:T(8,128)(2,1)S(1)}, u32[]{:S(2)}, u32[]{:S(2)}) %collective-permute-start.15) | collective-permute-done | bytes 262176 | tf_op jit(solution)/shard_map/ppermute | solution.py:486
  146.9 3.7 %collective-permute-done.20 = bf16[2,64,1024]{2,1,0:T(8,128)(2,1)S(1)} collective-permute-done((bf16[2,64,1024]{2,1,0:T(8,128)(2,1)S(1)}, bf16[2,64,1024]{2,1,0:T(8,128)(2,1)S(1)}, u32[]{:S(2)}, u32[]{:S(2)}) %collective-permute-start.20) | collective-permute-done | bytes 262176 | tf_op jit(solution)/shard_map/ppermute | solution.py:486
  152.1 10.5 %all-to-all-start = ((bf16[4,2,2,2,16,256]{5,4,1,3,2,0:T(8,128)(2,1)}), bf16[4,2,2,2,16,256]{5,4,1,3,2,0:T(8,128)(2,1)}, u32[]{:S(2)}, u32[]{:S(2)}) async-start(bf16[4,2,2,2,16,256]{5,4,1,3,2,0:T(8,128)(2,1)} %copy_bitcast_fusion), calls=%async_computation | async-start | bytes 524288 | tf_op jit(solution)/shard_map/all_to_all | solution.py:542
  168.1 5.6 %collective-permute-start.26 = (bf16[2,64,1024]{2,1,0:T(8,128)(2,1)}, bf16[2,64,1024]{2,1,0:T(8,128)(2,1)S(1)}, u32[]{:S(2)}, u32[]{:S(2)}) collective-permute-start(bf16[2,64,1024]{2,1,0:T(8,128)(2,1)} %fusion.5), channel_id=1, source_target_pairs={{0,8},{4,12},{8,0},{12,4},{1,9},{5,13},{9,1},{13,5},{2,10},{6,14},... | collective-permute-start | bytes 786440 | tf_op jit(solution)/shard_map/ppermute | solution.py:483
  176.0 6.7 %collective-permute-done.24 = bf16[2,64,1024]{2,1,0:T(8,128)(2,1)} collective-permute-done((bf16[2,64,1024]{2,1,0:T(8,128)(2,1)}, bf16[2,64,1024]{2,1,0:T(8,128)(2,1)}, u32[]{:S(2)}, u32[]{:S(2)}) %collective-permute-start.24) | collective-permute-done | bytes 262176 | tf_op jit(solution)/shard_map/ppermute | solution.py:486
  183.7 2.1 collective-permute-start.29
  185.8 6.5 %collective-permute-done.26.near2 = bf16[2,64,1024]{2,1,0:T(8,128)(2,1)S(1)} collective-permute-done((bf16[2,64,1024]{2,1,0:T(8,128)(2,1)}, bf16[2,64,1024]{2,1,0:T(8,128)(2,1)S(1)}, u32[]{:S(2)}, u32[]{:S(2)}) %collective-permute-start.26) | collective-permute-done | bytes 262176 | tf_op jit(solution)/shard_map/ppermute | solution.py:483
  192.3 5.2 %collective-permute-done.27.far2 = bf16[2,64,1024]{2,1,0:T(8,128)(2,1)} collective-permute-done((bf16[2,64,1024]{2,1,0:T(8,128)(2,1)}, bf16[2,64,1024]{2,1,0:T(8,128)(2,1)}, u32[]{:S(2)}, u32[]{:S(2)}) %collective-permute-start.27) | collective-permute-done | bytes 262176 | tf_op jit(solution)/shard_map/ppermute | solution.py:483
  200.0 2.1 %collective-permute-done.29.far1 = bf16[2,64,1024]{2,1,0:T(8,128)(2,1)S(1)} collective-permute-done((bf16[2,64,1024]{2,1,0:T(8,128)(2,1)S(1)}, bf16[2,64,1024]{2,1,0:T(8,128)(2,1)S(1)}, u32[]{:S(2)}, u32[]{:S(2)}) %collective-permute-start.29) | collective-permute-done | bytes 262176 | tf_op jit(solution)/shard_map/ppermute | solution.py:483
  202.2 5.6 %collective-permute-done.28.near1 = bf16[2,64,1024]{2,1,0:T(8,128)(2,1)S(1)} collective-permute-done((bf16[2,64,1024]{2,1,0:T(8,128)(2,1)S(1)}, bf16[2,64,1024]{2,1,0:T(8,128)(2,1)S(1)}, u32[]{:S(2)}, u32[]{:S(2)}) %collective-permute-start.28) | collective-permute-done | bytes 262176 | tf_op jit(solution)/shard_map/ppermute | solution.py:483
  207.8 2.2 %final.1 = bf16[4,64,1024]{2,1,0:T(8,128)(2,1)} custom-call(f32[4,2,64,1024]{3,2,1,0:T(8,128)S(1)} %get-tuple-element.110.own, bf16[4,2,64,1024]{3,2,1,0:T(8,128)(2,1)S(1)} %collective-permute-done.16.core, bf16[2,2,64,1024]{3,2,1,0:T(8,128)(2,1)} %collective-permute-done.25.near, bf16[2,64,1024]{2,1,0:T(8,128)(2,1)} %collective-permute-done.19.far, ...), custom_call_target="tpu_custom_call" | custom-call | tf_op jit(solution)/shard_map/final/pallas_call | solution.py:457
  (73 shorter events, 41.5 us)
Async XLA Ops:
  1.7 27.4 %collective-permute-start.1 = (bf16[64,4096]{1,0:T(8,128)(2,1)S(1)}, bf16[64,4096]{1,0:T(8,128)(2,1)S(1)}, u32[]{:S(2)}, u32[]{:S(2)}) collective-permute-start(bf16[64,4096]{1,0:T(8,128)(2,1)S(1)} %dynamic-slice_bitcast_fusion), channel_id=1, source_target_pairs={{0,8},{4,12},{8,0},{12,4},{1,9},{5,13},{9,1},{13,5},{2,10},{6,14},... | collective-permute-start | bytes 1572872 | tf_op jit(solution)/shard_map/ppermute | solution.py:483
  5.8 23.5 %collective-permute-start = (bf16[64,4096]{1,0:T(8,128)(2,1)S(1)}, bf16[64,4096]{1,0:T(8,128)(2,1)S(1)}, u32[]{:S(2)}, u32[]{:S(2)}) collective-permute-start(bf16[64,4096]{1,0:T(8,128)(2,1)S(1)} %dynamic-slice_bitcast_fusion), channel_id=1, source_target_pairs={{0,4},{4,0},{8,12},{12,8},{1,5},{5,1},{9,13},{13,9},{2,6},{6,2},{1... | collective-permute-start | bytes 1572872 | tf_op jit(solution)/shard_map/ppermute | solution.py:483
  29.3 12.9 %collective-permute-start.7 = (bf16[64,4096]{1,0:T(8,128)(2,1)S(1)}, bf16[64,4096]{1,0:T(8,128)(2,1)S(1)}, u32[]{:S(2)}, u32[]{:S(2)}) collective-permute-start(bf16[64,4096]{1,0:T(8,128)(2,1)S(1)} %collective-permute-done.refs_1_), channel_id=1, source_target_pairs={{0,2},{1,3},{2,0},{3,1},{4,6},{5,7},{6,4},{7,5},{8,10},{9,11},{10,... | collective-permute-start | bytes 1572872 | tf_op jit(solution)/shard_map/ppermute | solution.py:486
  30.8 28.6 %collective-permute-start.9 = (bf16[576,512]{1,0:T(8,128)(2,1)S(1)}, bf16[576,512]{1,0:T(8,128)(2,1)S(1)}, u32[]{:S(2)}, u32[]{:S(2)}) collective-permute-start(bf16[576,512]{1,0:T(8,128)(2,1)S(1)} %get-tuple-element.76), channel_id=1, source_target_pairs={{0,8},{4,12},{8,0},{12,4},{1,9},{5,13},{9,1},{13,5},{2,10},{6,14},... | collective-permute-start | bytes 1769480 | tf_op jit(solution)/shard_map/ppermute | solution.py:483
  42.1 27.0 %collective-permute-start.8 = (bf16[576,512]{1,0:T(8,128)(2,1)S(1)}, bf16[576,512]{1,0:T(8,128)(2,1)S(1)}, u32[]{:S(2)}, u32[]{:S(2)}) collective-permute-start(bf16[576,512]{1,0:T(8,128)(2,1)S(1)} %get-tuple-element.75), channel_id=1, source_target_pairs={{0,4},{4,0},{8,12},{12,8},{1,5},{5,1},{9,13},{13,9},{2,6},{6,2},{1... | collective-permute-start | bytes 1769480 | tf_op jit(solution)/shard_map/ppermute | solution.py:483
  43.6 11.6 %collective-permute-start.2 = (bf16[64,4096]{1,0:T(8,128)(2,1)S(1)}, bf16[64,4096]{1,0:T(8,128)(2,1)S(1)}, u32[]{:S(2)}, u32[]{:S(2)}) collective-permute-start(bf16[64,4096]{1,0:T(8,128)(2,1)S(1)} %collective-permute-done.1.refs_2_), channel_id=1, source_target_pairs={{0,2},{1,3},{2,0},{3,1},{4,6},{5,7},{6,4},{7,5},{8,10},{9,11},{10,... | collective-permute-start | bytes 1572872 | tf_op jit(solution)/shard_map/ppermute | solution.py:486
  45.0 45.0 %collective-permute-start.3 = (bf16[64,4096]{1,0:T(8,128)(2,1)S(1)}, bf16[64,4096]{1,0:T(8,128)(2,1)S(1)}, u32[]{:S(2)}, u32[]{:S(2)}) collective-permute-start(bf16[64,4096]{1,0:T(8,128)(2,1)S(1)} %collective-permute-done.1.refs_2_), channel_id=1, source_target_pairs={{0,4},{4,0},{8,12},{12,8},{1,5},{5,1},{9,13},{13,9},{2,6},{6,2},{1... | collective-permute-start | bytes 1572872 | tf_op jit(solution)/shard_map/ppermute | solution.py:483
  55.1 45.9 %collective-permute-start.5 = (bf16[576,512]{1,0:T(8,128)(2,1)S(1)}, bf16[576,512]{1,0:T(8,128)(2,1)S(1)}, u32[]{:S(2)}, u32[]{:S(2)}) collective-permute-start(bf16[576,512]{1,0:T(8,128)(2,1)S(1)} %get-tuple-element.66), channel_id=1, source_target_pairs={{0,12},{4,8},{8,4},{12,0},{1,13},{5,9},{9,5},{13,1},{2,14},{6,10},... | collective-permute-start | bytes 1769480 | tf_op jit(solution)/shard_map/ppermute | solution.py:483
  59.4 41.7 %collective-permute-start.11 = (bf16[576,512]{1,0:T(8,128)(2,1)S(1)}, bf16[576,512]{1,0:T(8,128)(2,1)S(1)}, u32[]{:S(2)}, u32[]{:S(2)}) collective-permute-start(bf16[576,512]{1,0:T(8,128)(2,1)S(1)} %collective-permute-done.9.z2), channel_id=1, source_target_pairs={{0,16},{16,0},{1,17},{17,1},{2,18},{18,2},{3,19},{19,3},{4,20},{20... | collective-permute-start | bytes 1769480 | tf_op jit(solution)/shard_map/ppermute | solution.py:489
  69.1 31.9 %collective-permute-start.10 = (bf16[576,512]{1,0:T(8,128)(2,1)S(1)}, bf16[576,512]{1,0:T(8,128)(2,1)S(1)}, u32[]{:S(2)}, u32[]{:S(2)}) collective-permute-start(bf16[576,512]{1,0:T(8,128)(2,1)S(1)} %collective-permute-done.8.z1), channel_id=1, source_target_pairs={{0,16},{16,0},{1,17},{17,1},{2,18},{18,2},{3,19},{19,3},{4,20},{20... | collective-permute-start | bytes 1769480 | tf_op jit(solution)/shard_map/ppermute | solution.py:489
  101.7 15.7 %collective-permute-start.6 = (bf16[576,512]{1,0:T(8,128)(2,1)S(1)}, bf16[576,512]{1,0:T(8,128)(2,1)S(1)}, u32[]{:S(2)}, u32[]{:S(2)}) collective-permute-start(bf16[576,512]{1,0:T(8,128)(2,1)S(1)} %collective-permute-done.5.refs_3_), channel_id=1, source_target_pairs={{0,16},{16,0},{1,17},{17,1},{2,18},{18,2},{3,19},{19,3},{4,20},{20... | collective-permute-start | bytes 1769480 | tf_op jit(solution)/shard_map/ppermute | solution.py:489
  102.8 14.7 %collective-permute-start.13 = (bf16[576,512]{1,0:T(8,128)(2,1)S(1)}, bf16[576,512]{1,0:T(8,128)(2,1)S(1)}, u32[]{:S(2)}, u32[]{:S(2)}) collective-permute-start(bf16[576,512]{1,0:T(8,128)(2,1)S(1)} %collective-permute-done.5.refs_3_), channel_id=1, source_target_pairs={{0,1},{1,0},{2,3},{3,2},{4,5},{5,4},{6,7},{7,6},{8,9},{9,8},{10,11... | collective-permute-start | bytes 1769480 | tf_op jit(solution)/shard_map/ppermute | solution.py:486
  137.3 13.3 %collective-permute-start.20 = (bf16[2,64,1024]{2,1,0:T(8,128)(2,1)S(1)}, bf16[2,64,1024]{2,1,0:T(8,128)(2,1)S(1)}, u32[]{:S(2)}, u32[]{:S(2)}) collective-permute-start(bf16[2,64,1024]{2,1,0:T(8,128)(2,1)S(1)} %get-tuple-element.95), channel_id=1, source_target_pairs={{0,2},{1,3},{2,0},{3,1},{4,6},{5,7},{6,4},{7,5},{8,10},{9,11},{10,... | collective-permute-start | bytes 786440 | tf_op jit(solution)/shard_map/ppermute | solution.py:486
  144.8 19.5 %collective-permute-start.22 = (bf16[2,64,1024]{2,1,0:T(8,128)(2,1)}, bf16[2,64,1024]{2,1,0:T(8,128)(2,1)}, u32[]{:S(2)}, u32[]{:S(2)}) collective-permute-start(bf16[2,64,1024]{2,1,0:T(8,128)(2,1)} %fusion.3), channel_id=1, source_target_pairs={{0,4},{4,0},{8,12},{12,8},{1,5},{5,1},{9,13},{13,9},{2,6},{6,2},{1... | collective-permute-start | bytes 786440 | tf_op jit(solution)/shard_map/ppermute | solution.py:483
  144.8 21.4 %collective-permute-start.18 = (bf16[2,64,1024]{2,1,0:T(8,128)(2,1)S(1)}, bf16[2,64,1024]{2,1,0:T(8,128)(2,1)}, u32[]{:S(2)}, u32[]{:S(2)}) collective-permute-start(bf16[2,64,1024]{2,1,0:T(8,128)(2,1)S(1)} %get-tuple-element.88), channel_id=1, source_target_pairs={{0,2},{1,3},{2,0},{3,1},{4,6},{5,7},{6,4},{7,5},{8,10},{9,11},{10,... | collective-permute-start | bytes 786440 | tf_op jit(solution)/shard_map/ppermute | solution.py:486
  146.1 16.6 %collective-permute-start.21 = (bf16[2,64,1024]{2,1,0:T(8,128)(2,1)}, bf16[2,64,1024]{2,1,0:T(8,128)(2,1)}, u32[]{:S(2)}, u32[]{:S(2)}) collective-permute-start(bf16[2,64,1024]{2,1,0:T(8,128)(2,1)} %get-tuple-element.100), channel_id=1, source_target_pairs={{0,3},{1,2},{2,1},{3,0},{4,7},{5,6},{6,5},{7,4},{8,11},{9,10},{10,... | collective-permute-start | bytes 786440 | tf_op jit(solution)/shard_map/ppermute | solution.py:486
  152.1 14.1 %collective-permute-start.23 = (bf16[2,64,1024]{2,1,0:T(8,128)(2,1)}, bf16[2,64,1024]{2,1,0:T(8,128)(2,1)}, u32[]{:S(2)}, u32[]{:S(2)}) collective-permute-start(bf16[2,64,1024]{2,1,0:T(8,128)(2,1)} %fusion.6), channel_id=1, source_target_pairs={{0,4},{4,0},{8,12},{12,8},{1,5},{5,1},{9,13},{13,9},{2,6},{6,2},{1... | collective-permute-start | bytes 786440 | tf_op jit(solution)/shard_map/ppermute | solution.py:483
  152.1 22.9 %all-to-all-start = ((bf16[4,2,2,2,16,256]{5,4,1,3,2,0:T(8,128)(2,1)}), bf16[4,2,2,2,16,256]{5,4,1,3,2,0:T(8,128)(2,1)}, u32[]{:S(2)}, u32[]{:S(2)}) async-start(bf16[4,2,2,2,16,256]{5,4,1,3,2,0:T(8,128)(2,1)} %copy_bitcast_fusion), calls=%async_computation | async-start | bytes 524288 | tf_op jit(solution)/shard_map/all_to_all | solution.py:542
  162.6 34.9 %collective-permute-start.25 = (bf16[2,2,64,1024]{3,2,1,0:T(8,128)(2,1)}, bf16[2,2,64,1024]{3,2,1,0:T(8,128)(2,1)}, u32[]{:S(2)}, u32[]{:S(2)}) collective-permute-start(bf16[2,2,64,1024]{3,2,1,0:T(8,128)(2,1)} %copy-done.6), channel_id=1, source_target_pairs={{0,2},{1,3},{2,0},{3,1},{4,6},{5,7},{6,4},{7,5},{8,10},{9,11},{10,... | collective-permute-start | bytes 1572872 | tf_op jit(solution)/shard_map/ppermute | solution.py:486
  166.2 16.5 %collective-permute-start.24 = (bf16[2,64,1024]{2,1,0:T(8,128)(2,1)}, bf16[2,64,1024]{2,1,0:T(8,128)(2,1)}, u32[]{:S(2)}, u32[]{:S(2)}) collective-permute-start(bf16[2,64,1024]{2,1,0:T(8,128)(2,1)} %get-tuple-element.109), channel_id=1, source_target_pairs={{0,3},{1,2},{2,1},{3,0},{4,7},{5,6},{6,5},{7,4},{8,11},{9,10},{10,... | collective-permute-start | bytes 786440 | tf_op jit(solution)/shard_map/ppermute | solution.py:486
  168.1 24.2 %collective-permute-start.26 = (bf16[2,64,1024]{2,1,0:T(8,128)(2,1)}, bf16[2,64,1024]{2,1,0:T(8,128)(2,1)S(1)}, u32[]{:S(2)}, u32[]{:S(2)}) collective-permute-start(bf16[2,64,1024]{2,1,0:T(8,128)(2,1)} %fusion.5), channel_id=1, source_target_pairs={{0,8},{4,12},{8,0},{12,4},{1,9},{5,13},{9,1},{13,5},{2,10},{6,14},... | collective-permute-start | bytes 786440 | tf_op jit(solution)/shard_map/ppermute | solution.py:483
  173.6 23.9 %collective-permute-start.27 = (bf16[2,64,1024]{2,1,0:T(8,128)(2,1)}, bf16[2,64,1024]{2,1,0:T(8,128)(2,1)}, u32[]{:S(2)}, u32[]{:S(2)}) collective-permute-start(bf16[2,64,1024]{2,1,0:T(8,128)(2,1)} %fusion.2), channel_id=1, source_target_pairs={{0,8},{4,12},{8,0},{12,4},{1,9},{5,13},{9,1},{13,5},{2,10},{6,14},... | collective-permute-start | bytes 786440 | tf_op jit(solution)/shard_map/ppermute | solution.py:483
  173.7 25.6 %collective-permute-start.19 = (bf16[2,64,1024]{2,1,0:T(8,128)(2,1)}, bf16[2,64,1024]{2,1,0:T(8,128)(2,1)}, u32[]{:S(2)}, u32[]{:S(2)}) collective-permute-start(bf16[2,64,1024]{2,1,0:T(8,128)(2,1)} %copy-done.7), channel_id=1, source_target_pairs={{0,3},{1,2},{2,1},{3,0},{4,7},{5,6},{6,5},{7,4},{8,11},{9,10},{10,... | collective-permute-start | bytes 786440 | tf_op jit(solution)/shard_map/ppermute | solution.py:486
  183.7 18.5 %collective-permute-start.29 = (bf16[2,64,1024]{2,1,0:T(8,128)(2,1)S(1)}, bf16[2,64,1024]{2,1,0:T(8,128)(2,1)S(1)}, u32[]{:S(2)}, u32[]{:S(2)}) collective-permute-start(bf16[2,64,1024]{2,1,0:T(8,128)(2,1)S(1)} %fusion), channel_id=1, source_target_pairs={{0,4},{4,0},{8,12},{12,8},{1,5},{5,1},{9,13},{13,9},{2,6},{6,2},{1... | collective-permute-start | bytes 786440 | tf_op jit(solution)/shard_map/ppermute | solution.py:483
  (16 other events, 131.3 us)

commit v6 on v5

--- a/solution.py
+++ b/solution.py
@@ -195,16 +195,6 @@
 
 def dot(a, b, dims=NN):
     return lax.dot_general(a, b, dims, preferred_element_type=F32)
-
-
-def partial_blocks(block, grad, weight, part):
-    def column(n, carry):
-        at = pl.ds(pl.multiple_of(block * 1024 + n * 256, 256), 256)
-        total = dot(grad[0], weight[0, at, :], NT) + dot(grad[1], weight[1, at, :], NT)
-        part[:, :, pl.ds(pl.multiple_of(n * 256, 256), 256)] = total.reshape(2, 256, 256)
-        return carry
-
-    lax.fori_loop(0, 4, column, 0)
 
 
 class Mover:
@@ -329,7 +319,7 @@
     (
         att_ref, qg_ref, own_ref,
         a3, b3, a2, b2, b1, a10, b0, core_ref,
-        w_s, qc_s, grad_s, part_s, sems,
+        w_s, qc_s, grad_s, sems,
     ) = refs[8:]
     s, g, h = lax.axis_index("seq"), lax.axis_index("grp"), lax.axis_index("head")
     c = lax.rem(h, 2)
@@ -387,8 +377,13 @@
             query_grad = dot(score_grad, keys)
             att_ref[slot, doc] = gather_heads(output).astype(BF)
             qg_ref[slot, doc] = gather_heads(query_grad).astype(BF)
-            grad_s[core, doc * 256 : (doc + 1) * 256, 0:256] = dot(score_grad, query, TN).astype(BF)
-            grad_s[core, doc * 256 : (doc + 1) * 256, 256:512] = dot(low, cot, TN).astype(BF)
+            key_grad = dot(score_grad, query, TN).astype(BF)
+            value_grad = dot(low, cot, TN).astype(BF)
+            for at in range(4):
+                first = lax.bitwise_xor(s, at) * 128 + doc * 64
+                to = pl.ds(pl.multiple_of(first, 64), 64)
+                grad_s[core, to, 0:256] = key_grad[at * 64 : at * 64 + 64]
+                grad_s[core, to, 256:512] = value_grad[at * 64 : at * 64 + 64]
 
     for copy in later:
         copy.wait()
@@ -400,11 +395,16 @@
         (1, cores),
         (0, owns),
     ):
-        partial_blocks(lax.bitwise_xor(h, flip), grad_s, w_s, part_s)
-        for k in range(4):
-            at = pl.ds(pl.multiple_of(lax.bitwise_xor(s, k) * 64, 64), 64)
-            for doc in range(2):
-                outs[k][doc] = part_s[doc, at, :].astype(outs[k].dtype)
+        block = lax.bitwise_xor(h, flip)
+        for n in range(4):
+            at = pl.ds(pl.multiple_of(block * 1024 + n * 256, 256), 256)
+            total = dot(grad_s[0], w_s[0, at, :], NT) + dot(grad_s[1], w_s[1, at, :], NT)
+            for k in range(4):
+                for doc in range(2):
+                    first = k * 128 + doc * 64
+                    outs[k][doc, :, n * 256 : n * 256 + 256] = total[first : first + 64].astype(
+                        outs[k].dtype
+                    )
 
 
 def main_call(lengths, arrays):
@@ -430,7 +430,6 @@
             pltpu.VMEM((2, 4096, 512), BF),
             pltpu.VMEM((2, 4, 64, 512), BF),
             pltpu.VMEM((2, 512, 512), BF),
-            pltpu.VMEM((2, 256, 1024), F32),
             pltpu.SemaphoreType.DMA((26,)),
         ],
         compiler_params=pltpu.CompilerParams(vmem_limit_bytes=34 * 1024 * 1024),
@@ -498,13 +497,11 @@
     z2 = along(m2, 2)
     e3 = along(e2, 1)
     x1, x2 = flip(e1, 2), flip(e2, 2)
-    x1, m1 = together(x1, m1)
-    z1 = along(m1, 1)
-    x2, m3 = together(x2, m3)
-    z3 = along(m3, 3)
+    e3, x1, x2, m1, m3 = together(e3, x1, x2, m1, m3)
+    z1, z3 = along(m1, 1), along(m3, 3)
     x3 = flip(e3, 2)
     y1, y2 = across(z1), across(z2)
-    x2, x3, z3, w_own = together(x2, x3, z3, w_own)
+    x3, z3, w_own = together(x3, z3, w_own)
     y3 = across(z3)
     packed = pack_call(w_own, z1, z2, y1, y2)
     packed_there = flip(packed, 1)
@@ -523,8 +520,7 @@
     b2, a2 = flip(b2, 3), flip(a2, 2)
     far3, own = together(summed(core[3], b3), own)
     far3 = along(far3, 1)
-    back = jnp.stack([front[0], other]).reshape(2, 2, 2, SEQ, 16, 256).transpose(3, 0, 1, 2, 4, 5)
-    near3, core, back = together(summed(own[3], a3), core, back)
+    near3, core = together(summed(own[3], a3), core)
     near3 = along(near3, 1)
     b2, b1, a10 = together(b2, b1, a10)
     b1, a10 = flip(b1, 3), flip(a10, 2)
@@ -534,7 +530,8 @@
     b0 = flip(b0, 3)
     near2, core = together(summed(own[2], a2, near3), core)
     near2 = along(near2, 2)
-    far1, own = together(summed(core[1], b1), own)
+    back = jnp.stack([front[0], other]).reshape(2, 2, 2, SEQ, 16, 256).transpose(3, 0, 1, 2, 4, 5)
+    far1, own, back = together(summed(core[1], b1), own, back)
     far1 = along(far1, 1)
     a10, near2, far2 = together(a10, near2, far2)
     near1 = along(summed(own[1], a10[0]), 1)

time: 211 us -> 195 us (0.924)
  waiting for transfers between devices: 120 us -> 102 us
  starting transfers between devices: 47.9 us -> 57.5 us
  Pallas kernels: 24.3 us -> 20.2 us
  other arithmetic: 8.08 us -> 5.08 us
    ppermute x12, starting transfers between devices: 21.4 us -> 33.5 us  [along(): return lax.ppermute(value, 'seq', [(a, a ^ k) for a in range(SEQ)])]
    ppermute x12, waiting for transfers between devices: 62 us -> 51.6 us  [along(): return lax.ppermute(value, 'seq', [(a, a ^ k) for a in range(SEQ)])]
    ppermute x15, waiting for transfers between devices: 52.3 us -> 45.2 us  [flip(): return lax.ppermute(value, 'head', [(a, a ^ bits) for a in range(4)])]
    all_to_all x1, starting transfers between devices: 10.5 us -> 5.45 us  [body(): back = lax.all_to_all(back, 'seq', split_axis=0, concat_axis=0, tiled=True)]
    pallas_call x1, Pallas kernels: 15.6 us -> 11.4 us  [main_call(): pl.pallas_call(main_kernel, out_shape=[front, front, jax.ShapeDtypeStruct...]
    convert_element_type x6, other arithmetic: 7.28 us -> 4.27 us  [summed(): return total.astype(BF)]
    unnamed x18 -> x16, local copies, waits for them, and re-layouts: 6.43 us -> 5.72 us
  transfers between devices with their start and end apart: 31 -> 31, of which waited for: 18 -> 21; matrix products, arithmetic and copies ran while one was open for 5% -> 3% of each run, Pallas kernels for 3% -> 3%
where the time goes in v6:
time: 195 us
  waiting for transfers between devices  102 us (52%)
  starting transfers between devices  57.5 us (29%)
  Pallas kernels  20.2 us (10%)
  local copies, waits for them, and re-layouts  8.48 us (4%)
  other arithmetic  5.08 us (3%)
    ppermute x12, waiting for transfers between devices, along(): return lax.ppermute(value, 'seq', [(a, a ^ k) for a in range(SEQ)])  51.6 us
    ppermute x15, waiting for transfers between devices, flip(): return lax.ppermute(value, 'head', [(a, a ^ bits) for a in range(4)])  45.2 us
    ppermute x12, starting transfers between devices, along(): return lax.ppermute(value, 'seq', [(a, a ^ k) for a in range(SEQ)])  33.5 us
    ppermute x15, starting transfers between devices, flip(): return lax.ppermute(value, 'head', [(a, a ^ bits) for a in range(4)])  13.9 us
    pallas_call x1, Pallas kernels, main_call(): pl.pallas_call(main_kernel, out_shape=[front, front, jax.ShapeDtypeStruct...  11.4 us
    ppermute x3, waiting for transfers between devices, across(): return lax.ppermute(value, 'grp', [(0, 1), (1, 0)])  5.75 us
    unnamed x16, local copies, waits for them, and re-layouts  5.72 us
    all_to_all x1, starting transfers between devices, body(): back = lax.all_to_all(back, 'seq', split_axis=0, concat_axis=0, tiled=True)  5.45 us
  transfers between devices with their start and end apart: 31, of which 21 were waited for; matrix products, arithmetic and copies ran while one was open for 3% of the time, Pallas kernels for 3%

profile of v6, /device:TPU:0, one launch (start us, length us, event | category | flops | bytes accessed | tf_op | source)
XLA Modules:
  0.0 194.6 jit_solution(6911920609456267757)
XLA Ops:
  1.7 4.1 %collective-permute-start.1 = (bf16[64,4096]{1,0:T(8,128)(2,1)S(1)}, bf16[64,4096]{1,0:T(8,128)(2,1)S(1)}, u32[]{:S(2)}, u32[]{:S(2)}) collective-permute-start(bf16[64,4096]{1,0:T(8,128)(2,1)S(1)} %dynamic-slice_bitcast_fusion), channel_id=1, source_target_pairs={{0,8},{4,12},{8,0},{12,4},{1,9},{5,13},{9,1},{13,5},{2,10},{6,14},... | collective-permute-start | bytes 1572872 | tf_op jit(solution)/shard_map/ppermute | solution.py:482
  14.6 14.4 %collective-permute-done.1.refs_2_ = bf16[64,4096]{1,0:T(8,128)(2,1)S(1)} collective-permute-done((bf16[64,4096]{1,0:T(8,128)(2,1)S(1)}, bf16[64,4096]{1,0:T(8,128)(2,1)S(1)}, u32[]{:S(2)}, u32[]{:S(2)}) %collective-permute-start.1) | collective-permute-done | bytes 524320 | tf_op jit(solution)/shard_map/ppermute | solution.py:482
  32.8 2.3 %collective-permute-start.9 = (bf16[576,512]{1,0:T(8,128)(2,1)S(1)}, bf16[576,512]{1,0:T(8,128)(2,1)S(1)}, u32[]{:S(2)}, u32[]{:S(2)}) collective-permute-start(bf16[576,512]{1,0:T(8,128)(2,1)S(1)} %get-tuple-element.76), channel_id=1, source_target_pairs={{0,8},{4,12},{8,0},{12,4},{1,9},{5,13},{9,1},{13,5},{2,10},{6,14},... | collective-permute-start | bytes 1769480 | tf_op jit(solution)/shard_map/ppermute | solution.py:482
  35.1 9.0 %collective-permute-done.3.refs_4_ = bf16[64,4096]{1,0:T(8,128)(2,1)S(1)} collective-permute-done((bf16[64,4096]{1,0:T(8,128)(2,1)S(1)}, bf16[64,4096]{1,0:T(8,128)(2,1)S(1)}, u32[]{:S(2)}, u32[]{:S(2)}) %collective-permute-start.3) | collective-permute-done | bytes 524320 | tf_op jit(solution)/shard_map/ppermute | solution.py:485
  44.1 9.2 %collective-permute-done.4.refs_5_ = bf16[64,4096]{1,0:T(8,128)(2,1)S(1)} collective-permute-done((bf16[64,4096]{1,0:T(8,128)(2,1)S(1)}, bf16[64,4096]{1,0:T(8,128)(2,1)S(1)}, u32[]{:S(2)}, u32[]{:S(2)}) %collective-permute-start.4) | collective-permute-done | bytes 524320 | tf_op jit(solution)/shard_map/ppermute | solution.py:485
  54.8 2.9 %collective-permute-start.6 = (bf16[576,512]{1,0:T(8,128)(2,1)S(1)}, bf16[576,512]{1,0:T(8,128)(2,1)S(1)}, u32[]{:S(2)}, u32[]{:S(2)}) collective-permute-start(bf16[576,512]{1,0:T(8,128)(2,1)S(1)} %get-tuple-element.68), channel_id=1, source_target_pairs={{0,12},{4,8},{8,4},{12,0},{1,13},{5,9},{9,5},{13,1},{2,14},{6,10},... | collective-permute-start | bytes 1769480 | tf_op jit(solution)/shard_map/ppermute | solution.py:482
  57.7 4.3 %collective-permute-done.9.z2 = bf16[576,512]{1,0:T(8,128)(2,1)S(1)} collective-permute-done((bf16[576,512]{1,0:T(8,128)(2,1)S(1)}, bf16[576,512]{1,0:T(8,128)(2,1)S(1)}, u32[]{:S(2)}, u32[]{:S(2)}) %collective-permute-start.9) | collective-permute-done | bytes 589856 | tf_op jit(solution)/shard_map/ppermute | solution.py:482
  63.5 6.6 %collective-permute-done.8.z1 = bf16[576,512]{1,0:T(8,128)(2,1)S(1)} collective-permute-done((bf16[576,512]{1,0:T(8,128)(2,1)S(1)}, bf16[576,512]{1,0:T(8,128)(2,1)S(1)}, u32[]{:S(2)}, u32[]{:S(2)}) %collective-permute-start.8) | collective-permute-done | bytes 589856 | tf_op jit(solution)/shard_map/ppermute | solution.py:482
  73.1 7.8 %collective-permute-done.5.refs_6_ = bf16[64,4096]{1,0:T(8,128)(2,1)S(1)} collective-permute-done((bf16[64,4096]{1,0:T(8,128)(2,1)S(1)}, bf16[64,4096]{1,0:T(8,128)(2,1)S(1)}, u32[]{:S(2)}, u32[]{:S(2)}) %collective-permute-start.5) | collective-permute-done | bytes 524320 | tf_op jit(solution)/shard_map/ppermute | solution.py:485
  80.8 3.3 %collective-permute-done.6.refs_3_ = bf16[576,512]{1,0:T(8,128)(2,1)S(1)} collective-permute-done((bf16[576,512]{1,0:T(8,128)(2,1)S(1)}, bf16[576,512]{1,0:T(8,128)(2,1)S(1)}, u32[]{:S(2)}, u32[]{:S(2)}) %collective-permute-start.6) | collective-permute-done | bytes 589856 | tf_op jit(solution)/shard_map/ppermute | solution.py:482
  86.9 4.2 %collective-permute-done.12.refs_8_.refs_5_ = bf16[3264,512]{1,0:T(8,128)(2,1)S(1)} collective-permute-done((bf16[3264,512]{1,0:T(8,128)(2,1)S(1)}, bf16[3264,512]{1,0:T(8,128)(2,1)S(1)}, u32[]{:S(2)}, u32[]{:S(2)}) %collective-permute-start.12) | collective-permute-done | bytes 3342368 | tf_op jit(solution)/shard_map/ppermute | solution.py:485
  91.1 4.4 %early.1 = (f32[2,512,512]{2,1,0:T(8,128)S(1)}, bf16[512,1024]{1,0:T(8,128)(2,1)S(1)}) custom-call(bf16[4,64,4096]{2,1,0:T(8,128)(2,1)S(1)} %copy-done, bf16[64,4096]{1,0:T(8,128)(2,1)S(1)} %collective-permute-done.refs_1_, bf16[64,4096]{1,0:T(8,128)(2,1)S(1)} %collective-permute-done.1.refs_2_, bf16[64,4096]{1,0:T(8,128)(2,1)S(1)} %collective-permute-done.2.refs_3_, ...), custom_call_target="tpu_custom_call" | custom-call | flops 1 | bytes 1 | tf_op jit(solution)/shard_map/early/pallas_call | solution.py:295
  95.5 5.4 %collective-permute-done.7.refs_4_ = bf16[576,512]{1,0:T(8,128)(2,1)S(1)} collective-permute-done((bf16[576,512]{1,0:T(8,128)(2,1)S(1)}, bf16[576,512]{1,0:T(8,128)(2,1)S(1)}, u32[]{:S(2)}, u32[]{:S(2)}) %collective-permute-start.7) | collective-permute-done | bytes 589856 | tf_op jit(solution)/shard_map/ppermute | solution.py:488
  102.9 11.4 %attend.1 = (bf16[2,2,64,256]{3,2,1,0:T(8,128)(2,1)S(1)}, bf16[2,2,64,256]{3,2,1,0:T(8,128)(2,1)S(1)}, f32[4,2,64,1024]{3,2,1,0:T(8,128)S(1)}, bf16[2,64,1024]{2...) custom-call(s32[4]{0:T(128)S(1)} %copy-done.7, ...), custom_call_target="tpu_custom_call" | custom-call | flops 6000000000 | bytes 25165824 | tf_op jit(solution)/shard_map/attend/pallas_call | solution.py:416
  117.4 5.2 %collective-permute-done.15 = bf16[2,64,1024]{2,1,0:T(8,128)(2,1)S(1)} collective-permute-done((bf16[2,64,1024]{2,1,0:T(8,128)(2,1)S(1)}, bf16[2,64,1024]{2,1,0:T(8,128)(2,1)S(1)}, u32[]{:S(2)}, u32[]{:S(2)}) %collective-permute-start.15) | collective-permute-done | bytes 262176 | tf_op jit(solution)/shard_map/ppermute | solution.py:485
  126.2 3.0 %collective-permute-done.20 = bf16[2,64,1024]{2,1,0:T(8,128)(2,1)S(1)} collective-permute-done((bf16[2,64,1024]{2,1,0:T(8,128)(2,1)S(1)}, bf16[2,64,1024]{2,1,0:T(8,128)(2,1)S(1)}, u32[]{:S(2)}, u32[]{:S(2)}) %collective-permute-start.20) | collective-permute-done | bytes 262176 | tf_op jit(solution)/shard_map/ppermute | solution.py:485
  133.9 2.2 %collective-permute-start.24 = (bf16[2,64,1024]{2,1,0:T(8,128)(2,1)S(1)}, bf16[2,64,1024]{2,1,0:T(8,128)(2,1)S(1)}, u32[]{:S(2)}, u32[]{:S(2)}) collective-permute-start(bf16[2,64,1024]{2,1,0:T(8,128)(2,1)S(1)} %get-tuple-element.106), channel_id=1, source_target_pairs={{0,3},{1,2},{2,1},{3,0},{4,7},{5,6},{6,5},{7,4},{8,11},{9,10},{10,... | collective-permute-start | bytes 786440 | tf_op jit(solution)/shard_map/ppermute | solution.py:485
  136.8 3.6 %collective-permute-done.18 = bf16[2,64,1024]{2,1,0:T(8,128)(2,1)S(1)} collective-permute-done((bf16[2,64,1024]{2,1,0:T(8,128)(2,1)S(1)}, bf16[2,64,1024]{2,1,0:T(8,128)(2,1)S(1)}, u32[]{:S(2)}, u32[]{:S(2)}) %collective-permute-start.18) | collective-permute-done | bytes 262176 | tf_op jit(solution)/shard_map/ppermute | solution.py:485
  142.7 15.5 %collective-permute-start.26 = (bf16[2,64,1024]{2,1,0:T(8,128)(2,1)}, bf16[2,64,1024]{2,1,0:T(8,128)(2,1)S(1)}, u32[]{:S(2)}, u32[]{:S(2)}) collective-permute-start(bf16[2,64,1024]{2,1,0:T(8,128)(2,1)} %fusion.5), channel_id=1, source_target_pairs={{0,8},{4,12},{8,0},{12,4},{1,9},{5,13},{9,1},{13,5},{2,10},{6,14},... | collective-permute-start | bytes 786440 | tf_op jit(solution)/shard_map/ppermute | solution.py:482
  159.0 5.5 %all-to-all-start = ((bf16[4,2,2,2,16,256]{5,4,1,3,2,0:T(8,128)(2,1)}), bf16[4,2,2,2,16,256]{5,4,1,3,2,0:T(8,128)(2,1)}, u32[]{:S(2)}, u32[]{:S(2)}) async-start(bf16[4,2,2,2,16,256]{5,4,1,3,2,0:T(8,128)(2,1)} %copy_bitcast_fusion), calls=%async_computation | async-start | bytes 524288 | tf_op jit(solution)/shard_map/all_to_all | solution.py:539
  167.2 12.1 %collective-permute-done.26.near2 = bf16[2,64,1024]{2,1,0:T(8,128)(2,1)S(1)} collective-permute-done((bf16[2,64,1024]{2,1,0:T(8,128)(2,1)}, bf16[2,64,1024]{2,1,0:T(8,128)(2,1)S(1)}, u32[]{:S(2)}, u32[]{:S(2)}) %collective-permute-start.26) | collective-permute-done | bytes 262176 | tf_op jit(solution)/shard_map/ppermute | solution.py:482
  179.3 4.4 %collective-permute-done.27.far2 = bf16[2,64,1024]{2,1,0:T(8,128)(2,1)} collective-permute-done((bf16[2,64,1024]{2,1,0:T(8,128)(2,1)}, bf16[2,64,1024]{2,1,0:T(8,128)(2,1)}, u32[]{:S(2)}, u32[]{:S(2)}) %collective-permute-start.27) | collective-permute-done | bytes 262176 | tf_op jit(solution)/shard_map/ppermute | solution.py:482
  187.3 4.9 %collective-permute-done.28.near1 = bf16[2,64,1024]{2,1,0:T(8,128)(2,1)} collective-permute-done((bf16[2,64,1024]{2,1,0:T(8,128)(2,1)}, bf16[2,64,1024]{2,1,0:T(8,128)(2,1)}, u32[]{:S(2)}, u32[]{:S(2)}) %collective-permute-start.28) | collective-permute-done | bytes 262176 | tf_op jit(solution)/shard_map/ppermute | solution.py:482
  192.2 2.4 %final.1 = bf16[4,64,1024]{2,1,0:T(8,128)(2,1)} custom-call(f32[4,2,64,1024]{3,2,1,0:T(8,128)S(1)} %get-tuple-element.110.own, bf16[4,2,64,1024]{3,2,1,0:T(8,128)(2,1)S(1)} %collective-permute-done.16.core, bf16[2,2,64,1024]{3,2,1,0:T(8,128)(2,1)} %collective-permute-done.25.near, bf16[2,64,1024]{2,1,0:T(8,128)(2,1)} %collective-permute-done.19.far, ...), custom_call_target="tpu_custom_call" | custom-call | tf_op jit(solution)/shard_map/final/pallas_call | solution.py:456
  (71 shorter events, 45.7 us)
Async XLA Ops:
  1.7 27.4 %collective-permute-start.1 = (bf16[64,4096]{1,0:T(8,128)(2,1)S(1)}, bf16[64,4096]{1,0:T(8,128)(2,1)S(1)}, u32[]{:S(2)}, u32[]{:S(2)}) collective-permute-start(bf16[64,4096]{1,0:T(8,128)(2,1)S(1)} %dynamic-slice_bitcast_fusion), channel_id=1, source_target_pairs={{0,8},{4,12},{8,0},{12,4},{1,9},{5,13},{9,1},{13,5},{2,10},{6,14},... | collective-permute-start | bytes 1572872 | tf_op jit(solution)/shard_map/ppermute | solution.py:482
  5.8 23.5 %collective-permute-start = (bf16[64,4096]{1,0:T(8,128)(2,1)S(1)}, bf16[64,4096]{1,0:T(8,128)(2,1)S(1)}, u32[]{:S(2)}, u32[]{:S(2)}) collective-permute-start(bf16[64,4096]{1,0:T(8,128)(2,1)S(1)} %dynamic-slice_bitcast_fusion), channel_id=1, source_target_pairs={{0,4},{4,0},{8,12},{12,8},{1,5},{5,1},{9,13},{13,9},{2,6},{6,2},{1... | collective-permute-start | bytes 1572872 | tf_op jit(solution)/shard_map/ppermute | solution.py:482
  29.3 14.9 %collective-permute-start.3 = (bf16[64,4096]{1,0:T(8,128)(2,1)S(1)}, bf16[64,4096]{1,0:T(8,128)(2,1)S(1)}, u32[]{:S(2)}, u32[]{:S(2)}) collective-permute-start(bf16[64,4096]{1,0:T(8,128)(2,1)S(1)} %collective-permute-done.refs_1_), channel_id=1, source_target_pairs={{0,2},{1,3},{2,0},{3,1},{4,6},{5,7},{6,4},{7,5},{8,10},{9,11},{10,... | collective-permute-start | bytes 1572872 | tf_op jit(solution)/shard_map/ppermute | solution.py:485
  30.8 22.6 %collective-permute-start.4 = (bf16[64,4096]{1,0:T(8,128)(2,1)S(1)}, bf16[64,4096]{1,0:T(8,128)(2,1)S(1)}, u32[]{:S(2)}, u32[]{:S(2)}) collective-permute-start(bf16[64,4096]{1,0:T(8,128)(2,1)S(1)} %collective-permute-done.1.refs_2_), channel_id=1, source_target_pairs={{0,2},{1,3},{2,0},{3,1},{4,6},{5,7},{6,4},{7,5},{8,10},{9,11},{10,... | collective-permute-start | bytes 1572872 | tf_op jit(solution)/shard_map/ppermute | solution.py:485
  31.3 23.3 %collective-permute-start.2 = (bf16[64,4096]{1,0:T(8,128)(2,1)S(1)}, bf16[64,4096]{1,0:T(8,128)(2,1)S(1)}, u32[]{:S(2)}, u32[]{:S(2)}) collective-permute-start(bf16[64,4096]{1,0:T(8,128)(2,1)S(1)} %collective-permute-done.1.refs_2_), channel_id=1, source_target_pairs={{0,4},{4,0},{8,12},{12,8},{1,5},{5,1},{9,13},{13,9},{2,6},{6,2},{1... | collective-permute-start | bytes 1572872 | tf_op jit(solution)/shard_map/ppermute | solution.py:482
  32.8 29.2 %collective-permute-start.9 = (bf16[576,512]{1,0:T(8,128)(2,1)S(1)}, bf16[576,512]{1,0:T(8,128)(2,1)S(1)}, u32[]{:S(2)}, u32[]{:S(2)}) collective-permute-start(bf16[576,512]{1,0:T(8,128)(2,1)S(1)} %get-tuple-element.76), channel_id=1, source_target_pairs={{0,8},{4,12},{8,0},{12,4},{1,9},{5,13},{9,1},{13,5},{2,10},{6,14},... | collective-permute-start | bytes 1769480 | tf_op jit(solution)/shard_map/ppermute | solution.py:482
  54.6 15.5 %collective-permute-start.8 = (bf16[576,512]{1,0:T(8,128)(2,1)S(1)}, bf16[576,512]{1,0:T(8,128)(2,1)S(1)}, u32[]{:S(2)}, u32[]{:S(2)}) collective-permute-start(bf16[576,512]{1,0:T(8,128)(2,1)S(1)} %get-tuple-element.75), channel_id=1, source_target_pairs={{0,4},{4,0},{8,12},{12,8},{1,5},{5,1},{9,13},{13,9},{2,6},{6,2},{1... | collective-permute-start | bytes 1769480 | tf_op jit(solution)/shard_map/ppermute | solution.py:482
  54.8 29.4 %collective-permute-start.6 = (bf16[576,512]{1,0:T(8,128)(2,1)S(1)}, bf16[576,512]{1,0:T(8,128)(2,1)S(1)}, u32[]{:S(2)}, u32[]{:S(2)}) collective-permute-start(bf16[576,512]{1,0:T(8,128)(2,1)S(1)} %get-tuple-element.68), channel_id=1, source_target_pairs={{0,12},{4,8},{8,4},{12,0},{1,13},{5,9},{9,5},{13,1},{2,14},{6,10},... | collective-permute-start | bytes 1769480 | tf_op jit(solution)/shard_map/ppermute | solution.py:482
  62.0 22.2 %collective-permute-start.11 = (bf16[576,512]{1,0:T(8,128)(2,1)S(1)}, bf16[576,512]{1,0:T(8,128)(2,1)S(1)}, u32[]{:S(2)}, u32[]{:S(2)}) collective-permute-start(bf16[576,512]{1,0:T(8,128)(2,1)S(1)} %collective-permute-done.9.z2), channel_id=1, source_target_pairs={{0,16},{16,0},{1,17},{17,1},{2,18},{18,2},{3,19},{19,3},{4,20},{20... | collective-permute-start | bytes 1769480 | tf_op jit(solution)/shard_map/ppermute | solution.py:488
  70.1 14.4 %collective-permute-start.10 = (bf16[576,512]{1,0:T(8,128)(2,1)S(1)}, bf16[576,512]{1,0:T(8,128)(2,1)S(1)}, u32[]{:S(2)}, u32[]{:S(2)}) collective-permute-start(bf16[576,512]{1,0:T(8,128)(2,1)S(1)} %collective-permute-done.8.z1), channel_id=1, source_target_pairs={{0,16},{16,0},{1,17},{17,1},{2,18},{18,2},{3,19},{19,3},{4,20},{20... | collective-permute-start | bytes 1769480 | tf_op jit(solution)/shard_map/ppermute | solution.py:488
  85.1 15.7 %collective-permute-start.7 = (bf16[576,512]{1,0:T(8,128)(2,1)S(1)}, bf16[576,512]{1,0:T(8,128)(2,1)S(1)}, u32[]{:S(2)}, u32[]{:S(2)}) collective-permute-start(bf16[576,512]{1,0:T(8,128)(2,1)S(1)} %collective-permute-done.6.refs_3_), channel_id=1, source_target_pairs={{0,16},{16,0},{1,17},{17,1},{2,18},{18,2},{3,19},{19,3},{4,20},{20... | collective-permute-start | bytes 1769480 | tf_op jit(solution)/shard_map/ppermute | solution.py:488
  86.7 14.2 %collective-permute-start.13 = (bf16[576,512]{1,0:T(8,128)(2,1)S(1)}, bf16[576,512]{1,0:T(8,128)(2,1)S(1)}, u32[]{:S(2)}, u32[]{:S(2)}) collective-permute-start(bf16[576,512]{1,0:T(8,128)(2,1)S(1)} %collective-permute-done.6.refs_3_), channel_id=1, source_target_pairs={{0,1},{1,0},{2,3},{3,2},{4,5},{5,4},{6,7},{7,6},{8,9},{9,8},{10,11... | collective-permute-start | bytes 1769480 | tf_op jit(solution)/shard_map/ppermute | solution.py:485
  116.2 13.0 %collective-permute-start.20 = (bf16[2,64,1024]{2,1,0:T(8,128)(2,1)S(1)}, bf16[2,64,1024]{2,1,0:T(8,128)(2,1)S(1)}, u32[]{:S(2)}, u32[]{:S(2)}) collective-permute-start(bf16[2,64,1024]{2,1,0:T(8,128)(2,1)S(1)} %get-tuple-element.95), channel_id=1, source_target_pairs={{0,2},{1,3},{2,0},{3,1},{4,6},{5,7},{6,4},{7,5},{8,10},{9,11},{10,... | collective-permute-start | bytes 786440 | tf_op jit(solution)/shard_map/ppermute | solution.py:485
  122.7 13.3 %collective-permute-start.22 = (bf16[2,64,1024]{2,1,0:T(8,128)(2,1)S(1)}, bf16[2,64,1024]{2,1,0:T(8,128)(2,1)S(1)}, u32[]{:S(2)}, u32[]{:S(2)}) collective-permute-start(bf16[2,64,1024]{2,1,0:T(8,128)(2,1)S(1)} %fusion.3), channel_id=1, source_target_pairs={{0,4},{4,0},{8,12},{12,8},{1,5},{5,1},{9,13},{13,9},{2,6},{6,2},{1... | collective-permute-start | bytes 786440 | tf_op jit(solution)/shard_map/ppermute | solution.py:482
  124.6 9.3 %collective-permute-start.21 = (bf16[2,64,1024]{2,1,0:T(8,128)(2,1)S(1)}, bf16[2,64,1024]{2,1,0:T(8,128)(2,1)S(1)}, u32[]{:S(2)}, u32[]{:S(2)}) collective-permute-start(bf16[2,64,1024]{2,1,0:T(8,128)(2,1)S(1)} %get-tuple-element.97), channel_id=1, source_target_pairs={{0,3},{1,2},{2,1},{3,0},{4,7},{5,6},{6,5},{7,4},{8,11},{9,10},{10,... | collective-permute-start | bytes 786440 | tf_op jit(solution)/shard_map/ppermute | solution.py:485
  129.3 12.7 %collective-permute-start.23 = (bf16[2,64,1024]{2,1,0:T(8,128)(2,1)S(1)}, bf16[2,64,1024]{2,1,0:T(8,128)(2,1)S(1)}, u32[]{:S(2)}, u32[]{:S(2)}) collective-permute-start(bf16[2,64,1024]{2,1,0:T(8,128)(2,1)S(1)} %fusion.6), channel_id=1, source_target_pairs={{0,4},{4,0},{8,12},{12,8},{1,5},{5,1},{9,13},{13,9},{2,6},{6,2},{1... | collective-permute-start | bytes 786440 | tf_op jit(solution)/shard_map/ppermute | solution.py:482
  131.1 9.3 %collective-permute-start.18 = (bf16[2,64,1024]{2,1,0:T(8,128)(2,1)S(1)}, bf16[2,64,1024]{2,1,0:T(8,128)(2,1)S(1)}, u32[]{:S(2)}, u32[]{:S(2)}) collective-permute-start(bf16[2,64,1024]{2,1,0:T(8,128)(2,1)S(1)} %get-tuple-element.88), channel_id=1, source_target_pairs={{0,2},{1,3},{2,0},{3,1},{4,6},{5,7},{6,4},{7,5},{8,10},{9,11},{10,... | collective-permute-start | bytes 786440 | tf_op jit(solution)/shard_map/ppermute | solution.py:485
  133.9 24.4 %collective-permute-start.24 = (bf16[2,64,1024]{2,1,0:T(8,128)(2,1)S(1)}, bf16[2,64,1024]{2,1,0:T(8,128)(2,1)S(1)}, u32[]{:S(2)}, u32[]{:S(2)}) collective-permute-start(bf16[2,64,1024]{2,1,0:T(8,128)(2,1)S(1)} %get-tuple-element.106), channel_id=1, source_target_pairs={{0,3},{1,2},{2,1},{3,0},{4,7},{5,6},{6,5},{7,4},{8,11},{9,10},{10,... | collective-permute-start | bytes 786440 | tf_op jit(solution)/shard_map/ppermute | solution.py:485
  140.4 43.4 %collective-permute-start.25 = (bf16[2,2,64,1024]{3,2,1,0:T(8,128)(2,1)}, bf16[2,2,64,1024]{3,2,1,0:T(8,128)(2,1)}, u32[]{:S(2)}, u32[]{:S(2)}) collective-permute-start(bf16[2,2,64,1024]{3,2,1,0:T(8,128)(2,1)} %get-tuple-element.111), channel_id=1, source_target_pairs={{0,2},{1,3},{2,0},{3,1},{4,6},{5,7},{6,4},{7,5},{8,10},{9,11},{10,... | collective-permute-start | bytes 1572872 | tf_op jit(solution)/shard_map/ppermute | solution.py:485
  142.7 36.6 %collective-permute-start.26 = (bf16[2,64,1024]{2,1,0:T(8,128)(2,1)}, bf16[2,64,1024]{2,1,0:T(8,128)(2,1)S(1)}, u32[]{:S(2)}, u32[]{:S(2)}) collective-permute-start(bf16[2,64,1024]{2,1,0:T(8,128)(2,1)} %fusion.5), channel_id=1, source_target_pairs={{0,8},{4,12},{8,0},{12,4},{1,9},{5,13},{9,1},{13,5},{2,10},{6,14},... | collective-permute-start | bytes 786440 | tf_op jit(solution)/shard_map/ppermute | solution.py:482
  158.2 25.6 %collective-permute-start.27 = (bf16[2,64,1024]{2,1,0:T(8,128)(2,1)}, bf16[2,64,1024]{2,1,0:T(8,128)(2,1)}, u32[]{:S(2)}, u32[]{:S(2)}) collective-permute-start(bf16[2,64,1024]{2,1,0:T(8,128)(2,1)} %fusion.2), channel_id=1, source_target_pairs={{0,8},{4,12},{8,0},{12,4},{1,9},{5,13},{9,1},{13,5},{2,10},{6,14},... | collective-permute-start | bytes 786440 | tf_op jit(solution)/shard_map/ppermute | solution.py:482
  159.0 26.5 %all-to-all-start = ((bf16[4,2,2,2,16,256]{5,4,1,3,2,0:T(8,128)(2,1)}), bf16[4,2,2,2,16,256]{5,4,1,3,2,0:T(8,128)(2,1)}, u32[]{:S(2)}, u32[]{:S(2)}) async-start(bf16[4,2,2,2,16,256]{5,4,1,3,2,0:T(8,128)(2,1)} %copy_bitcast_fusion), calls=%async_computation | async-start | bytes 524288 | tf_op jit(solution)/shard_map/all_to_all | solution.py:539
  164.4 22.1 %collective-permute-start.19 = (bf16[2,64,1024]{2,1,0:T(8,128)(2,1)}, bf16[2,64,1024]{2,1,0:T(8,128)(2,1)}, u32[]{:S(2)}, u32[]{:S(2)}) collective-permute-start(bf16[2,64,1024]{2,1,0:T(8,128)(2,1)} %copy-done.6), channel_id=1, source_target_pairs={{0,3},{1,2},{2,1},{3,0},{4,7},{5,6},{6,5},{7,4},{8,11},{9,10},{10,... | collective-permute-start | bytes 786440 | tf_op jit(solution)/shard_map/ppermute | solution.py:485
  165.5 21.8 %collective-permute-start.29 = (bf16[2,64,1024]{2,1,0:T(8,128)(2,1)}, bf16[2,64,1024]{2,1,0:T(8,128)(2,1)}, u32[]{:S(2)}, u32[]{:S(2)}) collective-permute-start(bf16[2,64,1024]{2,1,0:T(8,128)(2,1)} %fusion), channel_id=1, source_target_pairs={{0,4},{4,0},{8,12},{12,8},{1,5},{5,1},{9,13},{13,9},{2,6},{6,2},{1... | collective-permute-start | bytes 786440 | tf_op jit(solution)/shard_map/ppermute | solution.py:482
  (15 other events, 130.3 us)

commit v7 on v6

--- a/solution.py
+++ b/solution.py
@@ -132,7 +132,6 @@
 
 SEQ = 4
 PIECE = 512
-SENT = PIECE + 64
 
 
 def fits(mesh, encoder, key_weight, queries):
@@ -164,11 +163,12 @@
                     out_ref[t * TILE : (t + 1) * TILE, to : to + 128] = (
                         ref[row, at].astype(F32) * keep
                     ).astype(BF)
-        at = pl.ds(pl.multiple_of(column * 256, 256), 256)
-        out_ref[tiles * TILE :, 0:256] = query_ref[:, at]
-        out_ref[tiles * TILE :, 256:512] = cot_ref[:, at]
-
-    first, second, third = message_refs
+
+    first, second, third = message_refs[:3]
+    for k, ref in enumerate(message_refs[3:]):
+        at = pl.ds(pl.multiple_of(lax.bitwise_xor(s, k) * 256, 256), 256)
+        ref[:, 0:256] = query_ref[:, at]
+        ref[:, 256:512] = cot_ref[:, at]
     write(second, g * 8, 8, lax.bitwise_xor(s, 2))
     write(first, g * 8, 8, lax.bitwise_xor(s, 1))
     write(third, g * 8, 8, lax.bitwise_xor(s, 3))
@@ -177,12 +177,12 @@
 
 def prune(tile_mask, key_weight, value_weight, queries, cotangent):
     whole = pl.BlockSpec(memory_space=pltpu.VMEM)
-    rows = (2 * PIECE + 64, SENT, SENT, SENT)
+    shapes = [(2 * PIECE, 512)] + [(PIECE, 512)] * 3 + [(64, 512)] * 4
     return pl.pallas_call(
         prune_kernel,
-        out_shape=[jax.ShapeDtypeStruct((count, 512), BF) for count in rows],
+        out_shape=[jax.ShapeDtypeStruct(shape, BF) for shape in shapes],
         in_specs=[pl.BlockSpec(memory_space=pltpu.SMEM)] + [whole] * 4,
-        out_specs=[whole] * len(rows),
+        out_specs=[whole] * len(shapes),
         compiler_params=pltpu.CompilerParams(vmem_limit_bytes=12 * 1024 * 1024),
         name="prune",
     )(tile_mask, key_weight, value_weight, queries, cotangent)
@@ -219,15 +219,16 @@
 PACKED = 3 * 2 * PIECE
 
 
-def pack_kernel(own, z1, z2, y1, y2, out_ref, sems):
+def pack_kernel(own, z1, z2, y1, y2, q0, q1, q2, q3, out_ref, sems):
     g = lax.axis_index("grp")
-    pairs = [(own.at[0 : 2 * PIECE], out_ref.at[0 : 2 * PIECE])]
-    pairs.append((own.at[2 * PIECE : 2 * PIECE + 64], out_ref.at[PACKED : PACKED + 64]))
+    pairs = [(own, out_ref.at[0 : 2 * PIECE])]
     for k, z, y in ((1, z1, y1), (2, z2, y2)):
         for piece, side in ((z, g), (y, 1 - g)):
             first = pl.multiple_of(2 * PIECE * k + side * PIECE, PIECE)
-            pairs.append((piece.at[0:PIECE], out_ref.at[pl.ds(first, PIECE)]))
-        pairs.append((z.at[PIECE:SENT], out_ref.at[PACKED + 64 * k : PACKED + 64 * k + 64]))
+            pairs.append((piece, out_ref.at[pl.ds(first, PIECE)]))
+    for k, piece in enumerate((q0, q1, q2, q3)):
+        first = PACKED + 64 * lax.bitwise_xor(lax.axis_index("seq"), k)
+        pairs.append((piece, out_ref.at[pl.ds(pl.multiple_of(first, 64), 64)]))
     for copy in Mover(sems).start(pairs):
         copy.wait()
 
@@ -236,10 +237,10 @@
     here = pl.BlockSpec(memory_space=pl.ANY)
     return pl.pallas_call(
         pack_kernel,
-        out_shape=jax.ShapeDtypeStruct((PACKED + 192, 512), BF),
+        out_shape=jax.ShapeDtypeStruct((PACKED + 256, 512), BF),
         in_specs=[here] * len(arrays),
         out_specs=pl.BlockSpec(memory_space=pltpu.VMEM),
-        scratch_shapes=[pltpu.SemaphoreType.DMA((8,))],
+        scratch_shapes=[pltpu.SemaphoreType.DMA((9,))],
         compiler_params=pltpu.CompilerParams(vmem_limit_bytes=6 * 1024 * 1024),
         cost_estimate=pl.CostEstimate(flops=1, bytes_accessed=1, transcendentals=0),
         name="pack",
@@ -329,11 +330,9 @@
     for core, pieces in ((c, mine), (1 - c, theirs)):
         packed, z3, y3 = pieces
         for src, side in ((z3, g), (y3, 1 - g)):
-            pairs.append((src.at[0:PIECE], piece_rows(w_s, core, far, side * PIECE, PIECE)))
-        for k in range(3):
-            rows = packed.at[PACKED + 64 * k : PACKED + 64 * k + 64]
-            pairs.append((rows, qc_s.at[core, lax.bitwise_xor(s, k)]))
-        pairs.append((z3.at[PIECE:SENT], qc_s.at[core, far]))
+            pairs.append((src, piece_rows(w_s, core, far, side * PIECE, PIECE)))
+        for d in range(SEQ):
+            pairs.append((packed.at[PACKED + 64 * d : PACKED + 64 * d + 64], qc_s.at[core, d]))
     now = mover.start(pairs)
     later = mover.start(early_weights(w_s, c, s, mine[0], theirs[0]))
     for copy in now:
@@ -490,20 +489,24 @@
     e0 = lax.dynamic_index_in_dim(encoder, h, 0, keepdims=False)
     e2 = along(e0, 2)
     e1 = along(e0, 1)
-    w_own, m1, m2, m3 = prune(
+    w_own, m1, m2, m3, q0, q1, q2, q3 = prune(
         tile_mask, key_weight, value_weight, queries.reshape(64, 1024), cotangent.reshape(64, 1024)
     )
-    e1, e2, m2, w_own = together(e1, e2, m2, w_own)
-    z2 = along(m2, 2)
+    q1, q2, q3 = along(q1, 1), along(q2, 2), along(q3, 3)
+    e1, e2, m1, m2, q1, q2, q3 = together(e1, e2, m1, m2, q1, q2, q3)
+    z2, z1 = along(m2, 2), along(m1, 1)
     e3 = along(e2, 1)
     x1, x2 = flip(e1, 2), flip(e2, 2)
-    e3, x1, x2, m1, m3 = together(e3, x1, x2, m1, m3)
-    z1, z3 = along(m1, 1), along(m3, 3)
+    x1, x2, m3 = together(x1, x2, m3)
+    z3 = along(m3, 3)
+    x1, z2 = together(x1, z2)
+    x2, e3 = together(x2, e3)
+    y2 = across(z2)
     x3 = flip(e3, 2)
-    y1, y2 = across(z1), across(z2)
-    x3, z3, w_own = together(x3, z3, w_own)
+    y1 = across(z1)
+    z3, x3, w_own = together(z3, x3, w_own)
     y3 = across(z3)
-    packed = pack_call(w_own, z1, z2, y1, y2)
+    packed = pack_call(w_own, z1, z2, y1, y2, q0, q1, q2, q3)
     packed_there = flip(packed, 1)
     early = early_call([encoder, e1, e2, e3, x1, x2, x3, packed, packed_there])
     z3_there = flip(z3, 1)

time: 195 us -> 194 us (level)
  starting transfers between devices: 57.5 us -> 48.7 us
  waiting for transfers between devices: 102 us -> 110 us
    ppermute x12 -> x15, waiting for transfers between devices: 51.6 us -> 61.9 us  [along(): return lax.ppermute(value, 'seq', [(a, a ^ k) for a in range(SEQ)])]
    ppermute x15, waiting for transfers between devices: 45.2 us -> 35.4 us  [flip(): return lax.ppermute(value, 'head', [(a, a ^ bits) for a in range(4)])]
    ppermute x3, waiting for transfers between devices: 5.75 us -> 12.4 us  [across(): return lax.ppermute(value, 'grp', [(0, 1), (1, 0)])]
    ppermute x12 -> x15, starting transfers between devices: 33.5 us -> 27.2 us  [along(): return lax.ppermute(value, 'seq', [(a, a ^ k) for a in range(SEQ)])]
  transfers between devices with their start and end apart: 31 -> 34, of which waited for: 21 -> 20; matrix products, arithmetic and copies ran while one was open for 3% -> 4% of each run, Pallas kernels for 3% -> 3%
where the time goes in v7:
time: 194 us; the launch traced here: 193 us
  waiting for transfers between devices  110 us (57%)
  starting transfers between devices  48.7 us (25%)
  Pallas kernels  20.3 us (10%)
  local copies, waits for them, and re-layouts  8.48 us (4%)
  other arithmetic  5.09 us (3%)
    ppermute x15, waiting for transfers between devices, along(): return lax.ppermute(value, 'seq', [(a, a ^ k) for a in range(SEQ)])  61.9 us
    ppermute x15, waiting for transfers between devices, flip(): return lax.ppermute(value, 'head', [(a, a ^ bits) for a in range(4)])  35.4 us
    ppermute x15, starting transfers between devices, along(): return lax.ppermute(value, 'seq', [(a, a ^ k) for a in range(SEQ)])  27.2 us
    ppermute x15, starting transfers between devices, flip(): return lax.ppermute(value, 'head', [(a, a ^ bits) for a in range(4)])  13.8 us
    ppermute x3, waiting for transfers between devices, across(): return lax.ppermute(value, 'grp', [(0, 1), (1, 0)])  12.4 us
    pallas_call x1, Pallas kernels, main_call(): pl.pallas_call(main_kernel, out_shape=[front, front, jax.ShapeDtypeStruct...  11.4 us
    unnamed x16, local copies, waits for them, and re-layouts  5.72 us
    pallas_call x1, Pallas kernels, early_call(): pl.pallas_call(early_kernel, out_shape=[jax.ShapeDtypeStruct((2, 512, 512...  4.39 us
  transfers between devices with their start and end apart: 34, of which 20 were waited for; matrix products, arithmetic and copies ran while one was open for 4% of the time, Pallas kernels for 3%

profile of v7, /device:TPU:0, one launch (start us, length us, event | category | flops | bytes accessed | tf_op | source)
XLA Modules:
  0.0 193.3 jit_solution(2110046984912264901)
XLA Ops:
  1.7 4.1 %collective-permute-start.1 = (bf16[64,4096]{1,0:T(8,128)(2,1)S(1)}, bf16[64,4096]{1,0:T(8,128)(2,1)S(1)}, u32[]{:S(2)}, u32[]{:S(2)}) collective-permute-start(bf16[64,4096]{1,0:T(8,128)(2,1)S(1)} %dynamic-slice_bitcast_fusion), channel_id=1, source_target_pairs={{0,8},{4,12},{8,0},{12,4},{1,9},{5,13},{9,1},{13,5},{2,10},{6,14},... | collective-permute-start | bytes 1572872 | tf_op jit(solution)/shard_map/ppermute | solution.py:481
  15.2 3.9 %collective-permute-start.4 = (bf16[64,512]{1,0:T(8,128)(2,1)S(1)}, bf16[64,512]{1,0:T(8,128)(2,1)S(1)}, u32[]{:S(2)}, u32[]{:S(2)}) collective-permute-start(bf16[64,512]{1,0:T(8,128)(2,1)S(1)} %get-tuple-element.74), channel_id=1, source_target_pairs={{0,12},{4,8},{8,4},{12,0},{1,13},{5,9},{9,5},{13,1},{2,14},{6,10},... | collective-permute-start | bytes 196616 | tf_op jit(solution)/shard_map/ppermute | solution.py:481
  19.1 13.3 %collective-permute-done.2.q1 = bf16[64,512]{1,0:T(8,128)(2,1)S(1)} collective-permute-done((bf16[64,512]{1,0:T(8,128)(2,1)S(1)}, bf16[64,512]{1,0:T(8,128)(2,1)S(1)}, u32[]{:S(2)}, u32[]{:S(2)}) %collective-permute-start.2) | collective-permute-done | bytes 65568 | tf_op jit(solution)/shard_map/ppermute | solution.py:481
  41.3 7.9 %collective-permute-done.5.refs_4_ = bf16[64,4096]{1,0:T(8,128)(2,1)S(1)} collective-permute-done((bf16[64,4096]{1,0:T(8,128)(2,1)S(1)}, bf16[64,4096]{1,0:T(8,128)(2,1)S(1)}, u32[]{:S(2)}, u32[]{:S(2)}) %collective-permute-start.5) | collective-permute-done | bytes 524320 | tf_op jit(solution)/shard_map/ppermute | solution.py:484
  49.3 8.9 %collective-permute-done.6.refs_5_ = bf16[64,4096]{1,0:T(8,128)(2,1)S(1)} collective-permute-done((bf16[64,4096]{1,0:T(8,128)(2,1)S(1)}, bf16[64,4096]{1,0:T(8,128)(2,1)S(1)}, u32[]{:S(2)}, u32[]{:S(2)}) %collective-permute-start.6) | collective-permute-done | bytes 524320 | tf_op jit(solution)/shard_map/ppermute | solution.py:484
  58.2 4.3 %collective-permute-done.8.refs_3_ = bf16[64,4096]{1,0:T(8,128)(2,1)S(1)} collective-permute-done((bf16[64,4096]{1,0:T(8,128)(2,1)S(1)}, bf16[64,4096]{1,0:T(8,128)(2,1)S(1)}, u32[]{:S(2)}, u32[]{:S(2)}) %collective-permute-start.8) | collective-permute-done | bytes 524320 | tf_op jit(solution)/shard_map/ppermute | solution.py:481
  64.9 7.4 %collective-permute-done.12.z1 = bf16[512,512]{1,0:T(8,128)(2,1)S(1)} collective-permute-done((bf16[512,512]{1,0:T(8,128)(2,1)S(1)}, bf16[512,512]{1,0:T(8,128)(2,1)S(1)}, u32[]{:S(2)}, u32[]{:S(2)}) %collective-permute-start.12) | collective-permute-done | bytes 524320 | tf_op jit(solution)/shard_map/ppermute | solution.py:481
  74.3 11.5 %collective-permute-done.7.refs_3_ = bf16[512,512]{1,0:T(8,128)(2,1)S(1)} collective-permute-done((bf16[512,512]{1,0:T(8,128)(2,1)S(1)}, bf16[512,512]{1,0:T(8,128)(2,1)S(1)}, u32[]{:S(2)}, u32[]{:S(2)}) %collective-permute-start.7) | collective-permute-done | bytes 524320 | tf_op jit(solution)/shard_map/ppermute | solution.py:481
  87.2 7.2 %collective-permute-done.14.y2 = bf16[512,512]{1,0:T(8,128)(2,1)S(1)} collective-permute-done((bf16[512,512]{1,0:T(8,128)(2,1)S(1)}, bf16[512,512]{1,0:T(8,128)(2,1)S(1)}, u32[]{:S(2)}, u32[]{:S(2)}) %collective-permute-start.14) | collective-permute-done | bytes 524320 | tf_op jit(solution)/shard_map/ppermute | solution.py:487
  96.8 4.3 %collective-permute-done.15.refs_8_.refs_5_ = bf16[3328,512]{1,0:T(8,128)(2,1)S(1)} collective-permute-done((bf16[3328,512]{1,0:T(8,128)(2,1)S(1)}, bf16[3328,512]{1,0:T(8,128)(2,1)S(1)}, u32[]{:S(2)}, u32[]{:S(2)}) %collective-permute-start.15) | collective-permute-done | bytes 3407904 | tf_op jit(solution)/shard_map/ppermute | solution.py:484
  101.1 4.4 %early.1 = (f32[2,512,512]{2,1,0:T(8,128)S(1)}, bf16[512,1024]{1,0:T(8,128)(2,1)S(1)}) custom-call(bf16[4,64,4096]{2,1,0:T(8,128)(2,1)S(1)} %copy-done, bf16[64,4096]{1,0:T(8,128)(2,1)S(1)} %collective-permute-done.refs_1_, bf16[64,4096]{1,0:T(8,128)(2,1)S(1)} %collective-permute-done.1.refs_2_, bf16[64,4096]{1,0:T(8,128)(2,1)S(1)} %collective-permute-done.8.refs_3_, ...), custom_call_target="tpu_custom_call" | custom-call | flops 1 | bytes 1 | tf_op jit(solution)/shard_map/early/pallas_call | solution.py:296
  105.5 3.9 %collective-permute-done.10.refs_4_ = bf16[512,512]{1,0:T(8,128)(2,1)S(1)} collective-permute-done((bf16[512,512]{1,0:T(8,128)(2,1)S(1)}, bf16[512,512]{1,0:T(8,128)(2,1)S(1)}, u32[]{:S(2)}, u32[]{:S(2)}) %collective-permute-start.10) | collective-permute-done | bytes 524320 | tf_op jit(solution)/shard_map/ppermute | solution.py:487
  111.3 11.4 %attend.1 = (bf16[2,2,64,256]{3,2,1,0:T(8,128)(2,1)S(1)}, bf16[2,2,64,256]{3,2,1,0:T(8,128)(2,1)S(1)}, f32[4,2,64,1024]{3,2,1,0:T(8,128)S(1)}, bf16[2,64,1024]{2...) custom-call(s32[4]{0:T(128)S(1)} %copy-done.7, ...), custom_call_target="tpu_custom_call" | custom-call | flops 6000000000 | bytes 25165824 | tf_op jit(solution)/shard_map/attend/pallas_call | solution.py:415
  125.8 5.2 %collective-permute-done.18 = bf16[2,64,1024]{2,1,0:T(8,128)(2,1)S(1)} collective-permute-done((bf16[2,64,1024]{2,1,0:T(8,128)(2,1)S(1)}, bf16[2,64,1024]{2,1,0:T(8,128)(2,1)S(1)}, u32[]{:S(2)}, u32[]{:S(2)}) %collective-permute-start.18) | collective-permute-done | bytes 262176 | tf_op jit(solution)/shard_map/ppermute | solution.py:484
  131.1 2.6 %collective-permute-start.25 = (bf16[2,64,1024]{2,1,0:T(8,128)(2,1)S(1)}, bf16[2,64,1024]{2,1,0:T(8,128)(2,1)S(1)}, u32[]{:S(2)}, u32[]{:S(2)}) collective-permute-start(bf16[2,64,1024]{2,1,0:T(8,128)(2,1)S(1)} %fusion.3), channel_id=1, source_target_pairs={{0,4},{4,0},{8,12},{12,8},{1,5},{5,1},{9,13},{13,9},{2,6},{6,2},{1... | collective-permute-start | bytes 786440 | tf_op jit(solution)/shard_map/ppermute | solution.py:481
  135.3 2.3 %collective-permute-done.23 = bf16[2,64,1024]{2,1,0:T(8,128)(2,1)S(1)} collective-permute-done((bf16[2,64,1024]{2,1,0:T(8,128)(2,1)S(1)}, bf16[2,64,1024]{2,1,0:T(8,128)(2,1)S(1)}, u32[]{:S(2)}, u32[]{:S(2)}) %collective-permute-start.23) | collective-permute-done | bytes 262176 | tf_op jit(solution)/shard_map/ppermute | solution.py:484
  137.6 2.6 %collective-permute-start.26 = (bf16[2,64,1024]{2,1,0:T(8,128)(2,1)S(1)}, bf16[2,64,1024]{2,1,0:T(8,128)(2,1)S(1)}, u32[]{:S(2)}, u32[]{:S(2)}) collective-permute-start(bf16[2,64,1024]{2,1,0:T(8,128)(2,1)S(1)} %fusion.6), channel_id=1, source_target_pairs={{0,4},{4,0},{8,12},{12,8},{1,5},{5,1},{9,13},{13,9},{2,6},{6,2},{1... | collective-permute-start | bytes 786440 | tf_op jit(solution)/shard_map/ppermute | solution.py:481
  145.3 4.2 %collective-permute-done.21 = bf16[2,64,1024]{2,1,0:T(8,128)(2,1)S(1)} collective-permute-done((bf16[2,64,1024]{2,1,0:T(8,128)(2,1)S(1)}, bf16[2,64,1024]{2,1,0:T(8,128)(2,1)S(1)}, u32[]{:S(2)}, u32[]{:S(2)}) %collective-permute-start.21) | collective-permute-done | bytes 262176 | tf_op jit(solution)/shard_map/ppermute | solution.py:484
  151.8 3.7 %collective-permute-start.29 = (bf16[2,64,1024]{2,1,0:T(8,128)(2,1)}, bf16[2,64,1024]{2,1,0:T(8,128)(2,1)S(1)}, u32[]{:S(2)}, u32[]{:S(2)}) collective-permute-start(bf16[2,64,1024]{2,1,0:T(8,128)(2,1)} %fusion.5), channel_id=1, source_target_pairs={{0,8},{4,12},{8,0},{12,4},{1,9},{5,13},{9,1},{13,5},{2,10},{6,14},... | collective-permute-start | bytes 786440 | tf_op jit(solution)/shard_map/ppermute | solution.py:481
  156.3 4.2 %all-to-all-start = ((bf16[4,2,2,2,16,256]{5,4,1,3,2,0:T(8,128)(2,1)}), bf16[4,2,2,2,16,256]{5,4,1,3,2,0:T(8,128)(2,1)}, u32[]{:S(2)}, u32[]{:S(2)}) async-start(bf16[4,2,2,2,16,256]{5,4,1,3,2,0:T(8,128)(2,1)} %copy_bitcast_fusion), calls=%async_computation | async-start | bytes 524288 | tf_op jit(solution)/shard_map/all_to_all | solution.py:542
  163.3 12.3 %collective-permute-done.29.near2 = bf16[2,64,1024]{2,1,0:T(8,128)(2,1)S(1)} collective-permute-done((bf16[2,64,1024]{2,1,0:T(8,128)(2,1)}, bf16[2,64,1024]{2,1,0:T(8,128)(2,1)S(1)}, u32[]{:S(2)}, u32[]{:S(2)}) %collective-permute-start.29) | collective-permute-done | bytes 262176 | tf_op jit(solution)/shard_map/ppermute | solution.py:481
  175.5 5.7 %collective-permute-done.30.far2 = bf16[2,64,1024]{2,1,0:T(8,128)(2,1)} collective-permute-done((bf16[2,64,1024]{2,1,0:T(8,128)(2,1)}, bf16[2,64,1024]{2,1,0:T(8,128)(2,1)}, u32[]{:S(2)}, u32[]{:S(2)}) %collective-permute-start.30) | collective-permute-done | bytes 262176 | tf_op jit(solution)/shard_map/ppermute | solution.py:481
  185.6 5.4 %collective-permute-done.31.near1 = bf16[2,64,1024]{2,1,0:T(8,128)(2,1)} collective-permute-done((bf16[2,64,1024]{2,1,0:T(8,128)(2,1)}, bf16[2,64,1024]{2,1,0:T(8,128)(2,1)}, u32[]{:S(2)}, u32[]{:S(2)}) %collective-permute-start.31) | collective-permute-done | bytes 262176 | tf_op jit(solution)/shard_map/ppermute | solution.py:481
  191.0 2.4 %final.1 = bf16[4,64,1024]{2,1,0:T(8,128)(2,1)} custom-call(f32[4,2,64,1024]{3,2,1,0:T(8,128)S(1)} %get-tuple-element.128.own, bf16[4,2,64,1024]{3,2,1,0:T(8,128)(2,1)S(1)} %collective-permute-done.19.core, bf16[2,2,64,1024]{3,2,1,0:T(8,128)(2,1)} %collective-permute-done.28.near, bf16[2,64,1024]{2,1,0:T(8,128)(2,1)} %collective-permute-done.22.far, ...), custom_call_target="tpu_custom_call" | custom-call | tf_op jit(solution)/shard_map/final/pallas_call | solution.py:455
  (77 shorter events, 49.6 us)
Async XLA Ops:
  1.7 32.7 %collective-permute-start.1 = (bf16[64,4096]{1,0:T(8,128)(2,1)S(1)}, bf16[64,4096]{1,0:T(8,128)(2,1)S(1)}, u32[]{:S(2)}, u32[]{:S(2)}) collective-permute-start(bf16[64,4096]{1,0:T(8,128)(2,1)S(1)} %dynamic-slice_bitcast_fusion), channel_id=1, source_target_pairs={{0,8},{4,12},{8,0},{12,4},{1,9},{5,13},{9,1},{13,5},{2,10},{6,14},... | collective-permute-start | bytes 1572872 | tf_op jit(solution)/shard_map/ppermute | solution.py:481
  5.8 28.6 %collective-permute-start = (bf16[64,4096]{1,0:T(8,128)(2,1)S(1)}, bf16[64,4096]{1,0:T(8,128)(2,1)S(1)}, u32[]{:S(2)}, u32[]{:S(2)}) collective-permute-start(bf16[64,4096]{1,0:T(8,128)(2,1)S(1)} %dynamic-slice_bitcast_fusion), channel_id=1, source_target_pairs={{0,4},{4,0},{8,12},{12,8},{1,5},{5,1},{9,13},{13,9},{2,6},{6,2},{1... | collective-permute-start | bytes 1572872 | tf_op jit(solution)/shard_map/ppermute | solution.py:481
  14.6 17.7 %collective-permute-start.2 = (bf16[64,512]{1,0:T(8,128)(2,1)S(1)}, bf16[64,512]{1,0:T(8,128)(2,1)S(1)}, u32[]{:S(2)}, u32[]{:S(2)}) collective-permute-start(bf16[64,512]{1,0:T(8,128)(2,1)S(1)} %get-tuple-element.72), channel_id=1, source_target_pairs={{0,4},{4,0},{8,12},{12,8},{1,5},{5,1},{9,13},{13,9},{2,6},{6,2},{1... | collective-permute-start | bytes 196616 | tf_op jit(solution)/shard_map/ppermute | solution.py:481
  15.2 17.2 %collective-permute-start.3 = (bf16[64,512]{1,0:T(8,128)(2,1)S(1)}, bf16[64,512]{1,0:T(8,128)(2,1)S(1)}, u32[]{:S(2)}, u32[]{:S(2)}) collective-permute-start(bf16[64,512]{1,0:T(8,128)(2,1)S(1)} %get-tuple-element.73), channel_id=1, source_target_pairs={{0,8},{4,12},{8,0},{12,4},{1,9},{5,13},{9,1},{13,5},{2,10},{6,14},... | collective-permute-start | bytes 196616 | tf_op jit(solution)/shard_map/ppermute | solution.py:481
  15.2 19.2 %collective-permute-start.4 = (bf16[64,512]{1,0:T(8,128)(2,1)S(1)}, bf16[64,512]{1,0:T(8,128)(2,1)S(1)}, u32[]{:S(2)}, u32[]{:S(2)}) collective-permute-start(bf16[64,512]{1,0:T(8,128)(2,1)S(1)} %get-tuple-element.74), channel_id=1, source_target_pairs={{0,12},{4,8},{8,4},{12,0},{1,13},{5,9},{9,5},{13,1},{2,14},{6,10},... | collective-permute-start | bytes 196616 | tf_op jit(solution)/shard_map/ppermute | solution.py:481
  34.4 14.9 %collective-permute-start.5 = (bf16[64,4096]{1,0:T(8,128)(2,1)S(1)}, bf16[64,4096]{1,0:T(8,128)(2,1)S(1)}, u32[]{:S(2)}, u32[]{:S(2)}) collective-permute-start(bf16[64,4096]{1,0:T(8,128)(2,1)S(1)} %collective-permute-done.refs_1_), channel_id=1, source_target_pairs={{0,2},{1,3},{2,0},{3,1},{4,6},{5,7},{6,4},{7,5},{8,10},{9,11},{10,... | collective-permute-start | bytes 1572872 | tf_op jit(solution)/shard_map/ppermute | solution.py:484
  35.9 22.3 %collective-permute-start.6 = (bf16[64,4096]{1,0:T(8,128)(2,1)S(1)}, bf16[64,4096]{1,0:T(8,128)(2,1)S(1)}, u32[]{:S(2)}, u32[]{:S(2)}) collective-permute-start(bf16[64,4096]{1,0:T(8,128)(2,1)S(1)} %collective-permute-done.1.refs_2_), channel_id=1, source_target_pairs={{0,2},{1,3},{2,0},{3,1},{4,6},{5,7},{6,4},{7,5},{8,10},{9,11},{10,... | collective-permute-start | bytes 1572872 | tf_op jit(solution)/shard_map/ppermute | solution.py:484
  36.4 26.1 %collective-permute-start.8 = (bf16[64,4096]{1,0:T(8,128)(2,1)S(1)}, bf16[64,4096]{1,0:T(8,128)(2,1)S(1)}, u32[]{:S(2)}, u32[]{:S(2)}) collective-permute-start(bf16[64,4096]{1,0:T(8,128)(2,1)S(1)} %collective-permute-done.1.refs_2_), channel_id=1, source_target_pairs={{0,4},{4,0},{8,12},{12,8},{1,5},{5,1},{9,13},{13,9},{2,6},{6,2},{1... | collective-permute-start | bytes 1572872 | tf_op jit(solution)/shard_map/ppermute | solution.py:481
  37.4 27.5 %collective-permute-start.11 = (bf16[512,512]{1,0:T(8,128)(2,1)S(1)}, bf16[512,512]{1,0:T(8,128)(2,1)S(1)}, u32[]{:S(2)}, u32[]{:S(2)}) collective-permute-start(bf16[512,512]{1,0:T(8,128)(2,1)S(1)} %get-tuple-element.84), channel_id=1, source_target_pairs={{0,8},{4,12},{8,0},{12,4},{1,9},{5,13},{9,1},{13,5},{2,10},{6,14},... | collective-permute-start | bytes 1572872 | tf_op jit(solution)/shard_map/ppermute | solution.py:481
  39.5 32.8 %collective-permute-start.12 = (bf16[512,512]{1,0:T(8,128)(2,1)S(1)}, bf16[512,512]{1,0:T(8,128)(2,1)S(1)}, u32[]{:S(2)}, u32[]{:S(2)}) collective-permute-start(bf16[512,512]{1,0:T(8,128)(2,1)S(1)} %get-tuple-element.89), channel_id=1, source_target_pairs={{0,4},{4,0},{8,12},{12,8},{1,5},{5,1},{9,13},{13,9},{2,6},{6,2},{1... | collective-permute-start | bytes 1572872 | tf_op jit(solution)/shard_map/ppermute | solution.py:481
  64.0 21.8 %collective-permute-start.7 = (bf16[512,512]{1,0:T(8,128)(2,1)S(1)}, bf16[512,512]{1,0:T(8,128)(2,1)S(1)}, u32[]{:S(2)}, u32[]{:S(2)}) collective-permute-start(bf16[512,512]{1,0:T(8,128)(2,1)S(1)} %get-tuple-element.78), channel_id=1, source_target_pairs={{0,12},{4,8},{8,4},{12,0},{1,13},{5,9},{9,5},{13,1},{2,14},{6,10},... | collective-permute-start | bytes 1572872 | tf_op jit(solution)/shard_map/ppermute | solution.py:481
  72.3 14.9 %collective-permute-start.13 = (bf16[512,512]{1,0:T(8,128)(2,1)S(1)}, bf16[512,512]{1,0:T(8,128)(2,1)S(1)}, u32[]{:S(2)}, u32[]{:S(2)}) collective-permute-start(bf16[512,512]{1,0:T(8,128)(2,1)S(1)} %collective-permute-done.12.z1), channel_id=1, source_target_pairs={{0,16},{16,0},{1,17},{17,1},{2,18},{18,2},{3,19},{19,3},{4,20},{20... | collective-permute-start | bytes 1572872 | tf_op jit(solution)/shard_map/ppermute | solution.py:487
  73.8 20.5 %collective-permute-start.14 = (bf16[512,512]{1,0:T(8,128)(2,1)S(1)}, bf16[512,512]{1,0:T(8,128)(2,1)S(1)}, u32[]{:S(2)}, u32[]{:S(2)}) collective-permute-start(bf16[512,512]{1,0:T(8,128)(2,1)S(1)} %collective-permute-done.11.z2), channel_id=1, source_target_pairs={{0,16},{16,0},{1,17},{17,1},{2,18},{18,2},{3,19},{19,3},{4,20},{20... | collective-permute-start | bytes 1572872 | tf_op jit(solution)/shard_map/ppermute | solution.py:487
  95.1 14.3 %collective-permute-start.10 = (bf16[512,512]{1,0:T(8,128)(2,1)S(1)}, bf16[512,512]{1,0:T(8,128)(2,1)S(1)}, u32[]{:S(2)}, u32[]{:S(2)}) collective-permute-start(bf16[512,512]{1,0:T(8,128)(2,1)S(1)} %collective-permute-done.7.refs_3_), channel_id=1, source_target_pairs={{0,16},{16,0},{1,17},{17,1},{2,18},{18,2},{3,19},{19,3},{4,20},{20... | collective-permute-start | bytes 1572872 | tf_op jit(solution)/shard_map/ppermute | solution.py:487
  124.6 12.9 %collective-permute-start.23 = (bf16[2,64,1024]{2,1,0:T(8,128)(2,1)S(1)}, bf16[2,64,1024]{2,1,0:T(8,128)(2,1)S(1)}, u32[]{:S(2)}, u32[]{:S(2)}) collective-permute-start(bf16[2,64,1024]{2,1,0:T(8,128)(2,1)S(1)} %get-tuple-element.113), channel_id=1, source_target_pairs={{0,2},{1,3},{2,0},{3,1},{4,6},{5,7},{6,4},{7,5},{8,10},{9,11},{10,... | collective-permute-start | bytes 786440 | tf_op jit(solution)/shard_map/ppermute | solution.py:484
  131.1 13.3 %collective-permute-start.25 = (bf16[2,64,1024]{2,1,0:T(8,128)(2,1)S(1)}, bf16[2,64,1024]{2,1,0:T(8,128)(2,1)S(1)}, u32[]{:S(2)}, u32[]{:S(2)}) collective-permute-start(bf16[2,64,1024]{2,1,0:T(8,128)(2,1)S(1)} %fusion.3), channel_id=1, source_target_pairs={{0,4},{4,0},{8,12},{12,8},{1,5},{5,1},{9,13},{13,9},{2,6},{6,2},{1... | collective-permute-start | bytes 786440 | tf_op jit(solution)/shard_map/ppermute | solution.py:481
  137.6 13.4 %collective-permute-start.26 = (bf16[2,64,1024]{2,1,0:T(8,128)(2,1)S(1)}, bf16[2,64,1024]{2,1,0:T(8,128)(2,1)S(1)}, u32[]{:S(2)}, u32[]{:S(2)}) collective-permute-start(bf16[2,64,1024]{2,1,0:T(8,128)(2,1)S(1)} %fusion.6), channel_id=1, source_target_pairs={{0,4},{4,0},{8,12},{12,8},{1,5},{5,1},{9,13},{13,9},{2,6},{6,2},{1... | collective-permute-start | bytes 786440 | tf_op jit(solution)/shard_map/ppermute | solution.py:481
  142.5 13.1 %collective-permute-start.27 = (bf16[2,64,1024]{2,1,0:T(8,128)(2,1)S(1)}, bf16[2,64,1024]{2,1,0:T(8,128)(2,1)S(1)}, u32[]{:S(2)}, u32[]{:S(2)}) collective-permute-start(bf16[2,64,1024]{2,1,0:T(8,128)(2,1)S(1)} %get-tuple-element.124), channel_id=1, source_target_pairs={{0,3},{1,2},{2,1},{3,0},{4,7},{5,6},{6,5},{7,4},{8,11},{9,10},{10,... | collective-permute-start | bytes 786440 | tf_op jit(solution)/shard_map/ppermute | solution.py:484
  149.5 31.7 %collective-permute-start.28 = (bf16[2,2,64,1024]{3,2,1,0:T(8,128)(2,1)}, bf16[2,2,64,1024]{3,2,1,0:T(8,128)(2,1)}, u32[]{:S(2)}, u32[]{:S(2)}) collective-permute-start(bf16[2,2,64,1024]{3,2,1,0:T(8,128)(2,1)} %get-tuple-element.129), channel_id=1, source_target_pairs={{0,2},{1,3},{2,0},{3,1},{4,6},{5,7},{6,4},{7,5},{8,10},{9,11},{10,... | collective-permute-start | bytes 1572872 | tf_op jit(solution)/shard_map/ppermute | solution.py:484
  151.8 23.7 %collective-permute-start.29 = (bf16[2,64,1024]{2,1,0:T(8,128)(2,1)}, bf16[2,64,1024]{2,1,0:T(8,128)(2,1)S(1)}, u32[]{:S(2)}, u32[]{:S(2)}) collective-permute-start(bf16[2,64,1024]{2,1,0:T(8,128)(2,1)} %fusion.5), channel_id=1, source_target_pairs={{0,8},{4,12},{8,0},{12,4},{1,9},{5,13},{9,1},{13,5},{2,10},{6,14},... | collective-permute-start | bytes 786440 | tf_op jit(solution)/shard_map/ppermute | solution.py:481
  155.5 25.7 %collective-permute-start.30 = (bf16[2,64,1024]{2,1,0:T(8,128)(2,1)}, bf16[2,64,1024]{2,1,0:T(8,128)(2,1)}, u32[]{:S(2)}, u32[]{:S(2)}) collective-permute-start(bf16[2,64,1024]{2,1,0:T(8,128)(2,1)} %fusion.2), channel_id=1, source_target_pairs={{0,8},{4,12},{8,0},{12,4},{1,9},{5,13},{9,1},{13,5},{2,10},{6,14},... | collective-permute-start | bytes 786440 | tf_op jit(solution)/shard_map/ppermute | solution.py:481
  156.3 27.5 %all-to-all-start = ((bf16[4,2,2,2,16,256]{5,4,1,3,2,0:T(8,128)(2,1)}), bf16[4,2,2,2,16,256]{5,4,1,3,2,0:T(8,128)(2,1)}, u32[]{:S(2)}, u32[]{:S(2)}) async-start(bf16[4,2,2,2,16,256]{5,4,1,3,2,0:T(8,128)(2,1)} %copy_bitcast_fusion), calls=%async_computation | async-start | bytes 524288 | tf_op jit(solution)/shard_map/all_to_all | solution.py:542
  160.5 24.4 %collective-permute-start.22 = (bf16[2,64,1024]{2,1,0:T(8,128)(2,1)}, bf16[2,64,1024]{2,1,0:T(8,128)(2,1)}, u32[]{:S(2)}, u32[]{:S(2)}) collective-permute-start(bf16[2,64,1024]{2,1,0:T(8,128)(2,1)} %copy-done.6), channel_id=1, source_target_pairs={{0,3},{1,2},{2,1},{3,0},{4,7},{5,6},{6,5},{7,4},{8,11},{9,10},{10,... | collective-permute-start | bytes 786440 | tf_op jit(solution)/shard_map/ppermute | solution.py:484
  161.5 24.1 %collective-permute-start.32 = (bf16[2,64,1024]{2,1,0:T(8,128)(2,1)}, bf16[2,64,1024]{2,1,0:T(8,128)(2,1)}, u32[]{:S(2)}, u32[]{:S(2)}) collective-permute-start(bf16[2,64,1024]{2,1,0:T(8,128)(2,1)} %fusion), channel_id=1, source_target_pairs={{0,4},{4,0},{8,12},{12,8},{1,5},{5,1},{9,13},{13,9},{2,6},{6,2},{1... | collective-permute-start | bytes 786440 | tf_op jit(solution)/shard_map/ppermute | solution.py:481
  (18 other events, 134.5 us)

commit v8 on v7

--- a/solution.py
+++ b/solution.py
@@ -319,7 +319,7 @@
     mine, theirs = refs[2:5], refs[5:8]
     (
         att_ref, qg_ref, own_ref,
-        a3, b3, a2, b2, b1, a10, b0, core_ref,
+        a3, b3, a2, b2, b10, a10, core_ref,
         w_s, qc_s, grad_s, sems,
     ) = refs[8:]
     s, g, h = lax.axis_index("seq"), lax.axis_index("grp"), lax.axis_index("head")
@@ -390,7 +390,7 @@
     owns = [own_ref.at[k] for k in range(4)]
     for flip, outs in (
         (2, (a10.at[1], a10.at[0], a2, a3)),
-        (3, (b0, b1, b2, b3)),
+        (3, (b10.at[1], b10.at[0], b2, b3)),
         (1, cores),
         (0, owns),
     ):
@@ -419,12 +419,11 @@
             front,
             jax.ShapeDtypeStruct((4, 2, 64, 1024), F32),
         ]
-        + [piece] * 5
-        + [jax.ShapeDtypeStruct((2, 2, 64, 1024), BF)]
-        + [piece]
+        + [piece] * 4
+        + [jax.ShapeDtypeStruct((2, 2, 64, 1024), BF)] * 2
         + [jax.ShapeDtypeStruct((4, 2, 64, 1024), BF)],
         in_specs=[smem] + [vmem] * 2 + [here] * (len(arrays) - 2),
-        out_specs=[vmem] * 11,
+        out_specs=[vmem] * 10,
         scratch_shapes=[
             pltpu.VMEM((2, 4096, 512), BF),
             pltpu.VMEM((2, 4, 64, 512), BF),
@@ -443,7 +442,7 @@
     c = lax.rem(lax.axis_index("head"), 2)
     for i in range(2):
         mine = (own[0, i] + near[1, i].astype(F32)) + (near1[i].astype(F32) + near2[i].astype(F32))
-        theirs = (core[0, i].astype(F32) + far[i].astype(F32)) + (
+        theirs = (core[0, i].astype(F32) + far[1, i].astype(F32)) + (
             far1[i].astype(F32) + far2[i].astype(F32)
         )
         out_ref[2 * i + c] = mine.astype(BF)
@@ -503,6 +502,7 @@
     x2, e3 = together(x2, e3)
     y2 = across(z2)
     x3 = flip(e3, 2)
+    y2, z1 = together(y2, z1)
     y1 = across(z1)
     z3, x3, w_own = together(z3, x3, w_own)
     y3 = across(z3)
@@ -514,7 +514,7 @@
     y3_there = flip(y3, 1)
     outs = main_call(lengths, early + [packed, z3, y3, packed_there, z3_there, y3_there])
     att, qgrad, own = outs[:3]
-    a3, b3, a2, b2, b1, a10, b0, to_core = outs[3:]
+    a3, b3, a2, b2, b10, a10, to_core = outs[3:]
     from_core = flip(to_core, 1)
     front = jnp.stack([att, qgrad], axis=1)
     other = flip(front[1], 1)
@@ -525,27 +525,25 @@
     far3 = along(far3, 1)
     near3, core = together(summed(own[3], a3), core)
     near3 = along(near3, 1)
-    b2, b1, a10 = together(b2, b1, a10)
-    b1, a10 = flip(b1, 3), flip(a10, 2)
+    b2, b10, a10 = together(b2, b10, a10)
+    b10, a10 = flip(b10, 3), flip(a10, 2)
     far2, own = together(summed(core[2], b2, far3), own)
     far2 = along(far2, 2)
-    a2, b0 = together(a2, b0)
-    b0 = flip(b0, 3)
     near2, core = together(summed(own[2], a2, near3), core)
     near2 = along(near2, 2)
     back = jnp.stack([front[0], other]).reshape(2, 2, 2, SEQ, 16, 256).transpose(3, 0, 1, 2, 4, 5)
-    far1, own, back = together(summed(core[1], b1), own, back)
-    far1 = along(far1, 1)
-    a10, near2, far2 = together(a10, near2, far2)
-    near1 = along(summed(own[1], a10[0]), 1)
+    near1, core, back = together(summed(own[1], a10[0]), core, back)
+    near1 = along(near1, 1)
+    b10, near2, far2 = together(b10, near2, far2)
+    far1 = along(summed(core[1], b10[0]), 1)
     from_core = core
     back = lax.all_to_all(back, "seq", split_axis=0, concat_axis=0, tiled=True)
     back = back.transpose(2, 3, 1, 4, 0, 5).reshape(2, 2, 2, 16, 1024)
     back = jnp.where(c == 0, back, back[:, :, ::-1])
     back = back.reshape(2, DOCS, 16, 1024)
-    b0, back = together(b0, back)
+    a10, back = together(a10, back)
     encoder_grad = small_call(
-        final_kernel, (DOCS, 64, 1024), "final", own, from_core, a10, b0, near1, near2, far1, far2
+        final_kernel, (DOCS, 64, 1024), "final", own, from_core, a10, b10, near1, near2, far1, far2
     )
     return (back[0], back[1], encoder_grad)
 

time: 194 us -> 191 us (0.985)
  starting transfers between devices: 48.7 us -> 37.9 us
  waiting for transfers between devices: 110 us -> 116 us
    ppermute x15 -> x14, waiting for transfers between devices: 35.4 us -> 49 us  [flip(): return lax.ppermute(value, 'head', [(a, a ^ bits) for a in range(4)])]
    ppermute x15, starting transfers between devices: 27.2 us -> 17.2 us  [along(): return lax.ppermute(value, 'seq', [(a, a ^ k) for a in range(SEQ)])]
    ppermute x15, waiting for transfers between devices: 61.9 us -> 54 us  [along(): return lax.ppermute(value, 'seq', [(a, a ^ k) for a in range(SEQ)])]
    unnamed x16 -> x18, local copies, waits for them, and re-layouts: 5.72 us -> 7.58 us
    ppermute x15 -> x14, starting transfers between devices: 13.8 us -> 12 us  [flip(): return lax.ppermute(value, 'head', [(a, a ^ bits) for a in range(4)])]
  transfers between devices with their start and end apart: 34 -> 33, of which waited for: 20 -> 22; matrix products, arithmetic and copies ran while one was open for 4% -> 4% of each run, Pallas kernels for 3% -> 3%
where the time goes in v8:
time: 191 us
  waiting for transfers between devices  116 us (61%)
  starting transfers between devices  37.9 us (20%)
  Pallas kernels  20.2 us (11%)
  local copies, waits for them, and re-layouts  10.3 us (5%)
  other arithmetic  5.11 us (3%)
    ppermute x15, waiting for transfers between devices, along(): return lax.ppermute(value, 'seq', [(a, a ^ k) for a in range(SEQ)])  54 us
    ppermute x14, waiting for transfers between devices, flip(): return lax.ppermute(value, 'head', [(a, a ^ bits) for a in range(4)])  49 us
    ppermute x15, starting transfers between devices, along(): return lax.ppermute(value, 'seq', [(a, a ^ k) for a in range(SEQ)])  17.2 us
    ppermute x14, starting transfers between devices, flip(): return lax.ppermute(value, 'head', [(a, a ^ bits) for a in range(4)])  12 us
    ppermute x3, waiting for transfers between devices, across(): return lax.ppermute(value, 'grp', [(0, 1), (1, 0)])  11.6 us
    pallas_call x1, Pallas kernels, main_call(): pl.pallas_call(main_kernel, out_shape=[front, front, jax.ShapeDtypeStruct...  11.3 us
    unnamed x18, local copies, waits for them, and re-layouts  7.58 us
    ppermute x3, starting transfers between devices, across(): return lax.ppermute(value, 'grp', [(0, 1), (1, 0)])  4.62 us
  transfers between devices with their start and end apart: 33, of which 22 were waited for; matrix products, arithmetic and copies ran while one was open for 4% of the time, Pallas kernels for 3%

profile of v8, /device:TPU:0, one launch (start us, length us, event | category | flops | bytes accessed | tf_op | source)
XLA Modules:
  0.0 190.8 jit_solution(8972491123108977656)
XLA Ops:
  1.7 4.1 %collective-permute-start.1 = (bf16[64,4096]{1,0:T(8,128)(2,1)S(1)}, bf16[64,4096]{1,0:T(8,128)(2,1)S(1)}, u32[]{:S(2)}, u32[]{:S(2)}) collective-permute-start(bf16[64,4096]{1,0:T(8,128)(2,1)S(1)} %dynamic-slice_bitcast_fusion), channel_id=1, source_target_pairs={{0,8},{4,12},{8,0},{12,4},{1,9},{5,13},{9,1},{13,5},{2,10},{6,14},... | collective-permute-start | bytes 1572872 | tf_op jit(solution)/shard_map/ppermute | solution.py:480
  15.2 3.9 %collective-permute-start.4 = (bf16[64,512]{1,0:T(8,128)(2,1)S(1)}, bf16[64,512]{1,0:T(8,128)(2,1)S(1)}, u32[]{:S(2)}, u32[]{:S(2)}) collective-permute-start(bf16[64,512]{1,0:T(8,128)(2,1)S(1)} %get-tuple-element.73), channel_id=1, source_target_pairs={{0,12},{4,8},{8,4},{12,0},{1,13},{5,9},{9,5},{13,1},{2,14},{6,10},... | collective-permute-start | bytes 196616 | tf_op jit(solution)/shard_map/ppermute | solution.py:480
  19.1 13.3 %collective-permute-done.2.q1 = bf16[64,512]{1,0:T(8,128)(2,1)S(1)} collective-permute-done((bf16[64,512]{1,0:T(8,128)(2,1)S(1)}, bf16[64,512]{1,0:T(8,128)(2,1)S(1)}, u32[]{:S(2)}, u32[]{:S(2)}) %collective-permute-start.2) | collective-permute-done | bytes 65568 | tf_op jit(solution)/shard_map/ppermute | solution.py:480
  32.4 2.0 %collective-permute-done.4.q3 = bf16[64,512]{1,0:T(8,128)(2,1)S(1)} collective-permute-done((bf16[64,512]{1,0:T(8,128)(2,1)S(1)}, bf16[64,512]{1,0:T(8,128)(2,1)S(1)}, u32[]{:S(2)}, u32[]{:S(2)}) %collective-permute-start.4) | collective-permute-done | bytes 65568 | tf_op jit(solution)/shard_map/ppermute | solution.py:480
  36.4 2.9 %collective-permute-start.11 = (bf16[512,512]{1,0:T(8,128)(2,1)S(1)}, bf16[512,512]{1,0:T(8,128)(2,1)S(1)}, u32[]{:S(2)}, u32[]{:S(2)}) collective-permute-start(bf16[512,512]{1,0:T(8,128)(2,1)S(1)} %get-tuple-element.83), channel_id=1, source_target_pairs={{0,8},{4,12},{8,0},{12,4},{1,9},{5,13},{9,1},{13,5},{2,10},{6,14},... | collective-permute-start | bytes 1572872 | tf_op jit(solution)/shard_map/ppermute | solution.py:480
  41.3 7.9 %collective-permute-done.5.refs_4_ = bf16[64,4096]{1,0:T(8,128)(2,1)S(1)} collective-permute-done((bf16[64,4096]{1,0:T(8,128)(2,1)S(1)}, bf16[64,4096]{1,0:T(8,128)(2,1)S(1)}, u32[]{:S(2)}, u32[]{:S(2)}) %collective-permute-start.5) | collective-permute-done | bytes 524320 | tf_op jit(solution)/shard_map/ppermute | solution.py:483
  49.3 8.9 %collective-permute-done.6.refs_5_ = bf16[64,4096]{1,0:T(8,128)(2,1)S(1)} collective-permute-done((bf16[64,4096]{1,0:T(8,128)(2,1)S(1)}, bf16[64,4096]{1,0:T(8,128)(2,1)S(1)}, u32[]{:S(2)}, u32[]{:S(2)}) %collective-permute-start.6) | collective-permute-done | bytes 524320 | tf_op jit(solution)/shard_map/ppermute | solution.py:483
  58.2 4.0 %collective-permute-done.11.z2 = bf16[512,512]{1,0:T(8,128)(2,1)S(1)} collective-permute-done((bf16[512,512]{1,0:T(8,128)(2,1)S(1)}, bf16[512,512]{1,0:T(8,128)(2,1)S(1)}, u32[]{:S(2)}, u32[]{:S(2)}) %collective-permute-start.11) | collective-permute-done | bytes 524320 | tf_op jit(solution)/shard_map/ppermute | solution.py:480
  66.6 19.1 %collective-permute-done.13.z1 = bf16[512,512]{1,0:T(8,128)(2,1)S(1)} collective-permute-done((bf16[512,512]{1,0:T(8,128)(2,1)S(1)}, bf16[512,512]{1,0:T(8,128)(2,1)S(1)}, u32[]{:S(2)}, u32[]{:S(2)}) %collective-permute-start.13) | collective-permute-done | bytes 524320 | tf_op jit(solution)/shard_map/ppermute | solution.py:480
  87.3 7.7 %collective-permute-done.14.y1 = bf16[512,512]{1,0:T(8,128)(2,1)S(1)} collective-permute-done((bf16[512,512]{1,0:T(8,128)(2,1)S(1)}, bf16[512,512]{1,0:T(8,128)(2,1)S(1)}, u32[]{:S(2)}, u32[]{:S(2)}) %collective-permute-start.14) | collective-permute-done | bytes 524320 | tf_op jit(solution)/shard_map/ppermute | solution.py:486
  97.5 4.3 %collective-permute-done.15.refs_8_.refs_5_ = bf16[3328,512]{1,0:T(8,128)(2,1)S(1)} collective-permute-done((bf16[3328,512]{1,0:T(8,128)(2,1)S(1)}, bf16[3328,512]{1,0:T(8,128)(2,1)S(1)}, u32[]{:S(2)}, u32[]{:S(2)}) %collective-permute-start.15) | collective-permute-done | bytes 3407904 | tf_op jit(solution)/shard_map/ppermute | solution.py:483
  101.7 4.4 %early.1 = (f32[2,512,512]{2,1,0:T(8,128)S(1)}, bf16[512,1024]{1,0:T(8,128)(2,1)S(1)}) custom-call(bf16[4,64,4096]{2,1,0:T(8,128)(2,1)S(1)} %copy-done, bf16[64,4096]{1,0:T(8,128)(2,1)S(1)} %collective-permute-done.refs_1_, bf16[64,4096]{1,0:T(8,128)(2,1)S(1)} %collective-permute-done.1.refs_2_, bf16[64,4096]{1,0:T(8,128)(2,1)S(1)} %collective-permute-done.8.refs_3_, ...), custom_call_target="tpu_custom_call" | custom-call | flops 1 | bytes 1 | tf_op jit(solution)/shard_map/early/pallas_call | solution.py:296
  106.1 3.9 %collective-permute-done.10.refs_4_ = bf16[512,512]{1,0:T(8,128)(2,1)S(1)} collective-permute-done((bf16[512,512]{1,0:T(8,128)(2,1)S(1)}, bf16[512,512]{1,0:T(8,128)(2,1)S(1)}, u32[]{:S(2)}, u32[]{:S(2)}) %collective-permute-start.10) | collective-permute-done | bytes 524320 | tf_op jit(solution)/shard_map/ppermute | solution.py:486
  112.0 11.3 %attend.1 = (bf16[2,2,64,256]{3,2,1,0:T(8,128)(2,1)S(1)}, bf16[2,2,64,256]{3,2,1,0:T(8,128)(2,1)S(1)}, f32[4,2,64,1024]{3,2,1,0:T(8,128)S(1)}, bf16[2,64,1024]{2...) custom-call(s32[4]{0:T(128)S(1)} %copy-done.8, ...), custom_call_target="tpu_custom_call" | custom-call | flops 6000000000 | bytes 25165824 | tf_op jit(solution)/shard_map/attend/pallas_call | solution.py:415
  126.4 5.2 %collective-permute-done.18 = bf16[2,64,1024]{2,1,0:T(8,128)(2,1)S(1)} collective-permute-done((bf16[2,64,1024]{2,1,0:T(8,128)(2,1)S(1)}, bf16[2,64,1024]{2,1,0:T(8,128)(2,1)S(1)}, u32[]{:S(2)}, u32[]{:S(2)}) %collective-permute-start.18) | collective-permute-done | bytes 262176 | tf_op jit(solution)/shard_map/ppermute | solution.py:483
  133.6 4.5 %collective-permute-done.23 = bf16[2,64,1024]{2,1,0:T(8,128)(2,1)S(1)} collective-permute-done((bf16[2,64,1024]{2,1,0:T(8,128)(2,1)S(1)}, bf16[2,64,1024]{2,1,0:T(8,128)(2,1)S(1)}, u32[]{:S(2)}, u32[]{:S(2)}) %collective-permute-start.23) | collective-permute-done | bytes 262176 | tf_op jit(solution)/shard_map/ppermute | solution.py:483
  139.9 3.0 %collective-permute-done.21 = bf16[2,64,1024]{2,1,0:T(8,128)(2,1)S(1)} collective-permute-done((bf16[2,64,1024]{2,1,0:T(8,128)(2,1)S(1)}, bf16[2,64,1024]{2,1,0:T(8,128)(2,1)S(1)}, u32[]{:S(2)}, u32[]{:S(2)}) %collective-permute-start.21) | collective-permute-done | bytes 262176 | tf_op jit(solution)/shard_map/ppermute | solution.py:483
  147.2 2.2 %collective-permute-done.25 = bf16[2,64,1024]{2,1,0:T(8,128)(2,1)S(1)} collective-permute-done((bf16[2,64,1024]{2,1,0:T(8,128)(2,1)S(1)}, bf16[2,64,1024]{2,1,0:T(8,128)(2,1)S(1)}, u32[]{:S(2)}, u32[]{:S(2)}) %collective-permute-start.25) | collective-permute-done | bytes 262176 | tf_op jit(solution)/shard_map/ppermute | solution.py:483
  150.3 10.3 %collective-permute-done.22.near = bf16[2,2,64,1024]{3,2,1,0:T(8,128)(2,1)S(1)} collective-permute-done((bf16[2,2,64,1024]{3,2,1,0:T(8,128)(2,1)S(1)}, bf16[2,2,64,1024]{3,2,1,0:T(8,128)(2,1)S(1)}, u32[]{:S(2)}, u32[]{:S(2)}) %collective-permute-start.22) | collective-permute-done | bytes 524320 | tf_op jit(solution)/shard_map/ppermute | solution.py:483
  162.2 4.0 %all-to-all-start = ((bf16[4,2,2,2,16,256]{5,4,1,3,2,0:T(8,128)(2,1)}), bf16[4,2,2,2,16,256]{5,4,1,3,2,0:T(8,128)(2,1)}, u32[]{:S(2)}, u32[]{:S(2)}) async-start(bf16[4,2,2,2,16,256]{5,4,1,3,2,0:T(8,128)(2,1)} %copy_bitcast_fusion), calls=%async_computation | async-start | bytes 524288 | tf_op jit(solution)/shard_map/all_to_all | solution.py:540
  168.3 5.9 %collective-permute-done.28.near2 = bf16[2,64,1024]{2,1,0:T(8,128)(2,1)} collective-permute-done((bf16[2,64,1024]{2,1,0:T(8,128)(2,1)}, bf16[2,64,1024]{2,1,0:T(8,128)(2,1)}, u32[]{:S(2)}, u32[]{:S(2)}) %collective-permute-start.28) | collective-permute-done | bytes 262176 | tf_op jit(solution)/shard_map/ppermute | solution.py:480
  179.5 2.4 %collective-permute-done.30.near1 = bf16[2,64,1024]{2,1,0:T(8,128)(2,1)} collective-permute-done((bf16[2,64,1024]{2,1,0:T(8,128)(2,1)}, bf16[2,64,1024]{2,1,0:T(8,128)(2,1)}, u32[]{:S(2)}, u32[]{:S(2)}) %collective-permute-start.30) | collective-permute-done | bytes 262176 | tf_op jit(solution)/shard_map/ppermute | solution.py:480
  181.9 5.5 %collective-permute-done.31.far1 = bf16[2,64,1024]{2,1,0:T(8,128)(2,1)} collective-permute-done((bf16[2,64,1024]{2,1,0:T(8,128)(2,1)}, bf16[2,64,1024]{2,1,0:T(8,128)(2,1)}, u32[]{:S(2)}, u32[]{:S(2)}) %collective-permute-start.31) | collective-permute-done | bytes 262176 | tf_op jit(solution)/shard_map/ppermute | solution.py:480
  188.5 2.3 %final.1 = bf16[4,64,1024]{2,1,0:T(8,128)(2,1)} custom-call(f32[4,2,64,1024]{3,2,1,0:T(8,128)S(1)} %get-tuple-element.119.own, bf16[4,2,64,1024]{3,2,1,0:T(8,128)(2,1)S(1)} %collective-permute-done.19.core, bf16[2,2,64,1024]{3,2,1,0:T(8,128)(2,1)S(1)} %copy-done.4, bf16[2,2,64,1024]{3,2,1,0:T(8,128)(2,1)} %collective-permute-done.27.far, ...), custom_call_target="tpu_custom_call" | custom-call | tf_op jit(solution)/shard_map/final/pallas_call | solution.py:454
  (77 shorter events, 46.9 us)
Async XLA Ops:
  1.7 32.7 %collective-permute-start.1 = (bf16[64,4096]{1,0:T(8,128)(2,1)S(1)}, bf16[64,4096]{1,0:T(8,128)(2,1)S(1)}, u32[]{:S(2)}, u32[]{:S(2)}) collective-permute-start(bf16[64,4096]{1,0:T(8,128)(2,1)S(1)} %dynamic-slice_bitcast_fusion), channel_id=1, source_target_pairs={{0,8},{4,12},{8,0},{12,4},{1,9},{5,13},{9,1},{13,5},{2,10},{6,14},... | collective-permute-start | bytes 1572872 | tf_op jit(solution)/shard_map/ppermute | solution.py:480
  5.8 28.6 %collective-permute-start = (bf16[64,4096]{1,0:T(8,128)(2,1)S(1)}, bf16[64,4096]{1,0:T(8,128)(2,1)S(1)}, u32[]{:S(2)}, u32[]{:S(2)}) collective-permute-start(bf16[64,4096]{1,0:T(8,128)(2,1)S(1)} %dynamic-slice_bitcast_fusion), channel_id=1, source_target_pairs={{0,4},{4,0},{8,12},{12,8},{1,5},{5,1},{9,13},{13,9},{2,6},{6,2},{1... | collective-permute-start | bytes 1572872 | tf_op jit(solution)/shard_map/ppermute | solution.py:480
  14.6 17.7 %collective-permute-start.2 = (bf16[64,512]{1,0:T(8,128)(2,1)S(1)}, bf16[64,512]{1,0:T(8,128)(2,1)S(1)}, u32[]{:S(2)}, u32[]{:S(2)}) collective-permute-start(bf16[64,512]{1,0:T(8,128)(2,1)S(1)} %get-tuple-element.71), channel_id=1, source_target_pairs={{0,4},{4,0},{8,12},{12,8},{1,5},{5,1},{9,13},{13,9},{2,6},{6,2},{1... | collective-permute-start | bytes 196616 | tf_op jit(solution)/shard_map/ppermute | solution.py:480
  15.2 17.2 %collective-permute-start.3 = (bf16[64,512]{1,0:T(8,128)(2,1)S(1)}, bf16[64,512]{1,0:T(8,128)(2,1)S(1)}, u32[]{:S(2)}, u32[]{:S(2)}) collective-permute-start(bf16[64,512]{1,0:T(8,128)(2,1)S(1)} %get-tuple-element.72), channel_id=1, source_target_pairs={{0,8},{4,12},{8,0},{12,4},{1,9},{5,13},{9,1},{13,5},{2,10},{6,14},... | collective-permute-start | bytes 196616 | tf_op jit(solution)/shard_map/ppermute | solution.py:480
  15.2 19.2 %collective-permute-start.4 = (bf16[64,512]{1,0:T(8,128)(2,1)S(1)}, bf16[64,512]{1,0:T(8,128)(2,1)S(1)}, u32[]{:S(2)}, u32[]{:S(2)}) collective-permute-start(bf16[64,512]{1,0:T(8,128)(2,1)S(1)} %get-tuple-element.73), channel_id=1, source_target_pairs={{0,12},{4,8},{8,4},{12,0},{1,13},{5,9},{9,5},{13,1},{2,14},{6,10},... | collective-permute-start | bytes 196616 | tf_op jit(solution)/shard_map/ppermute | solution.py:480
  34.4 14.9 %collective-permute-start.5 = (bf16[64,4096]{1,0:T(8,128)(2,1)S(1)}, bf16[64,4096]{1,0:T(8,128)(2,1)S(1)}, u32[]{:S(2)}, u32[]{:S(2)}) collective-permute-start(bf16[64,4096]{1,0:T(8,128)(2,1)S(1)} %collective-permute-done.refs_1_), channel_id=1, source_target_pairs={{0,2},{1,3},{2,0},{3,1},{4,6},{5,7},{6,4},{7,5},{8,10},{9,11},{10,... | collective-permute-start | bytes 1572872 | tf_op jit(solution)/shard_map/ppermute | solution.py:483
  35.9 22.3 %collective-permute-start.6 = (bf16[64,4096]{1,0:T(8,128)(2,1)S(1)}, bf16[64,4096]{1,0:T(8,128)(2,1)S(1)}, u32[]{:S(2)}, u32[]{:S(2)}) collective-permute-start(bf16[64,4096]{1,0:T(8,128)(2,1)S(1)} %collective-permute-done.1.refs_2_), channel_id=1, source_target_pairs={{0,2},{1,3},{2,0},{3,1},{4,6},{5,7},{6,4},{7,5},{8,10},{9,11},{10,... | collective-permute-start | bytes 1572872 | tf_op jit(solution)/shard_map/ppermute | solution.py:483
  36.4 25.8 %collective-permute-start.11 = (bf16[512,512]{1,0:T(8,128)(2,1)S(1)}, bf16[512,512]{1,0:T(8,128)(2,1)S(1)}, u32[]{:S(2)}, u32[]{:S(2)}) collective-permute-start(bf16[512,512]{1,0:T(8,128)(2,1)S(1)} %get-tuple-element.83), channel_id=1, source_target_pairs={{0,8},{4,12},{8,0},{12,4},{1,9},{5,13},{9,1},{13,5},{2,10},{6,14},... | collective-permute-start | bytes 1572872 | tf_op jit(solution)/shard_map/ppermute | solution.py:480
  39.3 25.8 %collective-permute-start.8 = (bf16[64,4096]{1,0:T(8,128)(2,1)S(1)}, bf16[64,4096]{1,0:T(8,128)(2,1)S(1)}, u32[]{:S(2)}, u32[]{:S(2)}) collective-permute-start(bf16[64,4096]{1,0:T(8,128)(2,1)S(1)} %collective-permute-done.1.refs_2_), channel_id=1, source_target_pairs={{0,4},{4,0},{8,12},{12,8},{1,5},{5,1},{9,13},{13,9},{2,6},{6,2},{1... | collective-permute-start | bytes 1572872 | tf_op jit(solution)/shard_map/ppermute | solution.py:480
  39.5 46.3 %collective-permute-start.13 = (bf16[512,512]{1,0:T(8,128)(2,1)S(1)}, bf16[512,512]{1,0:T(8,128)(2,1)S(1)}, u32[]{:S(2)}, u32[]{:S(2)}) collective-permute-start(bf16[512,512]{1,0:T(8,128)(2,1)S(1)} %get-tuple-element.89), channel_id=1, source_target_pairs={{0,4},{4,0},{8,12},{12,8},{1,5},{5,1},{9,13},{13,9},{2,6},{6,2},{1... | collective-permute-start | bytes 1572872 | tf_op jit(solution)/shard_map/ppermute | solution.py:480
  62.2 23.6 %collective-permute-start.12 = (bf16[512,512]{1,0:T(8,128)(2,1)S(1)}, bf16[512,512]{1,0:T(8,128)(2,1)S(1)}, u32[]{:S(2)}, u32[]{:S(2)}) collective-permute-start(bf16[512,512]{1,0:T(8,128)(2,1)S(1)} %collective-permute-done.11.z2), channel_id=1, source_target_pairs={{0,16},{16,0},{1,17},{17,1},{2,18},{18,2},{3,19},{19,3},{4,20},{20... | collective-permute-start | bytes 1572872 | tf_op jit(solution)/shard_map/ppermute | solution.py:486
  65.1 22.1 %collective-permute-start.9 = (bf16[64,4096]{1,0:T(8,128)(2,1)S(1)}, bf16[64,4096]{1,0:T(8,128)(2,1)S(1)}, u32[]{:S(2)}, u32[]{:S(2)}) collective-permute-start(bf16[64,4096]{1,0:T(8,128)(2,1)S(1)} %collective-permute-done.8.refs_3_), channel_id=1, source_target_pairs={{0,2},{1,3},{2,0},{3,1},{4,6},{5,7},{6,4},{7,5},{8,10},{9,11},{10,... | collective-permute-start | bytes 1572872 | tf_op jit(solution)/shard_map/ppermute | solution.py:483
  66.6 20.7 %collective-permute-start.7 = (bf16[512,512]{1,0:T(8,128)(2,1)S(1)}, bf16[512,512]{1,0:T(8,128)(2,1)S(1)}, u32[]{:S(2)}, u32[]{:S(2)}) collective-permute-start(bf16[512,512]{1,0:T(8,128)(2,1)S(1)} %get-tuple-element.77), channel_id=1, source_target_pairs={{0,12},{4,8},{8,4},{12,0},{1,13},{5,9},{9,5},{13,1},{2,14},{6,10},... | collective-permute-start | bytes 1572872 | tf_op jit(solution)/shard_map/ppermute | solution.py:480
  95.7 14.3 %collective-permute-start.10 = (bf16[512,512]{1,0:T(8,128)(2,1)S(1)}, bf16[512,512]{1,0:T(8,128)(2,1)S(1)}, u32[]{:S(2)}, u32[]{:S(2)}) collective-permute-start(bf16[512,512]{1,0:T(8,128)(2,1)S(1)} %collective-permute-done.7.refs_3_), channel_id=1, source_target_pairs={{0,16},{16,0},{1,17},{17,1},{2,18},{18,2},{3,19},{19,3},{4,20},{20... | collective-permute-start | bytes 1572872 | tf_op jit(solution)/shard_map/ppermute | solution.py:486
  97.3 12.8 %collective-permute-start.16 = (bf16[512,512]{1,0:T(8,128)(2,1)S(1)}, bf16[512,512]{1,0:T(8,128)(2,1)S(1)}, u32[]{:S(2)}, u32[]{:S(2)}) collective-permute-start(bf16[512,512]{1,0:T(8,128)(2,1)S(1)} %collective-permute-done.7.refs_3_), channel_id=1, source_target_pairs={{0,1},{1,0},{2,3},{3,2},{4,5},{5,4},{6,7},{7,6},{8,9},{9,8},{10,11... | collective-permute-start | bytes 1572872 | tf_op jit(solution)/shard_map/ppermute | solution.py:483
  125.2 13.0 %collective-permute-start.23 = (bf16[2,64,1024]{2,1,0:T(8,128)(2,1)S(1)}, bf16[2,64,1024]{2,1,0:T(8,128)(2,1)S(1)}, u32[]{:S(2)}, u32[]{:S(2)}) collective-permute-start(bf16[2,64,1024]{2,1,0:T(8,128)(2,1)S(1)} %get-tuple-element.115), channel_id=1, source_target_pairs={{0,2},{1,3},{2,0},{3,1},{4,6},{5,7},{6,4},{7,5},{8,10},{9,11},{10,... | collective-permute-start | bytes 786440 | tf_op jit(solution)/shard_map/ppermute | solution.py:483
  133.5 11.5 %collective-permute-start.24 = (bf16[2,64,1024]{2,1,0:T(8,128)(2,1)S(1)}, bf16[2,64,1024]{2,1,0:T(8,128)(2,1)S(1)}, u32[]{:S(2)}, u32[]{:S(2)}) collective-permute-start(bf16[2,64,1024]{2,1,0:T(8,128)(2,1)S(1)} %fusion.2), channel_id=1, source_target_pairs={{0,4},{4,0},{8,12},{12,8},{1,5},{5,1},{9,13},{13,9},{2,6},{6,2},{1... | collective-permute-start | bytes 786440 | tf_op jit(solution)/shard_map/ppermute | solution.py:480
  142.8 17.8 %collective-permute-start.22 = (bf16[2,2,64,1024]{3,2,1,0:T(8,128)(2,1)S(1)}, bf16[2,2,64,1024]{3,2,1,0:T(8,128)(2,1)S(1)}, u32[]{:S(2)}, u32[]{:S(2)}) collective-permute-start(bf16[2,2,64,1024]{3,2,1,0:T(8,128)(2,1)S(1)} %get-tuple-element.110), channel_id=1, source_target_pairs={{0,2},{1,3},{2,0},{3,1},{4,6},{5,7},{6,4},{7,5},{8,10},{9,11},{10,... | collective-permute-start | bytes 1572872 | tf_op jit(solution)/shard_map/ppermute | solution.py:483
  145.9 22.3 %collective-permute-start.29 = (bf16[2,64,1024]{2,1,0:T(8,128)(2,1)}, bf16[2,64,1024]{2,1,0:T(8,128)(2,1)S(1)}, u32[]{:S(2)}, u32[]{:S(2)}) collective-permute-start(bf16[2,64,1024]{2,1,0:T(8,128)(2,1)} %fusion.1), channel_id=1, source_target_pairs={{0,8},{4,12},{8,0},{12,4},{1,9},{5,13},{9,1},{13,5},{2,10},{6,14},... | collective-permute-start | bytes 786440 | tf_op jit(solution)/shard_map/ppermute | solution.py:480
  145.9 28.2 %collective-permute-start.27 = (bf16[2,2,64,1024]{3,2,1,0:T(8,128)(2,1)}, bf16[2,2,64,1024]{3,2,1,0:T(8,128)(2,1)}, u32[]{:S(2)}, u32[]{:S(2)}) collective-permute-start(bf16[2,2,64,1024]{3,2,1,0:T(8,128)(2,1)} %get-tuple-element.128), channel_id=1, source_target_pairs={{0,3},{1,2},{2,1},{3,0},{4,7},{5,6},{6,5},{7,4},{8,11},{9,10},{10,... | collective-permute-start | bytes 1572872 | tf_op jit(solution)/shard_map/ppermute | solution.py:483
  150.2 23.9 %collective-permute-start.28 = (bf16[2,64,1024]{2,1,0:T(8,128)(2,1)}, bf16[2,64,1024]{2,1,0:T(8,128)(2,1)}, u32[]{:S(2)}, u32[]{:S(2)}) collective-permute-start(bf16[2,64,1024]{2,1,0:T(8,128)(2,1)} %fusion.4), channel_id=1, source_target_pairs={{0,8},{4,12},{8,0},{12,4},{1,9},{5,13},{9,1},{13,5},{2,10},{6,14},... | collective-permute-start | bytes 786440 | tf_op jit(solution)/shard_map/ppermute | solution.py:480
  162.2 15.5 %all-to-all-start = ((bf16[4,2,2,2,16,256]{5,4,1,3,2,0:T(8,128)(2,1)}), bf16[4,2,2,2,16,256]{5,4,1,3,2,0:T(8,128)(2,1)}, u32[]{:S(2)}, u32[]{:S(2)}) async-start(bf16[4,2,2,2,16,256]{5,4,1,3,2,0:T(8,128)(2,1)} %copy_bitcast_fusion), calls=%async_computation | async-start | bytes 524288 | tf_op jit(solution)/shard_map/all_to_all | solution.py:540
  166.3 15.6 %collective-permute-start.30 = (bf16[2,64,1024]{2,1,0:T(8,128)(2,1)}, bf16[2,64,1024]{2,1,0:T(8,128)(2,1)}, u32[]{:S(2)}, u32[]{:S(2)}) collective-permute-start(bf16[2,64,1024]{2,1,0:T(8,128)(2,1)} %fusion.6), channel_id=1, source_target_pairs={{0,4},{4,0},{8,12},{12,8},{1,5},{5,1},{9,13},{13,9},{2,6},{6,2},{1... | collective-permute-start | bytes 786440 | tf_op jit(solution)/shard_map/ppermute | solution.py:480
  175.9 11.5 %collective-permute-start.31 = (bf16[2,64,1024]{2,1,0:T(8,128)(2,1)}, bf16[2,64,1024]{2,1,0:T(8,128)(2,1)}, u32[]{:S(2)}, u32[]{:S(2)}) collective-permute-start(bf16[2,64,1024]{2,1,0:T(8,128)(2,1)} %fusion.7), channel_id=1, source_target_pairs={{0,4},{4,0},{8,12},{12,8},{1,5},{5,1},{9,13},{13,9},{2,6},{6,2},{1... | collective-permute-start | bytes 786440 | tf_op jit(solution)/shard_map/ppermute | solution.py:480
  (18 other events, 97.1 us)

commit v9 on v8

--- a/solution.py
+++ b/solution.py
@@ -487,24 +487,17 @@
 
     e0 = lax.dynamic_index_in_dim(encoder, h, 0, keepdims=False)
     e2 = along(e0, 2)
-    e1 = along(e0, 1)
     w_own, m1, m2, m3, q0, q1, q2, q3 = prune(
         tile_mask, key_weight, value_weight, queries.reshape(64, 1024), cotangent.reshape(64, 1024)
     )
+    z1 = along(m1, 1)
     q1, q2, q3 = along(q1, 1), along(q2, 2), along(q3, 3)
-    e1, e2, m1, m2, q1, q2, q3 = together(e1, e2, m1, m2, q1, q2, q3)
-    z2, z1 = along(m2, 2), along(m1, 1)
-    e3 = along(e2, 1)
-    x1, x2 = flip(e1, 2), flip(e2, 2)
-    x1, x2, m3 = together(x1, x2, m3)
-    z3 = along(m3, 3)
-    x1, z2 = together(x1, z2)
-    x2, e3 = together(x2, e3)
-    y2 = across(z2)
-    x3 = flip(e3, 2)
-    y2, z1 = together(y2, z1)
-    y1 = across(z1)
-    z3, x3, w_own = together(z3, x3, w_own)
+    e2, z1, q1, q2, q3, m2, e0 = together(e2, z1, q1, q2, q3, m2, e0)
+    e3, z2, x2, y1 = along(e2, 1), along(m2, 2), flip(e2, 2), across(z1)
+    e3, z2, x2, y1, m3, e0 = together(e3, z2, x2, y1, m3, e0)
+    z3, e1, y2, x3 = along(m3, 3), along(e0, 1), across(z2), flip(e3, 2)
+    x1 = flip(e1, 2)
+    z3, x3, e1, w_own = together(z3, x3, e1, w_own)
     y3 = across(z3)
     packed = pack_call(w_own, z1, z2, y1, y2, q0, q1, q2, q3)
     packed_there = flip(packed, 1)

time: 191 us -> 193 us (1.010)
  waiting for transfers between devices: 116 us -> 118 us
    ppermute x15, waiting for transfers between devices: 54 us -> 78.8 us  [along(): return lax.ppermute(value, 'seq', [(a, a ^ k) for a in range(SEQ)])]
    ppermute x14, waiting for transfers between devices: 49 us -> 37 us  [flip(): return lax.ppermute(value, 'head', [(a, a ^ bits) for a in range(4)])]
    ppermute x3, waiting for transfers between devices: 11.6 us -> 0.01 us  [across(): return lax.ppermute(value, 'grp', [(0, 1), (1, 0)])]
    ppermute x15, starting transfers between devices: 17.2 us -> 19.7 us  [along(): return lax.ppermute(value, 'seq', [(a, a ^ k) for a in range(SEQ)])]
  transfers between devices with their start and end apart: 33 -> 33, of which waited for: 22 -> 17; matrix products, arithmetic and copies ran while one was open for 4% -> 4% of each run, Pallas kernels for 3% -> 3%
where the time goes in v9:
time: 193 us
  waiting for transfers between devices  118 us (61%)
  starting transfers between devices  39 us (20%)
  Pallas kernels  20.2 us (10%)
  local copies, waits for them, and re-layouts  10.3 us (5%)
  other arithmetic  5.11 us (3%)
    ppermute x15, waiting for transfers between devices, along(): return lax.ppermute(value, 'seq', [(a, a ^ k) for a in range(SEQ)])  78.8 us
    ppermute x14, waiting for transfers between devices, flip(): return lax.ppermute(value, 'head', [(a, a ^ bits) for a in range(4)])  37 us
    ppermute x15, starting transfers between devices, along(): return lax.ppermute(value, 'seq', [(a, a ^ k) for a in range(SEQ)])  19.7 us
    ppermute x14, starting transfers between devices, flip(): return lax.ppermute(value, 'head', [(a, a ^ bits) for a in range(4)])  11.7 us
    pallas_call x1, Pallas kernels, main_call(): pl.pallas_call(main_kernel, out_shape=[front, front, jax.ShapeDtypeStruct...  11.3 us
    unnamed x18, local copies, waits for them, and re-layouts  7.58 us
    pallas_call x1, Pallas kernels, early_call(): pl.pallas_call(early_kernel, out_shape=[jax.ShapeDtypeStruct((2, 512, 512...  4.39 us
    convert_element_type x6, other arithmetic, summed(): return total.astype(BF)  4.28 us
  transfers between devices with their start and end apart: 33, of which 17 were waited for; matrix products, arithmetic and copies ran while one was open for 4% of the time, Pallas kernels for 3%

profile of v9, /device:TPU:0, one launch (start us, length us, event | category | flops | bytes accessed | tf_op | source)
XLA Modules:
  0.0 193.0 jit_solution(7850354060518947736)
XLA Ops:
  1.7 4.1 %collective-permute-start = (bf16[64,4096]{1,0:T(8,128)(2,1)S(1)}, bf16[64,4096]{1,0:T(8,128)(2,1)S(1)}, u32[]{:S(2)}, u32[]{:S(2)}) collective-permute-start(bf16[64,4096]{1,0:T(8,128)(2,1)S(1)} %dynamic-slice_bitcast_fusion), channel_id=1, source_target_pairs={{0,8},{4,12},{8,0},{12,4},{1,9},{5,13},{9,1},{13,5},{2,10},{6,14},... | collective-permute-start | bytes 1572872 | tf_op jit(solution)/shard_map/ppermute | solution.py:480
  15.2 3.9 %collective-permute-start.4 = (bf16[64,512]{1,0:T(8,128)(2,1)S(1)}, bf16[64,512]{1,0:T(8,128)(2,1)S(1)}, u32[]{:S(2)}, u32[]{:S(2)}) collective-permute-start(bf16[64,512]{1,0:T(8,128)(2,1)S(1)} %get-tuple-element.70), channel_id=1, source_target_pairs={{0,12},{4,8},{8,4},{12,0},{1,13},{5,9},{9,5},{13,1},{2,14},{6,10},... | collective-permute-start | bytes 196616 | tf_op jit(solution)/shard_map/ppermute | solution.py:480
  19.1 21.7 %collective-permute-done.2.q1 = bf16[64,512]{1,0:T(8,128)(2,1)S(1)} collective-permute-done((bf16[64,512]{1,0:T(8,128)(2,1)S(1)}, bf16[64,512]{1,0:T(8,128)(2,1)S(1)}, u32[]{:S(2)}, u32[]{:S(2)}) %collective-permute-start.2) | collective-permute-done | bytes 65568 | tf_op jit(solution)/shard_map/ppermute | solution.py:480
  44.4 2.5 %collective-permute-start.5 = (bf16[64,4096]{1,0:T(8,128)(2,1)S(1)}, bf16[64,4096]{1,0:T(8,128)(2,1)S(1)}, u32[]{:S(2)}, u32[]{:S(2)}) collective-permute-start(bf16[64,4096]{1,0:T(8,128)(2,1)S(1)} %collective-permute-done.refs_2_), channel_id=1, source_target_pairs={{0,4},{4,0},{8,12},{12,8},{1,5},{5,1},{9,13},{13,9},{2,6},{6,2},{1... | collective-permute-start | bytes 1572872 | tf_op jit(solution)/shard_map/ppermute | solution.py:480
  46.9 18.5 %collective-permute-done.6.z2 = bf16[512,512]{1,0:T(8,128)(2,1)S(1)} collective-permute-done((bf16[512,512]{1,0:T(8,128)(2,1)S(1)}, bf16[512,512]{1,0:T(8,128)(2,1)S(1)}, u32[]{:S(2)}, u32[]{:S(2)}) %collective-permute-start.6) | collective-permute-done | bytes 524320 | tf_op jit(solution)/shard_map/ppermute | solution.py:480
  65.4 2.5 %collective-permute-done.5.refs_3_ = bf16[64,4096]{1,0:T(8,128)(2,1)S(1)} collective-permute-done((bf16[64,4096]{1,0:T(8,128)(2,1)S(1)}, bf16[64,4096]{1,0:T(8,128)(2,1)S(1)}, u32[]{:S(2)}, u32[]{:S(2)}) %collective-permute-start.5) | collective-permute-done | bytes 524320 | tf_op jit(solution)/shard_map/ppermute | solution.py:480
  70.6 14.0 %collective-permute-done.9.refs_3_ = bf16[512,512]{1,0:T(8,128)(2,1)S(1)} collective-permute-done((bf16[512,512]{1,0:T(8,128)(2,1)S(1)}, bf16[512,512]{1,0:T(8,128)(2,1)S(1)}, u32[]{:S(2)}, u32[]{:S(2)}) %collective-permute-start.9) | collective-permute-done | bytes 524320 | tf_op jit(solution)/shard_map/ppermute | solution.py:480
  84.6 7.3 %collective-permute-done.11.refs_1_ = bf16[64,4096]{1,0:T(8,128)(2,1)S(1)} collective-permute-done((bf16[64,4096]{1,0:T(8,128)(2,1)S(1)}, bf16[64,4096]{1,0:T(8,128)(2,1)S(1)}, u32[]{:S(2)}, u32[]{:S(2)}) %collective-permute-start.11) | collective-permute-done | bytes 524320 | tf_op jit(solution)/shard_map/ppermute | solution.py:480
  95.7 11.3 %collective-permute-done.13.refs_4_ = bf16[64,4096]{1,0:T(8,128)(2,1)S(1)} collective-permute-done((bf16[64,4096]{1,0:T(8,128)(2,1)S(1)}, bf16[64,4096]{1,0:T(8,128)(2,1)S(1)}, u32[]{:S(2)}, u32[]{:S(2)}) %collective-permute-start.13) | collective-permute-done | bytes 524320 | tf_op jit(solution)/shard_map/ppermute | solution.py:483
  106.9 4.4 %early.1 = (f32[2,512,512]{2,1,0:T(8,128)S(1)}, bf16[512,1024]{1,0:T(8,128)(2,1)S(1)}) custom-call(bf16[4,64,4096]{2,1,0:T(8,128)(2,1)S(1)} %copy-done, bf16[64,4096]{1,0:T(8,128)(2,1)S(1)} %collective-permute-done.11.refs_1_, bf16[64,4096]{1,0:T(8,128)(2,1)S(1)} %collective-permute-done.refs_2_, bf16[64,4096]{1,0:T(8,128)(2,1)S(1)} %collective-permute-done.5.refs_3_, ...), custom_call_target="tpu_custom_call" | custom-call | flops 1 | bytes 1 | tf_op jit(solution)/shard_map/early/pallas_call | solution.py:296
  111.4 1.9 collective-permute-done.17.refs_7_
  113.3 11.3 %attend.1 = (bf16[2,2,64,256]{3,2,1,0:T(8,128)(2,1)S(1)}, bf16[2,2,64,256]{3,2,1,0:T(8,128)(2,1)S(1)}, f32[4,2,64,1024]{3,2,1,0:T(8,128)S(1)}, bf16[2,64,1024]{2...) custom-call(s32[4]{0:T(128)S(1)} %copy-done.8, ...), custom_call_target="tpu_custom_call" | custom-call | flops 6000000000 | bytes 25165824 | tf_op jit(solution)/shard_map/attend/pallas_call | solution.py:415
  127.7 5.2 %collective-permute-done.18 = bf16[2,64,1024]{2,1,0:T(8,128)(2,1)S(1)} collective-permute-done((bf16[2,64,1024]{2,1,0:T(8,128)(2,1)S(1)}, bf16[2,64,1024]{2,1,0:T(8,128)(2,1)S(1)}, u32[]{:S(2)}, u32[]{:S(2)}) %collective-permute-start.18) | collective-permute-done | bytes 262176 | tf_op jit(solution)/shard_map/ppermute | solution.py:483
  133.0 1.9 collective-permute-start.21
  135.4 4.2 %collective-permute-done.23 = bf16[2,64,1024]{2,1,0:T(8,128)(2,1)S(1)} collective-permute-done((bf16[2,64,1024]{2,1,0:T(8,128)(2,1)S(1)}, bf16[2,64,1024]{2,1,0:T(8,128)(2,1)S(1)}, u32[]{:S(2)}, u32[]{:S(2)}) %collective-permute-start.23) | collective-permute-done | bytes 262176 | tf_op jit(solution)/shard_map/ppermute | solution.py:483
  141.5 2.7 %collective-permute-done.21 = bf16[2,64,1024]{2,1,0:T(8,128)(2,1)S(1)} collective-permute-done((bf16[2,64,1024]{2,1,0:T(8,128)(2,1)S(1)}, bf16[2,64,1024]{2,1,0:T(8,128)(2,1)S(1)}, u32[]{:S(2)}, u32[]{:S(2)}) %collective-permute-start.21) | collective-permute-done | bytes 262176 | tf_op jit(solution)/shard_map/ppermute | solution.py:483
  149.0 1.8 collective-permute-done.25
  152.7 9.3 %collective-permute-done.22.near = bf16[2,2,64,1024]{3,2,1,0:T(8,128)(2,1)S(1)} collective-permute-done((bf16[2,2,64,1024]{3,2,1,0:T(8,128)(2,1)S(1)}, bf16[2,2,64,1024]{3,2,1,0:T(8,128)(2,1)S(1)}, u32[]{:S(2)}, u32[]{:S(2)}) %collective-permute-start.22) | collective-permute-done | bytes 524320 | tf_op jit(solution)/shard_map/ppermute | solution.py:483
  163.6 4.0 %all-to-all-start = ((bf16[4,2,2,2,16,256]{5,4,1,3,2,0:T(8,128)(2,1)}), bf16[4,2,2,2,16,256]{5,4,1,3,2,0:T(8,128)(2,1)}, u32[]{:S(2)}, u32[]{:S(2)}) async-start(bf16[4,2,2,2,16,256]{5,4,1,3,2,0:T(8,128)(2,1)} %copy_bitcast_fusion), calls=%async_computation | async-start | bytes 524288 | tf_op jit(solution)/shard_map/all_to_all | solution.py:533
  167.7 2.0 %collective-permute-start.30 = (bf16[2,64,1024]{2,1,0:T(8,128)(2,1)}, bf16[2,64,1024]{2,1,0:T(8,128)(2,1)}, u32[]{:S(2)}, u32[]{:S(2)}) collective-permute-start(bf16[2,64,1024]{2,1,0:T(8,128)(2,1)} %fusion.6), channel_id=1, source_target_pairs={{0,4},{4,0},{8,12},{12,8},{1,5},{5,1},{9,13},{13,9},{2,6},{6,2},{1... | collective-permute-start | bytes 786440 | tf_op jit(solution)/shard_map/ppermute | solution.py:480
  169.6 6.9 %collective-permute-done.28.near2 = bf16[2,64,1024]{2,1,0:T(8,128)(2,1)} collective-permute-done((bf16[2,64,1024]{2,1,0:T(8,128)(2,1)}, bf16[2,64,1024]{2,1,0:T(8,128)(2,1)}, u32[]{:S(2)}, u32[]{:S(2)}) %collective-permute-start.28) | collective-permute-done | bytes 262176 | tf_op jit(solution)/shard_map/ppermute | solution.py:480
  181.7 2.4 %collective-permute-done.30.near1 = bf16[2,64,1024]{2,1,0:T(8,128)(2,1)} collective-permute-done((bf16[2,64,1024]{2,1,0:T(8,128)(2,1)}, bf16[2,64,1024]{2,1,0:T(8,128)(2,1)}, u32[]{:S(2)}, u32[]{:S(2)}) %collective-permute-start.30) | collective-permute-done | bytes 262176 | tf_op jit(solution)/shard_map/ppermute | solution.py:480
  184.1 5.5 %collective-permute-done.31.far1 = bf16[2,64,1024]{2,1,0:T(8,128)(2,1)} collective-permute-done((bf16[2,64,1024]{2,1,0:T(8,128)(2,1)}, bf16[2,64,1024]{2,1,0:T(8,128)(2,1)}, u32[]{:S(2)}, u32[]{:S(2)}) %collective-permute-start.31) | collective-permute-done | bytes 262176 | tf_op jit(solution)/shard_map/ppermute | solution.py:480
  190.7 2.3 %final.1 = bf16[4,64,1024]{2,1,0:T(8,128)(2,1)} custom-call(f32[4,2,64,1024]{3,2,1,0:T(8,128)S(1)} %get-tuple-element.115.own, bf16[4,2,64,1024]{3,2,1,0:T(8,128)(2,1)S(1)} %collective-permute-done.19.core, bf16[2,2,64,1024]{3,2,1,0:T(8,128)(2,1)S(1)} %copy-done.4, bf16[2,2,64,1024]{3,2,1,0:T(8,128)(2,1)} %collective-permute-done.27.far, ...), custom_call_target="tpu_custom_call" | custom-call | tf_op jit(solution)/shard_map/final/pallas_call | solution.py:454
  (77 shorter events, 40.7 us)
Async XLA Ops:
  1.7 39.1 %collective-permute-start = (bf16[64,4096]{1,0:T(8,128)(2,1)S(1)}, bf16[64,4096]{1,0:T(8,128)(2,1)S(1)}, u32[]{:S(2)}, u32[]{:S(2)}) collective-permute-start(bf16[64,4096]{1,0:T(8,128)(2,1)S(1)} %dynamic-slice_bitcast_fusion), channel_id=1, source_target_pairs={{0,8},{4,12},{8,0},{12,4},{1,9},{5,13},{9,1},{13,5},{2,10},{6,14},... | collective-permute-start | bytes 1572872 | tf_op jit(solution)/shard_map/ppermute | solution.py:480
  13.1 27.8 %collective-permute-start.1 = (bf16[512,512]{1,0:T(8,128)(2,1)S(1)}, bf16[512,512]{1,0:T(8,128)(2,1)S(1)}, u32[]{:S(2)}, u32[]{:S(2)}) collective-permute-start(bf16[512,512]{1,0:T(8,128)(2,1)S(1)} %get-tuple-element.67), channel_id=1, source_target_pairs={{0,4},{4,0},{8,12},{12,8},{1,5},{5,1},{9,13},{13,9},{2,6},{6,2},{1... | collective-permute-start | bytes 1572872 | tf_op jit(solution)/shard_map/ppermute | solution.py:480
  14.7 26.1 %collective-permute-start.2 = (bf16[64,512]{1,0:T(8,128)(2,1)S(1)}, bf16[64,512]{1,0:T(8,128)(2,1)S(1)}, u32[]{:S(2)}, u32[]{:S(2)}) collective-permute-start(bf16[64,512]{1,0:T(8,128)(2,1)S(1)} %get-tuple-element.68), channel_id=1, source_target_pairs={{0,4},{4,0},{8,12},{12,8},{1,5},{5,1},{9,13},{13,9},{2,6},{6,2},{1... | collective-permute-start | bytes 196616 | tf_op jit(solution)/shard_map/ppermute | solution.py:480
  15.2 25.6 %collective-permute-start.3 = (bf16[64,512]{1,0:T(8,128)(2,1)S(1)}, bf16[64,512]{1,0:T(8,128)(2,1)S(1)}, u32[]{:S(2)}, u32[]{:S(2)}) collective-permute-start(bf16[64,512]{1,0:T(8,128)(2,1)S(1)} %get-tuple-element.69), channel_id=1, source_target_pairs={{0,8},{4,12},{8,0},{12,4},{1,9},{5,13},{9,1},{13,5},{2,10},{6,14},... | collective-permute-start | bytes 196616 | tf_op jit(solution)/shard_map/ppermute | solution.py:480
  15.2 25.6 %collective-permute-start.4 = (bf16[64,512]{1,0:T(8,128)(2,1)S(1)}, bf16[64,512]{1,0:T(8,128)(2,1)S(1)}, u32[]{:S(2)}, u32[]{:S(2)}) collective-permute-start(bf16[64,512]{1,0:T(8,128)(2,1)S(1)} %get-tuple-element.70), channel_id=1, source_target_pairs={{0,12},{4,8},{8,4},{12,0},{1,13},{5,9},{9,5},{13,1},{2,14},{6,10},... | collective-permute-start | bytes 196616 | tf_op jit(solution)/shard_map/ppermute | solution.py:480
  40.8 24.6 %collective-permute-start.6 = (bf16[512,512]{1,0:T(8,128)(2,1)S(1)}, bf16[512,512]{1,0:T(8,128)(2,1)S(1)}, u32[]{:S(2)}, u32[]{:S(2)}) collective-permute-start(bf16[512,512]{1,0:T(8,128)(2,1)S(1)} %get-tuple-element.73), channel_id=1, source_target_pairs={{0,8},{4,12},{8,0},{12,4},{1,9},{5,13},{9,1},{13,5},{2,10},{6,14},... | collective-permute-start | bytes 1572872 | tf_op jit(solution)/shard_map/ppermute | solution.py:480
  41.4 24.0 %collective-permute-start.8 = (bf16[512,512]{1,0:T(8,128)(2,1)S(1)}, bf16[512,512]{1,0:T(8,128)(2,1)S(1)}, u32[]{:S(2)}, u32[]{:S(2)}) collective-permute-start(bf16[512,512]{1,0:T(8,128)(2,1)S(1)} %collective-permute-done.1.z1), channel_id=1, source_target_pairs={{0,16},{16,0},{1,17},{17,1},{2,18},{18,2},{3,19},{19,3},{4,20},{20... | collective-permute-start | bytes 1572872 | tf_op jit(solution)/shard_map/ppermute | solution.py:486
  42.9 22.5 %collective-permute-start.7 = (bf16[64,4096]{1,0:T(8,128)(2,1)S(1)}, bf16[64,4096]{1,0:T(8,128)(2,1)S(1)}, u32[]{:S(2)}, u32[]{:S(2)}) collective-permute-start(bf16[64,4096]{1,0:T(8,128)(2,1)S(1)} %collective-permute-done.refs_2_), channel_id=1, source_target_pairs={{0,2},{1,3},{2,0},{3,1},{4,6},{5,7},{6,4},{7,5},{8,10},{9,11},{10,... | collective-permute-start | bytes 1572872 | tf_op jit(solution)/shard_map/ppermute | solution.py:483
  44.4 23.5 %collective-permute-start.5 = (bf16[64,4096]{1,0:T(8,128)(2,1)S(1)}, bf16[64,4096]{1,0:T(8,128)(2,1)S(1)}, u32[]{:S(2)}, u32[]{:S(2)}) collective-permute-start(bf16[64,4096]{1,0:T(8,128)(2,1)S(1)} %collective-permute-done.refs_2_), channel_id=1, source_target_pairs={{0,4},{4,0},{8,12},{12,8},{1,5},{5,1},{9,13},{13,9},{2,6},{6,2},{1... | collective-permute-start | bytes 1572872 | tf_op jit(solution)/shard_map/ppermute | solution.py:480
  67.9 16.7 %collective-permute-start.9 = (bf16[512,512]{1,0:T(8,128)(2,1)S(1)}, bf16[512,512]{1,0:T(8,128)(2,1)S(1)}, u32[]{:S(2)}, u32[]{:S(2)}) collective-permute-start(bf16[512,512]{1,0:T(8,128)(2,1)S(1)} %get-tuple-element.77), channel_id=1, source_target_pairs={{0,12},{4,8},{8,4},{12,0},{1,13},{5,9},{9,5},{13,1},{2,14},{6,10},... | collective-permute-start | bytes 1572872 | tf_op jit(solution)/shard_map/ppermute | solution.py:480
  69.4 22.4 %collective-permute-start.11 = (bf16[64,4096]{1,0:T(8,128)(2,1)S(1)}, bf16[64,4096]{1,0:T(8,128)(2,1)S(1)}, u32[]{:S(2)}, u32[]{:S(2)}) collective-permute-start(bf16[64,4096]{1,0:T(8,128)(2,1)S(1)} %dynamic-slice_bitcast_fusion), channel_id=1, source_target_pairs={{0,4},{4,0},{8,12},{12,8},{1,5},{5,1},{9,13},{13,9},{2,6},{6,2},{1... | collective-permute-start | bytes 1572872 | tf_op jit(solution)/shard_map/ppermute | solution.py:480
  69.4 22.4 %collective-permute-start.10 = (bf16[64,4096]{1,0:T(8,128)(2,1)S(1)}, bf16[64,4096]{1,0:T(8,128)(2,1)S(1)}, u32[]{:S(2)}, u32[]{:S(2)}) collective-permute-start(bf16[64,4096]{1,0:T(8,128)(2,1)S(1)} %collective-permute-done.5.refs_3_), channel_id=1, source_target_pairs={{0,2},{1,3},{2,0},{3,1},{4,6},{5,7},{6,4},{7,5},{8,10},{9,11},{10,... | collective-permute-start | bytes 1572872 | tf_op jit(solution)/shard_map/ppermute | solution.py:483
  70.0 21.8 %collective-permute-start.14 = (bf16[512,512]{1,0:T(8,128)(2,1)S(1)}, bf16[512,512]{1,0:T(8,128)(2,1)S(1)}, u32[]{:S(2)}, u32[]{:S(2)}) collective-permute-start(bf16[512,512]{1,0:T(8,128)(2,1)S(1)} %collective-permute-done.6.z2), channel_id=1, source_target_pairs={{0,16},{16,0},{1,17},{17,1},{2,18},{18,2},{3,19},{19,3},{4,20},{20... | collective-permute-start | bytes 1572872 | tf_op jit(solution)/shard_map/ppermute | solution.py:486
  92.5 14.4 %collective-permute-start.15 = (bf16[3328,512]{1,0:T(8,128)(2,1)S(1)}, bf16[3328,512]{1,0:T(8,128)(2,1)S(1)}, u32[]{:S(2)}, u32[]{:S(2)}) collective-permute-start(bf16[3328,512]{1,0:T(8,128)(2,1)S(1)} %pack.1.refs_7_.refs_2_), channel_id=1, source_target_pairs={{0,1},{1,0},{2,3},{3,2},{4,5},{5,4},{6,7},{7,6},{8,9},{9,8},{10,11... | collective-permute-start | bytes 10223624 | tf_op jit(solution)/shard_map/ppermute | solution.py:483
  92.6 14.3 %collective-permute-start.13 = (bf16[64,4096]{1,0:T(8,128)(2,1)S(1)}, bf16[64,4096]{1,0:T(8,128)(2,1)S(1)}, u32[]{:S(2)}, u32[]{:S(2)}) collective-permute-start(bf16[64,4096]{1,0:T(8,128)(2,1)S(1)} %collective-permute-done.11.refs_1_), channel_id=1, source_target_pairs={{0,2},{1,3},{2,0},{3,1},{4,6},{5,7},{6,4},{7,5},{8,10},{9,11},{10,... | collective-permute-start | bytes 1572872 | tf_op jit(solution)/shard_map/ppermute | solution.py:483
  94.2 17.2 %collective-permute-start.12 = (bf16[512,512]{1,0:T(8,128)(2,1)S(1)}, bf16[512,512]{1,0:T(8,128)(2,1)S(1)}, u32[]{:S(2)}, u32[]{:S(2)}) collective-permute-start(bf16[512,512]{1,0:T(8,128)(2,1)S(1)} %collective-permute-done.9.refs_3_), channel_id=1, source_target_pairs={{0,16},{16,0},{1,17},{17,1},{2,18},{18,2},{3,19},{19,3},{4,20},{20... | collective-permute-start | bytes 1572872 | tf_op jit(solution)/shard_map/ppermute | solution.py:486
  95.7 15.8 %collective-permute-start.16 = (bf16[512,512]{1,0:T(8,128)(2,1)S(1)}, bf16[512,512]{1,0:T(8,128)(2,1)S(1)}, u32[]{:S(2)}, u32[]{:S(2)}) collective-permute-start(bf16[512,512]{1,0:T(8,128)(2,1)S(1)} %collective-permute-done.9.refs_3_), channel_id=1, source_target_pairs={{0,1},{1,0},{2,3},{3,2},{4,5},{5,4},{6,7},{7,6},{8,9},{9,8},{10,11... | collective-permute-start | bytes 1572872 | tf_op jit(solution)/shard_map/ppermute | solution.py:483
  126.5 13.0 %collective-permute-start.23 = (bf16[2,64,1024]{2,1,0:T(8,128)(2,1)S(1)}, bf16[2,64,1024]{2,1,0:T(8,128)(2,1)S(1)}, u32[]{:S(2)}, u32[]{:S(2)}) collective-permute-start(bf16[2,64,1024]{2,1,0:T(8,128)(2,1)S(1)} %get-tuple-element.111), channel_id=1, source_target_pairs={{0,2},{1,3},{2,0},{3,1},{4,6},{5,7},{6,4},{7,5},{8,10},{9,11},{10,... | collective-permute-start | bytes 786440 | tf_op jit(solution)/shard_map/ppermute | solution.py:483
  144.2 17.8 %collective-permute-start.22 = (bf16[2,2,64,1024]{3,2,1,0:T(8,128)(2,1)S(1)}, bf16[2,2,64,1024]{3,2,1,0:T(8,128)(2,1)S(1)}, u32[]{:S(2)}, u32[]{:S(2)}) collective-permute-start(bf16[2,2,64,1024]{3,2,1,0:T(8,128)(2,1)S(1)} %get-tuple-element.106), channel_id=1, source_target_pairs={{0,2},{1,3},{2,0},{3,1},{4,6},{5,7},{6,4},{7,5},{8,10},{9,11},{10,... | collective-permute-start | bytes 1572872 | tf_op jit(solution)/shard_map/ppermute | solution.py:483
  147.3 22.3 %collective-permute-start.29 = (bf16[2,64,1024]{2,1,0:T(8,128)(2,1)}, bf16[2,64,1024]{2,1,0:T(8,128)(2,1)S(1)}, u32[]{:S(2)}, u32[]{:S(2)}) collective-permute-start(bf16[2,64,1024]{2,1,0:T(8,128)(2,1)} %fusion.1), channel_id=1, source_target_pairs={{0,8},{4,12},{8,0},{12,4},{1,9},{5,13},{9,1},{13,5},{2,10},{6,14},... | collective-permute-start | bytes 786440 | tf_op jit(solution)/shard_map/ppermute | solution.py:480
  148.4 28.1 %collective-permute-start.27 = (bf16[2,2,64,1024]{3,2,1,0:T(8,128)(2,1)}, bf16[2,2,64,1024]{3,2,1,0:T(8,128)(2,1)}, u32[]{:S(2)}, u32[]{:S(2)}) collective-permute-start(bf16[2,2,64,1024]{3,2,1,0:T(8,128)(2,1)} %get-tuple-element.124), channel_id=1, source_target_pairs={{0,3},{1,2},{2,1},{3,0},{4,7},{5,6},{6,5},{7,4},{8,11},{9,10},{10,... | collective-permute-start | bytes 1572872 | tf_op jit(solution)/shard_map/ppermute | solution.py:483
  151.6 24.9 %collective-permute-start.28 = (bf16[2,64,1024]{2,1,0:T(8,128)(2,1)}, bf16[2,64,1024]{2,1,0:T(8,128)(2,1)}, u32[]{:S(2)}, u32[]{:S(2)}) collective-permute-start(bf16[2,64,1024]{2,1,0:T(8,128)(2,1)} %fusion.4), channel_id=1, source_target_pairs={{0,8},{4,12},{8,0},{12,4},{1,9},{5,13},{9,1},{13,5},{2,10},{6,14},... | collective-permute-start | bytes 786440 | tf_op jit(solution)/shard_map/ppermute | solution.py:480
  163.6 16.3 %all-to-all-start = ((bf16[4,2,2,2,16,256]{5,4,1,3,2,0:T(8,128)(2,1)}), bf16[4,2,2,2,16,256]{5,4,1,3,2,0:T(8,128)(2,1)}, u32[]{:S(2)}, u32[]{:S(2)}) async-start(bf16[4,2,2,2,16,256]{5,4,1,3,2,0:T(8,128)(2,1)} %copy_bitcast_fusion), calls=%async_computation | async-start | bytes 524288 | tf_op jit(solution)/shard_map/all_to_all | solution.py:533
  167.7 16.4 %collective-permute-start.30 = (bf16[2,64,1024]{2,1,0:T(8,128)(2,1)}, bf16[2,64,1024]{2,1,0:T(8,128)(2,1)}, u32[]{:S(2)}, u32[]{:S(2)}) collective-permute-start(bf16[2,64,1024]{2,1,0:T(8,128)(2,1)} %fusion.6), channel_id=1, source_target_pairs={{0,4},{4,0},{8,12},{12,8},{1,5},{5,1},{9,13},{13,9},{2,6},{6,2},{1... | collective-permute-start | bytes 786440 | tf_op jit(solution)/shard_map/ppermute | solution.py:480
  (18 other events, 117.7 us)

commit v10 on v8

--- a/solution.py
+++ b/solution.py
@@ -518,8 +518,10 @@
     from_core = flip(to_core, 1)
     front = jnp.stack([att, qgrad], axis=1)
     other = flip(front[1], 1)
+    back = jnp.stack([front[0], other]).reshape(2, 2, 2, SEQ, 16, 256).transpose(3, 0, 1, 2, 4, 5)
     b3, a3 = flip(b3, 3), flip(a3, 2)
-    b3, core, other, b2, a2 = together(b3, from_core, other, b2, a2)
+    b3, core, b2, a2, back = together(b3, from_core, b2, a2, back)
+    back = lax.all_to_all(back, "seq", split_axis=0, concat_axis=0, tiled=True)
     b2, a2 = flip(b2, 3), flip(a2, 2)
     far3, own = together(summed(core[3], b3), own)
     far3 = along(far3, 1)
@@ -527,17 +529,16 @@
     near3 = along(near3, 1)
     b2, b10, a10 = together(b2, b10, a10)
     b10, a10 = flip(b10, 3), flip(a10, 2)
+    core, back = together(core, back)
     far2, own = together(summed(core[2], b2, far3), own)
     far2 = along(far2, 2)
     near2, core = together(summed(own[2], a2, near3), core)
     near2 = along(near2, 2)
-    back = jnp.stack([front[0], other]).reshape(2, 2, 2, SEQ, 16, 256).transpose(3, 0, 1, 2, 4, 5)
-    near1, core, back = together(summed(own[1], a10[0]), core, back)
+    near1, core = together(summed(own[1], a10[0]), core)
     near1 = along(near1, 1)
     b10, near2, far2 = together(b10, near2, far2)
     far1 = along(summed(core[1], b10[0]), 1)
     from_core = core
-    back = lax.all_to_all(back, "seq", split_axis=0, concat_axis=0, tiled=True)
     back = back.transpose(2, 3, 1, 4, 0, 5).reshape(2, 2, 2, 16, 1024)
     back = jnp.where(c == 0, back, back[:, :, ::-1])
     back = back.reshape(2, DOCS, 16, 1024)

time: 191 us -> 190 us (level)
  waiting for transfers between devices: 116 us -> 107 us
  other arithmetic: 5.11 us -> 9.95 us
  starting transfers between devices: 37.9 us -> 41.1 us
    ppermute x14, waiting for transfers between devices: 49 us -> 31.9 us  [flip(): return lax.ppermute(value, 'head', [(a, a ^ bits) for a in range(4)])]
    ppermute x15, waiting for transfers between devices: 54 us -> 63.6 us  [along(): return lax.ppermute(value, 'seq', [(a, a ^ k) for a in range(SEQ)])]
    convert_element_type x6, other arithmetic: 4.28 us -> 9.13 us  [summed(): return total.astype(BF)]
    ppermute x15, starting transfers between devices: 17.2 us -> 21.3 us  [along(): return lax.ppermute(value, 'seq', [(a, a ^ k) for a in range(SEQ)])]
    unnamed x18 -> x22, local copies, waits for them, and re-layouts: 7.58 us -> 7.1 us
  transfers between devices with their start and end apart: 33 -> 33, of which waited for: 22 -> 21; matrix products, arithmetic and copies ran while one was open for 4% -> 6% of each run, Pallas kernels for 3% -> 3%
where the time goes in v10:
time: 190 us; the launch traced here: 189 us
  waiting for transfers between devices  107 us (56%)
  starting transfers between devices  41.1 us (22%)
  Pallas kernels  20.2 us (11%)
  other arithmetic  9.95 us (5%)
  local copies, waits for them, and re-layouts  9.87 us (5%)
    ppermute x15, waiting for transfers between devices, along(): return lax.ppermute(value, 'seq', [(a, a ^ k) for a in range(SEQ)])  63.6 us
    ppermute x14, waiting for transfers between devices, flip(): return lax.ppermute(value, 'head', [(a, a ^ bits) for a in range(4)])  31.9 us
    ppermute x15, starting transfers between devices, along(): return lax.ppermute(value, 'seq', [(a, a ^ k) for a in range(SEQ)])  21.3 us
    ppermute x3, waiting for transfers between devices, across(): return lax.ppermute(value, 'grp', [(0, 1), (1, 0)])  11.6 us
    pallas_call x1, Pallas kernels, main_call(): pl.pallas_call(main_kernel, out_shape=[front, front, jax.ShapeDtypeStruct...  11.3 us
    ppermute x14, starting transfers between devices, flip(): return lax.ppermute(value, 'head', [(a, a ^ bits) for a in range(4)])  11 us
    convert_element_type x6, other arithmetic, summed(): return total.astype(BF)  9.13 us
    unnamed x22, local copies, waits for them, and re-layouts  7.1 us
  transfers between devices with their start and end apart: 33, of which 21 were waited for; matrix products, arithmetic and copies ran while one was open for 6% of the time, Pallas kernels for 3%

profile of v10, /device:TPU:0, one launch (start us, length us, event | category | flops | bytes accessed | tf_op | source)
XLA Modules:
  0.0 188.9 jit_solution(4572508427467430614)
XLA Ops:
  1.7 4.1 %collective-permute-start.1 = (bf16[64,4096]{1,0:T(8,128)(2,1)S(1)}, bf16[64,4096]{1,0:T(8,128)(2,1)S(1)}, u32[]{:S(2)}, u32[]{:S(2)}) collective-permute-start(bf16[64,4096]{1,0:T(8,128)(2,1)S(1)} %dynamic-slice_bitcast_fusion), channel_id=1, source_target_pairs={{0,8},{4,12},{8,0},{12,4},{1,9},{5,13},{9,1},{13,5},{2,10},{6,14},... | collective-permute-start | bytes 1572872 | tf_op jit(solution)/shard_map/ppermute | solution.py:480
  15.2 3.9 %collective-permute-start.4 = (bf16[64,512]{1,0:T(8,128)(2,1)S(1)}, bf16[64,512]{1,0:T(8,128)(2,1)S(1)}, u32[]{:S(2)}, u32[]{:S(2)}) collective-permute-start(bf16[64,512]{1,0:T(8,128)(2,1)S(1)} %get-tuple-element.74), channel_id=1, source_target_pairs={{0,12},{4,8},{8,4},{12,0},{1,13},{5,9},{9,5},{13,1},{2,14},{6,10},... | collective-permute-start | bytes 196616 | tf_op jit(solution)/shard_map/ppermute | solution.py:480
  19.1 13.3 %collective-permute-done.2.q1 = bf16[64,512]{1,0:T(8,128)(2,1)S(1)} collective-permute-done((bf16[64,512]{1,0:T(8,128)(2,1)S(1)}, bf16[64,512]{1,0:T(8,128)(2,1)S(1)}, u32[]{:S(2)}, u32[]{:S(2)}) %collective-permute-start.2) | collective-permute-done | bytes 65568 | tf_op jit(solution)/shard_map/ppermute | solution.py:480
  32.4 2.0 %collective-permute-done.4.q3 = bf16[64,512]{1,0:T(8,128)(2,1)S(1)} collective-permute-done((bf16[64,512]{1,0:T(8,128)(2,1)S(1)}, bf16[64,512]{1,0:T(8,128)(2,1)S(1)}, u32[]{:S(2)}, u32[]{:S(2)}) %collective-permute-start.4) | collective-permute-done | bytes 65568 | tf_op jit(solution)/shard_map/ppermute | solution.py:480
  36.4 2.9 %collective-permute-start.11 = (bf16[512,512]{1,0:T(8,128)(2,1)S(1)}, bf16[512,512]{1,0:T(8,128)(2,1)S(1)}, u32[]{:S(2)}, u32[]{:S(2)}) collective-permute-start(bf16[512,512]{1,0:T(8,128)(2,1)S(1)} %get-tuple-element.84), channel_id=1, source_target_pairs={{0,8},{4,12},{8,0},{12,4},{1,9},{5,13},{9,1},{13,5},{2,10},{6,14},... | collective-permute-start | bytes 1572872 | tf_op jit(solution)/shard_map/ppermute | solution.py:480
  41.3 7.9 %collective-permute-done.5.refs_4_ = bf16[64,4096]{1,0:T(8,128)(2,1)S(1)} collective-permute-done((bf16[64,4096]{1,0:T(8,128)(2,1)S(1)}, bf16[64,4096]{1,0:T(8,128)(2,1)S(1)}, u32[]{:S(2)}, u32[]{:S(2)}) %collective-permute-start.5) | collective-permute-done | bytes 524320 | tf_op jit(solution)/shard_map/ppermute | solution.py:483
  49.3 8.9 %collective-permute-done.6.refs_5_ = bf16[64,4096]{1,0:T(8,128)(2,1)S(1)} collective-permute-done((bf16[64,4096]{1,0:T(8,128)(2,1)S(1)}, bf16[64,4096]{1,0:T(8,128)(2,1)S(1)}, u32[]{:S(2)}, u32[]{:S(2)}) %collective-permute-start.6) | collective-permute-done | bytes 524320 | tf_op jit(solution)/shard_map/ppermute | solution.py:483
  58.2 4.0 %collective-permute-done.11.z2 = bf16[512,512]{1,0:T(8,128)(2,1)S(1)} collective-permute-done((bf16[512,512]{1,0:T(8,128)(2,1)S(1)}, bf16[512,512]{1,0:T(8,128)(2,1)S(1)}, u32[]{:S(2)}, u32[]{:S(2)}) %collective-permute-start.11) | collective-permute-done | bytes 524320 | tf_op jit(solution)/shard_map/ppermute | solution.py:480
  66.6 19.1 %collective-permute-done.13.z1 = bf16[512,512]{1,0:T(8,128)(2,1)S(1)} collective-permute-done((bf16[512,512]{1,0:T(8,128)(2,1)S(1)}, bf16[512,512]{1,0:T(8,128)(2,1)S(1)}, u32[]{:S(2)}, u32[]{:S(2)}) %collective-permute-start.13) | collective-permute-done | bytes 524320 | tf_op jit(solution)/shard_map/ppermute | solution.py:480
  87.3 7.7 %collective-permute-done.14.y1 = bf16[512,512]{1,0:T(8,128)(2,1)S(1)} collective-permute-done((bf16[512,512]{1,0:T(8,128)(2,1)S(1)}, bf16[512,512]{1,0:T(8,128)(2,1)S(1)}, u32[]{:S(2)}, u32[]{:S(2)}) %collective-permute-start.14) | collective-permute-done | bytes 524320 | tf_op jit(solution)/shard_map/ppermute | solution.py:486
  97.5 4.3 %collective-permute-done.15.refs_8_.refs_5_ = bf16[3328,512]{1,0:T(8,128)(2,1)S(1)} collective-permute-done((bf16[3328,512]{1,0:T(8,128)(2,1)S(1)}, bf16[3328,512]{1,0:T(8,128)(2,1)S(1)}, u32[]{:S(2)}, u32[]{:S(2)}) %collective-permute-start.15) | collective-permute-done | bytes 3407904 | tf_op jit(solution)/shard_map/ppermute | solution.py:483
  101.7 4.4 %early.1 = (f32[2,512,512]{2,1,0:T(8,128)S(1)}, bf16[512,1024]{1,0:T(8,128)(2,1)S(1)}) custom-call(bf16[4,64,4096]{2,1,0:T(8,128)(2,1)S(1)} %copy-done, bf16[64,4096]{1,0:T(8,128)(2,1)S(1)} %collective-permute-done.refs_1_, bf16[64,4096]{1,0:T(8,128)(2,1)S(1)} %collective-permute-done.1.refs_2_, bf16[64,4096]{1,0:T(8,128)(2,1)S(1)} %collective-permute-done.8.refs_3_, ...), custom_call_target="tpu_custom_call" | custom-call | flops 1 | bytes 1 | tf_op jit(solution)/shard_map/early/pallas_call | solution.py:296
  106.1 3.9 %collective-permute-done.10.refs_4_ = bf16[512,512]{1,0:T(8,128)(2,1)S(1)} collective-permute-done((bf16[512,512]{1,0:T(8,128)(2,1)S(1)}, bf16[512,512]{1,0:T(8,128)(2,1)S(1)}, u32[]{:S(2)}, u32[]{:S(2)}) %collective-permute-start.10) | collective-permute-done | bytes 524320 | tf_op jit(solution)/shard_map/ppermute | solution.py:486
  112.0 11.3 %attend.1 = (bf16[2,2,64,256]{3,2,1,0:T(8,128)(2,1)S(1)}, bf16[2,2,64,256]{3,2,1,0:T(8,128)(2,1)S(1)}, f32[4,2,64,1024]{3,2,1,0:T(8,128)S(1)}, bf16[2,64,1024]{2...) custom-call(s32[4]{0:T(128)S(1)} %copy-done.8, ...), custom_call_target="tpu_custom_call" | custom-call | flops 6000000000 | bytes 25165824 | tf_op jit(solution)/shard_map/attend/pallas_call | solution.py:415
  127.1 4.5 %collective-permute-done.18 = bf16[2,64,1024]{2,1,0:T(8,128)(2,1)S(1)} collective-permute-done((bf16[2,64,1024]{2,1,0:T(8,128)(2,1)S(1)}, bf16[2,64,1024]{2,1,0:T(8,128)(2,1)S(1)}, u32[]{:S(2)}, u32[]{:S(2)}) %collective-permute-start.18) | collective-permute-done | bytes 262176 | tf_op jit(solution)/shard_map/ppermute | solution.py:483
  132.3 4.0 %all-to-all-start = ((bf16[4,2,2,2,16,256]{5,4,1,3,2,0:T(8,128)(2,1)}), bf16[4,2,2,2,16,256]{5,4,1,3,2,0:T(8,128)(2,1)}, u32[]{:S(2)}, u32[]{:S(2)}) async-start(bf16[4,2,2,2,16,256]{5,4,1,3,2,0:T(8,128)(2,1)} %copy_bitcast_fusion), calls=%async_computation | async-start | bytes 524288 | tf_op jit(solution)/shard_map/all_to_all | solution.py:524
  136.4 1.9 %collective-permute-start.21 = (bf16[2,64,1024]{2,1,0:T(8,128)(2,1)S(1)}, bf16[2,64,1024]{2,1,0:T(8,128)(2,1)S(1)}, u32[]{:S(2)}, u32[]{:S(2)}) collective-permute-start(bf16[2,64,1024]{2,1,0:T(8,128)(2,1)S(1)} %get-tuple-element.108), channel_id=1, source_target_pairs={{0,3},{1,2},{2,1},{3,0},{4,7},{5,6},{6,5},{7,4},{8,11},{9,10},{10,... | collective-permute-start | bytes 786440 | tf_op jit(solution)/shard_map/ppermute | solution.py:483
  147.4 3.3 %collective-permute-done.24 = bf16[2,64,1024]{2,1,0:T(8,128)(2,1)} collective-permute-done((bf16[2,64,1024]{2,1,0:T(8,128)(2,1)}, bf16[2,64,1024]{2,1,0:T(8,128)(2,1)}, u32[]{:S(2)}, u32[]{:S(2)}) %collective-permute-start.24) | collective-permute-done | bytes 262176 | tf_op jit(solution)/shard_map/ppermute | solution.py:480
  154.4 3.1 %collective-permute-done.26 = bf16[2,64,1024]{2,1,0:T(8,128)(2,1)} collective-permute-done((bf16[2,64,1024]{2,1,0:T(8,128)(2,1)}, bf16[2,64,1024]{2,1,0:T(8,128)(2,1)}, u32[]{:S(2)}, u32[]{:S(2)}) %collective-permute-start.26) | collective-permute-done | bytes 262176 | tf_op jit(solution)/shard_map/ppermute | solution.py:480
  160.9 3.6 %collective-permute-done.22.near = bf16[2,2,64,1024]{3,2,1,0:T(8,128)(2,1)} collective-permute-done((bf16[2,2,64,1024]{3,2,1,0:T(8,128)(2,1)}, bf16[2,2,64,1024]{3,2,1,0:T(8,128)(2,1)}, u32[]{:S(2)}, u32[]{:S(2)}) %collective-permute-start.22) | collective-permute-done | bytes 524320 | tf_op jit(solution)/shard_map/ppermute | solution.py:483
  167.2 6.9 %collective-permute-done.29.far2 = bf16[2,64,1024]{2,1,0:T(8,128)(2,1)S(1)} collective-permute-done((bf16[2,64,1024]{2,1,0:T(8,128)(2,1)}, bf16[2,64,1024]{2,1,0:T(8,128)(2,1)S(1)}, u32[]{:S(2)}, u32[]{:S(2)}) %collective-permute-start.29) | collective-permute-done | bytes 262176 | tf_op jit(solution)/shard_map/ppermute | solution.py:480
  174.2 4.2 %collective-permute-done.28.near2 = bf16[2,64,1024]{2,1,0:T(8,128)(2,1)} collective-permute-done((bf16[2,64,1024]{2,1,0:T(8,128)(2,1)}, bf16[2,64,1024]{2,1,0:T(8,128)(2,1)}, u32[]{:S(2)}, u32[]{:S(2)}) %collective-permute-start.28) | collective-permute-done | bytes 262176 | tf_op jit(solution)/shard_map/ppermute | solution.py:480
  181.3 5.3 %collective-permute-done.31.far1 = bf16[2,64,1024]{2,1,0:T(8,128)(2,1)S(1)} collective-permute-done((bf16[2,64,1024]{2,1,0:T(8,128)(2,1)S(1)}, bf16[2,64,1024]{2,1,0:T(8,128)(2,1)S(1)}, u32[]{:S(2)}, u32[]{:S(2)}) %collective-permute-start.31) | collective-permute-done | bytes 262176 | tf_op jit(solution)/shard_map/ppermute | solution.py:480
  186.6 2.3 %final.1 = bf16[4,64,1024]{2,1,0:T(8,128)(2,1)} custom-call(f32[4,2,64,1024]{3,2,1,0:T(8,128)S(1)} %get-tuple-element.124.own, bf16[4,2,64,1024]{3,2,1,0:T(8,128)(2,1)S(1)} %collective-permute-done.19.core, bf16[2,2,64,1024]{3,2,1,0:T(8,128)(2,1)} %collective-permute-done.22.near, bf16[2,2,64,1024]{3,2,1,0:T(8,128)(2,1)} %collective-permute-done.27.far, ...), custom_call_target="tpu_custom_call" | custom-call | tf_op jit(solution)/shard_map/final/pallas_call | solution.py:454
  (81 shorter events, 51.3 us)
Async XLA Ops:
  1.7 32.7 %collective-permute-start.1 = (bf16[64,4096]{1,0:T(8,128)(2,1)S(1)}, bf16[64,4096]{1,0:T(8,128)(2,1)S(1)}, u32[]{:S(2)}, u32[]{:S(2)}) collective-permute-start(bf16[64,4096]{1,0:T(8,128)(2,1)S(1)} %dynamic-slice_bitcast_fusion), channel_id=1, source_target_pairs={{0,8},{4,12},{8,0},{12,4},{1,9},{5,13},{9,1},{13,5},{2,10},{6,14},... | collective-permute-start | bytes 1572872 | tf_op jit(solution)/shard_map/ppermute | solution.py:480
  5.8 28.6 %collective-permute-start = (bf16[64,4096]{1,0:T(8,128)(2,1)S(1)}, bf16[64,4096]{1,0:T(8,128)(2,1)S(1)}, u32[]{:S(2)}, u32[]{:S(2)}) collective-permute-start(bf16[64,4096]{1,0:T(8,128)(2,1)S(1)} %dynamic-slice_bitcast_fusion), channel_id=1, source_target_pairs={{0,4},{4,0},{8,12},{12,8},{1,5},{5,1},{9,13},{13,9},{2,6},{6,2},{1... | collective-permute-start | bytes 1572872 | tf_op jit(solution)/shard_map/ppermute | solution.py:480
  14.6 17.7 %collective-permute-start.2 = (bf16[64,512]{1,0:T(8,128)(2,1)S(1)}, bf16[64,512]{1,0:T(8,128)(2,1)S(1)}, u32[]{:S(2)}, u32[]{:S(2)}) collective-permute-start(bf16[64,512]{1,0:T(8,128)(2,1)S(1)} %get-tuple-element.72), channel_id=1, source_target_pairs={{0,4},{4,0},{8,12},{12,8},{1,5},{5,1},{9,13},{13,9},{2,6},{6,2},{1... | collective-permute-start | bytes 196616 | tf_op jit(solution)/shard_map/ppermute | solution.py:480
  15.2 17.2 %collective-permute-start.3 = (bf16[64,512]{1,0:T(8,128)(2,1)S(1)}, bf16[64,512]{1,0:T(8,128)(2,1)S(1)}, u32[]{:S(2)}, u32[]{:S(2)}) collective-permute-start(bf16[64,512]{1,0:T(8,128)(2,1)S(1)} %get-tuple-element.73), channel_id=1, source_target_pairs={{0,8},{4,12},{8,0},{12,4},{1,9},{5,13},{9,1},{13,5},{2,10},{6,14},... | collective-permute-start | bytes 196616 | tf_op jit(solution)/shard_map/ppermute | solution.py:480
  15.2 19.2 %collective-permute-start.4 = (bf16[64,512]{1,0:T(8,128)(2,1)S(1)}, bf16[64,512]{1,0:T(8,128)(2,1)S(1)}, u32[]{:S(2)}, u32[]{:S(2)}) collective-permute-start(bf16[64,512]{1,0:T(8,128)(2,1)S(1)} %get-tuple-element.74), channel_id=1, source_target_pairs={{0,12},{4,8},{8,4},{12,0},{1,13},{5,9},{9,5},{13,1},{2,14},{6,10},... | collective-permute-start | bytes 196616 | tf_op jit(solution)/shard_map/ppermute | solution.py:480
  34.4 14.9 %collective-permute-start.5 = (bf16[64,4096]{1,0:T(8,128)(2,1)S(1)}, bf16[64,4096]{1,0:T(8,128)(2,1)S(1)}, u32[]{:S(2)}, u32[]{:S(2)}) collective-permute-start(bf16[64,4096]{1,0:T(8,128)(2,1)S(1)} %collective-permute-done.refs_1_), channel_id=1, source_target_pairs={{0,2},{1,3},{2,0},{3,1},{4,6},{5,7},{6,4},{7,5},{8,10},{9,11},{10,... | collective-permute-start | bytes 1572872 | tf_op jit(solution)/shard_map/ppermute | solution.py:483
  35.9 22.3 %collective-permute-start.6 = (bf16[64,4096]{1,0:T(8,128)(2,1)S(1)}, bf16[64,4096]{1,0:T(8,128)(2,1)S(1)}, u32[]{:S(2)}, u32[]{:S(2)}) collective-permute-start(bf16[64,4096]{1,0:T(8,128)(2,1)S(1)} %collective-permute-done.1.refs_2_), channel_id=1, source_target_pairs={{0,2},{1,3},{2,0},{3,1},{4,6},{5,7},{6,4},{7,5},{8,10},{9,11},{10,... | collective-permute-start | bytes 1572872 | tf_op jit(solution)/shard_map/ppermute | solution.py:483
  36.4 25.8 %collective-permute-start.11 = (bf16[512,512]{1,0:T(8,128)(2,1)S(1)}, bf16[512,512]{1,0:T(8,128)(2,1)S(1)}, u32[]{:S(2)}, u32[]{:S(2)}) collective-permute-start(bf16[512,512]{1,0:T(8,128)(2,1)S(1)} %get-tuple-element.84), channel_id=1, source_target_pairs={{0,8},{4,12},{8,0},{12,4},{1,9},{5,13},{9,1},{13,5},{2,10},{6,14},... | collective-permute-start | bytes 1572872 | tf_op jit(solution)/shard_map/ppermute | solution.py:480
  39.3 25.8 %collective-permute-start.8 = (bf16[64,4096]{1,0:T(8,128)(2,1)S(1)}, bf16[64,4096]{1,0:T(8,128)(2,1)S(1)}, u32[]{:S(2)}, u32[]{:S(2)}) collective-permute-start(bf16[64,4096]{1,0:T(8,128)(2,1)S(1)} %collective-permute-done.1.refs_2_), channel_id=1, source_target_pairs={{0,4},{4,0},{8,12},{12,8},{1,5},{5,1},{9,13},{13,9},{2,6},{6,2},{1... | collective-permute-start | bytes 1572872 | tf_op jit(solution)/shard_map/ppermute | solution.py:480
  39.5 46.3 %collective-permute-start.13 = (bf16[512,512]{1,0:T(8,128)(2,1)S(1)}, bf16[512,512]{1,0:T(8,128)(2,1)S(1)}, u32[]{:S(2)}, u32[]{:S(2)}) collective-permute-start(bf16[512,512]{1,0:T(8,128)(2,1)S(1)} %get-tuple-element.90), channel_id=1, source_target_pairs={{0,4},{4,0},{8,12},{12,8},{1,5},{5,1},{9,13},{13,9},{2,6},{6,2},{1... | collective-permute-start | bytes 1572872 | tf_op jit(solution)/shard_map/ppermute | solution.py:480
  62.2 23.6 %collective-permute-start.12 = (bf16[512,512]{1,0:T(8,128)(2,1)S(1)}, bf16[512,512]{1,0:T(8,128)(2,1)S(1)}, u32[]{:S(2)}, u32[]{:S(2)}) collective-permute-start(bf16[512,512]{1,0:T(8,128)(2,1)S(1)} %collective-permute-done.11.z2), channel_id=1, source_target_pairs={{0,16},{16,0},{1,17},{17,1},{2,18},{18,2},{3,19},{19,3},{4,20},{20... | collective-permute-start | bytes 1572872 | tf_op jit(solution)/shard_map/ppermute | solution.py:486
  65.1 22.1 %collective-permute-start.9 = (bf16[64,4096]{1,0:T(8,128)(2,1)S(1)}, bf16[64,4096]{1,0:T(8,128)(2,1)S(1)}, u32[]{:S(2)}, u32[]{:S(2)}) collective-permute-start(bf16[64,4096]{1,0:T(8,128)(2,1)S(1)} %collective-permute-done.8.refs_3_), channel_id=1, source_target_pairs={{0,2},{1,3},{2,0},{3,1},{4,6},{5,7},{6,4},{7,5},{8,10},{9,11},{10,... | collective-permute-start | bytes 1572872 | tf_op jit(solution)/shard_map/ppermute | solution.py:483
  66.6 20.7 %collective-permute-start.7 = (bf16[512,512]{1,0:T(8,128)(2,1)S(1)}, bf16[512,512]{1,0:T(8,128)(2,1)S(1)}, u32[]{:S(2)}, u32[]{:S(2)}) collective-permute-start(bf16[512,512]{1,0:T(8,128)(2,1)S(1)} %get-tuple-element.78), channel_id=1, source_target_pairs={{0,12},{4,8},{8,4},{12,0},{1,13},{5,9},{9,5},{13,1},{2,14},{6,10},... | collective-permute-start | bytes 1572872 | tf_op jit(solution)/shard_map/ppermute | solution.py:480
  95.7 14.3 %collective-permute-start.10 = (bf16[512,512]{1,0:T(8,128)(2,1)S(1)}, bf16[512,512]{1,0:T(8,128)(2,1)S(1)}, u32[]{:S(2)}, u32[]{:S(2)}) collective-permute-start(bf16[512,512]{1,0:T(8,128)(2,1)S(1)} %collective-permute-done.7.refs_3_), channel_id=1, source_target_pairs={{0,16},{16,0},{1,17},{17,1},{2,18},{18,2},{3,19},{19,3},{4,20},{20... | collective-permute-start | bytes 1572872 | tf_op jit(solution)/shard_map/ppermute | solution.py:486
  97.3 12.8 %collective-permute-start.16 = (bf16[512,512]{1,0:T(8,128)(2,1)S(1)}, bf16[512,512]{1,0:T(8,128)(2,1)S(1)}, u32[]{:S(2)}, u32[]{:S(2)}) collective-permute-start(bf16[512,512]{1,0:T(8,128)(2,1)S(1)} %collective-permute-done.7.refs_3_), channel_id=1, source_target_pairs={{0,1},{1,0},{2,3},{3,2},{4,5},{5,4},{6,7},{7,6},{8,9},{9,8},{10,11... | collective-permute-start | bytes 1572872 | tf_op jit(solution)/shard_map/ppermute | solution.py:483
  125.2 16.4 %collective-permute-start.23 = (bf16[2,64,1024]{2,1,0:T(8,128)(2,1)}, bf16[2,64,1024]{2,1,0:T(8,128)(2,1)}, u32[]{:S(2)}, u32[]{:S(2)}) collective-permute-start(bf16[2,64,1024]{2,1,0:T(8,128)(2,1)} %get-tuple-element.116), channel_id=1, source_target_pairs={{0,2},{1,3},{2,0},{3,1},{4,6},{5,7},{6,4},{7,5},{8,10},{9,11},{10,... | collective-permute-start | bytes 786440 | tf_op jit(solution)/shard_map/ppermute | solution.py:483
  132.3 15.1 %all-to-all-start = ((bf16[4,2,2,2,16,256]{5,4,1,3,2,0:T(8,128)(2,1)}), bf16[4,2,2,2,16,256]{5,4,1,3,2,0:T(8,128)(2,1)}, u32[]{:S(2)}, u32[]{:S(2)}) async-start(bf16[4,2,2,2,16,256]{5,4,1,3,2,0:T(8,128)(2,1)} %copy_bitcast_fusion), calls=%async_computation | async-start | bytes 524288 | tf_op jit(solution)/shard_map/all_to_all | solution.py:524
  143.3 14.1 %collective-permute-start.26 = (bf16[2,64,1024]{2,1,0:T(8,128)(2,1)}, bf16[2,64,1024]{2,1,0:T(8,128)(2,1)}, u32[]{:S(2)}, u32[]{:S(2)}) collective-permute-start(bf16[2,64,1024]{2,1,0:T(8,128)(2,1)} %fusion.5), channel_id=1, source_target_pairs={{0,4},{4,0},{8,12},{12,8},{1,5},{5,1},{9,13},{13,9},{2,6},{6,2},{1... | collective-permute-start | bytes 786440 | tf_op jit(solution)/shard_map/ppermute | solution.py:480
  143.7 13.7 %collective-permute-start.25 = (bf16[2,64,1024]{2,1,0:T(8,128)(2,1)}, bf16[2,64,1024]{2,1,0:T(8,128)(2,1)}, u32[]{:S(2)}, u32[]{:S(2)}) collective-permute-start(bf16[2,64,1024]{2,1,0:T(8,128)(2,1)} %get-tuple-element.125), channel_id=1, source_target_pairs={{0,2},{1,3},{2,0},{3,1},{4,6},{5,7},{6,4},{7,5},{8,10},{9,11},{10,... | collective-permute-start | bytes 786440 | tf_op jit(solution)/shard_map/ppermute | solution.py:483
  145.1 19.5 %collective-permute-start.22 = (bf16[2,2,64,1024]{3,2,1,0:T(8,128)(2,1)}, bf16[2,2,64,1024]{3,2,1,0:T(8,128)(2,1)}, u32[]{:S(2)}, u32[]{:S(2)}) collective-permute-start(bf16[2,2,64,1024]{3,2,1,0:T(8,128)(2,1)} %copy-done.7), channel_id=1, source_target_pairs={{0,2},{1,3},{2,0},{3,1},{4,6},{5,7},{6,4},{7,5},{8,10},{9,11},{10,... | collective-permute-start | bytes 1572872 | tf_op jit(solution)/shard_map/ppermute | solution.py:483
  146.5 31.9 %collective-permute-start.27 = (bf16[2,2,64,1024]{3,2,1,0:T(8,128)(2,1)}, bf16[2,2,64,1024]{3,2,1,0:T(8,128)(2,1)}, u32[]{:S(2)}, u32[]{:S(2)}) collective-permute-start(bf16[2,2,64,1024]{3,2,1,0:T(8,128)(2,1)} %copy-done.6), channel_id=1, source_target_pairs={{0,3},{1,2},{2,1},{3,0},{4,7},{5,6},{6,5},{7,4},{8,11},{9,10},{10,... | collective-permute-start | bytes 1572872 | tf_op jit(solution)/shard_map/ppermute | solution.py:483
  152.6 21.6 %collective-permute-start.29 = (bf16[2,64,1024]{2,1,0:T(8,128)(2,1)}, bf16[2,64,1024]{2,1,0:T(8,128)(2,1)S(1)}, u32[]{:S(2)}, u32[]{:S(2)}) collective-permute-start(bf16[2,64,1024]{2,1,0:T(8,128)(2,1)} %fusion.1), channel_id=1, source_target_pairs={{0,8},{4,12},{8,0},{12,4},{1,9},{5,13},{9,1},{13,5},{2,10},{6,14},... | collective-permute-start | bytes 786440 | tf_op jit(solution)/shard_map/ppermute | solution.py:480
  159.3 19.1 %collective-permute-start.28 = (bf16[2,64,1024]{2,1,0:T(8,128)(2,1)}, bf16[2,64,1024]{2,1,0:T(8,128)(2,1)}, u32[]{:S(2)}, u32[]{:S(2)}) collective-permute-start(bf16[2,64,1024]{2,1,0:T(8,128)(2,1)} %fusion.4), channel_id=1, source_target_pairs={{0,8},{4,12},{8,0},{12,4},{1,9},{5,13},{9,1},{13,5},{2,10},{6,14},... | collective-permute-start | bytes 786440 | tf_op jit(solution)/shard_map/ppermute | solution.py:480
  165.5 15.8 %collective-permute-start.30 = (bf16[2,64,1024]{2,1,0:T(8,128)(2,1)S(1)}, bf16[2,64,1024]{2,1,0:T(8,128)(2,1)S(1)}, u32[]{:S(2)}, u32[]{:S(2)}) collective-permute-start(bf16[2,64,1024]{2,1,0:T(8,128)(2,1)S(1)} %fusion.6), channel_id=1, source_target_pairs={{0,4},{4,0},{8,12},{12,8},{1,5},{5,1},{9,13},{13,9},{2,6},{6,2},{1... | collective-permute-start | bytes 786440 | tf_op jit(solution)/shard_map/ppermute | solution.py:480
  (20 other events, 108.0 us)

commit v11 on v10

--- a/solution.py
+++ b/solution.py
@@ -491,13 +491,13 @@
     w_own, m1, m2, m3, q0, q1, q2, q3 = prune(
         tile_mask, key_weight, value_weight, queries.reshape(64, 1024), cotangent.reshape(64, 1024)
     )
-    q1, q2, q3 = along(q1, 1), along(q2, 2), along(q3, 3)
-    e1, e2, m1, m2, q1, q2, q3 = together(e1, e2, m1, m2, q1, q2, q3)
+    e1, e2, m1, m2 = together(e1, e2, m1, m2)
     z2, z1 = along(m2, 2), along(m1, 1)
     e3 = along(e2, 1)
     x1, x2 = flip(e1, 2), flip(e2, 2)
-    x1, x2, m3 = together(x1, x2, m3)
+    x1, x2, m3, q1, q2, q3 = together(x1, x2, m3, q1, q2, q3)
     z3 = along(m3, 3)
+    q1, q2, q3 = along(q1, 1), along(q2, 2), along(q3, 3)
     x1, z2 = together(x1, z2)
     x2, e3 = together(x2, e3)
     y2 = across(z2)

time: 190 us -> 186 us (0.979)
  waiting for transfers between devices: 107 us -> 90.8 us
  starting transfers between devices: 41.1 us -> 54.2 us
    ppermute x15, starting transfers between devices: 21.3 us -> 36.4 us  [along(): return lax.ppermute(value, 'seq', [(a, a ^ k) for a in range(SEQ)])]
    ppermute x15, waiting for transfers between devices: 63.6 us -> 52.2 us  [along(): return lax.ppermute(value, 'seq', [(a, a ^ k) for a in range(SEQ)])]
    ppermute x3, waiting for transfers between devices: 11.6 us -> 4.33 us  [across(): return lax.ppermute(value, 'grp', [(0, 1), (1, 0)])]
    ppermute x14, waiting for transfers between devices: 31.9 us -> 34.3 us  [flip(): return lax.ppermute(value, 'head', [(a, a ^ bits) for a in range(4)])]
  transfers between devices with their start and end apart: 33 -> 33, of which waited for: 21 -> 23; matrix products, arithmetic and copies ran while one was open for 6% -> 6% of each run, Pallas kernels for 3% -> 3%
where the time goes in v11:
time: 186 us
  waiting for transfers between devices  90.8 us (49%)
  starting transfers between devices  54.2 us (29%)
  Pallas kernels  20.2 us (11%)
  other arithmetic  9.96 us (5%)
  local copies, waits for them, and re-layouts  9.87 us (5%)
    ppermute x15, waiting for transfers between devices, along(): return lax.ppermute(value, 'seq', [(a, a ^ k) for a in range(SEQ)])  52.2 us
    ppermute x15, starting transfers between devices, along(): return lax.ppermute(value, 'seq', [(a, a ^ k) for a in range(SEQ)])  36.4 us
    ppermute x14, waiting for transfers between devices, flip(): return lax.ppermute(value, 'head', [(a, a ^ bits) for a in range(4)])  34.3 us
    pallas_call x1, Pallas kernels, main_call(): pl.pallas_call(main_kernel, out_shape=[front, front, jax.ShapeDtypeStruct...  11.3 us
    ppermute x14, starting transfers between devices, flip(): return lax.ppermute(value, 'head', [(a, a ^ bits) for a in range(4)])  10.8 us
    convert_element_type x6, other arithmetic, summed(): return total.astype(BF)  9.13 us
    unnamed x22, local copies, waits for them, and re-layouts  7.1 us
    pallas_call x1, Pallas kernels, early_call(): pl.pallas_call(early_kernel, out_shape=[jax.ShapeDtypeStruct((2, 512, 512...  4.39 us
  transfers between devices with their start and end apart: 33, of which 23 were waited for; matrix products, arithmetic and copies ran while one was open for 6% of the time, Pallas kernels for 3%

profile of v11, /device:TPU:0, one launch (start us, length us, event | category | flops | bytes accessed | tf_op | source)
XLA Modules:
  0.0 185.7 jit_solution(2327095933509060806)
XLA Ops:
  1.7 4.1 %collective-permute-start.1 = (bf16[64,4096]{1,0:T(8,128)(2,1)S(1)}, bf16[64,4096]{1,0:T(8,128)(2,1)S(1)}, u32[]{:S(2)}, u32[]{:S(2)}) collective-permute-start(bf16[64,4096]{1,0:T(8,128)(2,1)S(1)} %dynamic-slice_bitcast_fusion), channel_id=1, source_target_pairs={{0,8},{4,12},{8,0},{12,4},{1,9},{5,13},{9,1},{13,5},{2,10},{6,14},... | collective-permute-start | bytes 1572872 | tf_op jit(solution)/shard_map/ppermute | solution.py:480
  14.6 14.4 %collective-permute-done.1.refs_2_ = bf16[64,4096]{1,0:T(8,128)(2,1)S(1)} collective-permute-done((bf16[64,4096]{1,0:T(8,128)(2,1)S(1)}, bf16[64,4096]{1,0:T(8,128)(2,1)S(1)}, u32[]{:S(2)}, u32[]{:S(2)}) %collective-permute-start.1) | collective-permute-done | bytes 524320 | tf_op jit(solution)/shard_map/ppermute | solution.py:480
  32.7 2.4 %collective-permute-start.5 = (bf16[64,4096]{1,0:T(8,128)(2,1)S(1)}, bf16[64,4096]{1,0:T(8,128)(2,1)S(1)}, u32[]{:S(2)}, u32[]{:S(2)}) collective-permute-start(bf16[64,4096]{1,0:T(8,128)(2,1)S(1)} %collective-permute-done.1.refs_2_), channel_id=1, source_target_pairs={{0,4},{4,0},{8,12},{12,8},{1,5},{5,1},{9,13},{13,9},{2,6},{6,2},{1... | collective-permute-start | bytes 1572872 | tf_op jit(solution)/shard_map/ppermute | solution.py:480
  35.1 9.0 %collective-permute-done.2.refs_4_ = bf16[64,4096]{1,0:T(8,128)(2,1)S(1)} collective-permute-done((bf16[64,4096]{1,0:T(8,128)(2,1)S(1)}, bf16[64,4096]{1,0:T(8,128)(2,1)S(1)}, u32[]{:S(2)}, u32[]{:S(2)}) %collective-permute-start.2) | collective-permute-done | bytes 524320 | tf_op jit(solution)/shard_map/ppermute | solution.py:483
  44.1 9.2 %collective-permute-done.3.refs_5_ = bf16[64,4096]{1,0:T(8,128)(2,1)S(1)} collective-permute-done((bf16[64,4096]{1,0:T(8,128)(2,1)S(1)}, bf16[64,4096]{1,0:T(8,128)(2,1)S(1)}, u32[]{:S(2)}, u32[]{:S(2)}) %collective-permute-start.3) | collective-permute-done | bytes 524320 | tf_op jit(solution)/shard_map/ppermute | solution.py:483
  53.4 2.5 %collective-permute-done.8.z2 = bf16[512,512]{1,0:T(8,128)(2,1)S(1)} collective-permute-done((bf16[512,512]{1,0:T(8,128)(2,1)S(1)}, bf16[512,512]{1,0:T(8,128)(2,1)S(1)}, u32[]{:S(2)}, u32[]{:S(2)}) %collective-permute-start.8) | collective-permute-done | bytes 524320 | tf_op jit(solution)/shard_map/ppermute | solution.py:480
  58.7 3.9 %collective-permute-start.4 = (bf16[512,512]{1,0:T(8,128)(2,1)S(1)}, bf16[512,512]{1,0:T(8,128)(2,1)S(1)}, u32[]{:S(2)}, u32[]{:S(2)}) collective-permute-start(bf16[512,512]{1,0:T(8,128)(2,1)S(1)} %get-tuple-element.78), channel_id=1, source_target_pairs={{0,12},{4,8},{8,4},{12,0},{1,13},{5,9},{9,5},{13,1},{2,14},{6,10},... | collective-permute-start | bytes 1572872 | tf_op jit(solution)/shard_map/ppermute | solution.py:480
  62.6 4.9 %collective-permute-done.10.z1 = bf16[512,512]{1,0:T(8,128)(2,1)S(1)} collective-permute-done((bf16[512,512]{1,0:T(8,128)(2,1)S(1)}, bf16[512,512]{1,0:T(8,128)(2,1)S(1)}, u32[]{:S(2)}, u32[]{:S(2)}) %collective-permute-start.10) | collective-permute-done | bytes 524320 | tf_op jit(solution)/shard_map/ppermute | solution.py:480
  69.1 2.5 %collective-permute-start.12 = (bf16[64,512]{1,0:T(8,128)(2,1)S(1)}, bf16[64,512]{1,0:T(8,128)(2,1)S(1)}, u32[]{:S(2)}, u32[]{:S(2)}) collective-permute-start(bf16[64,512]{1,0:T(8,128)(2,1)S(1)} %get-tuple-element.94), channel_id=1, source_target_pairs={{0,4},{4,0},{8,12},{12,8},{1,5},{5,1},{9,13},{13,9},{2,6},{6,2},{1... | collective-permute-start | bytes 196616 | tf_op jit(solution)/shard_map/ppermute | solution.py:480
  71.6 14.2 %collective-permute-start.13 = (bf16[64,512]{1,0:T(8,128)(2,1)S(1)}, bf16[64,512]{1,0:T(8,128)(2,1)S(1)}, u32[]{:S(2)}, u32[]{:S(2)}) collective-permute-start(bf16[64,512]{1,0:T(8,128)(2,1)S(1)} %get-tuple-element.95), channel_id=1, source_target_pairs={{0,8},{4,12},{8,0},{12,4},{1,9},{5,13},{9,1},{13,5},{2,10},{6,14},... | collective-permute-start | bytes 196616 | tf_op jit(solution)/shard_map/ppermute | solution.py:480
  85.8 2.9 %collective-permute-done.13.q2 = bf16[64,512]{1,0:T(8,128)(2,1)S(1)} collective-permute-done((bf16[64,512]{1,0:T(8,128)(2,1)S(1)}, bf16[64,512]{1,0:T(8,128)(2,1)S(1)}, u32[]{:S(2)}, u32[]{:S(2)}) %collective-permute-start.13) | collective-permute-done | bytes 65568 | tf_op jit(solution)/shard_map/ppermute | solution.py:480
  88.7 3.1 %collective-permute-done.14.q3 = bf16[64,512]{1,0:T(8,128)(2,1)S(1)} collective-permute-done((bf16[64,512]{1,0:T(8,128)(2,1)S(1)}, bf16[64,512]{1,0:T(8,128)(2,1)S(1)}, u32[]{:S(2)}, u32[]{:S(2)}) %collective-permute-start.14) | collective-permute-done | bytes 65568 | tf_op jit(solution)/shard_map/ppermute | solution.py:480
  93.3 5.3 %collective-permute-done.15.refs_8_.refs_5_ = bf16[3328,512]{1,0:T(8,128)(2,1)S(1)} collective-permute-done((bf16[3328,512]{1,0:T(8,128)(2,1)S(1)}, bf16[3328,512]{1,0:T(8,128)(2,1)S(1)}, u32[]{:S(2)}, u32[]{:S(2)}) %collective-permute-start.15) | collective-permute-done | bytes 3407904 | tf_op jit(solution)/shard_map/ppermute | solution.py:483
  98.6 4.4 %early.1 = (f32[2,512,512]{2,1,0:T(8,128)S(1)}, bf16[512,1024]{1,0:T(8,128)(2,1)S(1)}) custom-call(bf16[4,64,4096]{2,1,0:T(8,128)(2,1)S(1)} %copy-done, bf16[64,4096]{1,0:T(8,128)(2,1)S(1)} %collective-permute-done.refs_1_, bf16[64,4096]{1,0:T(8,128)(2,1)S(1)} %collective-permute-done.1.refs_2_, bf16[64,4096]{1,0:T(8,128)(2,1)S(1)} %collective-permute-done.5.refs_3_, ...), custom_call_target="tpu_custom_call" | custom-call | flops 1 | bytes 1 | tf_op jit(solution)/shard_map/early/pallas_call | solution.py:296
  103.0 3.9 %collective-permute-done.7.refs_4_ = bf16[512,512]{1,0:T(8,128)(2,1)S(1)} collective-permute-done((bf16[512,512]{1,0:T(8,128)(2,1)S(1)}, bf16[512,512]{1,0:T(8,128)(2,1)S(1)}, u32[]{:S(2)}, u32[]{:S(2)}) %collective-permute-start.7) | collective-permute-done | bytes 524320 | tf_op jit(solution)/shard_map/ppermute | solution.py:486
  108.8 11.3 %attend.1 = (bf16[2,2,64,256]{3,2,1,0:T(8,128)(2,1)S(1)}, bf16[2,2,64,256]{3,2,1,0:T(8,128)(2,1)S(1)}, f32[4,2,64,1024]{3,2,1,0:T(8,128)S(1)}, bf16[2,64,1024]{2...) custom-call(s32[4]{0:T(128)S(1)} %copy-done.8, ...), custom_call_target="tpu_custom_call" | custom-call | flops 6000000000 | bytes 25165824 | tf_op jit(solution)/shard_map/attend/pallas_call | solution.py:415
  124.0 4.5 %collective-permute-done.18 = bf16[2,64,1024]{2,1,0:T(8,128)(2,1)S(1)} collective-permute-done((bf16[2,64,1024]{2,1,0:T(8,128)(2,1)S(1)}, bf16[2,64,1024]{2,1,0:T(8,128)(2,1)S(1)}, u32[]{:S(2)}, u32[]{:S(2)}) %collective-permute-start.18) | collective-permute-done | bytes 262176 | tf_op jit(solution)/shard_map/ppermute | solution.py:483
  129.2 4.0 %all-to-all-start = ((bf16[4,2,2,2,16,256]{5,4,1,3,2,0:T(8,128)(2,1)}), bf16[4,2,2,2,16,256]{5,4,1,3,2,0:T(8,128)(2,1)}, u32[]{:S(2)}, u32[]{:S(2)}) async-start(bf16[4,2,2,2,16,256]{5,4,1,3,2,0:T(8,128)(2,1)} %copy_bitcast_fusion), calls=%async_computation | async-start | bytes 524288 | tf_op jit(solution)/shard_map/all_to_all | solution.py:524
  144.3 3.3 %collective-permute-done.24 = bf16[2,64,1024]{2,1,0:T(8,128)(2,1)} collective-permute-done((bf16[2,64,1024]{2,1,0:T(8,128)(2,1)}, bf16[2,64,1024]{2,1,0:T(8,128)(2,1)}, u32[]{:S(2)}, u32[]{:S(2)}) %collective-permute-start.24) | collective-permute-done | bytes 262176 | tf_op jit(solution)/shard_map/ppermute | solution.py:480
  151.2 3.1 %collective-permute-done.26 = bf16[2,64,1024]{2,1,0:T(8,128)(2,1)} collective-permute-done((bf16[2,64,1024]{2,1,0:T(8,128)(2,1)}, bf16[2,64,1024]{2,1,0:T(8,128)(2,1)}, u32[]{:S(2)}, u32[]{:S(2)}) %collective-permute-start.26) | collective-permute-done | bytes 262176 | tf_op jit(solution)/shard_map/ppermute | solution.py:480
  157.8 3.6 %collective-permute-done.22.near = bf16[2,2,64,1024]{3,2,1,0:T(8,128)(2,1)} collective-permute-done((bf16[2,2,64,1024]{3,2,1,0:T(8,128)(2,1)}, bf16[2,2,64,1024]{3,2,1,0:T(8,128)(2,1)}, u32[]{:S(2)}, u32[]{:S(2)}) %collective-permute-start.22) | collective-permute-done | bytes 524320 | tf_op jit(solution)/shard_map/ppermute | solution.py:483
  164.1 6.9 %collective-permute-done.29.far2 = bf16[2,64,1024]{2,1,0:T(8,128)(2,1)S(1)} collective-permute-done((bf16[2,64,1024]{2,1,0:T(8,128)(2,1)}, bf16[2,64,1024]{2,1,0:T(8,128)(2,1)S(1)}, u32[]{:S(2)}, u32[]{:S(2)}) %collective-permute-start.29) | collective-permute-done | bytes 262176 | tf_op jit(solution)/shard_map/ppermute | solution.py:480
  171.0 4.2 %collective-permute-done.28.near2 = bf16[2,64,1024]{2,1,0:T(8,128)(2,1)} collective-permute-done((bf16[2,64,1024]{2,1,0:T(8,128)(2,1)}, bf16[2,64,1024]{2,1,0:T(8,128)(2,1)}, u32[]{:S(2)}, u32[]{:S(2)}) %collective-permute-start.28) | collective-permute-done | bytes 262176 | tf_op jit(solution)/shard_map/ppermute | solution.py:480
  178.2 5.3 %collective-permute-done.31.far1 = bf16[2,64,1024]{2,1,0:T(8,128)(2,1)S(1)} collective-permute-done((bf16[2,64,1024]{2,1,0:T(8,128)(2,1)S(1)}, bf16[2,64,1024]{2,1,0:T(8,128)(2,1)S(1)}, u32[]{:S(2)}, u32[]{:S(2)}) %collective-permute-start.31) | collective-permute-done | bytes 262176 | tf_op jit(solution)/shard_map/ppermute | solution.py:480
  (81 shorter events, 51.9 us)
Async XLA Ops:
  1.7 27.4 %collective-permute-start.1 = (bf16[64,4096]{1,0:T(8,128)(2,1)S(1)}, bf16[64,4096]{1,0:T(8,128)(2,1)S(1)}, u32[]{:S(2)}, u32[]{:S(2)}) collective-permute-start(bf16[64,4096]{1,0:T(8,128)(2,1)S(1)} %dynamic-slice_bitcast_fusion), channel_id=1, source_target_pairs={{0,8},{4,12},{8,0},{12,4},{1,9},{5,13},{9,1},{13,5},{2,10},{6,14},... | collective-permute-start | bytes 1572872 | tf_op jit(solution)/shard_map/ppermute | solution.py:480
  5.8 23.5 %collective-permute-start = (bf16[64,4096]{1,0:T(8,128)(2,1)S(1)}, bf16[64,4096]{1,0:T(8,128)(2,1)S(1)}, u32[]{:S(2)}, u32[]{:S(2)}) collective-permute-start(bf16[64,4096]{1,0:T(8,128)(2,1)S(1)} %dynamic-slice_bitcast_fusion), channel_id=1, source_target_pairs={{0,4},{4,0},{8,12},{12,8},{1,5},{5,1},{9,13},{13,9},{2,6},{6,2},{1... | collective-permute-start | bytes 1572872 | tf_op jit(solution)/shard_map/ppermute | solution.py:480
  29.3 14.9 %collective-permute-start.2 = (bf16[64,4096]{1,0:T(8,128)(2,1)S(1)}, bf16[64,4096]{1,0:T(8,128)(2,1)S(1)}, u32[]{:S(2)}, u32[]{:S(2)}) collective-permute-start(bf16[64,4096]{1,0:T(8,128)(2,1)S(1)} %collective-permute-done.refs_1_), channel_id=1, source_target_pairs={{0,2},{1,3},{2,0},{3,1},{4,6},{5,7},{6,4},{7,5},{8,10},{9,11},{10,... | collective-permute-start | bytes 1572872 | tf_op jit(solution)/shard_map/ppermute | solution.py:483
  30.8 22.6 %collective-permute-start.3 = (bf16[64,4096]{1,0:T(8,128)(2,1)S(1)}, bf16[64,4096]{1,0:T(8,128)(2,1)S(1)}, u32[]{:S(2)}, u32[]{:S(2)}) collective-permute-start(bf16[64,4096]{1,0:T(8,128)(2,1)S(1)} %collective-permute-done.1.refs_2_), channel_id=1, source_target_pairs={{0,2},{1,3},{2,0},{3,1},{4,6},{5,7},{6,4},{7,5},{8,10},{9,11},{10,... | collective-permute-start | bytes 1572872 | tf_op jit(solution)/shard_map/ppermute | solution.py:483
  31.3 24.5 %collective-permute-start.8 = (bf16[512,512]{1,0:T(8,128)(2,1)S(1)}, bf16[512,512]{1,0:T(8,128)(2,1)S(1)}, u32[]{:S(2)}, u32[]{:S(2)}) collective-permute-start(bf16[512,512]{1,0:T(8,128)(2,1)S(1)} %get-tuple-element.84), channel_id=1, source_target_pairs={{0,8},{4,12},{8,0},{12,4},{1,9},{5,13},{9,1},{13,5},{2,10},{6,14},... | collective-permute-start | bytes 1572872 | tf_op jit(solution)/shard_map/ppermute | solution.py:480
  32.7 24.8 %collective-permute-start.5 = (bf16[64,4096]{1,0:T(8,128)(2,1)S(1)}, bf16[64,4096]{1,0:T(8,128)(2,1)S(1)}, u32[]{:S(2)}, u32[]{:S(2)}) collective-permute-start(bf16[64,4096]{1,0:T(8,128)(2,1)S(1)} %collective-permute-done.1.refs_2_), channel_id=1, source_target_pairs={{0,4},{4,0},{8,12},{12,8},{1,5},{5,1},{9,13},{13,9},{2,6},{6,2},{1... | collective-permute-start | bytes 1572872 | tf_op jit(solution)/shard_map/ppermute | solution.py:480
  35.1 32.5 %collective-permute-start.10 = (bf16[512,512]{1,0:T(8,128)(2,1)S(1)}, bf16[512,512]{1,0:T(8,128)(2,1)S(1)}, u32[]{:S(2)}, u32[]{:S(2)}) collective-permute-start(bf16[512,512]{1,0:T(8,128)(2,1)S(1)} %get-tuple-element.90), channel_id=1, source_target_pairs={{0,4},{4,0},{8,12},{12,8},{1,5},{5,1},{9,13},{13,9},{2,6},{6,2},{1... | collective-permute-start | bytes 1572872 | tf_op jit(solution)/shard_map/ppermute | solution.py:480
  55.8 12.1 %collective-permute-start.9 = (bf16[512,512]{1,0:T(8,128)(2,1)S(1)}, bf16[512,512]{1,0:T(8,128)(2,1)S(1)}, u32[]{:S(2)}, u32[]{:S(2)}) collective-permute-start(bf16[512,512]{1,0:T(8,128)(2,1)S(1)} %collective-permute-done.8.z2), channel_id=1, source_target_pairs={{0,16},{16,0},{1,17},{17,1},{2,18},{18,2},{3,19},{19,3},{4,20},{20... | collective-permute-start | bytes 1572872 | tf_op jit(solution)/shard_map/ppermute | solution.py:486
  57.5 28.2 %collective-permute-start.6 = (bf16[64,4096]{1,0:T(8,128)(2,1)S(1)}, bf16[64,4096]{1,0:T(8,128)(2,1)S(1)}, u32[]{:S(2)}, u32[]{:S(2)}) collective-permute-start(bf16[64,4096]{1,0:T(8,128)(2,1)S(1)} %collective-permute-done.5.refs_3_), channel_id=1, source_target_pairs={{0,2},{1,3},{2,0},{3,1},{4,6},{5,7},{6,4},{7,5},{8,10},{9,11},{10,... | collective-permute-start | bytes 1572872 | tf_op jit(solution)/shard_map/ppermute | solution.py:483
  58.7 27.0 %collective-permute-start.4 = (bf16[512,512]{1,0:T(8,128)(2,1)S(1)}, bf16[512,512]{1,0:T(8,128)(2,1)S(1)}, u32[]{:S(2)}, u32[]{:S(2)}) collective-permute-start(bf16[512,512]{1,0:T(8,128)(2,1)S(1)} %get-tuple-element.78), channel_id=1, source_target_pairs={{0,12},{4,8},{8,4},{12,0},{1,13},{5,9},{9,5},{13,1},{2,14},{6,10},... | collective-permute-start | bytes 1572872 | tf_op jit(solution)/shard_map/ppermute | solution.py:480
  68.0 23.8 %collective-permute-start.11 = (bf16[512,512]{1,0:T(8,128)(2,1)S(1)}, bf16[512,512]{1,0:T(8,128)(2,1)S(1)}, u32[]{:S(2)}, u32[]{:S(2)}) collective-permute-start(bf16[512,512]{1,0:T(8,128)(2,1)S(1)} %collective-permute-done.10.z1), channel_id=1, source_target_pairs={{0,16},{16,0},{1,17},{17,1},{2,18},{18,2},{3,19},{19,3},{4,20},{20... | collective-permute-start | bytes 1572872 | tf_op jit(solution)/shard_map/ppermute | solution.py:486
  69.1 16.7 %collective-permute-start.12 = (bf16[64,512]{1,0:T(8,128)(2,1)S(1)}, bf16[64,512]{1,0:T(8,128)(2,1)S(1)}, u32[]{:S(2)}, u32[]{:S(2)}) collective-permute-start(bf16[64,512]{1,0:T(8,128)(2,1)S(1)} %get-tuple-element.94), channel_id=1, source_target_pairs={{0,4},{4,0},{8,12},{12,8},{1,5},{5,1},{9,13},{13,9},{2,6},{6,2},{1... | collective-permute-start | bytes 196616 | tf_op jit(solution)/shard_map/ppermute | solution.py:480
  71.6 17.1 %collective-permute-start.13 = (bf16[64,512]{1,0:T(8,128)(2,1)S(1)}, bf16[64,512]{1,0:T(8,128)(2,1)S(1)}, u32[]{:S(2)}, u32[]{:S(2)}) collective-permute-start(bf16[64,512]{1,0:T(8,128)(2,1)S(1)} %get-tuple-element.95), channel_id=1, source_target_pairs={{0,8},{4,12},{8,0},{12,4},{1,9},{5,13},{9,1},{13,5},{2,10},{6,14},... | collective-permute-start | bytes 196616 | tf_op jit(solution)/shard_map/ppermute | solution.py:480
  92.6 14.3 %collective-permute-start.7 = (bf16[512,512]{1,0:T(8,128)(2,1)S(1)}, bf16[512,512]{1,0:T(8,128)(2,1)S(1)}, u32[]{:S(2)}, u32[]{:S(2)}) collective-permute-start(bf16[512,512]{1,0:T(8,128)(2,1)S(1)} %collective-permute-done.4.refs_3_), channel_id=1, source_target_pairs={{0,16},{16,0},{1,17},{17,1},{2,18},{18,2},{3,19},{19,3},{4,20},{20... | collective-permute-start | bytes 1572872 | tf_op jit(solution)/shard_map/ppermute | solution.py:486
  93.1 13.8 %collective-permute-start.16 = (bf16[512,512]{1,0:T(8,128)(2,1)S(1)}, bf16[512,512]{1,0:T(8,128)(2,1)S(1)}, u32[]{:S(2)}, u32[]{:S(2)}) collective-permute-start(bf16[512,512]{1,0:T(8,128)(2,1)S(1)} %collective-permute-done.4.refs_3_), channel_id=1, source_target_pairs={{0,1},{1,0},{2,3},{3,2},{4,5},{5,4},{6,7},{7,6},{8,9},{9,8},{10,11... | collective-permute-start | bytes 1572872 | tf_op jit(solution)/shard_map/ppermute | solution.py:483
  122.1 16.5 %collective-permute-start.23 = (bf16[2,64,1024]{2,1,0:T(8,128)(2,1)}, bf16[2,64,1024]{2,1,0:T(8,128)(2,1)}, u32[]{:S(2)}, u32[]{:S(2)}) collective-permute-start(bf16[2,64,1024]{2,1,0:T(8,128)(2,1)} %get-tuple-element.116), channel_id=1, source_target_pairs={{0,2},{1,3},{2,0},{3,1},{4,6},{5,7},{6,4},{7,5},{8,10},{9,11},{10,... | collective-permute-start | bytes 786440 | tf_op jit(solution)/shard_map/ppermute | solution.py:483
  129.2 15.1 %all-to-all-start = ((bf16[4,2,2,2,16,256]{5,4,1,3,2,0:T(8,128)(2,1)}), bf16[4,2,2,2,16,256]{5,4,1,3,2,0:T(8,128)(2,1)}, u32[]{:S(2)}, u32[]{:S(2)}) async-start(bf16[4,2,2,2,16,256]{5,4,1,3,2,0:T(8,128)(2,1)} %copy_bitcast_fusion), calls=%async_computation | async-start | bytes 524288 | tf_op jit(solution)/shard_map/all_to_all | solution.py:524
  140.2 14.1 %collective-permute-start.26 = (bf16[2,64,1024]{2,1,0:T(8,128)(2,1)}, bf16[2,64,1024]{2,1,0:T(8,128)(2,1)}, u32[]{:S(2)}, u32[]{:S(2)}) collective-permute-start(bf16[2,64,1024]{2,1,0:T(8,128)(2,1)} %fusion.5), channel_id=1, source_target_pairs={{0,4},{4,0},{8,12},{12,8},{1,5},{5,1},{9,13},{13,9},{2,6},{6,2},{1... | collective-permute-start | bytes 786440 | tf_op jit(solution)/shard_map/ppermute | solution.py:480
  140.6 13.7 %collective-permute-start.25 = (bf16[2,64,1024]{2,1,0:T(8,128)(2,1)}, bf16[2,64,1024]{2,1,0:T(8,128)(2,1)}, u32[]{:S(2)}, u32[]{:S(2)}) collective-permute-start(bf16[2,64,1024]{2,1,0:T(8,128)(2,1)} %get-tuple-element.125), channel_id=1, source_target_pairs={{0,2},{1,3},{2,0},{3,1},{4,6},{5,7},{6,4},{7,5},{8,10},{9,11},{10,... | collective-permute-start | bytes 786440 | tf_op jit(solution)/shard_map/ppermute | solution.py:483
  141.9 19.5 %collective-permute-start.22 = (bf16[2,2,64,1024]{3,2,1,0:T(8,128)(2,1)}, bf16[2,2,64,1024]{3,2,1,0:T(8,128)(2,1)}, u32[]{:S(2)}, u32[]{:S(2)}) collective-permute-start(bf16[2,2,64,1024]{3,2,1,0:T(8,128)(2,1)} %copy-done.7), channel_id=1, source_target_pairs={{0,2},{1,3},{2,0},{3,1},{4,6},{5,7},{6,4},{7,5},{8,10},{9,11},{10,... | collective-permute-start | bytes 1572872 | tf_op jit(solution)/shard_map/ppermute | solution.py:483
  143.3 31.9 %collective-permute-start.27 = (bf16[2,2,64,1024]{3,2,1,0:T(8,128)(2,1)}, bf16[2,2,64,1024]{3,2,1,0:T(8,128)(2,1)}, u32[]{:S(2)}, u32[]{:S(2)}) collective-permute-start(bf16[2,2,64,1024]{3,2,1,0:T(8,128)(2,1)} %copy-done.6), channel_id=1, source_target_pairs={{0,3},{1,2},{2,1},{3,0},{4,7},{5,6},{6,5},{7,4},{8,11},{9,10},{10,... | collective-permute-start | bytes 1572872 | tf_op jit(solution)/shard_map/ppermute | solution.py:483
  149.5 21.6 %collective-permute-start.29 = (bf16[2,64,1024]{2,1,0:T(8,128)(2,1)}, bf16[2,64,1024]{2,1,0:T(8,128)(2,1)S(1)}, u32[]{:S(2)}, u32[]{:S(2)}) collective-permute-start(bf16[2,64,1024]{2,1,0:T(8,128)(2,1)} %fusion.1), channel_id=1, source_target_pairs={{0,8},{4,12},{8,0},{12,4},{1,9},{5,13},{9,1},{13,5},{2,10},{6,14},... | collective-permute-start | bytes 786440 | tf_op jit(solution)/shard_map/ppermute | solution.py:480
  156.2 19.1 %collective-permute-start.28 = (bf16[2,64,1024]{2,1,0:T(8,128)(2,1)}, bf16[2,64,1024]{2,1,0:T(8,128)(2,1)}, u32[]{:S(2)}, u32[]{:S(2)}) collective-permute-start(bf16[2,64,1024]{2,1,0:T(8,128)(2,1)} %fusion.4), channel_id=1, source_target_pairs={{0,8},{4,12},{8,0},{12,4},{1,9},{5,13},{9,1},{13,5},{2,10},{6,14},... | collective-permute-start | bytes 786440 | tf_op jit(solution)/shard_map/ppermute | solution.py:480
  162.4 15.7 %collective-permute-start.30 = (bf16[2,64,1024]{2,1,0:T(8,128)(2,1)S(1)}, bf16[2,64,1024]{2,1,0:T(8,128)(2,1)S(1)}, u32[]{:S(2)}, u32[]{:S(2)}) collective-permute-start(bf16[2,64,1024]{2,1,0:T(8,128)(2,1)S(1)} %fusion.6), channel_id=1, source_target_pairs={{0,4},{4,0},{8,12},{12,8},{1,5},{5,1},{9,13},{13,9},{2,6},{6,2},{1... | collective-permute-start | bytes 786440 | tf_op jit(solution)/shard_map/ppermute | solution.py:480
  (20 other events, 104.9 us)

commit v12 on v11

--- a/solution.py
+++ b/solution.py
@@ -493,8 +493,9 @@
     )
     e1, e2, m1, m2 = together(e1, e2, m1, m2)
     z2, z1 = along(m2, 2), along(m1, 1)
+    x1, x2 = flip(e1, 2), flip(e2, 2)
+    x1, e2 = together(x1, e2)
     e3 = along(e2, 1)
-    x1, x2 = flip(e1, 2), flip(e2, 2)
     x1, x2, m3, q1, q2, q3 = together(x1, x2, m3, q1, q2, q3)
     z3 = along(m3, 3)
     q1, q2, q3 = along(q1, 1), along(q2, 2), along(q3, 3)

time: 186 us -> 188 us (1.011)
    ppermute x14, waiting for transfers between devices: 34.3 us -> 31.8 us  [flip(): return lax.ppermute(value, 'head', [(a, a ^ bits) for a in range(4)])]
    ppermute x15, waiting for transfers between devices: 52.2 us -> 54.3 us  [along(): return lax.ppermute(value, 'seq', [(a, a ^ k) for a in range(SEQ)])]
  transfers between devices with their start and end apart: 33 -> 33, of which waited for: 23 -> 20; matrix products, arithmetic and copies ran while one was open for 6% -> 6% of each run, Pallas kernels for 3% -> 3%
where the time goes in v12:
time: 188 us; the launch traced here: 187 us
  waiting for transfers between devices  90.1 us (48%)
  starting transfers between devices  56 us (30%)
  Pallas kernels  20.2 us (11%)
  other arithmetic  9.96 us (5%)
  local copies, waits for them, and re-layouts  9.87 us (5%)
    ppermute x15, waiting for transfers between devices, along(): return lax.ppermute(value, 'seq', [(a, a ^ k) for a in range(SEQ)])  54.3 us
    ppermute x15, starting transfers between devices, along(): return lax.ppermute(value, 'seq', [(a, a ^ k) for a in range(SEQ)])  37.6 us
    ppermute x14, waiting for transfers between devices, flip(): return lax.ppermute(value, 'head', [(a, a ^ bits) for a in range(4)])  31.8 us
    pallas_call x1, Pallas kernels, main_call(): pl.pallas_call(main_kernel, out_shape=[front, front, jax.ShapeDtypeStruct...  11.3 us
    ppermute x14, starting transfers between devices, flip(): return lax.ppermute(value, 'head', [(a, a ^ bits) for a in range(4)])  11 us
    convert_element_type x6, other arithmetic, summed(): return total.astype(BF)  9.13 us
    unnamed x22, local copies, waits for them, and re-layouts  7.1 us
    pallas_call x1, Pallas kernels, early_call(): pl.pallas_call(early_kernel, out_shape=[jax.ShapeDtypeStruct((2, 512, 512...  4.39 us
  transfers between devices with their start and end apart: 33, of which 20 were waited for; matrix products, arithmetic and copies ran while one was open for 6% of the time, Pallas kernels for 3%

profile of v12, /device:TPU:0, one launch (start us, length us, event | category | flops | bytes accessed | tf_op | source)
XLA Modules:
  0.0 186.9 jit_solution(16876117232961305262)
XLA Ops:
  1.7 4.1 %collective-permute-start.1 = (bf16[64,4096]{1,0:T(8,128)(2,1)S(1)}, bf16[64,4096]{1,0:T(8,128)(2,1)S(1)}, u32[]{:S(2)}, u32[]{:S(2)}) collective-permute-start(bf16[64,4096]{1,0:T(8,128)(2,1)S(1)} %dynamic-slice_bitcast_fusion), channel_id=1, source_target_pairs={{0,8},{4,12},{8,0},{12,4},{1,9},{5,13},{9,1},{13,5},{2,10},{6,14},... | collective-permute-start | bytes 1572872 | tf_op jit(solution)/shard_map/ppermute | solution.py:480
  14.6 14.4 %collective-permute-done.1.refs_2_ = bf16[64,4096]{1,0:T(8,128)(2,1)S(1)} collective-permute-done((bf16[64,4096]{1,0:T(8,128)(2,1)S(1)}, bf16[64,4096]{1,0:T(8,128)(2,1)S(1)}, u32[]{:S(2)}, u32[]{:S(2)}) %collective-permute-start.1) | collective-permute-done | bytes 524320 | tf_op jit(solution)/shard_map/ppermute | solution.py:480
  32.7 2.4 %collective-permute-start.10 = (bf16[512,512]{1,0:T(8,128)(2,1)S(1)}, bf16[512,512]{1,0:T(8,128)(2,1)S(1)}, u32[]{:S(2)}, u32[]{:S(2)}) collective-permute-start(bf16[512,512]{1,0:T(8,128)(2,1)S(1)} %get-tuple-element.94), channel_id=1, source_target_pairs={{0,4},{4,0},{8,12},{12,8},{1,5},{5,1},{9,13},{13,9},{2,6},{6,2},{1... | collective-permute-start | bytes 1572872 | tf_op jit(solution)/shard_map/ppermute | solution.py:480
  35.1 9.0 %collective-permute-done.2.refs_4_ = bf16[64,4096]{1,0:T(8,128)(2,1)S(1)} collective-permute-done((bf16[64,4096]{1,0:T(8,128)(2,1)S(1)}, bf16[64,4096]{1,0:T(8,128)(2,1)S(1)}, u32[]{:S(2)}, u32[]{:S(2)}) %collective-permute-start.2) | collective-permute-done | bytes 524320 | tf_op jit(solution)/shard_map/ppermute | solution.py:483
  45.6 7.8 %collective-permute-done.3.refs_5_ = bf16[64,4096]{1,0:T(8,128)(2,1)S(1)} collective-permute-done((bf16[64,4096]{1,0:T(8,128)(2,1)S(1)}, bf16[64,4096]{1,0:T(8,128)(2,1)S(1)}, u32[]{:S(2)}, u32[]{:S(2)}) %collective-permute-start.3) | collective-permute-done | bytes 524320 | tf_op jit(solution)/shard_map/ppermute | solution.py:483
  53.4 2.5 %collective-permute-done.8.z2 = bf16[512,512]{1,0:T(8,128)(2,1)S(1)} collective-permute-done((bf16[512,512]{1,0:T(8,128)(2,1)S(1)}, bf16[512,512]{1,0:T(8,128)(2,1)S(1)}, u32[]{:S(2)}, u32[]{:S(2)}) %collective-permute-start.8) | collective-permute-done | bytes 524320 | tf_op jit(solution)/shard_map/ppermute | solution.py:480
  57.1 2.5 %collective-permute-start.4 = (bf16[512,512]{1,0:T(8,128)(2,1)S(1)}, bf16[512,512]{1,0:T(8,128)(2,1)S(1)}, u32[]{:S(2)}, u32[]{:S(2)}) collective-permute-start(bf16[512,512]{1,0:T(8,128)(2,1)S(1)} %get-tuple-element.81), channel_id=1, source_target_pairs={{0,12},{4,8},{8,4},{12,0},{1,13},{5,9},{9,5},{13,1},{2,14},{6,10},... | collective-permute-start | bytes 1572872 | tf_op jit(solution)/shard_map/ppermute | solution.py:480
  59.6 8.0 %collective-permute-done.5.refs_3_ = bf16[64,4096]{1,0:T(8,128)(2,1)S(1)} collective-permute-done((bf16[64,4096]{1,0:T(8,128)(2,1)S(1)}, bf16[64,4096]{1,0:T(8,128)(2,1)S(1)}, u32[]{:S(2)}, u32[]{:S(2)}) %collective-permute-start.5) | collective-permute-done | bytes 524320 | tf_op jit(solution)/shard_map/ppermute | solution.py:480
  70.6 2.5 %collective-permute-start.12 = (bf16[64,512]{1,0:T(8,128)(2,1)S(1)}, bf16[64,512]{1,0:T(8,128)(2,1)S(1)}, u32[]{:S(2)}, u32[]{:S(2)}) collective-permute-start(bf16[64,512]{1,0:T(8,128)(2,1)S(1)} %get-tuple-element.98), channel_id=1, source_target_pairs={{0,4},{4,0},{8,12},{12,8},{1,5},{5,1},{9,13},{13,9},{2,6},{6,2},{1... | collective-permute-start | bytes 196616 | tf_op jit(solution)/shard_map/ppermute | solution.py:480
  73.1 13.6 %collective-permute-start.13 = (bf16[64,512]{1,0:T(8,128)(2,1)S(1)}, bf16[64,512]{1,0:T(8,128)(2,1)S(1)}, u32[]{:S(2)}, u32[]{:S(2)}) collective-permute-start(bf16[64,512]{1,0:T(8,128)(2,1)S(1)} %get-tuple-element.99), channel_id=1, source_target_pairs={{0,8},{4,12},{8,0},{12,4},{1,9},{5,13},{9,1},{13,5},{2,10},{6,14},... | collective-permute-start | bytes 196616 | tf_op jit(solution)/shard_map/ppermute | solution.py:480
  86.7 2.9 %collective-permute-done.13.q2 = bf16[64,512]{1,0:T(8,128)(2,1)S(1)} collective-permute-done((bf16[64,512]{1,0:T(8,128)(2,1)S(1)}, bf16[64,512]{1,0:T(8,128)(2,1)S(1)}, u32[]{:S(2)}, u32[]{:S(2)}) %collective-permute-start.13) | collective-permute-done | bytes 65568 | tf_op jit(solution)/shard_map/ppermute | solution.py:480
  89.6 3.1 %collective-permute-done.14.q3 = bf16[64,512]{1,0:T(8,128)(2,1)S(1)} collective-permute-done((bf16[64,512]{1,0:T(8,128)(2,1)S(1)}, bf16[64,512]{1,0:T(8,128)(2,1)S(1)}, u32[]{:S(2)}, u32[]{:S(2)}) %collective-permute-start.14) | collective-permute-done | bytes 65568 | tf_op jit(solution)/shard_map/ppermute | solution.py:480
  94.3 5.3 %collective-permute-done.15.refs_8_.refs_5_ = bf16[3328,512]{1,0:T(8,128)(2,1)S(1)} collective-permute-done((bf16[3328,512]{1,0:T(8,128)(2,1)S(1)}, bf16[3328,512]{1,0:T(8,128)(2,1)S(1)}, u32[]{:S(2)}, u32[]{:S(2)}) %collective-permute-start.15) | collective-permute-done | bytes 3407904 | tf_op jit(solution)/shard_map/ppermute | solution.py:483
  99.5 4.4 %early.1 = (f32[2,512,512]{2,1,0:T(8,128)S(1)}, bf16[512,1024]{1,0:T(8,128)(2,1)S(1)}) custom-call(bf16[4,64,4096]{2,1,0:T(8,128)(2,1)S(1)} %copy-done, bf16[64,4096]{1,0:T(8,128)(2,1)S(1)} %collective-permute-done.refs_1_, bf16[64,4096]{1,0:T(8,128)(2,1)S(1)} %collective-permute-done.1.refs_2_, bf16[64,4096]{1,0:T(8,128)(2,1)S(1)} %collective-permute-done.5.refs_3_, ...), custom_call_target="tpu_custom_call" | custom-call | flops 1 | bytes 1 | tf_op jit(solution)/shard_map/early/pallas_call | solution.py:296
  103.9 3.9 %collective-permute-done.7.refs_4_ = bf16[512,512]{1,0:T(8,128)(2,1)S(1)} collective-permute-done((bf16[512,512]{1,0:T(8,128)(2,1)S(1)}, bf16[512,512]{1,0:T(8,128)(2,1)S(1)}, u32[]{:S(2)}, u32[]{:S(2)}) %collective-permute-start.7) | collective-permute-done | bytes 524320 | tf_op jit(solution)/shard_map/ppermute | solution.py:486
  109.8 11.3 %attend.1 = (bf16[2,2,64,256]{3,2,1,0:T(8,128)(2,1)S(1)}, bf16[2,2,64,256]{3,2,1,0:T(8,128)(2,1)S(1)}, f32[4,2,64,1024]{3,2,1,0:T(8,128)S(1)}, bf16[2,64,1024]{2...) custom-call(s32[4]{0:T(128)S(1)} %copy-done.8, ...), custom_call_target="tpu_custom_call" | custom-call | flops 6000000000 | bytes 25165824 | tf_op jit(solution)/shard_map/attend/pallas_call | solution.py:415
  124.8 4.7 %collective-permute-done.18 = bf16[2,64,1024]{2,1,0:T(8,128)(2,1)S(1)} collective-permute-done((bf16[2,64,1024]{2,1,0:T(8,128)(2,1)S(1)}, bf16[2,64,1024]{2,1,0:T(8,128)(2,1)S(1)}, u32[]{:S(2)}, u32[]{:S(2)}) %collective-permute-start.18) | collective-permute-done | bytes 262176 | tf_op jit(solution)/shard_map/ppermute | solution.py:483
  130.1 4.0 %all-to-all-start = ((bf16[4,2,2,2,16,256]{5,4,1,3,2,0:T(8,128)(2,1)}), bf16[4,2,2,2,16,256]{5,4,1,3,2,0:T(8,128)(2,1)}, u32[]{:S(2)}, u32[]{:S(2)}) async-start(bf16[4,2,2,2,16,256]{5,4,1,3,2,0:T(8,128)(2,1)} %copy_bitcast_fusion), calls=%async_computation | async-start | bytes 524288 | tf_op jit(solution)/shard_map/all_to_all | solution.py:525
  145.2 3.1 %collective-permute-done.24 = bf16[2,64,1024]{2,1,0:T(8,128)(2,1)} collective-permute-done((bf16[2,64,1024]{2,1,0:T(8,128)(2,1)}, bf16[2,64,1024]{2,1,0:T(8,128)(2,1)}, u32[]{:S(2)}, u32[]{:S(2)}) %collective-permute-start.24) | collective-permute-done | bytes 262176 | tf_op jit(solution)/shard_map/ppermute | solution.py:480
  158.7 2.7 %collective-permute-done.22.near = bf16[2,2,64,1024]{3,2,1,0:T(8,128)(2,1)} collective-permute-done((bf16[2,2,64,1024]{3,2,1,0:T(8,128)(2,1)}, bf16[2,2,64,1024]{3,2,1,0:T(8,128)(2,1)}, u32[]{:S(2)}, u32[]{:S(2)}) %collective-permute-start.22) | collective-permute-done | bytes 524320 | tf_op jit(solution)/shard_map/ppermute | solution.py:483
  164.1 7.6 %collective-permute-done.29.far2 = bf16[2,64,1024]{2,1,0:T(8,128)(2,1)S(1)} collective-permute-done((bf16[2,64,1024]{2,1,0:T(8,128)(2,1)}, bf16[2,64,1024]{2,1,0:T(8,128)(2,1)S(1)}, u32[]{:S(2)}, u32[]{:S(2)}) %collective-permute-start.29) | collective-permute-done | bytes 262176 | tf_op jit(solution)/shard_map/ppermute | solution.py:480
  171.8 4.6 %collective-permute-done.28.near2 = bf16[2,64,1024]{2,1,0:T(8,128)(2,1)} collective-permute-done((bf16[2,64,1024]{2,1,0:T(8,128)(2,1)}, bf16[2,64,1024]{2,1,0:T(8,128)(2,1)}, u32[]{:S(2)}, u32[]{:S(2)}) %collective-permute-start.28) | collective-permute-done | bytes 262176 | tf_op jit(solution)/shard_map/ppermute | solution.py:480
  178.6 6.0 %collective-permute-done.31.far1 = bf16[2,64,1024]{2,1,0:T(8,128)(2,1)S(1)} collective-permute-done((bf16[2,64,1024]{2,1,0:T(8,128)(2,1)S(1)}, bf16[2,64,1024]{2,1,0:T(8,128)(2,1)S(1)}, u32[]{:S(2)}, u32[]{:S(2)}) %collective-permute-start.31) | collective-permute-done | bytes 262176 | tf_op jit(solution)/shard_map/ppermute | solution.py:480
  184.6 2.3 %final.1 = bf16[4,64,1024]{2,1,0:T(8,128)(2,1)} custom-call(f32[4,2,64,1024]{3,2,1,0:T(8,128)S(1)} %get-tuple-element.128.own, bf16[4,2,64,1024]{3,2,1,0:T(8,128)(2,1)S(1)} %collective-permute-done.19.core, bf16[2,2,64,1024]{3,2,1,0:T(8,128)(2,1)} %collective-permute-done.22.near, bf16[2,2,64,1024]{3,2,1,0:T(8,128)(2,1)} %collective-permute-done.27.far, ...), custom_call_target="tpu_custom_call" | custom-call | tf_op jit(solution)/shard_map/final/pallas_call | solution.py:454
  (81 shorter events, 53.4 us)
Async XLA Ops:
  1.7 27.4 %collective-permute-start.1 = (bf16[64,4096]{1,0:T(8,128)(2,1)S(1)}, bf16[64,4096]{1,0:T(8,128)(2,1)S(1)}, u32[]{:S(2)}, u32[]{:S(2)}) collective-permute-start(bf16[64,4096]{1,0:T(8,128)(2,1)S(1)} %dynamic-slice_bitcast_fusion), channel_id=1, source_target_pairs={{0,8},{4,12},{8,0},{12,4},{1,9},{5,13},{9,1},{13,5},{2,10},{6,14},... | collective-permute-start | bytes 1572872 | tf_op jit(solution)/shard_map/ppermute | solution.py:480
  5.8 23.5 %collective-permute-start = (bf16[64,4096]{1,0:T(8,128)(2,1)S(1)}, bf16[64,4096]{1,0:T(8,128)(2,1)S(1)}, u32[]{:S(2)}, u32[]{:S(2)}) collective-permute-start(bf16[64,4096]{1,0:T(8,128)(2,1)S(1)} %dynamic-slice_bitcast_fusion), channel_id=1, source_target_pairs={{0,4},{4,0},{8,12},{12,8},{1,5},{5,1},{9,13},{13,9},{2,6},{6,2},{1... | collective-permute-start | bytes 1572872 | tf_op jit(solution)/shard_map/ppermute | solution.py:480
  29.3 14.9 %collective-permute-start.2 = (bf16[64,4096]{1,0:T(8,128)(2,1)S(1)}, bf16[64,4096]{1,0:T(8,128)(2,1)S(1)}, u32[]{:S(2)}, u32[]{:S(2)}) collective-permute-start(bf16[64,4096]{1,0:T(8,128)(2,1)S(1)} %collective-permute-done.refs_1_), channel_id=1, source_target_pairs={{0,2},{1,3},{2,0},{3,1},{4,6},{5,7},{6,4},{7,5},{8,10},{9,11},{10,... | collective-permute-start | bytes 1572872 | tf_op jit(solution)/shard_map/ppermute | solution.py:483
  30.8 22.6 %collective-permute-start.3 = (bf16[64,4096]{1,0:T(8,128)(2,1)S(1)}, bf16[64,4096]{1,0:T(8,128)(2,1)S(1)}, u32[]{:S(2)}, u32[]{:S(2)}) collective-permute-start(bf16[64,4096]{1,0:T(8,128)(2,1)S(1)} %collective-permute-done.1.refs_2_), channel_id=1, source_target_pairs={{0,2},{1,3},{2,0},{3,1},{4,6},{5,7},{6,4},{7,5},{8,10},{9,11},{10,... | collective-permute-start | bytes 1572872 | tf_op jit(solution)/shard_map/ppermute | solution.py:483
  31.3 24.5 %collective-permute-start.8 = (bf16[512,512]{1,0:T(8,128)(2,1)S(1)}, bf16[512,512]{1,0:T(8,128)(2,1)S(1)}, u32[]{:S(2)}, u32[]{:S(2)}) collective-permute-start(bf16[512,512]{1,0:T(8,128)(2,1)S(1)} %get-tuple-element.88), channel_id=1, source_target_pairs={{0,8},{4,12},{8,0},{12,4},{1,9},{5,13},{9,1},{13,5},{2,10},{6,14},... | collective-permute-start | bytes 1572872 | tf_op jit(solution)/shard_map/ppermute | solution.py:480
  32.7 36.4 %collective-permute-start.10 = (bf16[512,512]{1,0:T(8,128)(2,1)S(1)}, bf16[512,512]{1,0:T(8,128)(2,1)S(1)}, u32[]{:S(2)}, u32[]{:S(2)}) collective-permute-start(bf16[512,512]{1,0:T(8,128)(2,1)S(1)} %get-tuple-element.94), channel_id=1, source_target_pairs={{0,4},{4,0},{8,12},{12,8},{1,5},{5,1},{9,13},{13,9},{2,6},{6,2},{1... | collective-permute-start | bytes 1572872 | tf_op jit(solution)/shard_map/ppermute | solution.py:480
  44.1 23.4 %collective-permute-start.5 = (bf16[64,4096]{1,0:T(8,128)(2,1)S(1)}, bf16[64,4096]{1,0:T(8,128)(2,1)S(1)}, u32[]{:S(2)}, u32[]{:S(2)}) collective-permute-start(bf16[64,4096]{1,0:T(8,128)(2,1)S(1)} %collective-permute-done.1.refs_2_), channel_id=1, source_target_pairs={{0,4},{4,0},{8,12},{12,8},{1,5},{5,1},{9,13},{13,9},{2,6},{6,2},{1... | collective-permute-start | bytes 1572872 | tf_op jit(solution)/shard_map/ppermute | solution.py:480
  55.8 13.2 %collective-permute-start.9 = (bf16[512,512]{1,0:T(8,128)(2,1)S(1)}, bf16[512,512]{1,0:T(8,128)(2,1)S(1)}, u32[]{:S(2)}, u32[]{:S(2)}) collective-permute-start(bf16[512,512]{1,0:T(8,128)(2,1)S(1)} %collective-permute-done.8.z2), channel_id=1, source_target_pairs={{0,16},{16,0},{1,17},{17,1},{2,18},{18,2},{3,19},{19,3},{4,20},{20... | collective-permute-start | bytes 1572872 | tf_op jit(solution)/shard_map/ppermute | solution.py:486
  57.1 29.6 %collective-permute-start.4 = (bf16[512,512]{1,0:T(8,128)(2,1)S(1)}, bf16[512,512]{1,0:T(8,128)(2,1)S(1)}, u32[]{:S(2)}, u32[]{:S(2)}) collective-permute-start(bf16[512,512]{1,0:T(8,128)(2,1)S(1)} %get-tuple-element.81), channel_id=1, source_target_pairs={{0,12},{4,8},{8,4},{12,0},{1,13},{5,9},{9,5},{13,1},{2,14},{6,10},... | collective-permute-start | bytes 1572872 | tf_op jit(solution)/shard_map/ppermute | solution.py:480
  67.6 19.1 %collective-permute-start.6 = (bf16[64,4096]{1,0:T(8,128)(2,1)S(1)}, bf16[64,4096]{1,0:T(8,128)(2,1)S(1)}, u32[]{:S(2)}, u32[]{:S(2)}) collective-permute-start(bf16[64,4096]{1,0:T(8,128)(2,1)S(1)} %collective-permute-done.5.refs_3_), channel_id=1, source_target_pairs={{0,2},{1,3},{2,0},{3,1},{4,6},{5,7},{6,4},{7,5},{8,10},{9,11},{10,... | collective-permute-start | bytes 1572872 | tf_op jit(solution)/shard_map/ppermute | solution.py:483
  69.1 23.7 %collective-permute-start.11 = (bf16[512,512]{1,0:T(8,128)(2,1)S(1)}, bf16[512,512]{1,0:T(8,128)(2,1)S(1)}, u32[]{:S(2)}, u32[]{:S(2)}) collective-permute-start(bf16[512,512]{1,0:T(8,128)(2,1)S(1)} %collective-permute-done.10.z1), channel_id=1, source_target_pairs={{0,16},{16,0},{1,17},{17,1},{2,18},{18,2},{3,19},{19,3},{4,20},{20... | collective-permute-start | bytes 1572872 | tf_op jit(solution)/shard_map/ppermute | solution.py:486
  70.6 16.1 %collective-permute-start.12 = (bf16[64,512]{1,0:T(8,128)(2,1)S(1)}, bf16[64,512]{1,0:T(8,128)(2,1)S(1)}, u32[]{:S(2)}, u32[]{:S(2)}) collective-permute-start(bf16[64,512]{1,0:T(8,128)(2,1)S(1)} %get-tuple-element.98), channel_id=1, source_target_pairs={{0,4},{4,0},{8,12},{12,8},{1,5},{5,1},{9,13},{13,9},{2,6},{6,2},{1... | collective-permute-start | bytes 196616 | tf_op jit(solution)/shard_map/ppermute | solution.py:480
  73.1 16.6 %collective-permute-start.13 = (bf16[64,512]{1,0:T(8,128)(2,1)S(1)}, bf16[64,512]{1,0:T(8,128)(2,1)S(1)}, u32[]{:S(2)}, u32[]{:S(2)}) collective-permute-start(bf16[64,512]{1,0:T(8,128)(2,1)S(1)} %get-tuple-element.99), channel_id=1, source_target_pairs={{0,8},{4,12},{8,0},{12,4},{1,9},{5,13},{9,1},{13,5},{2,10},{6,14},... | collective-permute-start | bytes 196616 | tf_op jit(solution)/shard_map/ppermute | solution.py:480
  93.5 14.3 %collective-permute-start.7 = (bf16[512,512]{1,0:T(8,128)(2,1)S(1)}, bf16[512,512]{1,0:T(8,128)(2,1)S(1)}, u32[]{:S(2)}, u32[]{:S(2)}) collective-permute-start(bf16[512,512]{1,0:T(8,128)(2,1)S(1)} %collective-permute-done.4.refs_3_), channel_id=1, source_target_pairs={{0,16},{16,0},{1,17},{17,1},{2,18},{18,2},{3,19},{19,3},{4,20},{20... | collective-permute-start | bytes 1572872 | tf_op jit(solution)/shard_map/ppermute | solution.py:486
  94.1 13.8 %collective-permute-start.16 = (bf16[512,512]{1,0:T(8,128)(2,1)S(1)}, bf16[512,512]{1,0:T(8,128)(2,1)S(1)}, u32[]{:S(2)}, u32[]{:S(2)}) collective-permute-start(bf16[512,512]{1,0:T(8,128)(2,1)S(1)} %collective-permute-done.4.refs_3_), channel_id=1, source_target_pairs={{0,1},{1,0},{2,3},{3,2},{4,5},{5,4},{6,7},{7,6},{8,9},{9,8},{10,11... | collective-permute-start | bytes 1572872 | tf_op jit(solution)/shard_map/ppermute | solution.py:483
  122.1 16.5 %collective-permute-start.23 = (bf16[2,64,1024]{2,1,0:T(8,128)(2,1)}, bf16[2,64,1024]{2,1,0:T(8,128)(2,1)}, u32[]{:S(2)}, u32[]{:S(2)}) collective-permute-start(bf16[2,64,1024]{2,1,0:T(8,128)(2,1)} %get-tuple-element.120), channel_id=1, source_target_pairs={{0,2},{1,3},{2,0},{3,1},{4,6},{5,7},{6,4},{7,5},{8,10},{9,11},{10,... | collective-permute-start | bytes 786440 | tf_op jit(solution)/shard_map/ppermute | solution.py:483
  130.1 15.0 %all-to-all-start = ((bf16[4,2,2,2,16,256]{5,4,1,3,2,0:T(8,128)(2,1)}), bf16[4,2,2,2,16,256]{5,4,1,3,2,0:T(8,128)(2,1)}, u32[]{:S(2)}, u32[]{:S(2)}) async-start(bf16[4,2,2,2,16,256]{5,4,1,3,2,0:T(8,128)(2,1)} %copy_bitcast_fusion), calls=%async_computation | async-start | bytes 524288 | tf_op jit(solution)/shard_map/all_to_all | solution.py:525
  140.2 13.5 %collective-permute-start.26 = (bf16[2,64,1024]{2,1,0:T(8,128)(2,1)}, bf16[2,64,1024]{2,1,0:T(8,128)(2,1)}, u32[]{:S(2)}, u32[]{:S(2)}) collective-permute-start(bf16[2,64,1024]{2,1,0:T(8,128)(2,1)} %fusion.5), channel_id=1, source_target_pairs={{0,4},{4,0},{8,12},{12,8},{1,5},{5,1},{9,13},{13,9},{2,6},{6,2},{1... | collective-permute-start | bytes 786440 | tf_op jit(solution)/shard_map/ppermute | solution.py:480
  140.6 13.1 %collective-permute-start.25 = (bf16[2,64,1024]{2,1,0:T(8,128)(2,1)}, bf16[2,64,1024]{2,1,0:T(8,128)(2,1)}, u32[]{:S(2)}, u32[]{:S(2)}) collective-permute-start(bf16[2,64,1024]{2,1,0:T(8,128)(2,1)} %get-tuple-element.129), channel_id=1, source_target_pairs={{0,2},{1,3},{2,0},{3,1},{4,6},{5,7},{6,4},{7,5},{8,10},{9,11},{10,... | collective-permute-start | bytes 786440 | tf_op jit(solution)/shard_map/ppermute | solution.py:483
  142.8 18.6 %collective-permute-start.22 = (bf16[2,2,64,1024]{3,2,1,0:T(8,128)(2,1)}, bf16[2,2,64,1024]{3,2,1,0:T(8,128)(2,1)}, u32[]{:S(2)}, u32[]{:S(2)}) collective-permute-start(bf16[2,2,64,1024]{3,2,1,0:T(8,128)(2,1)} %copy-done.7), channel_id=1, source_target_pairs={{0,2},{1,3},{2,0},{3,1},{4,6},{5,7},{6,4},{7,5},{8,10},{9,11},{10,... | collective-permute-start | bytes 1572872 | tf_op jit(solution)/shard_map/ppermute | solution.py:483
  143.4 32.9 %collective-permute-start.27 = (bf16[2,2,64,1024]{3,2,1,0:T(8,128)(2,1)}, bf16[2,2,64,1024]{3,2,1,0:T(8,128)(2,1)}, u32[]{:S(2)}, u32[]{:S(2)}) collective-permute-start(bf16[2,2,64,1024]{3,2,1,0:T(8,128)(2,1)} %copy-done.6), channel_id=1, source_target_pairs={{0,3},{1,2},{2,1},{3,0},{4,7},{5,6},{6,5},{7,4},{8,11},{9,10},{10,... | collective-permute-start | bytes 1572872 | tf_op jit(solution)/shard_map/ppermute | solution.py:483
  150.1 21.6 %collective-permute-start.29 = (bf16[2,64,1024]{2,1,0:T(8,128)(2,1)}, bf16[2,64,1024]{2,1,0:T(8,128)(2,1)S(1)}, u32[]{:S(2)}, u32[]{:S(2)}) collective-permute-start(bf16[2,64,1024]{2,1,0:T(8,128)(2,1)} %fusion.1), channel_id=1, source_target_pairs={{0,8},{4,12},{8,0},{12,4},{1,9},{5,13},{9,1},{13,5},{2,10},{6,14},... | collective-permute-start | bytes 786440 | tf_op jit(solution)/shard_map/ppermute | solution.py:480
  155.5 20.8 %collective-permute-start.28 = (bf16[2,64,1024]{2,1,0:T(8,128)(2,1)}, bf16[2,64,1024]{2,1,0:T(8,128)(2,1)}, u32[]{:S(2)}, u32[]{:S(2)}) collective-permute-start(bf16[2,64,1024]{2,1,0:T(8,128)(2,1)} %fusion.4), channel_id=1, source_target_pairs={{0,8},{4,12},{8,0},{12,4},{1,9},{5,13},{9,1},{13,5},{2,10},{6,14},... | collective-permute-start | bytes 786440 | tf_op jit(solution)/shard_map/ppermute | solution.py:480
  162.4 16.2 %collective-permute-start.30 = (bf16[2,64,1024]{2,1,0:T(8,128)(2,1)S(1)}, bf16[2,64,1024]{2,1,0:T(8,128)(2,1)S(1)}, u32[]{:S(2)}, u32[]{:S(2)}) collective-permute-start(bf16[2,64,1024]{2,1,0:T(8,128)(2,1)S(1)} %fusion.6), channel_id=1, source_target_pairs={{0,4},{4,0},{8,12},{12,8},{1,5},{5,1},{9,13},{13,9},{2,6},{6,2},{1... | collective-permute-start | bytes 786440 | tf_op jit(solution)/shard_map/ppermute | solution.py:480
  (20 other events, 106.2 us)

commit v13 on v11

--- a/solution.py
+++ b/solution.py
@@ -520,7 +520,8 @@
     other = flip(front[1], 1)
     back = jnp.stack([front[0], other]).reshape(2, 2, 2, SEQ, 16, 256).transpose(3, 0, 1, 2, 4, 5)
     b3, a3 = flip(b3, 3), flip(a3, 2)
-    b3, core, b2, a2, back = together(b3, from_core, b2, a2, back)
+    b3, b2, a2 = together(b3, b2, a2)
+    b3, core, back = together(b3, from_core, back)
     back = lax.all_to_all(back, "seq", split_axis=0, concat_axis=0, tiled=True)
     b2, a2 = flip(b2, 3), flip(a2, 2)
     far3, own = together(summed(core[3], b3), own)

time: 186 us -> 193 us (1.038)
  waiting for transfers between devices: 90.8 us -> 100 us
    ppermute x15, waiting for transfers between devices: 52.2 us -> 56.6 us  [along(): return lax.ppermute(value, 'seq', [(a, a ^ k) for a in range(SEQ)])]
    ppermute x14, waiting for transfers between devices: 34.3 us -> 38.1 us  [flip(): return lax.ppermute(value, 'head', [(a, a ^ bits) for a in range(4)])]
    unnamed x22 -> x20, local copies, waits for them, and re-layouts: 7.1 us -> 5.73 us
  transfers between devices with their start and end apart: 33 -> 33, of which waited for: 23 -> 22; matrix products, arithmetic and copies ran while one was open for 6% -> 6% of each run, Pallas kernels for 3% -> 3%
where the time goes in v13:
time: 193 us; the launch traced here: 192 us
  waiting for transfers between devices  100 us (52%)
  starting transfers between devices  52.3 us (27%)
  Pallas kernels  20.2 us (10%)
  other arithmetic  9.99 us (5%)
  local copies, waits for them, and re-layouts  8.49 us (4%)
    ppermute x15, waiting for transfers between devices, along(): return lax.ppermute(value, 'seq', [(a, a ^ k) for a in range(SEQ)])  56.6 us
    ppermute x14, waiting for transfers between devices, flip(): return lax.ppermute(value, 'head', [(a, a ^ bits) for a in range(4)])  38.1 us
    ppermute x15, starting transfers between devices, along(): return lax.ppermute(value, 'seq', [(a, a ^ k) for a in range(SEQ)])  35.2 us
    pallas_call x1, Pallas kernels, main_call(): pl.pallas_call(main_kernel, out_shape=[front, front, jax.ShapeDtypeStruct...  11.3 us
    ppermute x14, starting transfers between devices, flip(): return lax.ppermute(value, 'head', [(a, a ^ bits) for a in range(4)])  10.2 us
    convert_element_type x6, other arithmetic, summed(): return total.astype(BF)  9.17 us
    unnamed x20, local copies, waits for them, and re-layouts  5.73 us
    pallas_call x1, Pallas kernels, early_call(): pl.pallas_call(early_kernel, out_shape=[jax.ShapeDtypeStruct((2, 512, 512...  4.39 us
  transfers between devices with their start and end apart: 33, of which 22 were waited for; matrix products, arithmetic and copies ran while one was open for 6% of the time, Pallas kernels for 3%

profile of v13, /device:TPU:0, one launch (start us, length us, event | category | flops | bytes accessed | tf_op | source)
XLA Modules:
  0.0 192.0 jit_solution(16558553874490472349)
XLA Ops:
  1.7 4.1 %collective-permute-start.1 = (bf16[64,4096]{1,0:T(8,128)(2,1)S(1)}, bf16[64,4096]{1,0:T(8,128)(2,1)S(1)}, u32[]{:S(2)}, u32[]{:S(2)}) collective-permute-start(bf16[64,4096]{1,0:T(8,128)(2,1)S(1)} %dynamic-slice_bitcast_fusion), channel_id=1, source_target_pairs={{0,8},{4,12},{8,0},{12,4},{1,9},{5,13},{9,1},{13,5},{2,10},{6,14},... | collective-permute-start | bytes 1572872 | tf_op jit(solution)/shard_map/ppermute | solution.py:480
  14.6 14.4 %collective-permute-done.1.refs_2_ = bf16[64,4096]{1,0:T(8,128)(2,1)S(1)} collective-permute-done((bf16[64,4096]{1,0:T(8,128)(2,1)S(1)}, bf16[64,4096]{1,0:T(8,128)(2,1)S(1)}, u32[]{:S(2)}, u32[]{:S(2)}) %collective-permute-start.1) | collective-permute-done | bytes 524320 | tf_op jit(solution)/shard_map/ppermute | solution.py:480
  32.7 2.4 %collective-permute-start.5 = (bf16[64,4096]{1,0:T(8,128)(2,1)S(1)}, bf16[64,4096]{1,0:T(8,128)(2,1)S(1)}, u32[]{:S(2)}, u32[]{:S(2)}) collective-permute-start(bf16[64,4096]{1,0:T(8,128)(2,1)S(1)} %collective-permute-done.1.refs_2_), channel_id=1, source_target_pairs={{0,4},{4,0},{8,12},{12,8},{1,5},{5,1},{9,13},{13,9},{2,6},{6,2},{1... | collective-permute-start | bytes 1572872 | tf_op jit(solution)/shard_map/ppermute | solution.py:480
  35.1 9.0 %collective-permute-done.2.refs_4_ = bf16[64,4096]{1,0:T(8,128)(2,1)S(1)} collective-permute-done((bf16[64,4096]{1,0:T(8,128)(2,1)S(1)}, bf16[64,4096]{1,0:T(8,128)(2,1)S(1)}, u32[]{:S(2)}, u32[]{:S(2)}) %collective-permute-start.2) | collective-permute-done | bytes 524320 | tf_op jit(solution)/shard_map/ppermute | solution.py:483
  44.1 9.2 %collective-permute-done.3.refs_5_ = bf16[64,4096]{1,0:T(8,128)(2,1)S(1)} collective-permute-done((bf16[64,4096]{1,0:T(8,128)(2,1)S(1)}, bf16[64,4096]{1,0:T(8,128)(2,1)S(1)}, u32[]{:S(2)}, u32[]{:S(2)}) %collective-permute-start.3) | collective-permute-done | bytes 524320 | tf_op jit(solution)/shard_map/ppermute | solution.py:483
  53.4 2.5 %collective-permute-done.8.z2 = bf16[512,512]{1,0:T(8,128)(2,1)S(1)} collective-permute-done((bf16[512,512]{1,0:T(8,128)(2,1)S(1)}, bf16[512,512]{1,0:T(8,128)(2,1)S(1)}, u32[]{:S(2)}, u32[]{:S(2)}) %collective-permute-start.8) | collective-permute-done | bytes 524320 | tf_op jit(solution)/shard_map/ppermute | solution.py:480
  58.7 3.9 %collective-permute-start.4 = (bf16[512,512]{1,0:T(8,128)(2,1)S(1)}, bf16[512,512]{1,0:T(8,128)(2,1)S(1)}, u32[]{:S(2)}, u32[]{:S(2)}) collective-permute-start(bf16[512,512]{1,0:T(8,128)(2,1)S(1)} %get-tuple-element.79), channel_id=1, source_target_pairs={{0,12},{4,8},{8,4},{12,0},{1,13},{5,9},{9,5},{13,1},{2,14},{6,10},... | collective-permute-start | bytes 1572872 | tf_op jit(solution)/shard_map/ppermute | solution.py:480
  62.6 4.9 %collective-permute-done.10.z1 = bf16[512,512]{1,0:T(8,128)(2,1)S(1)} collective-permute-done((bf16[512,512]{1,0:T(8,128)(2,1)S(1)}, bf16[512,512]{1,0:T(8,128)(2,1)S(1)}, u32[]{:S(2)}, u32[]{:S(2)}) %collective-permute-start.10) | collective-permute-done | bytes 524320 | tf_op jit(solution)/shard_map/ppermute | solution.py:480
  69.1 2.5 %collective-permute-start.12 = (bf16[64,512]{1,0:T(8,128)(2,1)S(1)}, bf16[64,512]{1,0:T(8,128)(2,1)S(1)}, u32[]{:S(2)}, u32[]{:S(2)}) collective-permute-start(bf16[64,512]{1,0:T(8,128)(2,1)S(1)} %get-tuple-element.95), channel_id=1, source_target_pairs={{0,4},{4,0},{8,12},{12,8},{1,5},{5,1},{9,13},{13,9},{2,6},{6,2},{1... | collective-permute-start | bytes 196616 | tf_op jit(solution)/shard_map/ppermute | solution.py:480
  71.6 14.2 %collective-permute-start.13 = (bf16[64,512]{1,0:T(8,128)(2,1)S(1)}, bf16[64,512]{1,0:T(8,128)(2,1)S(1)}, u32[]{:S(2)}, u32[]{:S(2)}) collective-permute-start(bf16[64,512]{1,0:T(8,128)(2,1)S(1)} %get-tuple-element.96), channel_id=1, source_target_pairs={{0,8},{4,12},{8,0},{12,4},{1,9},{5,13},{9,1},{13,5},{2,10},{6,14},... | collective-permute-start | bytes 196616 | tf_op jit(solution)/shard_map/ppermute | solution.py:480
  85.8 2.9 %collective-permute-done.13.q2 = bf16[64,512]{1,0:T(8,128)(2,1)S(1)} collective-permute-done((bf16[64,512]{1,0:T(8,128)(2,1)S(1)}, bf16[64,512]{1,0:T(8,128)(2,1)S(1)}, u32[]{:S(2)}, u32[]{:S(2)}) %collective-permute-start.13) | collective-permute-done | bytes 65568 | tf_op jit(solution)/shard_map/ppermute | solution.py:480
  88.7 3.1 %collective-permute-done.14.q3 = bf16[64,512]{1,0:T(8,128)(2,1)S(1)} collective-permute-done((bf16[64,512]{1,0:T(8,128)(2,1)S(1)}, bf16[64,512]{1,0:T(8,128)(2,1)S(1)}, u32[]{:S(2)}, u32[]{:S(2)}) %collective-permute-start.14) | collective-permute-done | bytes 65568 | tf_op jit(solution)/shard_map/ppermute | solution.py:480
  93.3 5.3 %collective-permute-done.15.refs_8_.refs_5_ = bf16[3328,512]{1,0:T(8,128)(2,1)S(1)} collective-permute-done((bf16[3328,512]{1,0:T(8,128)(2,1)S(1)}, bf16[3328,512]{1,0:T(8,128)(2,1)S(1)}, u32[]{:S(2)}, u32[]{:S(2)}) %collective-permute-start.15) | collective-permute-done | bytes 3407904 | tf_op jit(solution)/shard_map/ppermute | solution.py:483
  98.6 4.4 %early.1 = (f32[2,512,512]{2,1,0:T(8,128)S(1)}, bf16[512,1024]{1,0:T(8,128)(2,1)S(1)}) custom-call(bf16[4,64,4096]{2,1,0:T(8,128)(2,1)S(1)} %copy-done, bf16[64,4096]{1,0:T(8,128)(2,1)S(1)} %collective-permute-done.refs_1_, bf16[64,4096]{1,0:T(8,128)(2,1)S(1)} %collective-permute-done.1.refs_2_, bf16[64,4096]{1,0:T(8,128)(2,1)S(1)} %collective-permute-done.5.refs_3_, ...), custom_call_target="tpu_custom_call" | custom-call | flops 1 | bytes 1 | tf_op jit(solution)/shard_map/early/pallas_call | solution.py:296
  103.0 3.9 %collective-permute-done.7.refs_4_ = bf16[512,512]{1,0:T(8,128)(2,1)S(1)} collective-permute-done((bf16[512,512]{1,0:T(8,128)(2,1)S(1)}, bf16[512,512]{1,0:T(8,128)(2,1)S(1)}, u32[]{:S(2)}, u32[]{:S(2)}) %collective-permute-start.7) | collective-permute-done | bytes 524320 | tf_op jit(solution)/shard_map/ppermute | solution.py:486
  108.8 11.3 %attend.1 = (bf16[2,2,64,256]{3,2,1,0:T(8,128)(2,1)S(1)}, bf16[2,2,64,256]{3,2,1,0:T(8,128)(2,1)S(1)}, f32[4,2,64,1024]{3,2,1,0:T(8,128)S(1)}, bf16[2,64,1024]{2...) custom-call(s32[4]{0:T(128)S(1)} %copy-done.8, ...), custom_call_target="tpu_custom_call" | custom-call | flops 6000000000 | bytes 25165824 | tf_op jit(solution)/shard_map/attend/pallas_call | solution.py:415
  124.0 4.5 %collective-permute-done.18 = bf16[2,64,1024]{2,1,0:T(8,128)(2,1)S(1)} collective-permute-done((bf16[2,64,1024]{2,1,0:T(8,128)(2,1)S(1)}, bf16[2,64,1024]{2,1,0:T(8,128)(2,1)S(1)}, u32[]{:S(2)}, u32[]{:S(2)}) %collective-permute-start.18) | collective-permute-done | bytes 262176 | tf_op jit(solution)/shard_map/ppermute | solution.py:483
  130.9 4.0 %all-to-all-start = ((bf16[4,2,2,2,16,256]{5,4,1,3,2,0:T(8,128)(2,1)}), bf16[4,2,2,2,16,256]{5,4,1,3,2,0:T(8,128)(2,1)}, u32[]{:S(2)}, u32[]{:S(2)}) async-start(bf16[4,2,2,2,16,256]{5,4,1,3,2,0:T(8,128)(2,1)} %copy_bitcast_fusion), calls=%async_computation | async-start | bytes 524288 | tf_op jit(solution)/shard_map/all_to_all | solution.py:525
  143.4 4.9 %collective-permute-done.24 = bf16[2,64,1024]{2,1,0:T(8,128)(2,1)} collective-permute-done((bf16[2,64,1024]{2,1,0:T(8,128)(2,1)}, bf16[2,64,1024]{2,1,0:T(8,128)(2,1)}, u32[]{:S(2)}, u32[]{:S(2)}) %collective-permute-start.24) | collective-permute-done | bytes 262176 | tf_op jit(solution)/shard_map/ppermute | solution.py:480
  150.2 3.3 %collective-permute-done.26 = bf16[2,64,1024]{2,1,0:T(8,128)(2,1)} collective-permute-done((bf16[2,64,1024]{2,1,0:T(8,128)(2,1)}, bf16[2,64,1024]{2,1,0:T(8,128)(2,1)}, u32[]{:S(2)}, u32[]{:S(2)}) %collective-permute-start.26) | collective-permute-done | bytes 262176 | tf_op jit(solution)/shard_map/ppermute | solution.py:480
  160.4 7.5 %collective-permute-done.27.far = bf16[2,2,64,1024]{3,2,1,0:T(8,128)(2,1)} collective-permute-done((bf16[2,2,64,1024]{3,2,1,0:T(8,128)(2,1)}, bf16[2,2,64,1024]{3,2,1,0:T(8,128)(2,1)}, u32[]{:S(2)}, u32[]{:S(2)}) %collective-permute-start.27) | collective-permute-done | bytes 524320 | tf_op jit(solution)/shard_map/ppermute | solution.py:483
  167.9 6.8 %collective-permute-done.28.near2 = bf16[2,64,1024]{2,1,0:T(8,128)(2,1)S(1)} collective-permute-done((bf16[2,64,1024]{2,1,0:T(8,128)(2,1)}, bf16[2,64,1024]{2,1,0:T(8,128)(2,1)S(1)}, u32[]{:S(2)}, u32[]{:S(2)}) %collective-permute-start.28) | collective-permute-done | bytes 262176 | tf_op jit(solution)/shard_map/ppermute | solution.py:480
  174.7 5.6 %collective-permute-done.29.far2 = bf16[2,64,1024]{2,1,0:T(8,128)(2,1)} collective-permute-done((bf16[2,64,1024]{2,1,0:T(8,128)(2,1)}, bf16[2,64,1024]{2,1,0:T(8,128)(2,1)}, u32[]{:S(2)}, u32[]{:S(2)}) %collective-permute-start.29) | collective-permute-done | bytes 262176 | tf_op jit(solution)/shard_map/ppermute | solution.py:480
  182.2 7.4 %collective-permute-done.31.far1 = bf16[2,64,1024]{2,1,0:T(8,128)(2,1)S(1)} collective-permute-done((bf16[2,64,1024]{2,1,0:T(8,128)(2,1)S(1)}, bf16[2,64,1024]{2,1,0:T(8,128)(2,1)S(1)}, u32[]{:S(2)}, u32[]{:S(2)}) %collective-permute-start.31) | collective-permute-done | bytes 262176 | tf_op jit(solution)/shard_map/ppermute | solution.py:480
  (79 shorter events, 48.9 us)
Async XLA Ops:
  1.7 27.4 %collective-permute-start.1 = (bf16[64,4096]{1,0:T(8,128)(2,1)S(1)}, bf16[64,4096]{1,0:T(8,128)(2,1)S(1)}, u32[]{:S(2)}, u32[]{:S(2)}) collective-permute-start(bf16[64,4096]{1,0:T(8,128)(2,1)S(1)} %dynamic-slice_bitcast_fusion), channel_id=1, source_target_pairs={{0,8},{4,12},{8,0},{12,4},{1,9},{5,13},{9,1},{13,5},{2,10},{6,14},... | collective-permute-start | bytes 1572872 | tf_op jit(solution)/shard_map/ppermute | solution.py:480
  5.8 23.5 %collective-permute-start = (bf16[64,4096]{1,0:T(8,128)(2,1)S(1)}, bf16[64,4096]{1,0:T(8,128)(2,1)S(1)}, u32[]{:S(2)}, u32[]{:S(2)}) collective-permute-start(bf16[64,4096]{1,0:T(8,128)(2,1)S(1)} %dynamic-slice_bitcast_fusion), channel_id=1, source_target_pairs={{0,4},{4,0},{8,12},{12,8},{1,5},{5,1},{9,13},{13,9},{2,6},{6,2},{1... | collective-permute-start | bytes 1572872 | tf_op jit(solution)/shard_map/ppermute | solution.py:480
  29.3 14.9 %collective-permute-start.2 = (bf16[64,4096]{1,0:T(8,128)(2,1)S(1)}, bf16[64,4096]{1,0:T(8,128)(2,1)S(1)}, u32[]{:S(2)}, u32[]{:S(2)}) collective-permute-start(bf16[64,4096]{1,0:T(8,128)(2,1)S(1)} %collective-permute-done.refs_1_), channel_id=1, source_target_pairs={{0,2},{1,3},{2,0},{3,1},{4,6},{5,7},{6,4},{7,5},{8,10},{9,11},{10,... | collective-permute-start | bytes 1572872 | tf_op jit(solution)/shard_map/ppermute | solution.py:483
  30.8 22.6 %collective-permute-start.3 = (bf16[64,4096]{1,0:T(8,128)(2,1)S(1)}, bf16[64,4096]{1,0:T(8,128)(2,1)S(1)}, u32[]{:S(2)}, u32[]{:S(2)}) collective-permute-start(bf16[64,4096]{1,0:T(8,128)(2,1)S(1)} %collective-permute-done.1.refs_2_), channel_id=1, source_target_pairs={{0,2},{1,3},{2,0},{3,1},{4,6},{5,7},{6,4},{7,5},{8,10},{9,11},{10,... | collective-permute-start | bytes 1572872 | tf_op jit(solution)/shard_map/ppermute | solution.py:483
  31.3 24.5 %collective-permute-start.8 = (bf16[512,512]{1,0:T(8,128)(2,1)S(1)}, bf16[512,512]{1,0:T(8,128)(2,1)S(1)}, u32[]{:S(2)}, u32[]{:S(2)}) collective-permute-start(bf16[512,512]{1,0:T(8,128)(2,1)S(1)} %get-tuple-element.85), channel_id=1, source_target_pairs={{0,8},{4,12},{8,0},{12,4},{1,9},{5,13},{9,1},{13,5},{2,10},{6,14},... | collective-permute-start | bytes 1572872 | tf_op jit(solution)/shard_map/ppermute | solution.py:480
  32.7 24.8 %collective-permute-start.5 = (bf16[64,4096]{1,0:T(8,128)(2,1)S(1)}, bf16[64,4096]{1,0:T(8,128)(2,1)S(1)}, u32[]{:S(2)}, u32[]{:S(2)}) collective-permute-start(bf16[64,4096]{1,0:T(8,128)(2,1)S(1)} %collective-permute-done.1.refs_2_), channel_id=1, source_target_pairs={{0,4},{4,0},{8,12},{12,8},{1,5},{5,1},{9,13},{13,9},{2,6},{6,2},{1... | collective-permute-start | bytes 1572872 | tf_op jit(solution)/shard_map/ppermute | solution.py:480
  35.1 32.5 %collective-permute-start.10 = (bf16[512,512]{1,0:T(8,128)(2,1)S(1)}, bf16[512,512]{1,0:T(8,128)(2,1)S(1)}, u32[]{:S(2)}, u32[]{:S(2)}) collective-permute-start(bf16[512,512]{1,0:T(8,128)(2,1)S(1)} %get-tuple-element.91), channel_id=1, source_target_pairs={{0,4},{4,0},{8,12},{12,8},{1,5},{5,1},{9,13},{13,9},{2,6},{6,2},{1... | collective-permute-start | bytes 1572872 | tf_op jit(solution)/shard_map/ppermute | solution.py:480
  55.8 12.1 %collective-permute-start.9 = (bf16[512,512]{1,0:T(8,128)(2,1)S(1)}, bf16[512,512]{1,0:T(8,128)(2,1)S(1)}, u32[]{:S(2)}, u32[]{:S(2)}) collective-permute-start(bf16[512,512]{1,0:T(8,128)(2,1)S(1)} %collective-permute-done.8.z2), channel_id=1, source_target_pairs={{0,16},{16,0},{1,17},{17,1},{2,18},{18,2},{3,19},{19,3},{4,20},{20... | collective-permute-start | bytes 1572872 | tf_op jit(solution)/shard_map/ppermute | solution.py:486
  57.5 28.2 %collective-permute-start.6 = (bf16[64,4096]{1,0:T(8,128)(2,1)S(1)}, bf16[64,4096]{1,0:T(8,128)(2,1)S(1)}, u32[]{:S(2)}, u32[]{:S(2)}) collective-permute-start(bf16[64,4096]{1,0:T(8,128)(2,1)S(1)} %collective-permute-done.5.refs_3_), channel_id=1, source_target_pairs={{0,2},{1,3},{2,0},{3,1},{4,6},{5,7},{6,4},{7,5},{8,10},{9,11},{10,... | collective-permute-start | bytes 1572872 | tf_op jit(solution)/shard_map/ppermute | solution.py:483
  58.7 27.0 %collective-permute-start.4 = (bf16[512,512]{1,0:T(8,128)(2,1)S(1)}, bf16[512,512]{1,0:T(8,128)(2,1)S(1)}, u32[]{:S(2)}, u32[]{:S(2)}) collective-permute-start(bf16[512,512]{1,0:T(8,128)(2,1)S(1)} %get-tuple-element.79), channel_id=1, source_target_pairs={{0,12},{4,8},{8,4},{12,0},{1,13},{5,9},{9,5},{13,1},{2,14},{6,10},... | collective-permute-start | bytes 1572872 | tf_op jit(solution)/shard_map/ppermute | solution.py:480
  68.0 23.8 %collective-permute-start.11 = (bf16[512,512]{1,0:T(8,128)(2,1)S(1)}, bf16[512,512]{1,0:T(8,128)(2,1)S(1)}, u32[]{:S(2)}, u32[]{:S(2)}) collective-permute-start(bf16[512,512]{1,0:T(8,128)(2,1)S(1)} %collective-permute-done.10.z1), channel_id=1, source_target_pairs={{0,16},{16,0},{1,17},{17,1},{2,18},{18,2},{3,19},{19,3},{4,20},{20... | collective-permute-start | bytes 1572872 | tf_op jit(solution)/shard_map/ppermute | solution.py:486
  69.1 16.7 %collective-permute-start.12 = (bf16[64,512]{1,0:T(8,128)(2,1)S(1)}, bf16[64,512]{1,0:T(8,128)(2,1)S(1)}, u32[]{:S(2)}, u32[]{:S(2)}) collective-permute-start(bf16[64,512]{1,0:T(8,128)(2,1)S(1)} %get-tuple-element.95), channel_id=1, source_target_pairs={{0,4},{4,0},{8,12},{12,8},{1,5},{5,1},{9,13},{13,9},{2,6},{6,2},{1... | collective-permute-start | bytes 196616 | tf_op jit(solution)/shard_map/ppermute | solution.py:480
  71.6 17.1 %collective-permute-start.13 = (bf16[64,512]{1,0:T(8,128)(2,1)S(1)}, bf16[64,512]{1,0:T(8,128)(2,1)S(1)}, u32[]{:S(2)}, u32[]{:S(2)}) collective-permute-start(bf16[64,512]{1,0:T(8,128)(2,1)S(1)} %get-tuple-element.96), channel_id=1, source_target_pairs={{0,8},{4,12},{8,0},{12,4},{1,9},{5,13},{9,1},{13,5},{2,10},{6,14},... | collective-permute-start | bytes 196616 | tf_op jit(solution)/shard_map/ppermute | solution.py:480
  92.6 14.3 %collective-permute-start.7 = (bf16[512,512]{1,0:T(8,128)(2,1)S(1)}, bf16[512,512]{1,0:T(8,128)(2,1)S(1)}, u32[]{:S(2)}, u32[]{:S(2)}) collective-permute-start(bf16[512,512]{1,0:T(8,128)(2,1)S(1)} %collective-permute-done.4.refs_3_), channel_id=1, source_target_pairs={{0,16},{16,0},{1,17},{17,1},{2,18},{18,2},{3,19},{19,3},{4,20},{20... | collective-permute-start | bytes 1572872 | tf_op jit(solution)/shard_map/ppermute | solution.py:486
  93.1 13.8 %collective-permute-start.16 = (bf16[512,512]{1,0:T(8,128)(2,1)S(1)}, bf16[512,512]{1,0:T(8,128)(2,1)S(1)}, u32[]{:S(2)}, u32[]{:S(2)}) collective-permute-start(bf16[512,512]{1,0:T(8,128)(2,1)S(1)} %collective-permute-done.4.refs_3_), channel_id=1, source_target_pairs={{0,1},{1,0},{2,3},{3,2},{4,5},{5,4},{6,7},{7,6},{8,9},{9,8},{10,11... | collective-permute-start | bytes 1572872 | tf_op jit(solution)/shard_map/ppermute | solution.py:483
  122.1 16.6 %collective-permute-start.23 = (bf16[2,64,1024]{2,1,0:T(8,128)(2,1)}, bf16[2,64,1024]{2,1,0:T(8,128)(2,1)}, u32[]{:S(2)}, u32[]{:S(2)}) collective-permute-start(bf16[2,64,1024]{2,1,0:T(8,128)(2,1)} %get-tuple-element.118), channel_id=1, source_target_pairs={{0,2},{1,3},{2,0},{3,1},{4,6},{5,7},{6,4},{7,5},{8,10},{9,11},{10,... | collective-permute-start | bytes 786440 | tf_op jit(solution)/shard_map/ppermute | solution.py:483
  130.4 19.8 %collective-permute-start.25 = (bf16[2,64,1024]{2,1,0:T(8,128)(2,1)S(1)}, bf16[2,64,1024]{2,1,0:T(8,128)(2,1)}, u32[]{:S(2)}, u32[]{:S(2)}) collective-permute-start(bf16[2,64,1024]{2,1,0:T(8,128)(2,1)S(1)} %get-tuple-element.127), channel_id=1, source_target_pairs={{0,2},{1,3},{2,0},{3,1},{4,6},{5,7},{6,4},{7,5},{8,10},{9,11},{10,... | collective-permute-start | bytes 786440 | tf_op jit(solution)/shard_map/ppermute | solution.py:483
  130.9 12.5 %all-to-all-start = ((bf16[4,2,2,2,16,256]{5,4,1,3,2,0:T(8,128)(2,1)}), bf16[4,2,2,2,16,256]{5,4,1,3,2,0:T(8,128)(2,1)}, u32[]{:S(2)}, u32[]{:S(2)}) async-start(bf16[4,2,2,2,16,256]{5,4,1,3,2,0:T(8,128)(2,1)} %copy_bitcast_fusion), calls=%async_computation | async-start | bytes 524288 | tf_op jit(solution)/shard_map/all_to_all | solution.py:525
  140.4 13.2 %collective-permute-start.26 = (bf16[2,64,1024]{2,1,0:T(8,128)(2,1)}, bf16[2,64,1024]{2,1,0:T(8,128)(2,1)}, u32[]{:S(2)}, u32[]{:S(2)}) collective-permute-start(bf16[2,64,1024]{2,1,0:T(8,128)(2,1)} %fusion.5), channel_id=1, source_target_pairs={{0,4},{4,0},{8,12},{12,8},{1,5},{5,1},{9,13},{13,9},{2,6},{6,2},{1... | collective-permute-start | bytes 786440 | tf_op jit(solution)/shard_map/ppermute | solution.py:480
  140.4 18.9 %collective-permute-start.20 = (bf16[2,2,64,1024]{3,2,1,0:T(8,128)(2,1)}, bf16[2,2,64,1024]{3,2,1,0:T(8,128)(2,1)}, u32[]{:S(2)}, u32[]{:S(2)}) collective-permute-start(bf16[2,2,64,1024]{3,2,1,0:T(8,128)(2,1)} %copy-done.7), channel_id=1, source_target_pairs={{0,2},{1,3},{2,0},{3,1},{4,6},{5,7},{6,4},{7,5},{8,10},{9,11},{10,... | collective-permute-start | bytes 1572872 | tf_op jit(solution)/shard_map/ppermute | solution.py:483
  141.9 26.0 %collective-permute-start.27 = (bf16[2,2,64,1024]{3,2,1,0:T(8,128)(2,1)}, bf16[2,2,64,1024]{3,2,1,0:T(8,128)(2,1)}, u32[]{:S(2)}, u32[]{:S(2)}) collective-permute-start(bf16[2,2,64,1024]{3,2,1,0:T(8,128)(2,1)} %copy-done.6), channel_id=1, source_target_pairs={{0,3},{1,2},{2,1},{3,0},{4,7},{5,6},{6,5},{7,4},{8,11},{9,10},{10,... | collective-permute-start | bytes 1572872 | tf_op jit(solution)/shard_map/ppermute | solution.py:483
  155.4 19.3 %collective-permute-start.28 = (bf16[2,64,1024]{2,1,0:T(8,128)(2,1)}, bf16[2,64,1024]{2,1,0:T(8,128)(2,1)S(1)}, u32[]{:S(2)}, u32[]{:S(2)}) collective-permute-start(bf16[2,64,1024]{2,1,0:T(8,128)(2,1)} %fusion.4), channel_id=1, source_target_pairs={{0,8},{4,12},{8,0},{12,4},{1,9},{5,13},{9,1},{13,5},{2,10},{6,14},... | collective-permute-start | bytes 786440 | tf_op jit(solution)/shard_map/ppermute | solution.py:480
  157.2 23.2 %collective-permute-start.29 = (bf16[2,64,1024]{2,1,0:T(8,128)(2,1)}, bf16[2,64,1024]{2,1,0:T(8,128)(2,1)}, u32[]{:S(2)}, u32[]{:S(2)}) collective-permute-start(bf16[2,64,1024]{2,1,0:T(8,128)(2,1)} %fusion.1), channel_id=1, source_target_pairs={{0,8},{4,12},{8,0},{12,4},{1,9},{5,13},{9,1},{13,5},{2,10},{6,14},... | collective-permute-start | bytes 786440 | tf_op jit(solution)/shard_map/ppermute | solution.py:480
  160.3 21.9 %collective-permute-start.30 = (bf16[2,64,1024]{2,1,0:T(8,128)(2,1)S(1)}, bf16[2,64,1024]{2,1,0:T(8,128)(2,1)S(1)}, u32[]{:S(2)}, u32[]{:S(2)}) collective-permute-start(bf16[2,64,1024]{2,1,0:T(8,128)(2,1)S(1)} %fusion.6), channel_id=1, source_target_pairs={{0,4},{4,0},{8,12},{12,8},{1,5},{5,1},{9,13},{13,9},{2,6},{6,2},{1... | collective-permute-start | bytes 786440 | tf_op jit(solution)/shard_map/ppermute | solution.py:480
  (19 other events, 118.5 us)
